TPU v7x, 256 devices: a whole 4x4x8 slice. The times are simulated.
256 devices in a mesh: brick: 64 (over y, z, core), mp: 4 (over x).
Axes of the slice: x: 4, y: 4, z: 8, core: 2. Of those that a mesh axis runs over, the one named last changes fastest.
Arguments:
- voxel_feats: bfloat16 [196608, 512], P('brick'), may hold values from -6 to 6
- slot_rank: int32 [196608], P('brick'), may hold values from 0 to 131072, as said below
- curve_order: int32 [131072], P('brick'), may hold values from 0 to 196607, as said below
- patch_shift: int32 [1], replicated, may hold values from 1 to 1023
- qkv_weight: bfloat16 [512, 1536], P(None, 'mp')
- proj_weight: bfloat16 [512, 512], P('mp'), may hold values from -0.25 to 0.25
- up_weight: bfloat16 [512, 2048], P(None, 'mp'), may hold values from -0.25 to 0.25
- down_weight: bfloat16 [2048, 512], P('mp'), may hold values from -0.125 to 0.125
- norm_gains: float32 [2, 512], replicated, may hold values from 0.25 to 1.75
Outputs:
- voxel_out: bfloat16 [196608, 512], P('brick', 'mp')
Inputs may be any that keep to these rules, and one draw needn't show every extreme that they name: `slot_rank`: within each brick's 3072 slots the occupied ones come first and hold distinct curve positions in increasing order; the rest hold 131072. Every curve position lies in exactly one slot. Curve shard k is positions k * 2048 to (k + 1) * 2048 - 1 and draws its voxels only from bricks k - 1, k, k + 1 and k + 2 (mod 64). A brick holds at most 768 voxels of one shard, and some brick holds exactly 768 of some shard; some brick has all 3072 slots occupied. curve_order[p] = brick * 3072 + slot of the voxel at curve position p, the inverse of slot_rank on occupied slots.
All inputs are finite; a program needn't handle non-finite values.
Results may differ from a plain program's by a relative error of at most 0.012.
The roundings to bfloat16 on the way count: a program that leaves them out, or rounds other values in their place, can miss the bound.
Values may be sent and summed in bfloat16 or wider, within the bound.
No kernel may reach another device: no remote copies, remote signals or barrier semaphores. Data moves between devices by JAX's collectives and lax.ppermute only.
A program may use at most 128 MiB of HBM per device.

v0:
```python
import math

import jax
import jax.numpy as jnp
from jax import lax
from jax.sharding import PartitionSpec as P

HEADS = 32
PATCH = 1024


EPSILON = 1e-05


def shifted(value, axis, steps):
    count = lax.axis_size(axis)
    pairs = [(source, (source + steps) % count) for source in range(count)]
    return lax.ppermute(value, axis, pairs)


def cut_along(value, dim, devices):
    shape = value.shape
    blocks = value.reshape(*shape[:dim], devices, shape[dim] // devices, *shape[dim + 1 :])
    return jnp.moveaxis(blocks, dim, 0)


def summed_on_arrival(value, axis, dim):
    blocks = cut_along(value, dim, lax.axis_size(axis))
    arrived = lax.all_to_all(blocks, axis, split_axis=0, concat_axis=0, tiled=True)
    return arrived.astype(jnp.float32).sum(axis=0)


def layer_norm(values, gain):
    values = values.astype(jnp.float32)
    centred = values - jnp.mean(values, axis=-1, keepdims=True)
    spread = jnp.mean(centred * centred, axis=-1, keepdims=True)
    return (centred * lax.rsqrt(spread + EPSILON) * gain).astype(jnp.bfloat16)


def patch_attention(qkv_rows, heads_here, patch_len):
    row_count = qkv_rows.shape[0]
    head_dim = qkv_rows.shape[1] // (3 * heads_here)
    group_size = math.gcd(heads_here, 4)
    group_count = heads_here // group_size
    scale = head_dim ** (-0.5)

    def one_group(piece):
        scores = (
            jnp.einsum(
                "qhd,khd->hqk", piece[:, :, 0], piece[:, :, 1], preferred_element_type=jnp.float32
            )
            * scale
        )
        highest = jnp.max(scores, axis=-1, keepdims=True)
        weights_exp = jnp.exp(scores - highest)
        softmax_weights = (weights_exp / jnp.sum(weights_exp, axis=-1, keepdims=True)).astype(
            jnp.bfloat16
        )
        return jnp.einsum(
            "hqk,khd->qhd", softmax_weights, piece[:, :, 2], preferred_element_type=jnp.float32
        ).astype(jnp.bfloat16)

    def one_patch(block):
        pieces = jnp.moveaxis(block.reshape(patch_len, group_count, group_size, 3, head_dim), 1, 0)
        outputs = lax.map(one_group, pieces)
        return jnp.moveaxis(outputs, 0, 1).reshape(patch_len, heads_here * head_dim)

    blocks = qkv_rows.reshape(row_count // patch_len, patch_len, qkv_rows.shape[1])
    return lax.map(one_patch, blocks).reshape(row_count, heads_here * head_dim)


def per_device(
    voxel_feats,
    slot_rank,
    curve_order,
    patch_shift,
    qkv_weight,
    proj_weight,
    up_weight,
    down_weight,
    norm_gains,
):
    bricks = lax.axis_size("brick")
    model_parts = lax.axis_size("mp")
    my_index = lax.axis_index("brick")
    capacity = voxel_feats.shape[0]
    shard_rows = curve_order.shape[0]
    all_rows = shard_rows * bricks
    pair_rows = 3 * (shard_rows // 8)
    offset = patch_shift[0]
    brick_ids = jnp.arange(bricks, dtype=jnp.int32)
    lane_ids = jnp.arange(4, dtype=jnp.int32)
    live_slots = slot_rank < all_rows
    dest_shard = slot_rank // shard_rows
    run_starts = jnp.sum(
        (slot_rank[:, None] < (brick_ids * shard_rows)[None, :]).astype(jnp.int32), axis=0
    )
    live_count = jnp.sum(live_slots.astype(jnp.int32))
    run_stops = jnp.concatenate([run_starts[1:], live_count[None]])
    source_brick = curve_order // capacity
    source_slot = curve_order % capacity
    source_lane = (source_brick - my_index + 1) % bricks
    from_lane = source_lane[:, None] == lane_ids[None, :]
    first_slot = jnp.min(jnp.where(from_lane, source_slot[:, None], capacity), axis=0)
    first_of_row = jnp.sum(jnp.where(from_lane, first_slot[None, :], 0), axis=1)
    recv_index = source_lane * pair_rows + source_slot - first_of_row
    lanes_in = []
    for lane in range(4):
        step = lane - 1
        target = (my_index - step) % bricks
        slots = run_starts[target] + jnp.arange(pair_rows, dtype=jnp.int32)
        valid = slots < run_stops[target]
        rows = voxel_feats[jnp.minimum(slots, capacity - 1)]
        piece = jnp.where(valid[:, None], rows, jnp.zeros_like(rows))
        if step != 0:
            piece = shifted(piece, "brick", -step)
        lanes_in.append(piece)
    local_rows = jnp.concatenate(lanes_in, axis=0)[recv_index]
    head_next = shifted(local_rows[:PATCH], "brick", -1)
    window = lax.dynamic_slice_in_dim(
        jnp.concatenate([local_rows, head_next], axis=0), offset, shard_rows, 0
    )
    normed = layer_norm(window, norm_gains[0])
    qkv_rows = jnp.dot(normed, qkv_weight, preferred_element_type=jnp.float32).astype(jnp.bfloat16)
    heads_here = HEADS // model_parts
    attended = patch_attention(qkv_rows, heads_here, PATCH)
    head_partial = jnp.dot(attended, proj_weight, preferred_element_type=jnp.float32).astype(
        jnp.bfloat16
    )
    mixed = lax.psum(head_partial, "mp").astype(jnp.float32)
    hidden_state = (window.astype(jnp.float32) + mixed).astype(jnp.bfloat16)
    normed_two = layer_norm(hidden_state, norm_gains[1])
    expanded = jax.nn.gelu(
        jnp.dot(normed_two, up_weight, preferred_element_type=jnp.float32), approximate=False
    ).astype(jnp.bfloat16)
    mlp_terms = jnp.dot(expanded, down_weight, preferred_element_type=jnp.float32).astype(
        jnp.bfloat16
    )
    mlp_sum = summed_on_arrival(mlp_terms, "mp", 1)
    column_offset = lax.axis_index("mp") * mlp_sum.shape[1]
    hidden_part = lax.dynamic_slice_in_dim(hidden_state, column_offset, mlp_sum.shape[1], 1)
    result_window = (hidden_part.astype(jnp.float32) + mlp_sum).astype(jnp.bfloat16)
    tail_rows = shifted(result_window[shard_rows - PATCH :], "brick", 1)
    own_rows = lax.dynamic_slice_in_dim(
        jnp.concatenate([tail_rows, result_window], axis=0), PATCH - offset, shard_rows, 0
    )
    back_rows = (
        jnp.zeros((4 * pair_rows, own_rows.shape[1]), jnp.bfloat16).at[recv_index].set(own_rows)
    )
    back_rows = back_rows.reshape(4, pair_rows, own_rows.shape[1])
    lanes_out = []
    for lane in range(4):
        step = lane - 1
        piece = back_rows[lane]
        if step != 0:
            piece = shifted(piece, "brick", step)
        lanes_out.append(piece)
    returned = jnp.concatenate(lanes_out, axis=0)
    to_shard = dest_shard[:, None] == brick_ids[None, :]
    start_of_slot = jnp.sum(jnp.where(to_shard, run_starts[None, :], 0), axis=1)
    slot_ids = jnp.arange(capacity, dtype=jnp.int32)
    slot_lane = (my_index - dest_shard + 1) % bricks
    back_index = jnp.where(live_slots, slot_lane * pair_rows + slot_ids - start_of_slot, 0)
    picked = returned[back_index]
    return jnp.where(live_slots[:, None], picked, jnp.zeros_like(picked))


def solution(mesh):
    return jax.shard_map(
        per_device,
        mesh=mesh,
        in_specs=(
            P("brick", None),
            P("brick"),
            P("brick"),
            P(),
            P(None, "mp"),
            P("mp", None),
            P(None, "mp"),
            P("mp", None),
            P(),
        ),
        out_specs=P("brick", "mp"),
        check_vma=False,
    )
```

profile of v0, /device:TPU:1, one launch (start us, length us, event | category | flops | bytes accessed | tf_op | source)
XLA Modules:
  0.0 442.5 jit_solution(14720468173422895808)
XLA Ops:
  8.7 1.3 fusion.64
  13.4 1.3 add_compare_fusion.3
  14.8 3.3 gather_fusion
  18.1 2.2 broadcast_select_fusion.3
  20.3 3.0 collective-permute-start
  24.0 3.3 gather_fusion.2
  27.3 1.2 add_compare_fusion.1
  28.6 2.2 broadcast_select_fusion.1
  31.7 3.3 gather_fusion.3
  35.0 1.3 add_compare_fusion
  36.4 2.2 broadcast_select_fusion
  38.5 6.3 %collective-permute-start.2 = (bf16[768,512]{1,0:T(8,128)(2,1)}, bf16[768,512]{1,0:T(8,128)(2,1)}, u32[]{:S(2)}, u32[]{:S(2)}) collective-permute-start(bf16[768,512]{1,0:T(8,128)(2,1)} %broadcast_select_fusion), channel_id=1, source_target_pairs={{0,248},{4,252},{8,0},{12,4},{16,8},{20,12},{24,16},{28,20},{32,24... | collective-permute-start | bytes 2359304 | tf_op jit(solution)/shard_map/ppermute | solution.py:18
  45.5 3.3 gather_fusion.1
  48.8 1.2 add_compare_fusion.2
  50.9 1.3 broadcast_select_fusion.2
  52.2 9.7 %collective-permute-done.2 = bf16[768,512]{1,0:T(8,128)(2,1)} collective-permute-done((bf16[768,512]{1,0:T(8,128)(2,1)}, bf16[768,512]{1,0:T(8,128)(2,1)}, u32[]{:S(2)}, u32[]{:S(2)}) %collective-permute-start.2) | collective-permute-done | bytes 786464 | tf_op jit(solution)/shard_map/ppermute | solution.py:18
  61.9 3.0 pad_maximum_fusion
  64.8 11.5 %gather_fusion.4 = bf16[2048,512]{1,0:T(8,128)(2,1)} fusion(bf16[3072,512]{1,0:T(8,128)(2,1)} %pad_maximum_fusion, s32[2048]{0:T(1024)S(1)} %get-tuple-element.76), kind=kCustom, calls=%fused_computation.4 | custom fusion | bytes 4202496 | tf_op jit(solution)/shard_map/gather | solution.py:118
  76.3 2.3 slice.64
  78.7 1.8 collective-permute-start.3
  81.8 11.4 %collective-permute-done.3 = bf16[1024,512]{1,0:T(8,128)(2,1)} collective-permute-done((bf16[1024,512]{1,0:T(8,128)(2,1)}, bf16[1024,512]{1,0:T(8,128)(2,1)}, u32[]{:S(2)}, u32[]{:S(2)}) %collective-permute-start.3) | collective-permute-done | bytes 1048608 | tf_op jit(solution)/shard_map/ppermute | solution.py:18
  93.2 3.1 convert_reduce_fusion
  97.4 2.6 convolution_convert_fusion.2
  100.0 161.6 %while.21 = (s32[]{:T(128)}, bf16[2,1024,128]{2,1,0:T(8,128)(2,1)}, bf16[2,1024,384]{2,1,0:T(8,128)(2,1)}, s32[]{:T(128)}, s32[]{:T(128)}, /*index=5*/s32[]{:T(128)}) while((s32[]{:T(128)}, bf16[2,1024,128]{2,1,0:T(8,128)(2,1)}, bf16[2,1024,384]{2,1,0:T(8,128)(2,1)}, s32[]{:T(128)}, s32[]{:T(128)}, /*index=5*/s32[]{:T(128)}) %tuple.68), condition=%wide.region_11.12_spmd, body=%wide.region_6.11_spmd.sunk | while | flops 306255872 | bytes 72648360 | solution.py:69
  100.0 2.1 constant_dynamic-slice_fusion.5
  102.1 2.3 copy.34
  104.4 74.6 %while.22 = (s32[]{:T(128)}, bf16[2,1024,4,16]{1,3,2,0:T(8,128)(2,1)}, bf16[2,1024,4,3,16]{1,4,3,2,0:T(8,128)(2,1)}, s32[]{:T(128)}) while((s32[]{:T(128)}, bf16[2,1024,4,16]{1,3,2,0:T(8,128)(2,1)}, bf16[2,1024,4,3,16]{1,4,3,2,0:T(8,128)(2,1)}, s32[]{:T(128)}) %tuple.67), condition=%wide.region_10.10_spmd, body=%wide.region_7.9_spmd.sunk | while | flops 306255872 | bytes 68453432 | solution.py:65
  105.4 8.1 %fusion.121 = f32[4,1024,1024]{1,2,0:T(8,128)} fusion(bf16[1024,4,3,16]{0,3,1,2:T(8,128)(2,1)S(1)} %copy_bitcast_fusion.2), kind=kOutput, calls=%fused_computation.19.clone.1 | convolution fusion | flops 134217728 | bytes 17039360 | tf_op jit(solution)/shard_map/while/body/eval_jaxpr/while/body/eval_jaxpr/qhd,khd->hqk/dot_general | solution.py:49
  113.5 12.6 %fusion.122 = f32[4,1024]{1,0:T(4,128)S(1)} fusion(f32[4,1024,1024]{1,2,0:T(8,128)} %fusion.121), kind=kOutput, calls=%fused_computation.180.clone.1 | output fusion | flops 16778240 | bytes 16793600 | tf_op jit(solution)/shard_map/while/body/eval_jaxpr/while/body/eval_jaxpr/sub | solution.py:55
  126.1 15.6 %fusion.123 = bf16[2,1024,4,16]{1,3,2,0:T(8,128)(2,1)} fusion(bf16[2,1024,4,16]{1,3,2,0:T(8,128)(2,1)} %get-tuple-element.150, s32[]{:T(128)} %get-tuple-element.149, f32[4,1024]{1,0:T(4,128)S(1)} %fusion.122, bf16[1024,4,3,16]{0,3,1,2:T(8,128)(2,1)S(1)} %copy_bitcast_fusion.2, f32[4,1024,1024]{1,2,0:T(8,128)} %fusion.121), kind=kOutput, calls=%fused_computation.16.clone.1 | convolution fusion | flops 155259904 | bytes 33833472 | tf_op jit(solution)/shard_map/while/body/eval_jaxpr/while/body/eval_jaxpr/hqk,khd->qhd/dot_general | solution.py:59
  142.7 8.1 %fusion.121 = f32[4,1024,1024]{1,2,0:T(8,128)} fusion(bf16[1024,4,3,16]{0,3,1,2:T(8,128)(2,1)S(1)} %copy_bitcast_fusion.2), kind=kOutput, calls=%fused_computation.19.clone.1 | convolution fusion | flops 134217728 | bytes 17039360 | tf_op jit(solution)/shard_map/while/body/eval_jaxpr/while/body/eval_jaxpr/qhd,khd->hqk/dot_general | solution.py:49
  150.8 12.6 %fusion.122 = f32[4,1024]{1,0:T(4,128)S(1)} fusion(f32[4,1024,1024]{1,2,0:T(8,128)} %fusion.121), kind=kOutput, calls=%fused_computation.180.clone.1 | output fusion | flops 16778240 | bytes 16793600 | tf_op jit(solution)/shard_map/while/body/eval_jaxpr/while/body/eval_jaxpr/sub | solution.py:55
  163.4 15.6 %fusion.123 = bf16[2,1024,4,16]{1,3,2,0:T(8,128)(2,1)} fusion(bf16[2,1024,4,16]{1,3,2,0:T(8,128)(2,1)} %get-tuple-element.150, s32[]{:T(128)} %get-tuple-element.149, f32[4,1024]{1,0:T(4,128)S(1)} %fusion.122, bf16[1024,4,3,16]{0,3,1,2:T(8,128)(2,1)S(1)} %copy_bitcast_fusion.2, f32[4,1024,1024]{1,2,0:T(8,128)} %fusion.121), kind=kOutput, calls=%fused_computation.16.clone.1 | convolution fusion | flops 155259904 | bytes 33833472 | tf_op jit(solution)/shard_map/while/body/eval_jaxpr/while/body/eval_jaxpr/hqk,khd->qhd/dot_general | solution.py:59
  179.0 1.1 copy.35
  180.8 2.1 constant_dynamic-slice_fusion.5
  182.9 2.3 copy.34
  185.2 74.6 %while.22 = (s32[]{:T(128)}, bf16[2,1024,4,16]{1,3,2,0:T(8,128)(2,1)}, bf16[2,1024,4,3,16]{1,4,3,2,0:T(8,128)(2,1)}, s32[]{:T(128)}) while((s32[]{:T(128)}, bf16[2,1024,4,16]{1,3,2,0:T(8,128)(2,1)}, bf16[2,1024,4,3,16]{1,4,3,2,0:T(8,128)(2,1)}, s32[]{:T(128)}) %tuple.67), condition=%wide.region_10.10_spmd, body=%wide.region_7.9_spmd.sunk | while | flops 306255872 | bytes 68453432 | solution.py:65
  186.2 8.1 %fusion.121 = f32[4,1024,1024]{1,2,0:T(8,128)} fusion(bf16[1024,4,3,16]{0,3,1,2:T(8,128)(2,1)S(1)} %copy_bitcast_fusion.2), kind=kOutput, calls=%fused_computation.19.clone.1 | convolution fusion | flops 134217728 | bytes 17039360 | tf_op jit(solution)/shard_map/while/body/eval_jaxpr/while/body/eval_jaxpr/qhd,khd->hqk/dot_general | solution.py:49
  194.3 12.6 %fusion.122 = f32[4,1024]{1,0:T(4,128)S(1)} fusion(f32[4,1024,1024]{1,2,0:T(8,128)} %fusion.121), kind=kOutput, calls=%fused_computation.180.clone.1 | output fusion | flops 16778240 | bytes 16793600 | tf_op jit(solution)/shard_map/while/body/eval_jaxpr/while/body/eval_jaxpr/sub | solution.py:55
  206.9 15.6 %fusion.123 = bf16[2,1024,4,16]{1,3,2,0:T(8,128)(2,1)} fusion(bf16[2,1024,4,16]{1,3,2,0:T(8,128)(2,1)} %get-tuple-element.150, s32[]{:T(128)} %get-tuple-element.149, f32[4,1024]{1,0:T(4,128)S(1)} %fusion.122, bf16[1024,4,3,16]{0,3,1,2:T(8,128)(2,1)S(1)} %copy_bitcast_fusion.2, f32[4,1024,1024]{1,2,0:T(8,128)} %fusion.121), kind=kOutput, calls=%fused_computation.16.clone.1 | convolution fusion | flops 155259904 | bytes 33833472 | tf_op jit(solution)/shard_map/while/body/eval_jaxpr/while/body/eval_jaxpr/hqk,khd->qhd/dot_general | solution.py:59
  223.5 8.1 %fusion.121 = f32[4,1024,1024]{1,2,0:T(8,128)} fusion(bf16[1024,4,3,16]{0,3,1,2:T(8,128)(2,1)S(1)} %copy_bitcast_fusion.2), kind=kOutput, calls=%fused_computation.19.clone.1 | convolution fusion | flops 134217728 | bytes 17039360 | tf_op jit(solution)/shard_map/while/body/eval_jaxpr/while/body/eval_jaxpr/qhd,khd->hqk/dot_general | solution.py:49
  231.6 12.6 %fusion.122 = f32[4,1024]{1,0:T(4,128)S(1)} fusion(f32[4,1024,1024]{1,2,0:T(8,128)} %fusion.121), kind=kOutput, calls=%fused_computation.180.clone.1 | output fusion | flops 16778240 | bytes 16793600 | tf_op jit(solution)/shard_map/while/body/eval_jaxpr/while/body/eval_jaxpr/sub | solution.py:55
  244.2 15.6 %fusion.123 = bf16[2,1024,4,16]{1,3,2,0:T(8,128)(2,1)} fusion(bf16[2,1024,4,16]{1,3,2,0:T(8,128)(2,1)} %get-tuple-element.150, s32[]{:T(128)} %get-tuple-element.149, f32[4,1024]{1,0:T(4,128)S(1)} %fusion.122, bf16[1024,4,3,16]{0,3,1,2:T(8,128)(2,1)S(1)} %copy_bitcast_fusion.2, f32[4,1024,1024]{1,2,0:T(8,128)} %fusion.121), kind=kOutput, calls=%fused_computation.16.clone.1 | convolution fusion | flops 155259904 | bytes 33833472 | tf_op jit(solution)/shard_map/while/body/eval_jaxpr/while/body/eval_jaxpr/hqk,khd->qhd/dot_general | solution.py:59
  259.7 1.1 copy.35
  261.6 3.1 convolution_convert_fusion
  264.7 65.5 %all-reduce.2.cloned.1.call-done = bf16[2048,512]{1,0:T(8,128)(2,1)} async-done(((bf16[2048,512]{1,0:T(8,128)(2,1)}), bf16[2048,512]{1,0:T(8,128)(2,1)}) %all-reduce.2.cloned.1.call-update) | async-done | bytes 2097168 | tf_op jit(solution)/shard_map/psum | solution.py:130
  330.1 2.9 convert_reduce_fusion.1
  333.1 1.3 copy-done.2
  335.4 14.0 %convolution_convert_fusion.1 = bf16[2048,512]{0,1:T(8,128)(2,1)} fusion(bf16[512,512]{1,0:T(8,128)(2,1)} %param.20, bf16[512,512]{1,0:T(8,128)(2,1)} %param.19, bf16[2048,512]{1,0:T(8,128)(2,1)} %copy-done.2, f32[512]{0:T(512)S(1)} %bitcast.69, f32[2048]{0:T(1024)S(1)} %add_rsqrt_fusion, f32[2048]{0:T(1024)S(1)} %broadcast_multiply_fusion), kind=kOutput, calls=%fused_computation.68 | convolution fusion | flops 2221932544 | bytes 5261312 | tf_op jit(solution)/shard_map/dot_general | solution.py:136
  349.4 4.4 %all-to-all-start = ((bf16[4,2048,128]{1,2,0:T(8,128)(2,1)}), bf16[4,2048,128]{1,2,0:T(8,128)(2,1)}, u32[]{:S(2)}, u32[]{:S(2)}) async-start(bf16[4,2048,128]{1,2,0:T(8,128)(2,1)} %bitcast.67), calls=%async_computation | async-start | bytes 4194304 | tf_op jit(solution)/shard_map/all_to_all | solution.py:29
  353.9 25.6 %all-to-all-done = bf16[4,2048,128]{1,2,0:T(8,128)(2,1)} async-done(((bf16[4,2048,128]{1,2,0:T(8,128)(2,1)}), bf16[4,2048,128]{1,2,0:T(8,128)(2,1)}, u32[]{:S(2)}, u32[]{:S(2)}) %all-to-all-start) | async-done | bytes 2097184 | tf_op jit(solution)/shard_map/all_to_all | solution.py:29
  379.5 3.0 convert_reduce_fusion.2
  382.6 2.5 copy.24
  385.1 1.5 add_convert_fusion
  387.4 2.9 collective-permute-start.4
  390.3 3.3 collective-permute-done.4
  393.7 7.4 %scatter_custom_fusion = bf16[3072,128]{1,0:T(8,128)(2,1)} fusion(s32[2048]{0:T(1024)} %get-tuple-element.77, s32[]{:T(128)S(6)} %select_n.174, s32[]{:T(128)} %constant.86.clone.1, bf16[1024,128]{1,0:T(8,128)(2,1)} %collective-permute-done.4, bf16[]{:T(256)} %constant.218, bf16[2048,128]{1,0:T(8,128)(2,1)} %copy-done.3, bf16[]{:T(256)} %constant.82.clone.1), kind=kCustom, calls=%fused_computation.91 | custom fusion | flops 1048576 | bytes 1574404 | tf_op jit(solution)/shard_map/scatter | solution.py:148
  401.1 1.3 fusion.107
  402.4 4.8 %collective-permute-start.5 = (bf16[768,128]{1,0:T(8,128)(2,1)S(1)}, bf16[768,128]{1,0:T(8,128)(2,1)S(1)}, u32[]{:S(2)}, u32[]{:S(2)}) collective-permute-start(bf16[768,128]{1,0:T(8,128)(2,1)S(1)} %get-tuple-element.78), channel_id=1, source_target_pairs={{0,252},{4,0},{8,4},{12,8},{16,12},{20,16},{24,20},{28,24},{32,28}... | collective-permute-start | bytes 589832 | tf_op jit(solution)/shard_map/ppermute | solution.py:18
  407.2 1.2 collective-permute-done.5
  408.4 2.8 collective-permute-done.6
  411.2 8.0 %collective-permute-done.7 = bf16[768,128]{1,0:T(8,128)(2,1)S(1)} collective-permute-done((bf16[768,128]{1,0:T(8,128)(2,1)S(1)}, bf16[768,128]{1,0:T(8,128)(2,1)S(1)}, u32[]{:S(2)}, u32[]{:S(2)}) %collective-permute-start.7) | collective-permute-done | bytes 196640 | tf_op jit(solution)/shard_map/ppermute | solution.py:18
  420.2 12.1 %gather_fusion.5 = bf16[3072,128]{1,0:T(8,128)(2,1)} fusion(bf16[3072,128]{1,0:T(8,128)(2,1)} %pad_maximum_fusion.1, s32[3072]{0:T(1024)S(1)} %copy-done.4), kind=kCustom, calls=%fused_computation.5 | custom fusion | bytes 1585152 | tf_op jit(solution)/shard_map/gather | solution.py:164
  432.3 3.3 broadcast_select_fusion.4
  (66 shorter events, 18.5 us)
Async XLA Ops:
  6.5 8.2 %copy-start = (bf16[3072,512]{1,0:T(8,128)(2,1)S(1)}, bf16[3072,512]{1,0:T(8,128)(2,1)}, u32[]{:S(2)}) copy-start(bf16[3072,512]{1,0:T(8,128)(2,1)} %param.13) | copy-start | bytes 9437188
  6.5 323.6 %all-reduce.2.cloned.1.call-start = ((), (), s32[]{:S(2)}) async-start(), calls=%async_computation.1 | async-start | bytes 4194304 | tf_op jit(solution)/shard_map/psum | solution.py:130
  10.1 0.6 copy-start.6
  20.3 31.9 %collective-permute-start = (bf16[768,512]{1,0:T(8,128)(2,1)}, bf16[768,512]{1,0:T(8,128)(2,1)}, u32[]{:S(2)}, u32[]{:S(2)}) collective-permute-start(bf16[768,512]{1,0:T(8,128)(2,1)} %broadcast_select_fusion.3), channel_id=1, source_target_pairs={{0,4},{4,8},{8,12},{12,16},{16,20},{20,24},{24,28},{28,32},{32,36}... | collective-permute-start | bytes 2359304 | tf_op jit(solution)/shard_map/ppermute | solution.py:18
  30.8 21.4 %collective-permute-start.1 = (bf16[768,512]{1,0:T(8,128)(2,1)}, bf16[768,512]{1,0:T(8,128)(2,1)}, u32[]{:S(2)}, u32[]{:S(2)}) collective-permute-start(bf16[768,512]{1,0:T(8,128)(2,1)} %broadcast_select_fusion.1), channel_id=1, source_target_pairs={{0,252},{4,0},{8,4},{12,8},{16,12},{20,16},{24,20},{28,24},{32,28}... | collective-permute-start | bytes 2359304 | tf_op jit(solution)/shard_map/ppermute | solution.py:18
  36.3 12.5 %copy-start.5 = (s32[2048]{0:T(1024)S(1)}, s32[2048]{0:T(1024)}, u32[]{:S(2)}) copy-start(s32[2048]{0:T(1024)} %param.15) | copy-start | bytes 24580
  38.5 23.3 %collective-permute-start.2 = (bf16[768,512]{1,0:T(8,128)(2,1)}, bf16[768,512]{1,0:T(8,128)(2,1)}, u32[]{:S(2)}, u32[]{:S(2)}) collective-permute-start(bf16[768,512]{1,0:T(8,128)(2,1)} %broadcast_select_fusion), channel_id=1, source_target_pairs={{0,248},{4,252},{8,0},{12,4},{16,8},{20,12},{24,16},{28,20},{32,24... | collective-permute-start | bytes 2359304 | tf_op jit(solution)/shard_map/ppermute | solution.py:18
  64.8 16.3 %copy-start.8 = (f32[2,512]{1,0:T(2,128)S(1)}, f32[2,512]{1,0:T(2,128)}, u32[]{:S(2)}) copy-start(f32[2,512]{1,0:T(2,128)} %param.21) | copy-start | bytes 12292
  78.7 18.7 %copy-start.10 = (bf16[512,384]{1,0:T(8,128)(2,1)S(1)}, bf16[512,384]{1,0:T(8,128)(2,1)}, u32[]{:S(2)}) copy-start(bf16[512,384]{1,0:T(8,128)(2,1)} %param.17) | copy-start | bytes 1179652
  78.7 14.5 %collective-permute-start.3 = (bf16[1024,512]{1,0:T(8,128)(2,1)}, bf16[1024,512]{1,0:T(8,128)(2,1)}, u32[]{:S(2)}, u32[]{:S(2)}) collective-permute-start(bf16[1024,512]{1,0:T(8,128)(2,1)} %slice.64), channel_id=1, source_target_pairs={{0,252},{4,0},{8,4},{12,8},{16,12},{20,16},{24,20},{28,24},{32,28}... | collective-permute-start | bytes 3145736 | tf_op jit(solution)/shard_map/ppermute | solution.py:18
  96.3 3.7 copy-start.1
  264.7 70.8 %copy-start.9 = (f32[1,512]{1,0:T(1,128)S(1)}, f32[1,512]{1,0:T(1,128)}, u32[]{:S(2)}) copy-start(f32[1,512]{1,0:T(1,128)} %get-tuple-element.84) | copy-start | bytes 6148
  333.0 1.4 copy-start.2
  349.4 30.1 %all-to-all-start = ((bf16[4,2048,128]{1,2,0:T(8,128)(2,1)}), bf16[4,2048,128]{1,2,0:T(8,128)(2,1)}, u32[]{:S(2)}, u32[]{:S(2)}) async-start(bf16[4,2048,128]{1,2,0:T(8,128)(2,1)} %bitcast.67), calls=%async_computation | async-start | bytes 4194304 | tf_op jit(solution)/shard_map/all_to_all | solution.py:29
  385.1 35.1 %copy-start.4 = (s32[3072]{0:T(1024)S(1)}, s32[3072]{0:T(1024)}, u32[]{:S(2)}) copy-start(s32[3072]{0:T(1024)} %get-tuple-element.70) | copy-start | bytes 36868
  386.6 0.8 copy-start.3
  387.4 6.3 %collective-permute-start.4 = (bf16[1024,128]{1,0:T(8,128)(2,1)S(1)}, bf16[1024,128]{1,0:T(8,128)(2,1)}, u32[]{:S(2)}, u32[]{:S(2)}) collective-permute-start(bf16[1024,128]{1,0:T(8,128)(2,1)S(1)} %slice.65), channel_id=1, source_target_pairs={{0,4},{4,8},{8,12},{12,16},{16,20},{20,24},{24,28},{28,32},{32,36}... | collective-permute-start | bytes 786440 | tf_op jit(solution)/shard_map/ppermute | solution.py:18
  402.4 6.0 %collective-permute-start.5 = (bf16[768,128]{1,0:T(8,128)(2,1)S(1)}, bf16[768,128]{1,0:T(8,128)(2,1)S(1)}, u32[]{:S(2)}, u32[]{:S(2)}) collective-permute-start(bf16[768,128]{1,0:T(8,128)(2,1)S(1)} %get-tuple-element.78), channel_id=1, source_target_pairs={{0,252},{4,0},{8,4},{12,8},{16,12},{20,16},{24,20},{28,24},{32,28}... | collective-permute-start | bytes 589832 | tf_op jit(solution)/shard_map/ppermute | solution.py:18
  407.2 4.0 collective-permute-start.6
  407.2 12.0 %collective-permute-start.7 = (bf16[768,128]{1,0:T(8,128)(2,1)S(1)}, bf16[768,128]{1,0:T(8,128)(2,1)S(1)}, u32[]{:S(2)}, u32[]{:S(2)}) collective-permute-start(bf16[768,128]{1,0:T(8,128)(2,1)S(1)} %get-tuple-element.79), channel_id=1, source_target_pairs={{0,8},{4,12},{8,16},{12,20},{16,24},{20,28},{24,32},{28,36},{32,40... | collective-permute-start | bytes 589832 | tf_op jit(solution)/shard_map/ppermute | solution.py:18
  419.2 13.1 %copy-start.7 = (pred[3072]{0:T(1024)(128)(4,1)S(1)}, pred[3072]{0:T(1024)(128)(4,1)}, u32[]{:S(2)}) copy-start(pred[3072]{0:T(1024)(128)(4,1)} %copy-done.6) | copy-start | bytes 9220
Sparse Core Ops, SparseCore 0:
  264.8 65.3 all-reduce.1
where the time goes:
time: 444 us; the launch traced here: 442 us
  waiting for transfers between devices  128 us (29%)
  matrix products  114 us (26%)
  other arithmetic  98.9 us (22%)
  local copies, waits for them, and re-layouts  63.7 us (14%)
  starting transfers between devices  23.6 us (5%)
  between operations  14.3 us (3%)
    psum x1, waiting for transfers between devices, per_device(): mixed = lax.psum(head_partial, 'mp').astype(jnp.float32)  65.5 us
    dot_general x4, matrix products, one_group(): jnp.einsum('hqk,khd->qhd', softmax_weights, piece[:, :, 2], preferred_ele...  62.3 us
    sub x4, other arithmetic, one_group(): weights_exp = jnp.exp(scores - highest)  50.3 us
    ppermute x8, waiting for transfers between devices, shifted(): return lax.ppermute(value, axis, pairs)  36.4 us
    dot_general x4, matrix products, one_group(): jnp.einsum('qhd,khd->hqk', piece[:, :, 0], piece[:, :, 1], preferred_elem...  32.4 us
    all_to_all x1, waiting for transfers between devices, summed_on_arrival(): lax.all_to_all(blocks, axis, split_axis=0, concat_axis=0, tiled=True)  25.6 us
    ppermute x8, starting transfers between devices, shifted(): return lax.ppermute(value, axis, pairs)  19.1 us
    dot_general x1, matrix products, per_device(): jnp.dot(expanded, down_weight, preferred_element_type=jnp.float32)  14 us
  transfers between devices with their start and end apart: 10, of which 8 were waited for; matrix products, arithmetic and copies ran while one was open for 5% of the time, Pallas kernels for 0%

commit v1 on v0

v1 whole, which is shorter than its diff:
```python
import functools

import jax
import jax.numpy as jnp
from jax import lax
from jax.experimental import pallas as pl
from jax.experimental.pallas import tpu as pltpu
from jax.sharding import PartitionSpec as P

PATCH = 1024
HEAD_DIM = 16
GROUP_HEADS = 8
EPSILON = 1e-05
LOG2E = 1.4426950408889634

TILE = 16
BLOCK = 128
WINDOW = 160
MOST_RUN = 768
PIECE = MOST_RUN + TILE
LANES = 4
BLOCKS = PATCH // BLOCK

F32 = jnp.float32
BF16 = jnp.bfloat16

ANY = pl.BlockSpec(memory_space=pl.ANY)
VMEM = pl.BlockSpec(memory_space=pltpu.VMEM)
SMEM = pl.BlockSpec(memory_space=pltpu.SMEM)


def nt_dot(left, right):
    return lax.dot_general(left, right, (((1,), (1,)), ((), ())), preferred_element_type=F32)


def nn_dot(left, right):
    return jnp.dot(left, right, preferred_element_type=F32)


def tn_dot(left, right):
    return lax.dot_general(left, right, (((0,), (0,)), ((), ())), preferred_element_type=F32)


def aligned(value):
    return pl.multiple_of(value, TILE)


def shifted(value, axis, steps):
    count = lax.axis_size(axis)
    pairs = [(source, (source + steps) % count) for source in range(count)]
    return lax.ppermute(value, axis, pairs)


def layer_norm(values, gain):
    values = values.astype(F32)
    centred = values - jnp.mean(values, axis=-1, keepdims=True)
    spread = jnp.mean(centred * centred, axis=-1, keepdims=True)
    return (centred * lax.rsqrt(spread + EPSILON) * gain).astype(BF16)


def cut_kernel(start_ref, feats_ref, *rest):
    outs, (buffers, in_sems, out_sems) = rest[:3], rest[3:]
    order = (2, 1, 0)
    loads = [
        pltpu.make_async_copy(
            feats_ref.at[pl.ds(aligned(start_ref[i]), PIECE)], buffers.at[i], in_sems.at[i]
        )
        for i in range(3)
    ]
    stores = [
        pltpu.make_async_copy(buffers.at[i], outs[i], out_sems.at[i]) for i in range(3)
    ]
    for i in order:
        loads[i].start()
    for i in order:
        loads[i].wait()
        stores[i].start()
    for i in order:
        stores[i].wait()


def cut_windows(starts, feats):
    piece = jax.ShapeDtypeStruct((PIECE, feats.shape[1]), feats.dtype)
    return pl.pallas_call(
        cut_kernel,
        out_shape=(piece,) * 3,
        in_specs=[SMEM, ANY],
        out_specs=(ANY,) * 3,
        scratch_shapes=[
            pltpu.VMEM((3, PIECE, feats.shape[1]), feats.dtype),
            pltpu.SemaphoreType.DMA((3,)),
            pltpu.SemaphoreType.DMA((3,)),
        ],
        name="cut_windows",
    )(starts, feats)


def gather_block(table_ref, block, spots, lane_refs):
    windows = [
        lane_refs[lane][pl.ds(aligned(table_ref[block, lane]), WINDOW), :]
        for lane in range(LANES)
    ]
    stacked = jnp.concatenate(windows, axis=0)
    hots = []
    lanes_iota = lax.broadcasted_iota(jnp.int32, (BLOCK, 128), 1)
    for chunk in range(LANES * WINDOW // 128):
        hots.append(jnp.where(spots == lanes_iota + chunk * 128, 1.0, 0.0).astype(BF16))
    hot = jnp.concatenate(hots, axis=1)
    return nn_dot(hot, stacked).astype(BF16)


def head_kernel(
    table_ref, start_ref, spots_ref, feats_ref, lane0_ref, lane2_ref, lane3_ref, out_ref, own_ref, sem
):
    load = pltpu.make_async_copy(
        feats_ref.at[pl.ds(aligned(start_ref[0]), PIECE)], own_ref, sem
    )
    load.start()
    load.wait()
    lane_refs = (lane0_ref, own_ref, lane2_ref, lane3_ref)

    def step(block, carry):
        rows = pl.ds(pl.multiple_of(block * BLOCK, BLOCK), BLOCK)
        out_ref[rows, :] = gather_block(table_ref, block, spots_ref[rows, :], lane_refs)
        return carry

    lax.fori_loop(0, BLOCKS, step, 0)


def head_rows(table, start, spots, feats, lanes):
    width = feats.shape[1]
    return pl.pallas_call(
        head_kernel,
        out_shape=jax.ShapeDtypeStruct((PATCH, width), BF16),
        in_specs=[SMEM, SMEM, VMEM, ANY, VMEM, VMEM, VMEM],
        out_specs=VMEM,
        scratch_shapes=[pltpu.VMEM((PIECE, width), BF16), pltpu.SemaphoreType.DMA],
        cost_estimate=pl.CostEstimate(
            flops=2 * PATCH * 768 * width, bytes_accessed=5 << 20, transcendentals=0
        ),
        name="head_rows",
    )(table, start, spots, feats, *lanes)


def attend_kernel(with_head, groups, queries, *refs):
    table_ref, start_ref, spots_ref, feats_ref = refs[:4]
    lane0_ref, lane2_ref, lane3_ref = refs[4:7]
    gain_ref = refs[7]
    qkv_refs = refs[8 : 8 + groups]
    proj_refs = refs[8 + groups : 8 + 2 * groups]
    at = 8 + 2 * groups
    if with_head:
        extra_ref = refs[at]
        at += 1
    out_ref = refs[at]
    own_ref, rows_ref, normed_ref, keys_ref, values_ref, query_ref, mixed_ref, score_ref, sem = refs[
        at + 1 :
    ]
    load = pltpu.make_async_copy(
        feats_ref.at[pl.ds(aligned(start_ref[0]), PIECE)], own_ref, sem
    )
    load.start()
    load.wait()
    lane_refs = (lane0_ref, own_ref, lane2_ref, lane3_ref)
    gain = gain_ref[0:1, :]

    def gather_step(block, carry):
        rows = pl.ds(pl.multiple_of(block * BLOCK, BLOCK), BLOCK)
        found = gather_block(table_ref, block, spots_ref[rows, :], lane_refs)
        if with_head:
            found = found + extra_ref[rows, :]
        rows_ref[rows, :] = found
        normed_ref[rows, :] = layer_norm(found, gain)
        return carry

    lax.fori_loop(0, BLOCKS, gather_step, 0)
    own_rows = pl.ds(pl.multiple_of(start_ref[1], queries), queries)
    span = GROUP_HEADS * HEAD_DIM
    for group in range(groups):
        weight = qkv_refs[group]
        query = nt_dot(weight[0:span, :], normed_ref[own_rows, :])
        query_ref[group] = (query * (HEAD_DIM ** (-0.5) * LOG2E)).astype(BF16)
        for part in range(4):
            rows = slice(part * 256, (part + 1) * 256)
            normed = normed_ref[rows, :]
            keys_ref[group, rows, :] = nt_dot(normed, weight[span : 2 * span, :]).astype(BF16)
            values_ref[group, :, rows] = nt_dot(weight[2 * span : 3 * span, :], normed).astype(BF16)

    head_of_row = lax.broadcasted_iota(jnp.int32, (span, queries), 0) // HEAD_DIM
    ones = jnp.ones((HEAD_DIM, PATCH), BF16)

    def head_step(head, carry):
        mine = head_of_row == head
        rows = pl.ds(pl.multiple_of(head * HEAD_DIM, HEAD_DIM), HEAD_DIM)
        for group in range(groups):
            query = query_ref[group]
            query = jnp.where(mine, query, jnp.zeros_like(query))
            slot = group % 2
            highest = None
            for part in range(4):
                keys = slice(part * 256, (part + 1) * 256)
                scores = nn_dot(keys_ref[group, keys, :], query)
                score_ref[slot, keys, :] = scores
                top = jnp.max(scores, axis=0, keepdims=True)
                highest = top if highest is None else jnp.maximum(highest, top)
            values = jnp.concatenate([values_ref[group, rows, :], ones], axis=0)
            total = None
            for part in range(4):
                keys = slice(part * 256, (part + 1) * 256)
                weights = jnp.exp2(score_ref[slot, keys, :] - highest).astype(BF16)
                term = nn_dot(values[:, keys], weights)
                total = term if total is None else total + term
            mixed_ref[group, rows, :] = (
                total[:HEAD_DIM] / total[HEAD_DIM : HEAD_DIM + 1]
            ).astype(BF16)
        return carry

    lax.fori_loop(0, GROUP_HEADS, head_step, 0)
    mixed = None
    for group in range(groups):
        term = tn_dot(mixed_ref[group], proj_refs[group][...]).astype(BF16).astype(F32)
        mixed = term if mixed is None else mixed + term
    out_ref[...] = (rows_ref[own_rows, :].astype(F32) + mixed).astype(BF16)


def attend(table, start, spots, feats, lanes, gains, qkv, proj, extra, queries):
    width = feats.shape[1]
    groups = len(qkv)
    span = GROUP_HEADS * HEAD_DIM
    operands = [table, start, spots, feats, *lanes, gains, *qkv, *proj]
    specs = [SMEM, SMEM, VMEM, ANY] + [VMEM] * (4 + 2 * groups)
    if extra is not None:
        operands.append(extra)
        specs.append(VMEM)
    return pl.pallas_call(
        functools.partial(attend_kernel, extra is not None, groups, queries),
        out_shape=jax.ShapeDtypeStruct((queries, width), BF16),
        in_specs=specs,
        out_specs=VMEM,
        scratch_shapes=[
            pltpu.VMEM((PIECE, width), BF16),
            pltpu.VMEM((PATCH, width), BF16),
            pltpu.VMEM((PATCH, width), BF16),
            pltpu.VMEM((groups, PATCH, span), BF16),
            pltpu.VMEM((groups, span, PATCH), BF16),
            pltpu.VMEM((groups, span, queries), BF16),
            pltpu.VMEM((groups, span, queries), BF16),
            pltpu.VMEM((2, PATCH, queries), F32),
            pltpu.SemaphoreType.DMA,
        ],
        cost_estimate=pl.CostEstimate(
            flops=40 * 10**9, bytes_accessed=10 << 20, transcendentals=8 << 20
        ),
        name="attend",
    )(*operands)


def mlp_kernel(groups, hidden_ref, gain_ref, *refs):
    up_refs, down_refs = refs[:groups], refs[groups : 2 * groups]
    out_ref, wide_ref = refs[2 * groups :]
    hidden = hidden_ref[...]
    normed = layer_norm(hidden, gain_ref[1:2, :])
    for group in range(groups):
        wide = nn_dot(normed, up_refs[group][...])
        wide_ref[group] = (wide * (0.5 + 0.5 * lax.erf(wide * 0.5**0.5))).astype(BF16)
    total = None
    for group in range(groups):
        term = nn_dot(wide_ref[group], down_refs[group][...]).astype(BF16).astype(F32)
        total = term if total is None else total + term
    result = (hidden.astype(F32) + total).astype(BF16)
    width = result.shape[1] // groups
    for group in range(groups):
        out_ref[group] = result[:, group * width : (group + 1) * width]


def mlp(hidden, gains, up, down):
    groups = len(up)
    rows, width = hidden.shape
    return pl.pallas_call(
        functools.partial(mlp_kernel, groups),
        out_shape=jax.ShapeDtypeStruct((groups, rows, width // groups), BF16),
        in_specs=[VMEM] * (2 + 2 * groups),
        out_specs=VMEM,
        scratch_shapes=[pltpu.VMEM((groups, rows, up[0].shape[1]), BF16)],
        cost_estimate=pl.CostEstimate(
            flops=4 * rows * width * up[0].shape[1] * groups,
            bytes_accessed=5 << 20,
            transcendentals=0,
        ),
        name="mlp",
    )(hidden, gains, *up, *down)


def pack_kernel(table_ref, spots_ref, tail_ref, first_ref, last_ref, *rest):
    outs, lanes_ref = rest[:LANES], rest[LANES]
    lanes_ref[...] = jnp.zeros_like(lanes_ref)
    tall = lax.broadcasted_iota(jnp.int32, (LANES * WINDOW, BLOCK), 0)
    for part, source in enumerate((tail_ref, first_ref, last_ref)):

        def step(block, carry):
            place = part * BLOCKS + block
            spots = spots_ref[pl.ds(place, 1), :]
            hot = jnp.where(tall == spots, 1.0, 0.0).astype(BF16)
            rows = source[pl.ds(pl.multiple_of(block * BLOCK, BLOCK), BLOCK), :]
            sent = nn_dot(hot, rows).astype(BF16)
            for lane in range(LANES):
                window = pl.ds(aligned(table_ref[place, lane]), WINDOW)
                lanes_ref[lane, window, :] = (
                    lanes_ref[lane, window, :] + sent[lane * WINDOW : (lane + 1) * WINDOW]
                )
            return carry

        lax.fori_loop(0, BLOCKS, step, 0)
    for lane in range(LANES):
        outs[lane][...] = lanes_ref[lane]


def pack_lanes(table, spots, tail, first, last):
    width = tail.shape[1]
    return pl.pallas_call(
        pack_kernel,
        out_shape=(jax.ShapeDtypeStruct((PIECE, width), BF16),) * LANES,
        in_specs=[SMEM] + [VMEM] * 4,
        out_specs=(VMEM,) * LANES,
        scratch_shapes=[pltpu.VMEM((LANES, PIECE, width), BF16)],
        name="pack_lanes",
    )(table, spots, tail, first, last)


def place_kernel(spans_ref, *refs):
    pieces, out_ref = refs[:LANES], refs[LANES]
    out_ref[...] = jnp.zeros_like(out_ref)
    row = lax.broadcasted_iota(jnp.int32, (PIECE, out_ref.shape[1]), 0)
    for lane in range(LANES):
        start = aligned(spans_ref[lane, 0])
        slots = row + start
        mine = (slots >= spans_ref[lane, 1]) & (slots < spans_ref[lane, 2])
        window = pl.ds(start, PIECE)
        out_ref[window, :] = jnp.where(mine, pieces[lane][...], out_ref[window, :])


def place_rows(spans, pieces, capacity):
    width = pieces[0].shape[1]
    return pl.pallas_call(
        place_kernel,
        out_shape=jax.ShapeDtypeStruct((capacity, width), BF16),
        in_specs=[SMEM] + [VMEM] * LANES,
        out_specs=VMEM,
        name="place_rows",
    )(spans, *pieces)


def ring_gather(block):
    half = block.shape[0] // 2
    ahead = shifted(block, "mp", 1)
    behind = shifted(block, "mp", -1)
    far = jnp.concatenate(
        [shifted(ahead[:half], "mp", 1), shifted(behind[half:], "mp", -1)], axis=0
    )
    return [block, ahead, far, behind]


def per_device(
    voxel_feats,
    slot_rank,
    curve_order,
    patch_shift,
    qkv_weight,
    proj_weight,
    up_weight,
    down_weight,
    norm_gains,
):
    bricks = lax.axis_size("brick")
    parts = lax.axis_size("mp")
    me = lax.axis_index("brick")
    capacity = voxel_feats.shape[0]
    shard = curve_order.shape[0]
    queries = PATCH // parts
    offset = patch_shift[0]
    lane_ids = jnp.arange(LANES, dtype=jnp.int32)
    last_start = capacity - PIECE

    targets = (me - lane_ids + 1) % bricks
    ends = jnp.stack([targets, targets + 1]) * shard
    counts = jnp.sum((slot_rank[None, None, :] < ends[:, :, None]).astype(jnp.int32), axis=2)
    run_start = jnp.minimum(counts[0] // TILE * TILE, last_start)
    spans = jnp.stack([run_start, counts[0], counts[1]], axis=1)

    piece0, piece2, piece3 = cut_windows(
        jnp.stack([run_start[0], run_start[2], run_start[3]]), voxel_feats
    )
    lane3 = shifted(piece3, "brick", -2)
    lane2 = shifted(piece2, "brick", -1)
    lane0 = shifted(piece0, "brick", 1)
    lanes = (lane0, lane2, lane3)

    span = GROUP_HEADS * HEAD_DIM
    column = jnp.arange(3 * span, dtype=jnp.int32)
    place = (column // HEAD_DIM % 3) * span + column // (3 * HEAD_DIM) * HEAD_DIM + column % HEAD_DIM
    order = (place[None, :] == column[:, None]).astype(BF16)
    qkv_rows = nt_dot(order, qkv_weight).astype(BF16)
    early = ring_gather(jnp.concatenate([qkv_rows, proj_weight], axis=0))
    late = ring_gather(jnp.concatenate([up_weight, down_weight], axis=0))
    qkv = [block[: 3 * span] for block in early]
    proj = [block[3 * span :] for block in early]
    up = [block[: up_weight.shape[0]] for block in late]
    down = [block[up_weight.shape[0] :] for block in late]

    source = curve_order // capacity
    slot = curve_order - source * capacity
    lane = (source - me + 1) % bricks
    from_lane = lane[None, :] == lane_ids[:, None]
    first_slot = jnp.min(jnp.where(from_lane, slot[None, :], capacity), axis=1)
    lane_start = jnp.minimum(first_slot // TILE * TILE, last_start)
    position = jnp.arange(shard, dtype=jnp.int32)
    block_first = jnp.arange(3 * BLOCKS, dtype=jnp.int32) * BLOCK + offset - PATCH
    before = jnp.sum(
        (from_lane[None, :, :] & (position[None, None, :] < block_first[:, None, None])).astype(
            jnp.int32
        ),
        axis=2,
    )
    table = jnp.clip(
        (first_slot - lane_start)[None, :] + before, 0, PIECE - WINDOW
    ) // TILE * TILE
    base = jnp.sum(jnp.where(from_lane, (lane_ids * WINDOW - lane_start)[:, None], 0), axis=0)
    fill = jnp.full((PATCH,), -1, jnp.int32)
    lane_wide = lax.dynamic_slice_in_dim(
        jnp.concatenate([fill, lane, fill]), offset, shard + PATCH, 0
    )
    spot_wide = lax.dynamic_slice_in_dim(
        jnp.concatenate([fill, slot + base, fill]), offset, shard + PATCH, 0
    )
    lane_wide = lane_wide.reshape(3 * BLOCKS, BLOCK)
    spot_wide = spot_wide.reshape(3 * BLOCKS, BLOCK)
    table_of = jnp.sum(
        jnp.where(lane_wide[:, :, None] == lane_ids[None, None, :], table[:, None, :], 0), axis=2
    )
    spots = jnp.where(lane_wide < 0, -1, spot_wide - table_of)
    tall = jnp.broadcast_to(spots.reshape(3, PATCH, 1), (3, PATCH, 128))

    own_start = jnp.stack([run_start[1], lax.axis_index("mp") * queries])
    head = head_rows(table[:BLOCKS], own_start, tall[0], voxel_feats, lanes)
    head_next = shifted(head, "brick", -1)
    common = (own_start, norm_gains, qkv, proj)

    def hidden_of(part, extra):
        rows = slice(part * BLOCKS, (part + 1) * BLOCKS)
        return attend(
            table[rows], own_start, tall[part], voxel_feats, lanes, norm_gains, qkv, proj, extra, queries
        )

    def columns_of(result):
        arrived = lax.all_to_all(result, "mp", split_axis=0, concat_axis=0, tiled=True)
        return arrived.reshape(PATCH, arrived.shape[2])

    first = columns_of(mlp(hidden_of(1, None), norm_gains, up, down))
    last = columns_of(mlp(hidden_of(2, head_next), norm_gains, up, down))
    tail = shifted(last, "brick", 1)
    back0, back1, back2, back3 = pack_lanes(table, spots, tail, first, last)
    pieces = (
        shifted(back0, "brick", -1),
        back1,
        shifted(back2, "brick", 1),
        shifted(back3, "brick", 2),
    )
    return place_rows(spans, pieces, capacity)


def solution(mesh):
    return jax.shard_map(
        per_device,
        mesh=mesh,
        in_specs=(
            P("brick", None),
            P("brick"),
            P("brick"),
            P(),
            P(None, "mp"),
            P("mp", None),
            P(None, "mp"),
            P("mp", None),
            P(),
        ),
        out_specs=P("brick", "mp"),
        check_vma=False,
    )
```

time: 444 us -> 184 us (0.41)
  matrix products: 114 us -> 0.41 us
  waiting for transfers between devices: 128 us -> 32.5 us
  other arithmetic: 98.9 us -> 7.41 us
  Pallas kernels: 0 us -> 83.1 us
  local copies, waits for them, and re-layouts: 63.7 us -> 15.5 us
  starting transfers between devices: 23.6 us -> 43.8 us
  between operations: 14.3 us -> 1.02 us
    dot_general x11 -> x1, matrix products: 114 us -> 0.41 us  [nt_dot(): lax.dot_general(left, right, (((1,), (1,)), ((), ())), preferred_element_...]
    pallas_call x0 -> x8, Pallas kernels: none -> 83.1 us  [the longest x2 55 us: attend(): pl.pallas_call(functools.partial(attend_kernel, extra is not None, groups...]
    psum x1 -> x0, waiting for transfers between devices: 65.5 us -> none  [per_device(): mixed = lax.psum(head_partial, 'mp').astype(jnp.float32)]
    sub x4, other arithmetic: 50.3 us -> 0.05 us  [the longest x1 0.02 us: per_device(): slot = curve_order - source * capacity]
    gather x6 -> x0, local copies, waits for them, and re-layouts: 37 us -> none  [the longest x4 13.3 us: per_device(): rows = voxel_feats[jnp.minimum(slots, capacity - 1)]]
    all_to_all x1 -> x2, waiting for transfers between devices: 25.6 us -> 5.43 us  [columns_of(): lax.all_to_all(result, 'mp', split_axis=0, concat_axis=0, tiled=True)]
    ppermute x8 -> x16, starting transfers between devices: 19.1 us -> 35.9 us  [shifted(): return lax.ppermute(value, axis, pairs)]
    select_n x11 -> x3, other arithmetic: 14.8 us -> 0.74 us  [the longest x2 0.72 us: per_device(): spots = jnp.where(lane_wide < 0, -1, spot_wide - table_of)]
  transfers between devices with their start and end apart: 10 -> 18, of which waited for: 8 -> 7; matrix products, arithmetic and copies ran while one was open for 5% -> 9% of each run, Pallas kernels for 0% -> 36%
where the time goes in v1:
time: 184 us
  Pallas kernels  83.1 us (45%)
  starting transfers between devices  43.8 us (24%)
  waiting for transfers between devices  32.5 us (18%)
  local copies, waits for them, and re-layouts  15.5 us (8%)
  other arithmetic  7.41 us (4%)
    pallas_call x2, Pallas kernels, attend(): pl.pallas_call(functools.partial(attend_kernel, extra is not None, groups...  55 us
    ppermute x16, starting transfers between devices, shifted(): return lax.ppermute(value, axis, pairs)  35.9 us
    ppermute x16, waiting for transfers between devices, shifted(): return lax.ppermute(value, axis, pairs)  27.1 us
    pallas_call x2, Pallas kernels, mlp(): pl.pallas_call(functools.partial(mlp_kernel, groups), out_shape=jax.Shape...  8.84 us
    all_to_all x2, starting transfers between devices, columns_of(): lax.all_to_all(result, 'mp', split_axis=0, concat_axis=0, tiled=True)  7.88 us
    pallas_call x1, Pallas kernels, pack_lanes(): pl.pallas_call(pack_kernel, out_shape=(jax.ShapeDtypeStruct((PIECE, width...  7.09 us
    pallas_call x1, Pallas kernels, head_rows(): pl.pallas_call(head_kernel, out_shape=jax.ShapeDtypeStruct((PATCH, width)...  6.11 us
    all_to_all x2, waiting for transfers between devices, columns_of(): lax.all_to_all(result, 'mp', split_axis=0, concat_axis=0, tiled=True)  5.43 us
  transfers between devices with their start and end apart: 18, of which 7 were waited for; matrix products, arithmetic and copies ran while one was open for 9% of the time, Pallas kernels for 36%

profile of v1, /device:TPU:1, one launch (start us, length us, event | category | flops | bytes accessed | tf_op | source)
XLA Modules:
  0.0 183.7 jit_solution(4549759934577599646)
XLA Ops:
  0.1 1.0 convert_reduce_fusion.1
  1.1 0.6 fusion.36
  1.8 1.2 pad_add_fusion.2.start_ref
  3.0 3.4 %cut_windows.1 = (bf16[784,512]{1,0:T(8,128)(2,1)}, bf16[784,512]{1,0:T(8,128)(2,1)}, bf16[784,512]{1,0:T(8,128)(2,1)}) custom-call(s32[3]{0:T(128)} %pad_add_fusion.2.start_ref, bf16[3072,512]{1,0:T(8,128)(2,1)} %refs_3_.3), custom_call_target="tpu_custom_call" | custom-call | tf_op jit(solution)/shard_map/cut_windows/pallas_call | solution.py:84
  6.4 3.1 %collective-permute-start = (bf16[784,512]{1,0:T(8,128)(2,1)}, bf16[784,512]{1,0:T(8,128)(2,1)S(1)}, u32[]{:S(2)}, u32[]{:S(2)}) collective-permute-start(bf16[784,512]{1,0:T(8,128)(2,1)} %get-tuple-element.12), channel_id=1, source_target_pairs={{0,4},{4,8},{8,12},{12,16},{16,20},{20,24},{24,28},{28,32},{32,36}... | collective-permute-start | bytes 2408456 | tf_op jit(solution)/shard_map/ppermute | solution.py:51
  9.5 0.3 collective-permute-start.1
  9.8 6.3 %collective-permute-start.2 = (bf16[784,512]{1,0:T(8,128)(2,1)}, bf16[784,512]{1,0:T(8,128)(2,1)}, u32[]{:S(2)}, u32[]{:S(2)}) collective-permute-start(bf16[784,512]{1,0:T(8,128)(2,1)} %get-tuple-element.14), channel_id=1, source_target_pairs={{0,248},{4,252},{8,0},{12,4},{16,8},{20,12},{24,16},{28,20},{32,24... | collective-permute-start | bytes 2408456 | tf_op jit(solution)/shard_map/ppermute | solution.py:51
  16.1 0.4 convolution_convert_fusion.refs_8_
  16.6 0.7 copy-done.10
  17.3 0.8 pad_maximum_fusion
  18.1 1.2 collective-permute-start.3
  19.3 0.8 constant_dynamic-update-slice_fusion.1
  20.2 0.8 constant_dynamic-update-slice_fusion
  21.0 1.2 collective-permute-start.8
  22.9 0.1 iota_compare_fusion.2
  23.1 0.2 convert_reduce_fusion
  23.3 0.1 select_reduce_fusion.2
  23.6 0.1 select_reduce_fusion.1
  23.9 0.7 fusion.7
  24.8 0.6 fusion.34
  25.4 1.5 collective-permute-start.5
  26.9 1.2 pad_add_fusion.1.start_ref.refs_1_
  28.1 1.8 %collective-permute-done.1.lane2_ref.refs_5_ = bf16[784,512]{1,0:T(8,128)(2,1)} collective-permute-done((bf16[784,512]{1,0:T(8,128)(2,1)}, bf16[784,512]{1,0:T(8,128)(2,1)}, u32[]{:S(2)}, u32[]{:S(2)}) %collective-permute-start.1) | collective-permute-done | bytes 802848 | tf_op jit(solution)/shard_map/ppermute | solution.py:51
  29.9 2.4 %collective-permute-start.10 = (bf16[1024,512]{1,0:T(8,128)(2,1)}, bf16[1024,512]{1,0:T(8,128)(2,1)S(1)}, u32[]{:S(2)}, u32[]{:S(2)}) collective-permute-start(bf16[1024,512]{1,0:T(8,128)(2,1)} %constant_dynamic-update-slice_fusion), channel_id=1, source_target_pairs={{0,3},{1,0},{2,1},{3,2},{4,7},{5,4},{6,5},{7,6},{8,11},{9,8},{10,9... | collective-permute-start | bytes 3145736 | tf_op jit(solution)/shard_map/ppermute | solution.py:51
  32.3 0.6 fusion.35
  32.9 1.2 collective-permute-done.2.lane3_ref.refs_6_
  34.1 1.0 broadcast_in_dim.86.spots_ref
  35.1 6.1 %head_rows.1 = bf16[1024,512]{1,0:T(8,128)(2,1)} custom-call(s32[8,4]{1,0:T(8,128)} %get-tuple-element.31.table_ref, s32[2]{0:T(128)} %pad_add_fusion.1.start_ref.refs_1_, s32[1024,128]{1,0:T(8,128)} %broadcast_in_dim.86.spots_ref, bf16[3072,512]{1,0:T(8,128)(2,1)} %refs_3_.3, bf16[784,512]{1,0:T(8,128)(2,1)} %copy-done.9, ...), custom_call_target="tpu_custom_call" | custom-call | flops 805306368 | bytes 5242880 | tf_op jit(solution)/shard_map/head_rows/pallas_call | solution.py:132
  41.3 9.0 %collective-permute-start.7 = (bf16[1024,512]{1,0:T(8,128)(2,1)}, bf16[1024,512]{1,0:T(8,128)(2,1)}, u32[]{:S(2)}, u32[]{:S(2)}) collective-permute-start(bf16[1024,512]{1,0:T(8,128)(2,1)} %head_rows.1), channel_id=1, source_target_pairs={{0,252},{4,0},{8,4},{12,8},{16,12},{20,16},{24,20},{28,24},{32,28}... | collective-permute-start | bytes 3145736 | tf_op jit(solution)/shard_map/ppermute | solution.py:51
  50.3 2.6 %collective-permute-start.6 = (bf16[256,512]{1,0:T(8,128)(2,1)S(1)}, bf16[256,512]{1,0:T(8,128)(2,1)S(1)}, u32[]{:S(2)}, u32[]{:S(2)}) collective-permute-start(bf16[256,512]{1,0:T(8,128)(2,1)S(1)} %slice.107), channel_id=1, source_target_pairs={{0,3},{1,0},{2,1},{3,2},{4,7},{5,4},{6,5},{7,6},{8,11},{9,8},{10,9... | collective-permute-start | bytes 786440 | tf_op jit(solution)/shard_map/ppermute | solution.py:51
  52.9 0.8 slice.105.refs_9_
  53.7 0.8 slice.108.refs_11_
  54.5 0.7 slice.109.refs_13_
  55.2 0.7 slice.111.refs_15_
  55.9 8.8 %collective-permute-done.6 = bf16[256,512]{1,0:T(8,128)(2,1)S(1)} collective-permute-done((bf16[256,512]{1,0:T(8,128)(2,1)S(1)}, bf16[256,512]{1,0:T(8,128)(2,1)S(1)}, u32[]{:S(2)}, u32[]{:S(2)}) %collective-permute-start.6) | collective-permute-done | bytes 262176 | tf_op jit(solution)/shard_map/ppermute | solution.py:51
  64.7 0.7 slice.110.refs_14_
  65.3 0.8 pad_maximum_fusion.1.refs_10_
  66.1 0.9 fusion.33
  67.0 0.9 collective-permute-start.9
  67.9 0.9 fusion.32
  68.8 1.8 collective-permute-start.11
  70.7 1.0 broadcast_in_dim.84.refs_2_
  71.7 27.7 %attend.2.hidden_ref = bf16[256,512]{1,0:T(8,128)(2,1)} custom-call(s32[8,4]{1,0:T(8,128)} %get-tuple-element.32.refs_0_, s32[2]{0:T(128)} %pad_add_fusion.1.start_ref.refs_1_, s32[1024,128]{1,0:T(8,128)} %broadcast_in_dim.84.refs_2_, bf16[3072,512]{1,0:T(8,128)(2,1)} %refs_3_.3, bf16[784,512]{1,0:T(8,128)(2,1)} %copy-done.9, ...), custom_call_target="tpu_custom_call" | custom-call | flops 40000000000 | bytes 10485760 | tf_op jit(solution)/shard_map/attend/pallas_call | solution.py:235
  99.4 0.8 copy-done.5
  100.2 0.2 copy-done.6
  100.3 4.4 %mlp.2 = bf16[4,256,128]{2,1,0:T(8,128)(2,1)} custom-call(bf16[256,512]{1,0:T(8,128)(2,1)} %attend.2.hidden_ref, f32[2,512]{1,0:T(2,128)} %gain_ref.3, bf16[512,512]{1,0:T(8,128)(2,1)} %refs_0_.3, bf16[512,512]{1,0:T(8,128)(2,1)} %copy-done.3, bf16[512,512]{1,0:T(8,128)(2,1)} %copy-done.5, bf16[512,512]{1,0:T(8,128)(2,1)} %get-tuple-element.24.refs_3_, ...), custom_call_target="tpu_custom_call" | custom-call | flops 1073741824 | bytes 5242880 | tf_op jit(solution)/shard_map/mlp/pallas_call | solution.py:279
  104.7 3.4 %all-to-all-start = ((bf16[4,256,128]{2,1,0:T(8,128)(2,1)}), bf16[4,256,128]{2,1,0:T(8,128)(2,1)S(1)}, u32[]{:S(2)}, u32[]{:S(2)}) async-start(bf16[4,256,128]{2,1,0:T(8,128)(2,1)} %mlp.2), calls=%async_computation | async-start | bytes 524288 | tf_op jit(solution)/shard_map/all_to_all | solution.py:455
  108.2 1.0 broadcast_in_dim.88.refs_2_
  109.2 27.3 %attend.3.hidden_ref = bf16[256,512]{1,0:T(8,128)(2,1)} custom-call(s32[8,4]{1,0:T(8,128)} %get-tuple-element.30.refs_0_, s32[2]{0:T(128)} %pad_add_fusion.1.start_ref.refs_1_, s32[1024,128]{1,0:T(8,128)} %broadcast_in_dim.88.refs_2_, bf16[3072,512]{1,0:T(8,128)(2,1)} %refs_3_.3, bf16[784,512]{1,0:T(8,128)(2,1)} %copy-done.9, ...), custom_call_target="tpu_custom_call" | custom-call | flops 40000000000 | bytes 10485760 | tf_op jit(solution)/shard_map/attend/pallas_call | solution.py:235
  136.5 0.9 collective-permute-start.12
  137.4 4.4 %mlp.3 = bf16[4,256,128]{2,1,0:T(8,128)(2,1)} custom-call(bf16[256,512]{1,0:T(8,128)(2,1)} %attend.3.hidden_ref, f32[2,512]{1,0:T(2,128)} %gain_ref.3, bf16[512,512]{1,0:T(8,128)(2,1)} %refs_0_.3, bf16[512,512]{1,0:T(8,128)(2,1)} %copy-done.3, bf16[512,512]{1,0:T(8,128)(2,1)} %copy-done.5, bf16[512,512]{1,0:T(8,128)(2,1)} %get-tuple-element.24.refs_3_, ...), custom_call_target="tpu_custom_call" | custom-call | flops 1073741824 | bytes 5242880 | tf_op jit(solution)/shard_map/mlp/pallas_call | solution.py:279
  141.8 4.5 %all-to-all-start.1 = ((bf16[4,256,128]{2,1,0:T(8,128)(2,1)}), bf16[4,256,128]{2,1,0:T(8,128)(2,1)S(1)}, u32[]{:S(2)}, u32[]{:S(2)}) async-start(bf16[4,256,128]{2,1,0:T(8,128)(2,1)} %mlp.3), calls=%async_computation.1 | async-start | bytes 524288 | tf_op jit(solution)/shard_map/all_to_all | solution.py:455
  146.3 0.1 copy.22
  146.4 5.4 %all-to-all-done.1 = bf16[4,256,128]{2,1,0:T(8,128)(2,1)S(1)} async-done(((bf16[4,256,128]{2,1,0:T(8,128)(2,1)}), bf16[4,256,128]{2,1,0:T(8,128)(2,1)S(1)}, u32[]{:S(2)}, u32[]{:S(2)}) %all-to-all-start.1) | async-done | bytes 262176 | tf_op jit(solution)/shard_map/all_to_all | solution.py:455
  151.8 0.7 copy-done.8
  152.6 7.1 %pack_lanes.1 = (bf16[784,128]{1,0:T(8,128)(2,1)}, bf16[784,128]{1,0:T(8,128)(2,1)}, bf16[784,128]{1,0:T(8,128)(2,1)}, bf16[784,128]{1,0:T(8,128)(2,1)}) custom-call(s32[24,4]{1,0:T(8,128)} %copy-done.15, s32[24,128]{1,0:T(8,128)} %get-tuple-element.19.spots_ref, bf16[1024,128]{1,0:T(8,128)(2,1)} %copy-done.11, bf16[1024,128]{1,0:T(8,128)(2,1)} %bitcast.36, ...), custom_call_target="tpu_custom_call" | custom-call | tf_op jit(solution)/shard_map/pack_lanes/pallas_call | solution.py:320
  159.7 4.7 %collective-permute-start.13 = (bf16[784,128]{1,0:T(8,128)(2,1)}, bf16[784,128]{1,0:T(8,128)(2,1)S(1)}, u32[]{:S(2)}, u32[]{:S(2)}) collective-permute-start(bf16[784,128]{1,0:T(8,128)(2,1)} %get-tuple-element.15), channel_id=1, source_target_pairs={{0,252},{4,0},{8,4},{12,8},{16,12},{20,16},{24,20},{28,24},{32,28}... | collective-permute-start | bytes 602120 | tf_op jit(solution)/shard_map/ppermute | solution.py:51
  164.4 0.1 copy.27
  164.5 0.7 pad_add_fusion.spans_ref
  165.2 0.9 collective-permute-done.13.refs_0_
  166.1 3.1 %collective-permute-done.14.refs_2_ = bf16[784,128]{1,0:T(8,128)(2,1)S(1)} collective-permute-done((bf16[784,128]{1,0:T(8,128)(2,1)}, bf16[784,128]{1,0:T(8,128)(2,1)S(1)}, u32[]{:S(2)}, u32[]{:S(2)}) %collective-permute-start.14) | collective-permute-done | bytes 200736 | tf_op jit(solution)/shard_map/ppermute | solution.py:51
  169.2 11.1 %collective-permute-done.15.refs_3_ = bf16[784,128]{1,0:T(8,128)(2,1)S(1)} collective-permute-done((bf16[784,128]{1,0:T(8,128)(2,1)}, bf16[784,128]{1,0:T(8,128)(2,1)S(1)}, u32[]{:S(2)}, u32[]{:S(2)}) %collective-permute-start.15) | collective-permute-done | bytes 200736 | tf_op jit(solution)/shard_map/ppermute | solution.py:51
  180.3 0.7 copy-done.14
  181.0 2.7 %place_rows.1 = bf16[3072,128]{1,0:T(8,128)(2,1)} custom-call(s32[4,3]{1,0:T(4,128)} %pad_add_fusion.spans_ref, bf16[784,128]{1,0:T(8,128)(2,1)} %copy-done.12, bf16[784,128]{1,0:T(8,128)(2,1)} %get-tuple-element.16.refs_1_, bf16[784,128]{1,0:T(8,128)(2,1)} %copy-done.13, bf16[784,128]{1,0:T(8,128)(2,1)} %copy-done.14), custom_call_target="tpu_custom_call" | custom-call | tf_op jit(solution)/shard_map/place_rows/pallas_call | solution.py:344
  (77 shorter events, 1.0 us)
Async XLA Ops:
  0.0 16.1 %copy-start = (bf16[512,384]{1,0:T(8,128)(2,1)S(1)}, bf16[512,384]{1,0:T(8,128)(2,1)}, u32[]{:S(2)}) copy-start(bf16[512,384]{1,0:T(8,128)(2,1)} %param.13) | copy-start | bytes 1179652
  0.0 17.3 %copy-start.16 = (bf16[128,512]{1,0:T(8,128)(2,1)S(1)}, bf16[128,512]{1,0:T(8,128)(2,1)}, u32[]{:S(2)}) copy-start(bf16[128,512]{1,0:T(8,128)(2,1)} %refs_12_.3) | copy-start | bytes 393220
  0.0 19.3 %copy-start.1 = (bf16[512,512]{1,0:T(8,128)(2,1)S(1)}, bf16[512,512]{1,0:T(8,128)(2,1)}, u32[]{:S(2)}) copy-start(bf16[512,512]{1,0:T(8,128)(2,1)} %refs_0_.3) | copy-start | bytes 1572868
  0.0 20.2 %copy-start.2 = (bf16[512,512]{1,0:T(8,128)(2,1)S(1)}, bf16[512,512]{1,0:T(8,128)(2,1)}, u32[]{:S(2)}) copy-start(bf16[512,512]{1,0:T(8,128)(2,1)} %refs_4_.3) | copy-start | bytes 1572868
  1.1 15.0 %copy-start.19 = (s32[2,4]{1,0:T(2,128)}, s32[2,4]{1,0:T(2,128)S(1)}, u32[]{:S(2)}) copy-start(s32[2,4]{1,0:T(2,128)S(1)} %convert_reduce_fusion.1) | copy-start | bytes 100
  3.0 20.0 %copy-start.17 = (s32[2048]{0:T(1024)S(1)}, s32[2048]{0:T(1024)}, u32[]{:S(2)}) copy-start(s32[2048]{0:T(1024)} %param.11) | copy-start | bytes 24580
  6.4 19.0 %collective-permute-start = (bf16[784,512]{1,0:T(8,128)(2,1)}, bf16[784,512]{1,0:T(8,128)(2,1)S(1)}, u32[]{:S(2)}, u32[]{:S(2)}) collective-permute-start(bf16[784,512]{1,0:T(8,128)(2,1)} %get-tuple-element.12), channel_id=1, source_target_pairs={{0,4},{4,8},{8,12},{12,16},{16,20},{20,24},{24,28},{28,32},{32,36}... | collective-permute-start | bytes 2408456 | tf_op jit(solution)/shard_map/ppermute | solution.py:51
  9.5 20.4 %collective-permute-start.1 = (bf16[784,512]{1,0:T(8,128)(2,1)}, bf16[784,512]{1,0:T(8,128)(2,1)}, u32[]{:S(2)}, u32[]{:S(2)}) collective-permute-start(bf16[784,512]{1,0:T(8,128)(2,1)} %get-tuple-element.13), channel_id=1, source_target_pairs={{0,252},{4,0},{8,4},{12,8},{16,12},{20,16},{24,20},{28,24},{32,28}... | collective-permute-start | bytes 2408456 | tf_op jit(solution)/shard_map/ppermute | solution.py:51
  9.8 24.4 %collective-permute-start.2 = (bf16[784,512]{1,0:T(8,128)(2,1)}, bf16[784,512]{1,0:T(8,128)(2,1)}, u32[]{:S(2)}, u32[]{:S(2)}) collective-permute-start(bf16[784,512]{1,0:T(8,128)(2,1)} %get-tuple-element.14), channel_id=1, source_target_pairs={{0,248},{4,252},{8,0},{12,4},{16,8},{20,12},{24,16},{28,20},{32,24... | collective-permute-start | bytes 2408456 | tf_op jit(solution)/shard_map/ppermute | solution.py:51
  16.6 0.7 copy-start.10
  18.1 34.7 %collective-permute-start.3 = (bf16[512,512]{1,0:T(8,128)(2,1)}, bf16[512,512]{1,0:T(8,128)(2,1)S(1)}, u32[]{:S(2)}, u32[]{:S(2)}) collective-permute-start(bf16[512,512]{1,0:T(8,128)(2,1)} %pad_maximum_fusion), channel_id=1, source_target_pairs={{0,1},{1,2},{2,3},{3,0},{4,5},{5,6},{6,7},{7,4},{8,9},{9,10},{10,1... | collective-permute-start | bytes 1572872 | tf_op jit(solution)/shard_map/ppermute | solution.py:51
  21.0 45.1 %collective-permute-start.8 = (bf16[1024,512]{1,0:T(8,128)(2,1)}, bf16[1024,512]{1,0:T(8,128)(2,1)S(1)}, u32[]{:S(2)}, u32[]{:S(2)}) collective-permute-start(bf16[1024,512]{1,0:T(8,128)(2,1)} %constant_dynamic-update-slice_fusion), channel_id=1, source_target_pairs={{0,1},{1,2},{2,3},{3,0},{4,5},{5,6},{6,7},{7,4},{8,9},{9,10},{10,1... | collective-permute-start | bytes 3145736 | tf_op jit(solution)/shard_map/ppermute | solution.py:51
  23.5 17.7 %copy-start.15 = (s32[24,4]{1,0:T(8,128)}, s32[24,4]{1,0:T(8,128)S(1)}, u32[]{:S(2)}) copy-start(s32[24,4]{1,0:T(8,128)S(1)} %fusion.6.table_ref) | copy-start | bytes 1156
  25.4 2.7 %copy-start.9 = (bf16[784,512]{1,0:T(8,128)(2,1)}, bf16[784,512]{1,0:T(8,128)(2,1)S(1)}, u32[]{:S(2)}) copy-start(bf16[784,512]{1,0:T(8,128)(2,1)S(1)} %collective-permute-done.lane0_ref.refs_4_) | copy-start | bytes 2408452
  25.4 24.9 %collective-permute-start.5 = (bf16[512,512]{1,0:T(8,128)(2,1)}, bf16[512,512]{1,0:T(8,128)(2,1)S(1)}, u32[]{:S(2)}, u32[]{:S(2)}) collective-permute-start(bf16[512,512]{1,0:T(8,128)(2,1)} %pad_maximum_fusion), channel_id=1, source_target_pairs={{0,3},{1,0},{2,1},{3,2},{4,7},{5,4},{6,5},{7,6},{8,11},{9,8},{10,9... | collective-permute-start | bytes 1572872 | tf_op jit(solution)/shard_map/ppermute | solution.py:51
  29.9 38.0 %collective-permute-start.10 = (bf16[1024,512]{1,0:T(8,128)(2,1)}, bf16[1024,512]{1,0:T(8,128)(2,1)S(1)}, u32[]{:S(2)}, u32[]{:S(2)}) collective-permute-start(bf16[1024,512]{1,0:T(8,128)(2,1)} %constant_dynamic-update-slice_fusion), channel_id=1, source_target_pairs={{0,3},{1,0},{2,1},{3,2},{4,7},{5,4},{6,5},{7,6},{8,11},{9,8},{10,9... | collective-permute-start | bytes 3145736 | tf_op jit(solution)/shard_map/ppermute | solution.py:51
  41.3 29.4 %collective-permute-start.7 = (bf16[1024,512]{1,0:T(8,128)(2,1)}, bf16[1024,512]{1,0:T(8,128)(2,1)}, u32[]{:S(2)}, u32[]{:S(2)}) collective-permute-start(bf16[1024,512]{1,0:T(8,128)(2,1)} %head_rows.1), channel_id=1, source_target_pairs={{0,252},{4,0},{8,4},{12,8},{16,12},{20,16},{24,20},{28,24},{32,28}... | collective-permute-start | bytes 3145736 | tf_op jit(solution)/shard_map/ppermute | solution.py:51
  50.3 14.4 %collective-permute-start.6 = (bf16[256,512]{1,0:T(8,128)(2,1)S(1)}, bf16[256,512]{1,0:T(8,128)(2,1)S(1)}, u32[]{:S(2)}, u32[]{:S(2)}) collective-permute-start(bf16[256,512]{1,0:T(8,128)(2,1)S(1)} %slice.107), channel_id=1, source_target_pairs={{0,3},{1,0},{2,1},{3,2},{4,7},{5,4},{6,5},{7,6},{8,11},{9,8},{10,9... | collective-permute-start | bytes 786440 | tf_op jit(solution)/shard_map/ppermute | solution.py:51
  52.9 12.5 %collective-permute-start.4 = (bf16[256,512]{1,0:T(8,128)(2,1)S(1)}, bf16[256,512]{1,0:T(8,128)(2,1)S(1)}, u32[]{:S(2)}, u32[]{:S(2)}) collective-permute-start(bf16[256,512]{1,0:T(8,128)(2,1)S(1)} %slice.106), channel_id=1, source_target_pairs={{0,1},{1,2},{2,3},{3,0},{4,5},{5,6},{6,7},{7,4},{8,9},{9,10},{10,1... | collective-permute-start | bytes 786440 | tf_op jit(solution)/shard_map/ppermute | solution.py:51
  54.5 16.1 %copy-start.18 = (s32[1,1024,1]{1,0,2:T(1,128)S(1)}, s32[1,1024,1]{1,0,2:T(1,128)}, u32[]{:S(2)}) copy-start(s32[1,1024,1]{1,0,2:T(1,128)} %get-tuple-element.29) | copy-start | bytes 12292
  67.0 32.3 %copy-start.3 = (bf16[512,512]{1,0:T(8,128)(2,1)}, bf16[512,512]{1,0:T(8,128)(2,1)S(1)}, u32[]{:S(2)}) copy-start(bf16[512,512]{1,0:T(8,128)(2,1)S(1)} %get-tuple-element.26.refs_1_) | copy-start | bytes 1572868
  67.0 32.3 %collective-permute-start.9 = (bf16[512,512]{1,0:T(8,128)(2,1)S(1)}, bf16[512,512]{1,0:T(8,128)(2,1)S(1)}, u32[]{:S(2)}, u32[]{:S(2)}) collective-permute-start(bf16[512,512]{1,0:T(8,128)(2,1)S(1)} %get-tuple-element.26.refs_1_), channel_id=1, source_target_pairs={{0,1},{1,2},{2,3},{3,0},{4,5},{5,6},{6,7},{7,4},{8,9},{9,10},{10,1... | collective-permute-start | bytes 1572872 | tf_op jit(solution)/shard_map/ppermute | solution.py:51
  68.8 30.5 %copy-start.4 = (bf16[512,512]{1,0:T(8,128)(2,1)}, bf16[512,512]{1,0:T(8,128)(2,1)S(1)}, u32[]{:S(2)}) copy-start(bf16[512,512]{1,0:T(8,128)(2,1)S(1)} %get-tuple-element.23.refs_7_) | copy-start | bytes 1572868
  68.8 30.6 %collective-permute-start.11 = (bf16[512,512]{1,0:T(8,128)(2,1)S(1)}, bf16[512,512]{1,0:T(8,128)(2,1)S(1)}, u32[]{:S(2)}, u32[]{:S(2)}) collective-permute-start(bf16[512,512]{1,0:T(8,128)(2,1)S(1)} %get-tuple-element.23.refs_7_), channel_id=1, source_target_pairs={{0,3},{1,0},{2,1},{3,2},{4,7},{5,4},{6,5},{7,6},{8,11},{9,8},{10,9... | collective-permute-start | bytes 1572872 | tf_op jit(solution)/shard_map/ppermute | solution.py:51
  99.4 0.8 copy-start.5
  99.4 0.9 copy-start.6
  104.7 31.7 %all-to-all-start = ((bf16[4,256,128]{2,1,0:T(8,128)(2,1)}), bf16[4,256,128]{2,1,0:T(8,128)(2,1)S(1)}, u32[]{:S(2)}, u32[]{:S(2)}) async-start(bf16[4,256,128]{2,1,0:T(8,128)(2,1)} %mlp.2), calls=%async_computation | async-start | bytes 524288 | tf_op jit(solution)/shard_map/all_to_all | solution.py:455
  136.5 9.8 %copy-start.20 = (s32[2,4]{1,0:T(2,128)S(1)}, s32[2,4]{1,0:T(2,128)}, u32[]{:S(2)}) copy-start(s32[2,4]{1,0:T(2,128)} %copy-done.19) | copy-start | bytes 100
  136.5 15.3 %copy-start.7 = (bf16[4,256,128]{2,1,0:T(8,128)(2,1)}, bf16[4,256,128]{2,1,0:T(8,128)(2,1)S(1)}, u32[]{:S(2)}) copy-start(bf16[4,256,128]{2,1,0:T(8,128)(2,1)S(1)} %all-to-all-done) | copy-start | bytes 786436
  136.5 15.3 %collective-permute-start.12 = (bf16[1024,128]{1,0:T(8,128)(2,1)S(1)}, bf16[1024,128]{1,0:T(8,128)(2,1)S(1)}, u32[]{:S(2)}, u32[]{:S(2)}) collective-permute-start(bf16[1024,128]{1,0:T(8,128)(2,1)S(1)} %bitcast.34), channel_id=1, source_target_pairs={{0,4},{4,8},{8,12},{12,16},{16,20},{20,24},{24,28},{28,32},{32,36}... | collective-permute-start | bytes 786440 | tf_op jit(solution)/shard_map/ppermute | solution.py:51
  141.8 10.0 %all-to-all-start.1 = ((bf16[4,256,128]{2,1,0:T(8,128)(2,1)}), bf16[4,256,128]{2,1,0:T(8,128)(2,1)S(1)}, u32[]{:S(2)}, u32[]{:S(2)}) async-start(bf16[4,256,128]{2,1,0:T(8,128)(2,1)} %mlp.3), calls=%async_computation.1 | async-start | bytes 524288 | tf_op jit(solution)/shard_map/all_to_all | solution.py:455
  151.8 0.7 copy-start.8
  151.8 0.8 copy-start.11
  159.7 6.4 %collective-permute-start.13 = (bf16[784,128]{1,0:T(8,128)(2,1)}, bf16[784,128]{1,0:T(8,128)(2,1)S(1)}, u32[]{:S(2)}, u32[]{:S(2)}) collective-permute-start(bf16[784,128]{1,0:T(8,128)(2,1)} %get-tuple-element.15), channel_id=1, source_target_pairs={{0,252},{4,0},{8,4},{12,8},{16,12},{20,16},{24,20},{28,24},{32,28}... | collective-permute-start | bytes 602120 | tf_op jit(solution)/shard_map/ppermute | solution.py:51
  164.4 4.8 %collective-permute-start.14 = (bf16[784,128]{1,0:T(8,128)(2,1)}, bf16[784,128]{1,0:T(8,128)(2,1)S(1)}, u32[]{:S(2)}, u32[]{:S(2)}) collective-permute-start(bf16[784,128]{1,0:T(8,128)(2,1)} %get-tuple-element.17), channel_id=1, source_target_pairs={{0,4},{4,8},{8,12},{12,16},{16,20},{20,24},{24,28},{28,32},{32,36}... | collective-permute-start | bytes 602120 | tf_op jit(solution)/shard_map/ppermute | solution.py:51
  164.4 15.9 %collective-permute-start.15 = (bf16[784,128]{1,0:T(8,128)(2,1)}, bf16[784,128]{1,0:T(8,128)(2,1)S(1)}, u32[]{:S(2)}, u32[]{:S(2)}) collective-permute-start(bf16[784,128]{1,0:T(8,128)(2,1)} %get-tuple-element.18), channel_id=1, source_target_pairs={{0,8},{4,12},{8,16},{12,20},{16,24},{20,28},{24,32},{28,36},{32,40... | collective-permute-start | bytes 602120 | tf_op jit(solution)/shard_map/ppermute | solution.py:51
  166.1 14.3 %copy-start.12 = (bf16[784,128]{1,0:T(8,128)(2,1)}, bf16[784,128]{1,0:T(8,128)(2,1)S(1)}, u32[]{:S(2)}) copy-start(bf16[784,128]{1,0:T(8,128)(2,1)S(1)} %collective-permute-done.13.refs_0_) | copy-start | bytes 602116
  169.2 11.1 %copy-start.13 = (bf16[784,128]{1,0:T(8,128)(2,1)}, bf16[784,128]{1,0:T(8,128)(2,1)S(1)}, u32[]{:S(2)}) copy-start(bf16[784,128]{1,0:T(8,128)(2,1)S(1)} %collective-permute-done.14.refs_2_) | copy-start | bytes 602116
  180.3 0.7 copy-start.14

commit v2 on v0

v2 whole, which is shorter than its diff:
```python
import functools

import jax
import jax.numpy as jnp
from jax import lax
from jax.experimental import pallas as pl
from jax.experimental.pallas import tpu as pltpu
from jax.sharding import PartitionSpec as P

PATCH = 1024
HEAD_DIM = 16
GROUP_HEADS = 8
EPSILON = 1e-05
LOG2E = 1.4426950408889634

TILE = 16
BLOCK = 128
WINDOW = 160
MOST_RUN = 768
PIECE = MOST_RUN + TILE
LANES = 4
BLOCKS = PATCH // BLOCK

F32 = jnp.float32
BF16 = jnp.bfloat16

ANY = pl.BlockSpec(memory_space=pl.ANY)
VMEM = pl.BlockSpec(memory_space=pltpu.VMEM)
SMEM = pl.BlockSpec(memory_space=pltpu.SMEM)
HBM = pl.BlockSpec(memory_space=pltpu.HBM)


def nt_dot(left, right):
    return lax.dot_general(left, right, (((1,), (1,)), ((), ())), preferred_element_type=F32)


def nn_dot(left, right):
    return jnp.dot(left, right, preferred_element_type=F32)


def tn_dot(left, right):
    return lax.dot_general(left, right, (((0,), (0,)), ((), ())), preferred_element_type=F32)


def aligned(value):
    return pl.multiple_of(value, TILE)


def shifted(value, axis, steps):
    count = lax.axis_size(axis)
    pairs = [(source, (source + steps) % count) for source in range(count)]
    return lax.ppermute(value, axis, pairs)


def layer_norm(values, gain):
    values = values.astype(F32)
    centred = values - jnp.mean(values, axis=-1, keepdims=True)
    spread = jnp.mean(centred * centred, axis=-1, keepdims=True)
    return (centred * lax.rsqrt(spread + EPSILON) * gain).astype(BF16)


def window_start(first, capacity):
    return aligned(jnp.minimum(lax.div(first, TILE) * TILE, capacity - PIECE))


def cut_kernel(bricks, shard, ranks_ref, feats_ref, *rest):
    outs, counts_ref, sems = rest[:LANES], rest[LANES], rest[LANES + 1]
    capacity = feats_ref.shape[0]
    me = lax.axis_index("brick")
    ranks = ranks_ref[...]
    loads = []
    for lane in (3, 2, 0, 1):
        target = lax.rem(me - lane + 1 + bricks, bricks)
        first = jnp.sum((ranks < target * shard).astype(jnp.int32))
        counts_ref[0, lane] = first
        rows = pl.ds(window_start(first, capacity), PIECE)
        loads.append(pltpu.make_async_copy(feats_ref.at[rows], outs[lane], sems.at[lane]))
        loads[-1].start()
    for lane in range(LANES):
        target = lax.rem(me - lane + 1 + bricks, bricks)
        counts_ref[1, lane] = jnp.sum((ranks < (target + 1) * shard).astype(jnp.int32))
    for load in loads:
        load.wait()


def cut_windows(bricks, shard, ranks, feats):
    piece = jax.ShapeDtypeStruct((PIECE, feats.shape[1]), feats.dtype)
    return pl.pallas_call(
        functools.partial(cut_kernel, bricks, shard),
        out_shape=(piece,) * LANES + (jax.ShapeDtypeStruct((2, LANES), jnp.int32),),
        in_specs=[VMEM, HBM],
        out_specs=(VMEM,) * LANES + (SMEM,),
        scratch_shapes=[pltpu.SemaphoreType.DMA((LANES,))],
        compiler_params=pltpu.CompilerParams(vmem_limit_bytes=8 << 20),
        name="cut_windows",
    )(ranks, feats)


def index_kernel(bricks, capacity, shift_ref, order_ref, after_ref, spots_ref, table_ref, wide_ref):
    me = lax.axis_index("brick")
    order = order_ref[...]
    rows = order.shape[0]
    lane_of = jnp.zeros_like(order)
    spot_of = jnp.zeros_like(order)
    column = lax.broadcasted_iota(jnp.int32, (1, BLOCK), 1)
    leads = jnp.zeros((1, BLOCK), F32)
    for lane in range(LANES):
        source = lax.rem(me + lane - 1 + bricks, bricks)
        slot = order - source * capacity
        mine = (slot >= 0) & (slot < capacity)
        first = jnp.min(jnp.where(mine, slot, capacity), keepdims=True)
        start = jnp.minimum(first & -TILE, capacity - PIECE)
        lane_of = jnp.where(mine, lane, lane_of)
        spot_of = jnp.where(mine, slot - start + lane * WINDOW, spot_of)
        leads = jnp.where(column == lane, (first - start).astype(F32), leads)
    ahead = PATCH - shift_ref[0]
    down, across = lax.div(ahead, BLOCK), lax.rem(ahead, BLOCK)
    wide_ref[...] = jnp.full_like(wide_ref, -1)
    for index, value in enumerate((lane_of, spot_of)):
        turned = pltpu.roll(value, across, 1)
        wide_ref[index, 0, pl.ds(down, rows), :] = turned
        wide_ref[index, 1, pl.ds(down + 1, rows), :] = turned
    height = spots_ref.shape[0]
    near = lax.broadcasted_iota(jnp.int32, (height, BLOCK), 1) >= across
    lane_wide = jnp.where(near, wide_ref[0, 0, :height, :], wide_ref[0, 1, :height, :])
    spot_wide = jnp.where(near, wide_ref[1, 0, :height, :], wide_ref[1, 1, :height, :])
    held = jnp.zeros((height, BLOCK), F32)
    wide_column = lax.broadcasted_iota(jnp.int32, (height, BLOCK), 1)
    for lane in range(LANES):
        found = jnp.sum((lane_wide == lane).astype(F32), axis=1, keepdims=True)
        held = jnp.where(wide_column == lane, found, held)
    below = lax.broadcasted_iota(jnp.int32, (height, height), 1) < lax.broadcasted_iota(
        jnp.int32, (height, height), 0
    )
    before = nn_dot(below.astype(F32).astype(BF16), held.astype(BF16))
    table = jnp.minimum((leads + before).astype(jnp.int32) & -TILE, PIECE - WINDOW)
    table_ref[...] = table
    spots = spot_wide
    for lane in range(LANES):
        spots = jnp.where(lane_wide == lane, spot_wide - table[:, lane : lane + 1], spots)
    spots_ref[...] = jnp.where(lane_wide < 0, -1, spots)


def index_tables(bricks, capacity, shift, order, after):
    height = 3 * BLOCKS
    table = jax.ShapeDtypeStruct((height, BLOCK), jnp.int32)
    return pl.pallas_call(
        functools.partial(index_kernel, bricks, capacity),
        out_shape=(table, table),
        in_specs=[SMEM, VMEM, HBM],
        out_specs=(VMEM, VMEM),
        scratch_shapes=[pltpu.VMEM((2, 2, height + 2 * BLOCKS, BLOCK), jnp.int32)],
        compiler_params=pltpu.CompilerParams(vmem_limit_bytes=4 << 20),
        name="index_tables",
    )(shift, order, after)


def hot_rows(spots):
    tall = lax.broadcasted_iota(jnp.int32, (LANES * WINDOW, BLOCK), 0)
    return jnp.where(tall == spots, 1.0, 0.0).astype(BF16)


def gather_block(table_ref, spots_ref, place, lane_refs):
    windows = [
        lane_refs[lane][pl.ds(aligned(table_ref[place, lane]), WINDOW), :]
        for lane in range(LANES)
    ]
    stacked = jnp.concatenate(windows, axis=0)
    return tn_dot(hot_rows(spots_ref[place : place + 1, :]), stacked).astype(BF16)


def head_kernel(table_ref, spots_ref, *refs):
    out_ref = refs[-1]
    for block in range(BLOCKS):
        rows = slice(block * BLOCK, (block + 1) * BLOCK)
        out_ref[rows, :] = gather_block(table_ref, spots_ref, block, refs[:LANES])


def head_rows(table, spots, lanes, after):
    width = lanes[0].shape[1]
    return pl.pallas_call(
        head_kernel,
        out_shape=jax.ShapeDtypeStruct((PATCH, width), BF16),
        in_specs=[SMEM] + [VMEM] * (1 + LANES) + [ANY] * len(after),
        out_specs=VMEM,
        cost_estimate=pl.CostEstimate(
            flops=2 * PATCH * 768 * width, bytes_accessed=5 << 20, transcendentals=0
        ),
        compiler_params=pltpu.CompilerParams(vmem_limit_bytes=12 << 20),
        name="head_rows",
    )(table, spots, *lanes, *after)


def project_kernel(part, extras, table_ref, spots_ref, *refs):
    lane_refs, gain_ref = refs[:LANES], refs[LANES]
    near_ref, ahead_ref, far_a_ref, far_b_ref, behind_ref = refs[LANES + 1 : LANES + 6]
    extra_ref = refs[LANES + 6]
    own_ref, keys_ref, values_ref, query_ref, rows_ref, normed_ref, stack_ref = refs[-7:]
    queries = own_ref.shape[0]
    span = GROUP_HEADS * HEAD_DIM
    for group, ref in enumerate((near_ref, ahead_ref, None, behind_ref)):
        for kind in range(3):
            if ref is None:
                source = (far_a_ref, far_b_ref)[kind // 2]
                at = kind % 2 * span
            else:
                source, at = ref, kind * span
            stack_ref[kind, group * span : (group + 1) * span, :] = source[at : at + span, :]
    gain = gain_ref[0:1, :]
    for quarter in range(4):
        for block in range(quarter * 2, quarter * 2 + 2):
            rows = slice(block * BLOCK, (block + 1) * BLOCK)
            found = gather_block(table_ref, spots_ref, part * BLOCKS + BLOCKS + block, lane_refs)
            if part == 1:
                found = found + extra_ref[rows, :]
            rows_ref[rows, :] = found
            normed_ref[rows, :] = layer_norm(found, gain)
        rows = slice(quarter * 256, (quarter + 1) * 256)
        normed = normed_ref[rows, :]
        keys_ref[rows, :] = nt_dot(normed, stack_ref[1]).astype(BF16)
        values_ref[:, rows] = nt_dot(stack_ref[2], normed).astype(BF16)
    own_rows = pl.ds(pl.multiple_of(lax.axis_index("mp") * queries, queries), queries)
    own_ref[...] = rows_ref[own_rows, :]
    query = nt_dot(stack_ref[0], normed_ref[own_rows, :])
    query_ref[...] = (query * (HEAD_DIM ** (-0.5) * LOG2E)).astype(BF16)


def project(part, table, spots, lanes, gains, early, extra, queries):
    width = lanes[0].shape[1]
    shape = lambda *dims: jax.ShapeDtypeStruct(dims, BF16)
    return pl.pallas_call(
        functools.partial(project_kernel, part, len(extra)),
        out_shape=(shape(queries, width), shape(PATCH, width), shape(width, PATCH), shape(width, queries)),
        in_specs=[SMEM] + [VMEM] * (LANES + 7) + ([VMEM] + [ANY] * (len(extra) - 1) if part else [ANY] * len(extra)),
        out_specs=(VMEM,) * 4,
        scratch_shapes=[
            pltpu.VMEM((PATCH, width), BF16),
            pltpu.VMEM((PATCH, width), BF16),
            pltpu.VMEM((3, width, width), BF16),
        ],
        cost_estimate=pl.CostEstimate(flops=10 * 10**9, bytes_accessed=10 << 20, transcendentals=0),
        compiler_params=pltpu.CompilerParams(vmem_limit_bytes=20 << 20),
        name="project_last" if part else "project_first",
    )(table, spots, *lanes, gains, *early, *extra)


def attend_kernel(after, own_ref, keys_ref, values_ref, query_ref, *refs):
    near_ref, ahead_ref, far_b_ref, behind_ref = refs[:4]
    out_ref, mixed_ref, score_ref = refs[4 + after :]
    queries = own_ref.shape[0]
    groups = 4
    span = GROUP_HEADS * HEAD_DIM

    head_of_row = lax.broadcasted_iota(jnp.int32, (span, queries), 0) // HEAD_DIM
    ones = jnp.ones((HEAD_DIM, BLOCK), BF16)

    def query_of(group, head):
        query = query_ref[group * span : (group + 1) * span, :]
        return jnp.where(head_of_row == head, query, jnp.zeros_like(query))

    def score(slot, group, query, chunk, highest):
        rows = slice(chunk * BLOCK, (chunk + 1) * BLOCK)
        scores = nn_dot(keys_ref[rows, group * span : (group + 1) * span], query)
        score_ref[slot, rows, :] = scores
        top = jnp.max(scores.reshape(BLOCK // 8, 8, queries), axis=0)
        return top if highest is None else jnp.maximum(highest, top)

    highest = None
    query = query_of(0, 0)
    for chunk in range(BLOCKS):
        highest = score(0, 0, query, chunk, highest)

    def head_step(head, highest):
        for group in range(groups):
            top = jnp.max(highest, axis=0, keepdims=True)
            later = (group + 1) % groups
            query = query_of(later, head if later else jnp.minimum(head + 1, GROUP_HEADS - 1))
            rows = pl.ds(pl.multiple_of(group * span + head * HEAD_DIM, HEAD_DIM), HEAD_DIM)
            total, highest = None, None
            for chunk in range(BLOCKS):
                keys = slice(chunk * BLOCK, (chunk + 1) * BLOCK)
                highest = score(later % 2, later, query, chunk, highest)
                weights = jnp.exp2(score_ref[group % 2, keys, :] - top).astype(BF16)
                values = jnp.concatenate([values_ref[rows, keys], ones], axis=0)
                term = nn_dot(values, weights)
                total = term if total is None else total + term
            mixed_ref[rows, :] = (total[:HEAD_DIM] / total[HEAD_DIM : HEAD_DIM + 1]).astype(BF16)
        return highest

    lax.fori_loop(0, GROUP_HEADS, head_step, highest)
    mixed = None
    for group in range(groups):
        rows = slice(group * span, (group + 1) * span)
        weight = (near_ref, ahead_ref, far_b_ref, behind_ref)[group]
        weight = weight[span : 2 * span, :] if group == 2 else weight[3 * span :, :]
        term = tn_dot(mixed_ref[rows, :], weight).astype(BF16).astype(F32)
        mixed = term if mixed is None else mixed + term
    out_ref[...] = (own_ref[...].astype(F32) + mixed).astype(BF16)


def attend(part, projected, early, after):
    queries, width = projected[0].shape
    near, ahead, far_a, far_b, behind = early
    return pl.pallas_call(
        functools.partial(attend_kernel, len(after)),
        out_shape=jax.ShapeDtypeStruct((queries, width), BF16),
        in_specs=[VMEM] * 8 + [ANY] * len(after),
        out_specs=VMEM,
        scratch_shapes=[
            pltpu.VMEM((width, queries), BF16),
            pltpu.VMEM((2, PATCH, queries), F32),
        ],
        cost_estimate=pl.CostEstimate(
            flops=30 * 10**9, bytes_accessed=5 << 20, transcendentals=8 << 20
        ),
        compiler_params=pltpu.CompilerParams(vmem_limit_bytes=16 << 20),
        name="attend_last" if part else "attend_first",
    )(*projected, near, ahead, far_b, behind, *after)


def mlp_kernel(groups, hidden_ref, gain_ref, *refs):
    up_refs, down_refs = refs[:groups], refs[groups : 2 * groups]
    wide_ref, before_ref, result_ref = refs[-3:]
    outs = refs[-3 - groups : -3]
    queries, width = hidden_ref.shape
    normed = layer_norm(hidden_ref[...], gain_ref[1:2, :])
    pieces = [(group, chunk) for group in range(groups) for chunk in range(queries // BLOCK)]

    def widen(index):
        group, chunk = pieces[index]
        before_ref[index % 2] = nn_dot(normed[chunk * BLOCK : (chunk + 1) * BLOCK], up_refs[group][...])

    widen(0)
    for index, (group, chunk) in enumerate(pieces):
        if index + 1 < len(pieces):
            widen(index + 1)
        wide = before_ref[index % 2]
        wide_ref[group, chunk * BLOCK : (chunk + 1) * BLOCK, :] = (
            wide * (0.5 + 0.5 * lax.erf(wide * 0.5**0.5))
        ).astype(BF16)
    total = None
    for group in range(groups):
        term = nn_dot(wide_ref[group], down_refs[group][...]).astype(BF16).astype(F32)
        total = term if total is None else total + term
    result_ref[...] = (hidden_ref[...].astype(F32) + total).astype(BF16)
    cut = width // groups
    rank = lax.axis_index("mp")
    for step in range(groups):
        column = pl.multiple_of(lax.rem(rank + step, groups) * cut, cut)
        outs[step][...] = result_ref[:, pl.ds(column, cut)]


def mlp(hidden, gains, up, down, after):
    groups = len(up)
    rows, width = hidden.shape
    middle = up[0].shape[1]
    return pl.pallas_call(
        functools.partial(mlp_kernel, groups),
        out_shape=(jax.ShapeDtypeStruct((rows, width // groups), BF16),) * groups,
        in_specs=[VMEM] * (2 + 2 * groups) + [ANY] * len(after),
        out_specs=(VMEM,) * groups,
        scratch_shapes=[
            pltpu.VMEM((groups, rows, middle), BF16),
            pltpu.VMEM((2, BLOCK, middle), F32),
            pltpu.VMEM((rows, width), BF16),
        ],
        cost_estimate=pl.CostEstimate(
            flops=4 * rows * width * middle * groups, bytes_accessed=5 << 20, transcendentals=0
        ),
        compiler_params=pltpu.CompilerParams(vmem_limit_bytes=16 << 20),
        name="mlp",
    )(hidden, gains, *up, *down, *after)


def pack_kernel(shift_ref, table_ref, spots_ref, *rest):
    sources, rest = rest[:12], rest[12:]
    outs, lanes_ref, rows_ref = rest[:LANES], rest[LANES], rest[LANES + 1]
    queries = sources[0].shape[0]
    lanes_ref[...] = jnp.zeros_like(lanes_ref)
    rank = lax.axis_index("mp")
    for index, source in enumerate(sources):
        sender = lax.rem(rank - index % 4 + 4, 4)
        at = pl.multiple_of(index // 4 * PATCH + sender * queries, queries)
        rows_ref[pl.ds(at, queries), :] = source[...]
    begin = lax.div(PATCH - shift_ref[0], BLOCK)
    for step in range(2 * BLOCKS + 1):
        place = jnp.minimum(begin + step, 3 * BLOCKS - 1)
        fresh = begin + step < 3 * BLOCKS
        spots = jnp.where(fresh, spots_ref[pl.ds(place, 1), :], -1)
        rows = rows_ref[pl.ds(pl.multiple_of(place * BLOCK, BLOCK), BLOCK), :]
        sent = nn_dot(hot_rows(spots), rows).astype(BF16)
        for lane in range(LANES):
            window = pl.ds(aligned(table_ref[place, lane]), WINDOW)
            lanes_ref[lane, window, :] = (
                lanes_ref[lane, window, :] + sent[lane * WINDOW : (lane + 1) * WINDOW]
            )
    for lane in range(LANES):
        outs[lane][...] = lanes_ref[lane]


def pack_lanes(shift, table, spots, sources):
    width = sources[0].shape[1]
    return pl.pallas_call(
        pack_kernel,
        out_shape=(jax.ShapeDtypeStruct((PIECE, width), BF16),) * LANES,
        in_specs=[SMEM, SMEM] + [VMEM] * (1 + len(sources)),
        out_specs=(VMEM,) * LANES,
        scratch_shapes=[
            pltpu.VMEM((LANES, PIECE, width), BF16),
            pltpu.VMEM((3 * PATCH, width), BF16),
        ],
        compiler_params=pltpu.CompilerParams(vmem_limit_bytes=12 << 20),
        name="pack_lanes",
    )(shift, table, spots, *sources)


def place_kernel(counts_ref, *refs):
    pieces, out_ref = refs[:LANES], refs[LANES]
    capacity = out_ref.shape[0]
    out_ref[...] = jnp.zeros_like(out_ref)
    row = lax.broadcasted_iota(jnp.int32, (PIECE, out_ref.shape[1]), 0)
    for lane in range(LANES):
        start = window_start(counts_ref[0, lane], capacity)
        slots = row + start
        mine = (slots >= counts_ref[0, lane]) & (slots < counts_ref[1, lane])
        window = pl.ds(start, PIECE)
        out_ref[window, :] = jnp.where(mine, pieces[lane][...], out_ref[window, :])


def place_rows(counts, pieces, capacity):
    width = pieces[0].shape[1]
    return pl.pallas_call(
        place_kernel,
        out_shape=jax.ShapeDtypeStruct((capacity, width), BF16),
        in_specs=[SMEM] + [VMEM] * LANES,
        out_specs=VMEM,
        compiler_params=pltpu.CompilerParams(vmem_limit_bytes=12 << 20),
        name="place_rows",
    )(counts, *pieces)


def per_device(
    voxel_feats,
    slot_rank,
    curve_order,
    patch_shift,
    qkv_weight,
    proj_weight,
    up_weight,
    down_weight,
    norm_gains,
):
    bricks = lax.axis_size("brick")
    parts = lax.axis_size("mp")
    capacity, width = voxel_feats.shape
    shard = curve_order.shape[0]
    queries = PATCH // parts

    piece0, own, piece2, piece3, counts = cut_windows(
        bricks, shard, slot_rank.reshape(capacity // 128, 128), voxel_feats
    )
    lane3 = shifted(piece3, "brick", -2)
    lane2 = shifted(piece2, "brick", -1)
    lane0 = shifted(piece0, "brick", 1)
    lanes = (lane0, own, lane2, lane3)
    counts, qkv_weight, proj_weight = lax.optimization_barrier((counts, qkv_weight, proj_weight))

    span = GROUP_HEADS * HEAD_DIM
    column = jnp.arange(3 * span, dtype=jnp.int32)
    place = (column // HEAD_DIM % 3) * span + column // (3 * HEAD_DIM) * HEAD_DIM + column % HEAD_DIM
    order = (place[None, :] == column[:, None]).astype(BF16)
    qkv_rows = nt_dot(order, qkv_weight).astype(BF16)
    near = jnp.concatenate([qkv_rows, proj_weight], axis=0)
    ahead, behind = shifted(near, "mp", 1), shifted(near, "mp", -1)
    half = near.shape[0] // 2
    far_a, far_b = shifted(ahead[:half], "mp", 1), shifted(behind[half:], "mp", -1)
    early = (near, ahead, far_a, far_b, behind)
    ahead, behind, up_out, down_out = lax.optimization_barrier(
        (ahead, behind, up_weight, down_weight)
    )
    up_ahead, up_behind = shifted(up_out, "mp", 1), shifted(up_out, "mp", -1)
    down_ahead, down_behind = shifted(down_out, "mp", 1), shifted(down_out, "mp", -1)

    spots, table = index_tables(
        bricks, capacity, patch_shift, curve_order.reshape(shard // BLOCK, BLOCK), near
    )
    head = head_rows(table, spots, lanes, (far_a, far_b))
    head_next = shifted(head, "brick", -1)
    common = (table, spots, lanes, norm_gains, early)
    projected = project(0, *common, (head,), queries)
    up_ahead, down_behind, *projected = lax.optimization_barrier(
        (up_ahead, down_behind, *projected)
    )
    up_far, down_far = shifted(up_ahead, "mp", 1), shifted(down_behind, "mp", -1)
    up = (up_weight, up_ahead, up_far, up_behind)
    down = (down_weight, down_ahead, down_far, down_behind)
    hidden = attend(0, projected, early, ())
    projected = project(1, *common, (head_next, hidden), queries)
    blocks = mlp(hidden, norm_gains, up, down, (projected[0],))
    first = [blocks[0]] + [shifted(blocks[step], "mp", step) for step in range(1, parts)]
    hidden = attend(1, projected, early, (blocks[0],))
    blocks = mlp(hidden, norm_gains, up, down, ())
    last = [blocks[0]] + [shifted(blocks[step], "mp", step) for step in range(1, parts)]

    def onward(step):
        pairs = [
            (brick * parts + rank, (brick + 1) % bricks * parts + (rank + step) % parts)
            for brick in range(bricks)
            for rank in range(parts)
        ]
        return lax.ppermute(blocks[step], ("brick", "mp"), pairs)

    tail = [onward(step) for step in range(parts)]
    back0, back1, back2, back3 = pack_lanes(patch_shift, table, spots, (*tail, *first, *last))
    pieces = (
        shifted(back0, "brick", -1),
        back1,
        shifted(back2, "brick", 1),
        shifted(back3, "brick", 2),
    )
    return place_rows(counts, pieces, capacity)


def solution(mesh):
    return jax.shard_map(
        per_device,
        mesh=mesh,
        in_specs=(
            P("brick", None),
            P("brick"),
            P("brick"),
            P(),
            P(None, "mp"),
            P("mp", None),
            P(None, "mp"),
            P("mp", None),
            P(),
        ),
        out_specs=P("brick", "mp"),
        check_vma=False,
    )
```

time: 444 us -> 133 us (0.30)
  matrix products: 114 us -> 0.41 us
  other arithmetic: 98.9 us -> 0.05 us
  waiting for transfers between devices: 128 us -> 33.7 us
  local copies, waits for them, and re-layouts: 63.7 us -> 2.71 us
  Pallas kernels: 0 us -> 40.7 us
  starting transfers between devices: 23.6 us -> 54.2 us
  between operations: 14.3 us -> 0.86 us
    dot_general x11 -> x1, matrix products: 114 us -> 0.41 us  [nt_dot(): lax.dot_general(left, right, (((1,), (1,)), ((), ())), preferred_element_...]
    psum x1 -> x0, waiting for transfers between devices: 65.5 us -> none  [per_device(): mixed = lax.psum(head_partial, 'mp').astype(jnp.float32)]
    sub x4 -> x0, other arithmetic: 50.3 us -> none  [one_group(): weights_exp = jnp.exp(scores - highest)]
    pallas_call x0 -> x11, Pallas kernels: none -> 40.7 us  [the longest x2 21.1 us: attend(): pl.pallas_call(functools.partial(attend_kernel, len(after)), out_shape=ja...]
    gather x6 -> x0, local copies, waits for them, and re-layouts: 37 us -> none  [the longest x4 13.3 us: per_device(): rows = voxel_feats[jnp.minimum(slots, capacity - 1)]]
    all_to_all x1 -> x0, waiting for transfers between devices: 25.6 us -> none  [summed_on_arrival(): lax.all_to_all(blocks, axis, split_axis=0, concat_axis=0, tiled=True)]
    ppermute x8 -> x23, starting transfers between devices: 19.1 us -> 43.2 us  [shifted(): return lax.ppermute(value, axis, pairs)]
    select_n x11 -> x0, other arithmetic: 14.8 us -> none  [the longest x4 7.88 us: per_device(): piece = jnp.where(valid[:, None], rows, jnp.zeros_like(rows))]
  transfers between devices with their start and end apart: 10 -> 27, of which waited for: 8 -> 11; matrix products, arithmetic and copies ran while one was open for 5% -> 0% of each run, Pallas kernels for 0% -> 16%
where the time goes in v2:
time: 133 us
  starting transfers between devices  54.2 us (41%)
  Pallas kernels  40.7 us (31%)
  waiting for transfers between devices  33.7 us (25%)
  local copies, waits for them, and re-layouts  2.71 us (2%)
    ppermute x23, starting transfers between devices, shifted(): return lax.ppermute(value, axis, pairs)  43.2 us
    ppermute x23, waiting for transfers between devices, shifted(): return lax.ppermute(value, axis, pairs)  32.4 us
    pallas_call x2, Pallas kernels, attend(): pl.pallas_call(functools.partial(attend_kernel, len(after)), out_shape=ja...  21.1 us
    ppermute x4, starting transfers between devices, onward(): return lax.ppermute(blocks[step], ('brick', 'mp'), pairs)  10.9 us
    pallas_call x2, Pallas kernels, project(): pl.pallas_call(functools.partial(project_kernel, part, len(extra)), out_s...  8.49 us
    pallas_call x2, Pallas kernels, mlp(): pl.pallas_call(functools.partial(mlp_kernel, groups), out_shape=(jax.Shap...  3.27 us
    unnamed x16, local copies, waits for them, and re-layouts  2.67 us
  transfers between devices with their start and end apart: 27, of which 11 were waited for; matrix products, arithmetic and copies ran while one was open for 0% of the time, Pallas kernels for 16%

profile of v2, /device:TPU:1, one launch (start us, length us, event | category | flops | bytes accessed | tf_op | source)
XLA Modules:
  0.0 132.6 jit_solution(1516262622842949706)
XLA Ops:
  0.0 1.9 %copy-done.1 = bf16[3072,512]{1,0:T(8,128)(2,1)S(1)} copy-done((bf16[3072,512]{1,0:T(8,128)(2,1)S(1)}, bf16[3072,512]{1,0:T(8,128)(2,1)}, u32[]{:S(2)}) %copy-start.1) | copy-done | bytes 3145752
  1.9 0.7 copy-done.5
  2.7 1.6 %cut_windows.1 = (bf16[784,512]{1,0:T(8,128)(2,1)S(1)}, bf16[784,512]{1,0:T(8,128)(2,1)S(1)}, bf16[784,512]{1,0:T(8,128)(2,1)S(1)}, bf16[784,512]{1,0:T(8,128)(2,1)S(1)}, s32[2,4]{1,0:T(2,128)S(1)}) custom-call(s32[24,128]{1,0:T(8,128)S(1)} %bitcast.3, bf16[3072,512]{1,0:T(8,128)(2,1)S(1)} %copy-done.1), custom_call_target="tpu_custom_call" | custom-call | tf_op jit(solution)/shard_map/cut_windows/pallas_call | solution.py:88
  4.3 3.1 %collective-permute-start = (bf16[784,512]{1,0:T(8,128)(2,1)S(1)}, bf16[784,512]{1,0:T(8,128)(2,1)S(1)}, u32[]{:S(2)}, u32[]{:S(2)}) collective-permute-start(bf16[784,512]{1,0:T(8,128)(2,1)S(1)} %get-tuple-element.49), channel_id=1, source_target_pairs={{0,4},{4,8},{8,12},{12,16},{16,20},{20,24},{24,28},{28,32},{32,36}... | collective-permute-start | bytes 2408456 | tf_op jit(solution)/shard_map/ppermute | solution.py:52
  7.4 0.3 collective-permute-start.1
  7.7 6.3 %collective-permute-start.2 = (bf16[784,512]{1,0:T(8,128)(2,1)S(1)}, bf16[784,512]{1,0:T(8,128)(2,1)S(1)}, u32[]{:S(2)}, u32[]{:S(2)}) collective-permute-start(bf16[784,512]{1,0:T(8,128)(2,1)S(1)} %get-tuple-element.52), channel_id=1, source_target_pairs={{0,248},{4,252},{8,0},{12,4},{16,8},{20,12},{24,16},{28,20},{32,24... | collective-permute-start | bytes 2408456 | tf_op jit(solution)/shard_map/ppermute | solution.py:52
  14.0 0.4 convolution_convert_fusion
  14.5 0.0 copy-start.4
  14.5 2.6 %collective-permute-start.5 = (bf16[512,512]{1,0:T(8,128)(2,1)S(1)}, bf16[512,512]{1,0:T(8,128)(2,1)S(1)}, u32[]{:S(2)}, u32[]{:S(2)}) collective-permute-start(bf16[512,512]{1,0:T(8,128)(2,1)S(1)} %pad_maximum_fusion.after_ref.refs_5_.refs_0_), channel_id=1, source_target_pairs={{0,3},{1,0},{2,1},{3,2},{4,7},{5,4},{6,5},{7,6},{8,11},{9,8},{10,9... | collective-permute-start | bytes 1572872 | tf_op jit(solution)/shard_map/ppermute | solution.py:52
  17.0 0.0 collective-permute-start.3
  17.0 9.3 %collective-permute-done.5.refs_9_.refs_3_ = bf16[512,512]{1,0:T(8,128)(2,1)S(1)} collective-permute-done((bf16[512,512]{1,0:T(8,128)(2,1)S(1)}, bf16[512,512]{1,0:T(8,128)(2,1)S(1)}, u32[]{:S(2)}, u32[]{:S(2)}) %collective-permute-start.5) | collective-permute-done | bytes 524320 | tf_op jit(solution)/shard_map/ppermute | solution.py:52
  26.4 3.5 %collective-permute-start.6 = (bf16[256,512]{1,0:T(8,128)(2,1)S(1)}, bf16[256,512]{1,0:T(8,128)(2,1)S(1)}, u32[]{:S(2)}, u32[]{:S(2)}) collective-permute-start(bf16[256,512]{1,0:T(8,128)(2,1)S(1)} %slice.9), channel_id=1, source_target_pairs={{0,3},{1,0},{2,1},{3,2},{4,7},{5,4},{6,5},{7,6},{8,11},{9,8},{10,9... | collective-permute-start | bytes 786440 | tf_op jit(solution)/shard_map/ppermute | solution.py:52
  29.9 0.0 collective-permute-done.3.refs_6_.refs_1_
  29.9 0.1 collective-permute-start.4
  30.7 0.6 index_tables.1
  31.3 1.9 %collective-permute-done.6.refs_5_.refs_8_.refs_2_ = bf16[256,512]{1,0:T(8,128)(2,1)S(1)} collective-permute-done((bf16[256,512]{1,0:T(8,128)(2,1)S(1)}, bf16[256,512]{1,0:T(8,128)(2,1)S(1)}, u32[]{:S(2)}, u32[]{:S(2)}) %collective-permute-start.6) | collective-permute-done | bytes 262176 | tf_op jit(solution)/shard_map/ppermute | solution.py:52
  33.2 0.0 collective-permute-start.8
  33.2 3.2 %collective-permute-done.4.refs_4_.refs_7_ = bf16[256,512]{1,0:T(8,128)(2,1)S(1)} collective-permute-done((bf16[256,512]{1,0:T(8,128)(2,1)S(1)}, bf16[256,512]{1,0:T(8,128)(2,1)S(1)}, u32[]{:S(2)}, u32[]{:S(2)}) %collective-permute-start.4) | collective-permute-done | bytes 262176 | tf_op jit(solution)/shard_map/ppermute | solution.py:52
  36.4 0.0 collective-permute-start.11
  36.4 1.4 %collective-permute-start.9 = (bf16[512,512]{1,0:T(8,128)(2,1)S(1)}, bf16[512,512]{1,0:T(8,128)(2,1)S(1)}, u32[]{:S(2)}, u32[]{:S(2)}) collective-permute-start(bf16[512,512]{1,0:T(8,128)(2,1)S(1)} %copy-done.3), channel_id=1, source_target_pairs={{0,3},{1,0},{2,1},{3,2},{4,7},{5,4},{6,5},{7,6},{8,11},{9,8},{10,9... | collective-permute-start | bytes 1572872 | tf_op jit(solution)/shard_map/ppermute | solution.py:52
  37.8 0.0 collective-permute-done.1.refs_2_
  37.8 0.2 collective-permute-start.12
  38.0 1.8 %head_rows.1.refs_10_ = bf16[1024,512]{1,0:T(8,128)(2,1)S(1)} custom-call(s32[24,128]{1,0:T(8,128)S(1)} %get-tuple-element.47.table_ref, s32[24,128]{1,0:T(8,128)S(1)} %get-tuple-element.48.spots_ref, bf16[784,512]{1,0:T(8,128)(2,1)S(1)} %collective-permute-done.refs_0_, bf16[784,512]{1,0:T(8,128)(2,1)S(1)} %get-tuple-element.50.refs_1_, ...), custom_call_target="tpu_custom_call" | custom-call | flops 805306368 | bytes 5242880 | tf_op jit(solution)/shard_map/head_rows/pallas_call | solution.py:181
  39.8 7.7 %collective-permute-start.7 = (bf16[1024,512]{1,0:T(8,128)(2,1)S(1)}, bf16[1024,512]{1,0:T(8,128)(2,1)S(1)}, u32[]{:S(2)}, u32[]{:S(2)}) collective-permute-start(bf16[1024,512]{1,0:T(8,128)(2,1)S(1)} %head_rows.1.refs_10_), channel_id=1, source_target_pairs={{0,252},{4,0},{8,4},{12,8},{16,12},{20,16},{24,20},{28,24},{32,28}... | collective-permute-start | bytes 3145736 | tf_op jit(solution)/shard_map/ppermute | solution.py:52
  47.5 4.3 %project_first.1 = (bf16[256,512]{1,0:T(8,128)(2,1)S(1)}, bf16[1024,512]{1,0:T(8,128)(2,1)S(1)}, bf16[512,1024]{1,0:T(8,128)(2,1)S(1)}, bf16[512,256]{1,0:T(8,128)(2,1)S(1)}) custom-call(s32[24,128]{1,0:T(8,128)S(1)} %get-tuple-element.47.table_ref, s32[24,128]{1,0:T(8,128)S(1)} %get-tuple-element.48.spots_ref, ...), custom_call_target="tpu_custom_call" | custom-call | flops 10000000000 | bytes 10485760 | tf_op jit(solution)/shard_map/project_first/pallas_call | solution.py:231
  51.8 2.5 %collective-permute-done.9.refs_7_ = bf16[512,512]{1,0:T(8,128)(2,1)S(1)} collective-permute-done((bf16[512,512]{1,0:T(8,128)(2,1)S(1)}, bf16[512,512]{1,0:T(8,128)(2,1)S(1)}, u32[]{:S(2)}, u32[]{:S(2)}) %collective-permute-start.9) | collective-permute-done | bytes 524320 | tf_op jit(solution)/shard_map/ppermute | solution.py:52
  54.3 0.0 collective-permute-start.10
  54.3 2.7 %collective-permute-start.13 = (bf16[512,512]{1,0:T(8,128)(2,1)S(1)}, bf16[512,512]{1,0:T(8,128)(2,1)S(1)}, u32[]{:S(2)}, u32[]{:S(2)}) collective-permute-start(bf16[512,512]{1,0:T(8,128)(2,1)S(1)} %collective-permute-done.9.refs_7_), channel_id=1, source_target_pairs={{0,3},{1,0},{2,1},{3,2},{4,7},{5,4},{6,5},{7,6},{8,11},{9,8},{10,9... | collective-permute-start | bytes 1572872 | tf_op jit(solution)/shard_map/ppermute | solution.py:52
  56.9 10.5 %attend_first.1.refs_11_.hidden_ref = bf16[256,512]{1,0:T(8,128)(2,1)S(1)} custom-call(bf16[256,512]{1,0:T(8,128)(2,1)S(1)} %get-tuple-element.59.own_ref, bf16[1024,512]{1,0:T(8,128)(2,1)S(1)} %get-tuple-element.60.keys_ref, bf16[512,1024]{1,0:T(8,128)(2,1)S(1)} %get-tuple-element.61.values_ref, bf16[512,256]{1,0:T(8,128)(2,1)S(1)} %get-tuple-element.62.query_ref, ...), custom_call_target="tpu_custom_call" | custom-call | flops 30000001024 | bytes 5242880 | tf_op jit(solution)/shard_map/attend_first/pallas_call | solution.py:304
  67.5 4.2 %project_last.1 = (bf16[256,512]{1,0:T(8,128)(2,1)S(1)}, bf16[1024,512]{1,0:T(8,128)(2,1)S(1)}, bf16[512,1024]{1,0:T(8,128)(2,1)S(1)}, bf16[512,256]{1,0:T(8,128)(2,1)S(1)}) custom-call(s32[24,128]{1,0:T(8,128)S(1)} %get-tuple-element.47.table_ref, s32[24,128]{1,0:T(8,128)S(1)} %get-tuple-element.48.spots_ref, ...), custom_call_target="tpu_custom_call" | custom-call | flops 10000000000 | bytes 10485760 | tf_op jit(solution)/shard_map/project_last/pallas_call | solution.py:231
  71.7 0.0 collective-permute-done.11.refs_3_
  71.7 0.0 collective-permute-done.12.refs_5_
  71.8 0.0 collective-permute-done.13.refs_6_
  71.8 1.6 %mlp.2 = (bf16[256,128]{1,0:T(8,128)(2,1)S(1)}, bf16[256,128]{1,0:T(8,128)(2,1)S(1)}, bf16[256,128]{1,0:T(8,128)(2,1)S(1)}, bf16[256,128]{1,0:T(8,128)(2,1)S(1)}) custom-call(bf16[256,512]{1,0:T(8,128)(2,1)S(1)} %attend_first.1.refs_11_.hidden_ref, f32[2,512]{1,0:T(2,128)S(1)} %copy-done.4, bf16[512,512]{1,0:T(8,128)(2,1)S(1)} %copy-done.2, ...), custom_call_target="tpu_custom_call" | custom-call | flops 1073741824 | bytes 5242880 | tf_op jit(solution)/shard_map/mlp/pallas_call | solution.py:357
  73.4 10.5 %attend_last.1.hidden_ref = bf16[256,512]{1,0:T(8,128)(2,1)S(1)} custom-call(bf16[256,512]{1,0:T(8,128)(2,1)S(1)} %get-tuple-element.63.refs_8_.own_ref, bf16[1024,512]{1,0:T(8,128)(2,1)S(1)} %get-tuple-element.64.keys_ref, bf16[512,1024]{1,0:T(8,128)(2,1)S(1)} %get-tuple-element.65.values_ref, bf16[512,256]{1,0:T(8,128)(2,1)S(1)} %get-tuple-element.66.query_ref, ...), custom_call_target="tpu_custom_call" | custom-call | flops 30000001024 | bytes 5242880 | tf_op jit(solution)/shard_map/attend_last/pallas_call | solution.py:304
  83.9 1.6 %mlp.3 = (bf16[256,128]{1,0:T(8,128)(2,1)S(1)}, bf16[256,128]{1,0:T(8,128)(2,1)S(1)}, bf16[256,128]{1,0:T(8,128)(2,1)S(1)}, bf16[256,128]{1,0:T(8,128)(2,1)S(1)}) custom-call(bf16[256,512]{1,0:T(8,128)(2,1)S(1)} %attend_last.1.hidden_ref, f32[2,512]{1,0:T(2,128)S(1)} %copy-done.4, bf16[512,512]{1,0:T(8,128)(2,1)S(1)} %copy-done.2, ...), custom_call_target="tpu_custom_call" | custom-call | flops 1073741824 | bytes 5242880 | tf_op jit(solution)/shard_map/mlp/pallas_call | solution.py:357
  85.6 6.4 %collective-permute-start.14 = (bf16[256,128]{1,0:T(8,128)(2,1)S(1)}, bf16[256,128]{1,0:T(8,128)(2,1)S(1)}, u32[]{:S(2)}, u32[]{:S(2)}) collective-permute-start(bf16[256,128]{1,0:T(8,128)(2,1)S(1)} %get-tuple-element.70.rest_8_), channel_id=1, source_target_pairs={{0,4},{1,5},{2,6},{3,7},{4,8},{5,9},{6,10},{7,11},{8,12},{9,13},{1... | collective-permute-start | bytes 196616 | tf_op jit(solution)/shard_map/ppermute | solution.py:511
  92.0 0.0 collective-permute-start.15
  92.0 2.8 %collective-permute-start.16 = (bf16[256,128]{1,0:T(8,128)(2,1)S(1)}, bf16[256,128]{1,0:T(8,128)(2,1)S(1)}, u32[]{:S(2)}, u32[]{:S(2)}) collective-permute-start(bf16[256,128]{1,0:T(8,128)(2,1)S(1)} %get-tuple-element.72), channel_id=1, source_target_pairs={{0,6},{1,7},{2,4},{3,5},{4,10},{5,11},{6,8},{7,9},{8,14},{9,15},{1... | collective-permute-start | bytes 196616 | tf_op jit(solution)/shard_map/ppermute | solution.py:511
  94.8 1.7 %collective-permute-start.17 = (bf16[256,128]{1,0:T(8,128)(2,1)S(1)}, bf16[256,128]{1,0:T(8,128)(2,1)S(1)}, u32[]{:S(2)}, u32[]{:S(2)}) collective-permute-start(bf16[256,128]{1,0:T(8,128)(2,1)S(1)} %get-tuple-element.73), channel_id=1, source_target_pairs={{0,7},{1,4},{2,5},{3,6},{4,11},{5,8},{6,9},{7,10},{8,15},{9,12},{1... | collective-permute-start | bytes 196616 | tf_op jit(solution)/shard_map/ppermute | solution.py:511
  96.5 0.6 collective-permute-start.21
  97.1 0.6 collective-permute-done.14.rest_0_
  97.7 1.0 collective-permute-start.22
  98.7 0.7 collective-permute-done.15.rest_1_
  99.3 1.4 %collective-permute-start.23 = (bf16[256,128]{1,0:T(8,128)(2,1)S(1)}, bf16[256,128]{1,0:T(8,128)(2,1)S(1)}, u32[]{:S(2)}, u32[]{:S(2)}) collective-permute-start(bf16[256,128]{1,0:T(8,128)(2,1)S(1)} %get-tuple-element.73), channel_id=1, source_target_pairs={{0,3},{1,0},{2,1},{3,2},{4,7},{5,4},{6,5},{7,6},{8,11},{9,8},{10,9... | collective-permute-start | bytes 196616 | tf_op jit(solution)/shard_map/ppermute | solution.py:52
  100.8 0.0 collective-permute-done.16.rest_2_
  100.8 0.5 collective-permute-start.18
  101.2 0.0 collective-permute-done.17.rest_3_
  101.2 4.0 %collective-permute-start.19 = (bf16[256,128]{1,0:T(8,128)(2,1)S(1)}, bf16[256,128]{1,0:T(8,128)(2,1)S(1)}, u32[]{:S(2)}, u32[]{:S(2)}) collective-permute-start(bf16[256,128]{1,0:T(8,128)(2,1)S(1)} %get-tuple-element.75), channel_id=1, source_target_pairs={{0,2},{1,3},{2,0},{3,1},{4,6},{5,7},{6,4},{7,5},{8,10},{9,11},{10,... | collective-permute-start | bytes 196616 | tf_op jit(solution)/shard_map/ppermute | solution.py:52
  105.2 0.0 collective-permute-done.21.rest_9_
  105.2 2.1 %collective-permute-start.20 = (bf16[256,128]{1,0:T(8,128)(2,1)S(1)}, bf16[256,128]{1,0:T(8,128)(2,1)S(1)}, u32[]{:S(2)}, u32[]{:S(2)}) collective-permute-start(bf16[256,128]{1,0:T(8,128)(2,1)S(1)} %get-tuple-element.76), channel_id=1, source_target_pairs={{0,3},{1,0},{2,1},{3,2},{4,7},{5,4},{6,5},{7,6},{8,11},{9,8},{10,9... | collective-permute-start | bytes 196616 | tf_op jit(solution)/shard_map/ppermute | solution.py:52
  107.3 0.0 collective-permute-done.22.rest_10_
  107.3 0.0 collective-permute-done.23.rest_11_
  107.3 0.0 collective-permute-done.18.rest_5_
  107.3 0.3 collective-permute-done.19.rest_6_
  107.6 1.2 collective-permute-done.20.rest_7_
  108.8 1.9 %pack_lanes.1 = (bf16[784,128]{1,0:T(8,128)(2,1)S(1)}, bf16[784,128]{1,0:T(8,128)(2,1)S(1)}, bf16[784,128]{1,0:T(8,128)(2,1)S(1)}, bf16[784,128]{1,0:T(8,128)(2,1)S(1)}) custom-call(s32[1]{0:T(128)S(6)} %copy.10.shift_ref, s32[24,128]{1,0:T(8,128)S(1)} %get-tuple-element.47.table_ref, s32[24,128]{1,0:T(8,128)S(1)} %get-tuple-element.48.spots_ref, ...), custom_call_target="tpu_custom_call" | custom-call | tf_op jit(solution)/shard_map/pack_lanes/pallas_call | solution.py:403
  110.7 5.8 %collective-permute-start.24 = (bf16[784,128]{1,0:T(8,128)(2,1)S(1)}, bf16[784,128]{1,0:T(8,128)(2,1)S(1)}, u32[]{:S(2)}, u32[]{:S(2)}) collective-permute-start(bf16[784,128]{1,0:T(8,128)(2,1)S(1)} %get-tuple-element.77), channel_id=1, source_target_pairs={{0,252},{4,0},{8,4},{12,8},{16,12},{20,16},{24,20},{28,24},{32,28}... | collective-permute-start | bytes 602120 | tf_op jit(solution)/shard_map/ppermute | solution.py:52
  116.5 0.0 collective-permute-start.25
  116.5 0.2 collective-permute-start.26
  116.7 1.7 %collective-permute-done.24.refs_0_ = bf16[784,128]{1,0:T(8,128)(2,1)S(1)} collective-permute-done((bf16[784,128]{1,0:T(8,128)(2,1)S(1)}, bf16[784,128]{1,0:T(8,128)(2,1)S(1)}, u32[]{:S(2)}, u32[]{:S(2)}) %collective-permute-start.24) | collective-permute-done | bytes 200736 | tf_op jit(solution)/shard_map/ppermute | solution.py:52
  118.3 1.1 collective-permute-done.25.refs_2_
  119.5 11.1 %collective-permute-done.26.refs_3_ = bf16[784,128]{1,0:T(8,128)(2,1)S(1)} collective-permute-done((bf16[784,128]{1,0:T(8,128)(2,1)S(1)}, bf16[784,128]{1,0:T(8,128)(2,1)S(1)}, u32[]{:S(2)}, u32[]{:S(2)}) %collective-permute-start.26) | collective-permute-done | bytes 200736 | tf_op jit(solution)/shard_map/ppermute | solution.py:52
  130.6 2.0 %place_rows.1 = bf16[3072,128]{1,0:T(8,128)(2,1)} custom-call(s32[2,4]{1,0:T(2,128)S(1)} %get-tuple-element.44.counts_ref, bf16[784,128]{1,0:T(8,128)(2,1)S(1)} %collective-permute-done.24.refs_0_, bf16[784,128]{1,0:T(8,128)(2,1)S(1)} %get-tuple-element.78.refs_1_, bf16[784,128]{1,0:T(8,128)(2,1)S(1)} %collective-permute-done.25.refs_2_, ...), custom_call_target="tpu_custom_call" | custom-call | tf_op jit(solution)/shard_map/place_rows/pallas_call | solution.py:432
  (22 shorter events, 0.1 us)
Async XLA Ops:
  0.0 14.0 %copy-start = (bf16[512,384]{1,0:T(8,128)(2,1)S(1)}, bf16[512,384]{1,0:T(8,128)(2,1)}, u32[]{:S(2)}) copy-start(bf16[512,384]{1,0:T(8,128)(2,1)} %param.13) | copy-start | bytes 1179652
  0.0 1.9 %copy-start.1 = (bf16[3072,512]{1,0:T(8,128)(2,1)S(1)}, bf16[3072,512]{1,0:T(8,128)(2,1)}, u32[]{:S(2)}) copy-start(bf16[3072,512]{1,0:T(8,128)(2,1)} %feats_ref.1) | copy-start | bytes 9437188
  1.9 0.7 copy-start.5
  2.7 11.8 %copy-start.7 = (bf16[128,512]{1,0:T(8,128)(2,1)S(1)}, bf16[128,512]{1,0:T(8,128)(2,1)}, u32[]{:S(2)}) copy-start(bf16[128,512]{1,0:T(8,128)(2,1)} %param.14) | copy-start | bytes 393220
  2.7 28.0 %copy-start.6 = (s32[2048]{0:T(1024)S(1)}, s32[2048]{0:T(1024)}, u32[]{:S(2)}) copy-start(s32[2048]{0:T(1024)} %param.11) | copy-start | bytes 24580
  2.7 30.6 %copy-start.2 = (bf16[512,512]{1,0:T(8,128)(2,1)S(1)}, bf16[512,512]{1,0:T(8,128)(2,1)}, u32[]{:S(2)}) copy-start(bf16[512,512]{1,0:T(8,128)(2,1)} %refs_0_.3) | copy-start | bytes 1572868
  2.7 33.8 %copy-start.3 = (bf16[512,512]{1,0:T(8,128)(2,1)S(1)}, bf16[512,512]{1,0:T(8,128)(2,1)}, u32[]{:S(2)}) copy-start(bf16[512,512]{1,0:T(8,128)(2,1)} %refs_4_.7) | copy-start | bytes 1572868
  4.3 32.1 %collective-permute-start = (bf16[784,512]{1,0:T(8,128)(2,1)S(1)}, bf16[784,512]{1,0:T(8,128)(2,1)S(1)}, u32[]{:S(2)}, u32[]{:S(2)}) collective-permute-start(bf16[784,512]{1,0:T(8,128)(2,1)S(1)} %get-tuple-element.49), channel_id=1, source_target_pairs={{0,4},{4,8},{8,12},{12,16},{16,20},{20,24},{24,28},{28,32},{32,36}... | collective-permute-start | bytes 2408456 | tf_op jit(solution)/shard_map/ppermute | solution.py:52
  7.4 30.4 %collective-permute-start.1 = (bf16[784,512]{1,0:T(8,128)(2,1)S(1)}, bf16[784,512]{1,0:T(8,128)(2,1)S(1)}, u32[]{:S(2)}, u32[]{:S(2)}) collective-permute-start(bf16[784,512]{1,0:T(8,128)(2,1)S(1)} %get-tuple-element.51), channel_id=1, source_target_pairs={{0,252},{4,0},{8,4},{12,8},{16,12},{20,16},{24,20},{28,24},{32,28}... | collective-permute-start | bytes 2408456 | tf_op jit(solution)/shard_map/ppermute | solution.py:52
  7.7 30.3 %collective-permute-start.2 = (bf16[784,512]{1,0:T(8,128)(2,1)S(1)}, bf16[784,512]{1,0:T(8,128)(2,1)S(1)}, u32[]{:S(2)}, u32[]{:S(2)}) collective-permute-start(bf16[784,512]{1,0:T(8,128)(2,1)S(1)} %get-tuple-element.52), channel_id=1, source_target_pairs={{0,248},{4,252},{8,0},{12,4},{16,8},{20,12},{24,16},{28,20},{32,24... | collective-permute-start | bytes 2408456 | tf_op jit(solution)/shard_map/ppermute | solution.py:52
  14.5 33.0 %copy-start.4 = (f32[2,512]{1,0:T(2,128)S(1)}, f32[2,512]{1,0:T(2,128)}, u32[]{:S(2)}) copy-start(f32[2,512]{1,0:T(2,128)} %gain_ref.3) | copy-start | bytes 12292
  14.5 11.9 %collective-permute-start.5 = (bf16[512,512]{1,0:T(8,128)(2,1)S(1)}, bf16[512,512]{1,0:T(8,128)(2,1)S(1)}, u32[]{:S(2)}, u32[]{:S(2)}) collective-permute-start(bf16[512,512]{1,0:T(8,128)(2,1)S(1)} %pad_maximum_fusion.after_ref.refs_5_.refs_0_), channel_id=1, source_target_pairs={{0,3},{1,0},{2,1},{3,2},{4,7},{5,4},{6,5},{7,6},{8,11},{9,8},{10,9... | collective-permute-start | bytes 1572872 | tf_op jit(solution)/shard_map/ppermute | solution.py:52
  17.0 12.9 %collective-permute-start.3 = (bf16[512,512]{1,0:T(8,128)(2,1)S(1)}, bf16[512,512]{1,0:T(8,128)(2,1)S(1)}, u32[]{:S(2)}, u32[]{:S(2)}) collective-permute-start(bf16[512,512]{1,0:T(8,128)(2,1)S(1)} %pad_maximum_fusion.after_ref.refs_5_.refs_0_), channel_id=1, source_target_pairs={{0,1},{1,2},{2,3},{3,0},{4,5},{5,6},{6,7},{7,4},{8,9},{9,10},{10,1... | collective-permute-start | bytes 1572872 | tf_op jit(solution)/shard_map/ppermute | solution.py:52
  26.4 6.8 %collective-permute-start.6 = (bf16[256,512]{1,0:T(8,128)(2,1)S(1)}, bf16[256,512]{1,0:T(8,128)(2,1)S(1)}, u32[]{:S(2)}, u32[]{:S(2)}) collective-permute-start(bf16[256,512]{1,0:T(8,128)(2,1)S(1)} %slice.9), channel_id=1, source_target_pairs={{0,3},{1,0},{2,1},{3,2},{4,7},{5,4},{6,5},{7,6},{8,11},{9,8},{10,9... | collective-permute-start | bytes 786440 | tf_op jit(solution)/shard_map/ppermute | solution.py:52
  29.9 6.5 %collective-permute-start.4 = (bf16[256,512]{1,0:T(8,128)(2,1)S(1)}, bf16[256,512]{1,0:T(8,128)(2,1)S(1)}, u32[]{:S(2)}, u32[]{:S(2)}) collective-permute-start(bf16[256,512]{1,0:T(8,128)(2,1)S(1)} %slice.8), channel_id=1, source_target_pairs={{0,1},{1,2},{2,3},{3,0},{4,5},{5,6},{6,7},{7,4},{8,9},{9,10},{10,1... | collective-permute-start | bytes 786440 | tf_op jit(solution)/shard_map/ppermute | solution.py:52
  33.2 18.5 %collective-permute-start.8 = (bf16[512,512]{1,0:T(8,128)(2,1)S(1)}, bf16[512,512]{1,0:T(8,128)(2,1)S(1)}, u32[]{:S(2)}, u32[]{:S(2)}) collective-permute-start(bf16[512,512]{1,0:T(8,128)(2,1)S(1)} %copy-done.2), channel_id=1, source_target_pairs={{0,1},{1,2},{2,3},{3,0},{4,5},{5,6},{6,7},{7,4},{8,9},{9,10},{10,1... | collective-permute-start | bytes 1572872 | tf_op jit(solution)/shard_map/ppermute | solution.py:52
  36.4 35.3 %collective-permute-start.11 = (bf16[512,512]{1,0:T(8,128)(2,1)S(1)}, bf16[512,512]{1,0:T(8,128)(2,1)S(1)}, u32[]{:S(2)}, u32[]{:S(2)}) collective-permute-start(bf16[512,512]{1,0:T(8,128)(2,1)S(1)} %copy-done.2), channel_id=1, source_target_pairs={{0,3},{1,0},{2,1},{3,2},{4,7},{5,4},{6,5},{7,6},{8,11},{9,8},{10,9... | collective-permute-start | bytes 1572872 | tf_op jit(solution)/shard_map/ppermute | solution.py:52
  36.4 17.8 %collective-permute-start.9 = (bf16[512,512]{1,0:T(8,128)(2,1)S(1)}, bf16[512,512]{1,0:T(8,128)(2,1)S(1)}, u32[]{:S(2)}, u32[]{:S(2)}) collective-permute-start(bf16[512,512]{1,0:T(8,128)(2,1)S(1)} %copy-done.3), channel_id=1, source_target_pairs={{0,3},{1,0},{2,1},{3,2},{4,7},{5,4},{6,5},{7,6},{8,11},{9,8},{10,9... | collective-permute-start | bytes 1572872 | tf_op jit(solution)/shard_map/ppermute | solution.py:52
  37.8 33.9 %collective-permute-start.12 = (bf16[512,512]{1,0:T(8,128)(2,1)S(1)}, bf16[512,512]{1,0:T(8,128)(2,1)S(1)}, u32[]{:S(2)}, u32[]{:S(2)}) collective-permute-start(bf16[512,512]{1,0:T(8,128)(2,1)S(1)} %copy-done.3), channel_id=1, source_target_pairs={{0,1},{1,2},{2,3},{3,0},{4,5},{5,6},{6,7},{7,4},{8,9},{9,10},{10,1... | collective-permute-start | bytes 1572872 | tf_op jit(solution)/shard_map/ppermute | solution.py:52
  39.8 27.7 %collective-permute-start.7 = (bf16[1024,512]{1,0:T(8,128)(2,1)S(1)}, bf16[1024,512]{1,0:T(8,128)(2,1)S(1)}, u32[]{:S(2)}, u32[]{:S(2)}) collective-permute-start(bf16[1024,512]{1,0:T(8,128)(2,1)S(1)} %head_rows.1.refs_10_), channel_id=1, source_target_pairs={{0,252},{4,0},{8,4},{12,8},{16,12},{20,16},{24,20},{28,24},{32,28}... | collective-permute-start | bytes 3145736 | tf_op jit(solution)/shard_map/ppermute | solution.py:52
  54.3 17.5 %collective-permute-start.10 = (bf16[512,512]{1,0:T(8,128)(2,1)S(1)}, bf16[512,512]{1,0:T(8,128)(2,1)S(1)}, u32[]{:S(2)}, u32[]{:S(2)}) collective-permute-start(bf16[512,512]{1,0:T(8,128)(2,1)S(1)} %collective-permute-done.8.refs_1_), channel_id=1, source_target_pairs={{0,1},{1,2},{2,3},{3,0},{4,5},{5,6},{6,7},{7,4},{8,9},{9,10},{10,1... | collective-permute-start | bytes 1572872 | tf_op jit(solution)/shard_map/ppermute | solution.py:52
  54.3 17.5 %collective-permute-start.13 = (bf16[512,512]{1,0:T(8,128)(2,1)S(1)}, bf16[512,512]{1,0:T(8,128)(2,1)S(1)}, u32[]{:S(2)}, u32[]{:S(2)}) collective-permute-start(bf16[512,512]{1,0:T(8,128)(2,1)S(1)} %collective-permute-done.9.refs_7_), channel_id=1, source_target_pairs={{0,3},{1,0},{2,1},{3,2},{4,7},{5,4},{6,5},{7,6},{8,11},{9,8},{10,9... | collective-permute-start | bytes 1572872 | tf_op jit(solution)/shard_map/ppermute | solution.py:52
  85.6 12.1 %collective-permute-start.14 = (bf16[256,128]{1,0:T(8,128)(2,1)S(1)}, bf16[256,128]{1,0:T(8,128)(2,1)S(1)}, u32[]{:S(2)}, u32[]{:S(2)}) collective-permute-start(bf16[256,128]{1,0:T(8,128)(2,1)S(1)} %get-tuple-element.70.rest_8_), channel_id=1, source_target_pairs={{0,4},{1,5},{2,6},{3,7},{4,8},{5,9},{6,10},{7,11},{8,12},{9,13},{1... | collective-permute-start | bytes 196616 | tf_op jit(solution)/shard_map/ppermute | solution.py:511
  92.0 7.4 %collective-permute-start.15 = (bf16[256,128]{1,0:T(8,128)(2,1)S(1)}, bf16[256,128]{1,0:T(8,128)(2,1)S(1)}, u32[]{:S(2)}, u32[]{:S(2)}) collective-permute-start(bf16[256,128]{1,0:T(8,128)(2,1)S(1)} %get-tuple-element.71), channel_id=1, source_target_pairs={{0,5},{1,6},{2,7},{3,4},{4,9},{5,10},{6,11},{7,8},{8,13},{9,14},{1... | collective-permute-start | bytes 196616 | tf_op jit(solution)/shard_map/ppermute | solution.py:511
  92.0 8.8 %collective-permute-start.16 = (bf16[256,128]{1,0:T(8,128)(2,1)S(1)}, bf16[256,128]{1,0:T(8,128)(2,1)S(1)}, u32[]{:S(2)}, u32[]{:S(2)}) collective-permute-start(bf16[256,128]{1,0:T(8,128)(2,1)S(1)} %get-tuple-element.72), channel_id=1, source_target_pairs={{0,6},{1,7},{2,4},{3,5},{4,10},{5,11},{6,8},{7,9},{8,14},{9,15},{1... | collective-permute-start | bytes 196616 | tf_op jit(solution)/shard_map/ppermute | solution.py:511
  94.8 6.4 %collective-permute-start.17 = (bf16[256,128]{1,0:T(8,128)(2,1)S(1)}, bf16[256,128]{1,0:T(8,128)(2,1)S(1)}, u32[]{:S(2)}, u32[]{:S(2)}) collective-permute-start(bf16[256,128]{1,0:T(8,128)(2,1)S(1)} %get-tuple-element.73), channel_id=1, source_target_pairs={{0,7},{1,4},{2,5},{3,6},{4,11},{5,8},{6,9},{7,10},{8,15},{9,12},{1... | collective-permute-start | bytes 196616 | tf_op jit(solution)/shard_map/ppermute | solution.py:511
  96.5 8.7 %collective-permute-start.21 = (bf16[256,128]{1,0:T(8,128)(2,1)S(1)}, bf16[256,128]{1,0:T(8,128)(2,1)S(1)}, u32[]{:S(2)}, u32[]{:S(2)}) collective-permute-start(bf16[256,128]{1,0:T(8,128)(2,1)S(1)} %get-tuple-element.71), channel_id=1, source_target_pairs={{0,1},{1,2},{2,3},{3,0},{4,5},{5,6},{6,7},{7,4},{8,9},{9,10},{10,1... | collective-permute-start | bytes 196616 | tf_op jit(solution)/shard_map/ppermute | solution.py:52
  97.7 9.6 %collective-permute-start.22 = (bf16[256,128]{1,0:T(8,128)(2,1)S(1)}, bf16[256,128]{1,0:T(8,128)(2,1)S(1)}, u32[]{:S(2)}, u32[]{:S(2)}) collective-permute-start(bf16[256,128]{1,0:T(8,128)(2,1)S(1)} %get-tuple-element.72), channel_id=1, source_target_pairs={{0,2},{1,3},{2,0},{3,1},{4,6},{5,7},{6,4},{7,5},{8,10},{9,11},{10,... | collective-permute-start | bytes 196616 | tf_op jit(solution)/shard_map/ppermute | solution.py:52
  99.3 7.9 %collective-permute-start.23 = (bf16[256,128]{1,0:T(8,128)(2,1)S(1)}, bf16[256,128]{1,0:T(8,128)(2,1)S(1)}, u32[]{:S(2)}, u32[]{:S(2)}) collective-permute-start(bf16[256,128]{1,0:T(8,128)(2,1)S(1)} %get-tuple-element.73), channel_id=1, source_target_pairs={{0,3},{1,0},{2,1},{3,2},{4,7},{5,4},{6,5},{7,6},{8,11},{9,8},{10,9... | collective-permute-start | bytes 196616 | tf_op jit(solution)/shard_map/ppermute | solution.py:52
  100.8 6.5 %collective-permute-start.18 = (bf16[256,128]{1,0:T(8,128)(2,1)S(1)}, bf16[256,128]{1,0:T(8,128)(2,1)S(1)}, u32[]{:S(2)}, u32[]{:S(2)}) collective-permute-start(bf16[256,128]{1,0:T(8,128)(2,1)S(1)} %get-tuple-element.74), channel_id=1, source_target_pairs={{0,1},{1,2},{2,3},{3,0},{4,5},{5,6},{6,7},{7,4},{8,9},{9,10},{10,1... | collective-permute-start | bytes 196616 | tf_op jit(solution)/shard_map/ppermute | solution.py:52
  101.2 6.3 %collective-permute-start.19 = (bf16[256,128]{1,0:T(8,128)(2,1)S(1)}, bf16[256,128]{1,0:T(8,128)(2,1)S(1)}, u32[]{:S(2)}, u32[]{:S(2)}) collective-permute-start(bf16[256,128]{1,0:T(8,128)(2,1)S(1)} %get-tuple-element.75), channel_id=1, source_target_pairs={{0,2},{1,3},{2,0},{3,1},{4,6},{5,7},{6,4},{7,5},{8,10},{9,11},{10,... | collective-permute-start | bytes 196616 | tf_op jit(solution)/shard_map/ppermute | solution.py:52
  105.2 3.5 %collective-permute-start.20 = (bf16[256,128]{1,0:T(8,128)(2,1)S(1)}, bf16[256,128]{1,0:T(8,128)(2,1)S(1)}, u32[]{:S(2)}, u32[]{:S(2)}) collective-permute-start(bf16[256,128]{1,0:T(8,128)(2,1)S(1)} %get-tuple-element.76), channel_id=1, source_target_pairs={{0,3},{1,0},{2,1},{3,2},{4,7},{5,4},{6,5},{7,6},{8,11},{9,8},{10,9... | collective-permute-start | bytes 196616 | tf_op jit(solution)/shard_map/ppermute | solution.py:52
  110.7 7.7 %collective-permute-start.24 = (bf16[784,128]{1,0:T(8,128)(2,1)S(1)}, bf16[784,128]{1,0:T(8,128)(2,1)S(1)}, u32[]{:S(2)}, u32[]{:S(2)}) collective-permute-start(bf16[784,128]{1,0:T(8,128)(2,1)S(1)} %get-tuple-element.77), channel_id=1, source_target_pairs={{0,252},{4,0},{8,4},{12,8},{16,12},{20,16},{24,20},{28,24},{32,28}... | collective-permute-start | bytes 602120 | tf_op jit(solution)/shard_map/ppermute | solution.py:52
  116.5 3.0 %collective-permute-start.25 = (bf16[784,128]{1,0:T(8,128)(2,1)S(1)}, bf16[784,128]{1,0:T(8,128)(2,1)S(1)}, u32[]{:S(2)}, u32[]{:S(2)}) collective-permute-start(bf16[784,128]{1,0:T(8,128)(2,1)S(1)} %get-tuple-element.79), channel_id=1, source_target_pairs={{0,4},{4,8},{8,12},{12,16},{16,20},{20,24},{24,28},{28,32},{32,36}... | collective-permute-start | bytes 602120 | tf_op jit(solution)/shard_map/ppermute | solution.py:52
  116.5 14.1 %collective-permute-start.26 = (bf16[784,128]{1,0:T(8,128)(2,1)S(1)}, bf16[784,128]{1,0:T(8,128)(2,1)S(1)}, u32[]{:S(2)}, u32[]{:S(2)}) collective-permute-start(bf16[784,128]{1,0:T(8,128)(2,1)S(1)} %get-tuple-element.80), channel_id=1, source_target_pairs={{0,8},{4,12},{8,16},{12,20},{16,24},{20,28},{24,32},{28,36},{32,40... | collective-permute-start | bytes 602120 | tf_op jit(solution)/shard_map/ppermute | solution.py:52

commit v3 on v2

--- a/solution.py
+++ b/solution.py
@@ -20,6 +20,7 @@
 PIECE = MOST_RUN + TILE
 LANES = 4
 BLOCKS = PATCH // BLOCK
+
 
 F32 = jnp.float32
 BF16 = jnp.bfloat16
@@ -91,7 +92,7 @@
         in_specs=[VMEM, HBM],
         out_specs=(VMEM,) * LANES + (SMEM,),
         scratch_shapes=[pltpu.SemaphoreType.DMA((LANES,))],
-        compiler_params=pltpu.CompilerParams(vmem_limit_bytes=8 << 20),
+        compiler_params=pltpu.CompilerParams(vmem_limit_bytes=60 << 20),
         name="cut_windows",
     )(ranks, feats)
 
@@ -191,7 +192,7 @@
     )(table, spots, *lanes, *after)
 
 
-def project_kernel(part, extras, table_ref, spots_ref, *refs):
+def project_kernel(part, table_ref, spots_ref, *refs):
     lane_refs, gain_ref = refs[:LANES], refs[LANES]
     near_ref, ahead_ref, far_a_ref, far_b_ref, behind_ref = refs[LANES + 1 : LANES + 6]
     extra_ref = refs[LANES + 6]
@@ -229,7 +230,7 @@
     width = lanes[0].shape[1]
     shape = lambda *dims: jax.ShapeDtypeStruct(dims, BF16)
     return pl.pallas_call(
-        functools.partial(project_kernel, part, len(extra)),
+        functools.partial(project_kernel, part),
         out_shape=(shape(queries, width), shape(PATCH, width), shape(width, PATCH), shape(width, queries)),
         in_specs=[SMEM] + [VMEM] * (LANES + 7) + ([VMEM] + [ANY] * (len(extra) - 1) if part else [ANY] * len(extra)),
         out_specs=(VMEM,) * 4,
@@ -244,12 +245,12 @@
     )(table, spots, *lanes, gains, *early, *extra)
 
 
-def attend_kernel(after, own_ref, keys_ref, values_ref, query_ref, *refs):
-    near_ref, ahead_ref, far_b_ref, behind_ref = refs[:4]
-    out_ref, mixed_ref, score_ref = refs[4 + after :]
-    queries = own_ref.shape[0]
-    groups = 4
+def attend_kernel(groups, final, keys_ref, values_ref, query_ref, *refs):
+    mixed_ref, score_ref = refs[-2:]
+    out_ref = refs[-3] if final else None
+    queries = query_ref.shape[1]
     span = GROUP_HEADS * HEAD_DIM
+    first = groups[0]
 
     head_of_row = lax.broadcasted_iota(jnp.int32, (span, queries), 0) // HEAD_DIM
     ones = jnp.ones((HEAD_DIM, BLOCK), BF16)
@@ -266,56 +267,72 @@
         return top if highest is None else jnp.maximum(highest, top)
 
     highest = None
-    query = query_of(0, 0)
+    query = query_of(first, 0)
     for chunk in range(BLOCKS):
-        highest = score(0, 0, query, chunk, highest)
+        highest = score(0, first, query, chunk, highest)
 
     def head_step(head, highest):
-        for group in range(groups):
+        for index, group in enumerate(groups):
             top = jnp.max(highest, axis=0, keepdims=True)
-            later = (group + 1) % groups
-            query = query_of(later, head if later else jnp.minimum(head + 1, GROUP_HEADS - 1))
+            last = index + 1 == len(groups)
+            later = groups[0] if last else groups[index + 1]
+            query = query_of(later, jnp.minimum(head + 1, GROUP_HEADS - 1) if last else head)
             rows = pl.ds(pl.multiple_of(group * span + head * HEAD_DIM, HEAD_DIM), HEAD_DIM)
             total, highest = None, None
             for chunk in range(BLOCKS):
                 keys = slice(chunk * BLOCK, (chunk + 1) * BLOCK)
-                highest = score(later % 2, later, query, chunk, highest)
-                weights = jnp.exp2(score_ref[group % 2, keys, :] - top).astype(BF16)
+                highest = score((index + 1) % 2, later, query, chunk, highest)
+                weights = jnp.exp2(score_ref[index % 2, keys, :] - top).astype(BF16)
                 values = jnp.concatenate([values_ref[rows, keys], ones], axis=0)
                 term = nn_dot(values, weights)
                 total = term if total is None else total + term
-            mixed_ref[rows, :] = (total[:HEAD_DIM] / total[HEAD_DIM : HEAD_DIM + 1]).astype(BF16)
+            held = pl.ds(pl.multiple_of((group - first) * span + head * HEAD_DIM, HEAD_DIM), HEAD_DIM)
+            mixed_ref[held, :] = (total[:HEAD_DIM] / total[HEAD_DIM : HEAD_DIM + 1]).astype(BF16)
         return highest
 
     lax.fori_loop(0, GROUP_HEADS, head_step, highest)
+    if not final:
+        return
+    own_ref, near_ref, ahead_ref, far_b_ref, behind_ref = refs[:5]
     mixed = None
-    for group in range(groups):
-        rows = slice(group * span, (group + 1) * span)
+    for group in range(4):
+        if group < first:
+            held = refs[5][group * span : (group + 1) * span, :]
+        else:
+            held = mixed_ref[(group - first) * span : (group - first + 1) * span, :]
         weight = (near_ref, ahead_ref, far_b_ref, behind_ref)[group]
         weight = weight[span : 2 * span, :] if group == 2 else weight[3 * span :, :]
-        term = tn_dot(mixed_ref[rows, :], weight).astype(BF16).astype(F32)
+        term = tn_dot(held, weight).astype(BF16).astype(F32)
         mixed = term if mixed is None else mixed + term
     out_ref[...] = (own_ref[...].astype(F32) + mixed).astype(BF16)
 
 
-def attend(part, projected, early, after):
-    queries, width = projected[0].shape
-    near, ahead, far_a, far_b, behind = early
-    return pl.pallas_call(
-        functools.partial(attend_kernel, len(after)),
-        out_shape=jax.ShapeDtypeStruct((queries, width), BF16),
-        in_specs=[VMEM] * 8 + [ANY] * len(after),
+def attend(groups, projected, early, prior, after):
+    own, keys, values, query = projected
+    queries, width = own.shape
+    span = GROUP_HEADS * HEAD_DIM
+    height = len(groups) * span
+    final = groups[-1] == 3
+    near, ahead, _, far_b, behind = early
+    operands = [keys, values, query]
+    if final:
+        operands += [own, near, ahead, far_b, behind, *prior]
+    scratch = [pltpu.VMEM((2, PATCH, queries), F32)]
+    if final:
+        scratch = [pltpu.VMEM((height, queries), BF16)] + scratch
+    return pl.pallas_call(
+        functools.partial(attend_kernel, groups, final),
+        out_shape=jax.ShapeDtypeStruct((queries, width) if final else (height, queries), BF16),
+        in_specs=[VMEM] * len(operands) + [ANY] * len(after),
         out_specs=VMEM,
-        scratch_shapes=[
-            pltpu.VMEM((width, queries), BF16),
-            pltpu.VMEM((2, PATCH, queries), F32),
-        ],
+        scratch_shapes=scratch,
         cost_estimate=pl.CostEstimate(
-            flops=30 * 10**9, bytes_accessed=5 << 20, transcendentals=8 << 20
+            flops=8 * 10**9 * len(groups),
+            bytes_accessed=5 << 20,
+            transcendentals=(2 << 20) * len(groups),
         ),
         compiler_params=pltpu.CompilerParams(vmem_limit_bytes=16 << 20),
-        name="attend_last" if part else "attend_first",
-    )(*projected, near, ahead, far_b, behind, *after)
+    )(*operands, *after)
 
 
 def mlp_kernel(groups, hidden_ref, gain_ref, *refs):
@@ -439,7 +456,7 @@
     )(counts, *pieces)
 
 
-def per_device(
+def body(
     voxel_feats,
     slot_rank,
     curve_order,
@@ -452,7 +469,7 @@
 ):
     bricks = lax.axis_size("brick")
     parts = lax.axis_size("mp")
-    capacity, width = voxel_feats.shape
+    capacity, _ = voxel_feats.shape
     shard = curve_order.shape[0]
     queries = PATCH // parts
 
@@ -487,20 +504,15 @@
     head = head_rows(table, spots, lanes, (far_a, far_b))
     head_next = shifted(head, "brick", -1)
     common = (table, spots, lanes, norm_gains, early)
-    projected = project(0, *common, (head,), queries)
-    up_ahead, down_behind, *projected = lax.optimization_barrier(
-        (up_ahead, down_behind, *projected)
-    )
+    patch0 = project(0, *common, (head,), queries)
+    mixed = attend((0, 1), patch0, early, (), ())
+    up_ahead, down_behind, mixed = lax.optimization_barrier((up_ahead, down_behind, mixed))
     up_far, down_far = shifted(up_ahead, "mp", 1), shifted(down_behind, "mp", -1)
     up = (up_weight, up_ahead, up_far, up_behind)
     down = (down_weight, down_ahead, down_far, down_behind)
-    hidden = attend(0, projected, early, ())
-    projected = project(1, *common, (head_next, hidden), queries)
-    blocks = mlp(hidden, norm_gains, up, down, (projected[0],))
-    first = [blocks[0]] + [shifted(blocks[step], "mp", step) for step in range(1, parts)]
-    hidden = attend(1, projected, early, (blocks[0],))
-    blocks = mlp(hidden, norm_gains, up, down, ())
-    last = [blocks[0]] + [shifted(blocks[step], "mp", step) for step in range(1, parts)]
+    patch1 = project(1, *common, (head_next, mixed), queries)
+
+    blocks = mlp(attend((0, 1, 2, 3), patch1, early, (), ()), norm_gains, up, down, ())
 
     def onward(step):
         pairs = [
@@ -510,7 +522,14 @@
         ]
         return lax.ppermute(blocks[step], ("brick", "mp"), pairs)
 
-    tail = [onward(step) for step in range(parts)]
+    tail, last = [], [blocks[0]]
+    for step in range(parts):
+        tail.append(onward(step))
+        if step:
+            last.append(shifted(blocks[step], "mp", step))
+    hidden = attend((2, 3), patch0, early, (mixed,), (blocks[0],))
+    blocks = mlp(hidden, norm_gains, up, down, ())
+    first = [blocks[0]] + [shifted(blocks[step], "mp", step) for step in range(1, parts)]
     back0, back1, back2, back3 = pack_lanes(patch_shift, table, spots, (*tail, *first, *last))
     pieces = (
         shifted(back0, "brick", -1),
@@ -523,7 +542,7 @@
 
 def solution(mesh):
     return jax.shard_map(
-        per_device,
+        body,
         mesh=mesh,
         in_specs=(
             P("brick", None),

time: 133 us -> 122 us (0.917)
  waiting for transfers between devices: 33.7 us -> 25.5 us
  Pallas kernels: 40.7 us -> 45.2 us
  starting transfers between devices: 54.2 us -> 49.8 us
  local copies, waits for them, and re-layouts: 2.71 us -> 0.07 us
    ppermute x23, waiting for transfers between devices: 32.4 us -> 25.5 us  [shifted(): return lax.ppermute(value, axis, pairs)]
    ppermute x4, starting transfers between devices: 10.9 us -> 6.84 us  [onward(): return lax.ppermute(blocks[step], ('brick', 'mp'), pairs)]
    pallas_call x1, Pallas kernels: 1.62 us -> 4.55 us  [cut_windows(): pl.pallas_call(functools.partial(cut_kernel, bricks, shard), out_shape=(p...]
    unnamed x16, local copies, waits for them, and re-layouts: 2.67 us -> 0.04 us
    pallas_call x4 -> x5, Pallas kernels: 29.6 us -> 31.1 us  [the longest x3 22.6 us: attend(): pl.pallas_call(functools.partial(attend_kernel, groups, final), out_shape...]
  transfers between devices with their start and end apart: 27 -> 27, of which waited for: 11 -> 8; matrix products, arithmetic and copies ran while one was open for 0% -> 0% of each run, Pallas kernels for 16% -> 29%
where the time goes in v3:
time: 122 us
  starting transfers between devices  49.8 us (41%)
  Pallas kernels  45.2 us (37%)
  waiting for transfers between devices  25.5 us (21%)
    ppermute x23, starting transfers between devices, shifted(): return lax.ppermute(value, axis, pairs)  43 us
    ppermute x23, waiting for transfers between devices, shifted(): return lax.ppermute(value, axis, pairs)  25.5 us
    pallas_call x3, Pallas kernels, attend(): pl.pallas_call(functools.partial(attend_kernel, groups, final), out_shape...  22.6 us
    pallas_call x2, Pallas kernels, project(): pl.pallas_call(functools.partial(project_kernel, part), out_shape=(shape(...  8.5 us
    ppermute x4, starting transfers between devices, onward(): return lax.ppermute(blocks[step], ('brick', 'mp'), pairs)  6.84 us
    pallas_call x1, Pallas kernels, cut_windows(): pl.pallas_call(functools.partial(cut_kernel, bricks, shard), out_shape=(p...  4.55 us
    pallas_call x2, Pallas kernels, mlp(): pl.pallas_call(functools.partial(mlp_kernel, groups), out_shape=(jax.Shap...  3.24 us
  transfers between devices with their start and end apart: 27, of which 8 were waited for; matrix products, arithmetic and copies ran while one was open for 0% of the time, Pallas kernels for 29%

profile of v3, /device:TPU:1, one launch (start us, length us, event | category | flops | bytes accessed | tf_op | source)
XLA Modules:
  0.0 121.9 jit_solution(3191284185858582205)
XLA Ops:
  0.0 4.5 %cut_windows.1 = (bf16[784,512]{1,0:T(8,128)(2,1)}, bf16[784,512]{1,0:T(8,128)(2,1)}, bf16[784,512]{1,0:T(8,128)(2,1)}, bf16[784,512]{1,0:T(8,128)(2,1)}, s32[2,4]{1,0:T(2,128)}) custom-call(s32[24,128]{1,0:T(8,128)} %bitcast.4, bf16[3072,512]{1,0:T(8,128)(2,1)} %feats_ref.1), custom_call_target="tpu_custom_call" | custom-call | tf_op jit(solution)/shard_map/cut_windows/pallas_call | solution.py:89
  4.6 3.1 %collective-permute-start = (bf16[784,512]{1,0:T(8,128)(2,1)}, bf16[784,512]{1,0:T(8,128)(2,1)S(1)}, u32[]{:S(2)}, u32[]{:S(2)}) collective-permute-start(bf16[784,512]{1,0:T(8,128)(2,1)} %get-tuple-element.46), channel_id=1, source_target_pairs={{0,4},{4,8},{8,12},{12,16},{16,20},{20,24},{24,28},{28,32},{32,36}... | collective-permute-start | bytes 2408456 | tf_op jit(solution)/shard_map/ppermute | solution.py:53
  7.7 0.3 collective-permute-start.1
  8.0 6.3 %collective-permute-start.2 = (bf16[784,512]{1,0:T(8,128)(2,1)}, bf16[784,512]{1,0:T(8,128)(2,1)S(1)}, u32[]{:S(2)}, u32[]{:S(2)}) collective-permute-start(bf16[784,512]{1,0:T(8,128)(2,1)} %get-tuple-element.49), channel_id=1, source_target_pairs={{0,248},{4,252},{8,0},{12,4},{16,8},{20,12},{24,16},{28,20},{32,24... | collective-permute-start | bytes 2408456 | tf_op jit(solution)/shard_map/ppermute | solution.py:53
  14.3 0.4 convolution_convert_fusion
  14.8 0.0 copy-start.4
  14.8 1.3 %collective-permute-start.3 = (bf16[512,512]{1,0:T(8,128)(2,1)S(1)}, bf16[512,512]{1,0:T(8,128)(2,1)S(1)}, u32[]{:S(2)}, u32[]{:S(2)}) collective-permute-start(bf16[512,512]{1,0:T(8,128)(2,1)S(1)} %pad_maximum_fusion.after_ref.refs_5_.refs_1_), channel_id=1, source_target_pairs={{0,1},{1,2},{2,3},{3,0},{4,5},{5,6},{6,7},{7,4},{8,9},{9,10},{10,1... | collective-permute-start | bytes 1572872 | tf_op jit(solution)/shard_map/ppermute | solution.py:53
  16.1 1.5 %collective-permute-start.5 = (bf16[512,512]{1,0:T(8,128)(2,1)S(1)}, bf16[512,512]{1,0:T(8,128)(2,1)S(1)}, u32[]{:S(2)}, u32[]{:S(2)}) collective-permute-start(bf16[512,512]{1,0:T(8,128)(2,1)S(1)} %pad_maximum_fusion.after_ref.refs_5_.refs_1_), channel_id=1, source_target_pairs={{0,3},{1,0},{2,1},{3,2},{4,7},{5,4},{6,5},{7,6},{8,11},{9,8},{10,9... | collective-permute-start | bytes 1572872 | tf_op jit(solution)/shard_map/ppermute | solution.py:53
  17.5 10.1 %collective-permute-done.3.refs_6_.refs_2_ = bf16[512,512]{1,0:T(8,128)(2,1)S(1)} collective-permute-done((bf16[512,512]{1,0:T(8,128)(2,1)S(1)}, bf16[512,512]{1,0:T(8,128)(2,1)S(1)}, u32[]{:S(2)}, u32[]{:S(2)}) %collective-permute-start.3) | collective-permute-done | bytes 524320 | tf_op jit(solution)/shard_map/ppermute | solution.py:53
  27.6 0.1 collective-permute-start.4
  27.7 0.0 collective-permute-done.5.refs_9_.refs_4_
  27.8 2.7 %collective-permute-start.6 = (bf16[256,512]{1,0:T(8,128)(2,1)S(1)}, bf16[256,512]{1,0:T(8,128)(2,1)S(1)}, u32[]{:S(2)}, u32[]{:S(2)}) collective-permute-start(bf16[256,512]{1,0:T(8,128)(2,1)S(1)} %slice.9), channel_id=1, source_target_pairs={{0,3},{1,0},{2,1},{3,2},{4,7},{5,4},{6,5},{7,6},{8,11},{9,8},{10,9... | collective-permute-start | bytes 786440 | tf_op jit(solution)/shard_map/ppermute | solution.py:53
  31.2 0.6 index_tables.1
  31.8 2.4 %collective-permute-done.4.refs_4_.refs_7_ = bf16[256,512]{1,0:T(8,128)(2,1)S(1)} collective-permute-done((bf16[256,512]{1,0:T(8,128)(2,1)S(1)}, bf16[256,512]{1,0:T(8,128)(2,1)S(1)}, u32[]{:S(2)}, u32[]{:S(2)}) %collective-permute-start.4) | collective-permute-done | bytes 262176 | tf_op jit(solution)/shard_map/ppermute | solution.py:53
  34.2 0.0 collective-permute-start.8
  34.2 0.0 collective-permute-done.6.refs_5_.refs_8_.refs_3_
  34.2 2.8 %collective-permute-start.11 = (bf16[512,512]{1,0:T(8,128)(2,1)S(1)}, bf16[512,512]{1,0:T(8,128)(2,1)S(1)}, u32[]{:S(2)}, u32[]{:S(2)}) collective-permute-start(bf16[512,512]{1,0:T(8,128)(2,1)S(1)} %copy-done.1), channel_id=1, source_target_pairs={{0,3},{1,0},{2,1},{3,2},{4,7},{5,4},{6,5},{7,6},{8,11},{9,8},{10,9... | collective-permute-start | bytes 1572872 | tf_op jit(solution)/shard_map/ppermute | solution.py:53
  36.9 0.0 collective-permute-done.refs_0_
  36.9 0.1 collective-permute-start.9
  37.0 0.0 collective-permute-done.1.refs_2_
  37.0 1.4 %collective-permute-start.12 = (bf16[512,512]{1,0:T(8,128)(2,1)S(1)}, bf16[512,512]{1,0:T(8,128)(2,1)S(1)}, u32[]{:S(2)}, u32[]{:S(2)}) collective-permute-start(bf16[512,512]{1,0:T(8,128)(2,1)S(1)} %copy-done.2), channel_id=1, source_target_pairs={{0,1},{1,2},{2,3},{3,0},{4,5},{5,6},{6,7},{7,4},{8,9},{9,10},{10,1... | collective-permute-start | bytes 1572872 | tf_op jit(solution)/shard_map/ppermute | solution.py:53
  38.4 0.0 collective-permute-done.2.refs_3_
  38.4 1.8 %head_rows.1.refs_10_ = bf16[1024,512]{1,0:T(8,128)(2,1)S(1)} custom-call(s32[24,128]{1,0:T(8,128)S(1)} %get-tuple-element.44.table_ref, s32[24,128]{1,0:T(8,128)S(1)} %get-tuple-element.45.spots_ref, bf16[784,512]{1,0:T(8,128)(2,1)S(1)} %collective-permute-done.refs_0_, bf16[784,512]{1,0:T(8,128)(2,1)S(1)} %copy-done.3, ...), custom_call_target="tpu_custom_call" | custom-call | flops 805306368 | bytes 5242880 | tf_op jit(solution)/shard_map/head_rows/pallas_call | solution.py:182
  40.2 5.3 %collective-permute-start.7 = (bf16[1024,512]{1,0:T(8,128)(2,1)S(1)}, bf16[1024,512]{1,0:T(8,128)(2,1)S(1)}, u32[]{:S(2)}, u32[]{:S(2)}) collective-permute-start(bf16[1024,512]{1,0:T(8,128)(2,1)S(1)} %head_rows.1.refs_10_), channel_id=1, source_target_pairs={{0,252},{4,0},{8,4},{12,8},{16,12},{20,16},{24,20},{28,24},{32,28}... | collective-permute-start | bytes 3145736 | tf_op jit(solution)/shard_map/ppermute | solution.py:53
  45.5 4.3 %project_first.1 = (bf16[256,512]{1,0:T(8,128)(2,1)S(1)}, bf16[1024,512]{1,0:T(8,128)(2,1)S(1)}, bf16[512,1024]{1,0:T(8,128)(2,1)S(1)}, bf16[512,256]{1,0:T(8,128)(2,1)S(1)}) custom-call(s32[24,128]{1,0:T(8,128)S(1)} %get-tuple-element.44.table_ref, s32[24,128]{1,0:T(8,128)S(1)} %get-tuple-element.45.spots_ref, ...), custom_call_target="tpu_custom_call" | custom-call | flops 10000000000 | bytes 10485760 | tf_op jit(solution)/shard_map/project_first/pallas_call | solution.py:232
  49.8 5.8 %shard_map.91.refs_11_.refs_5_ = bf16[256,256]{1,0:T(8,128)(2,1)S(1)} custom-call(bf16[1024,512]{1,0:T(8,128)(2,1)S(1)} %get-tuple-element.52.keys_ref, bf16[512,1024]{1,0:T(8,128)(2,1)S(1)} %get-tuple-element.53.values_ref, bf16[512,256]{1,0:T(8,128)(2,1)S(1)} %get-tuple-element.54.query_ref), custom_call_target="tpu_custom_call" | custom-call | flops 16000000000 | bytes 5242880 | tf_op jit(solution)/shard_map/pallas_call | solution.py:323
  55.6 0.0 collective-permute-done.8.refs_1_
  55.6 0.5 collective-permute-start.10
  56.2 2.5 %collective-permute-start.13 = (bf16[512,512]{1,0:T(8,128)(2,1)S(1)}, bf16[512,512]{1,0:T(8,128)(2,1)S(1)}, u32[]{:S(2)}, u32[]{:S(2)}) collective-permute-start(bf16[512,512]{1,0:T(8,128)(2,1)S(1)} %collective-permute-done.9.refs_7_), channel_id=1, source_target_pairs={{0,3},{1,0},{2,1},{3,2},{4,7},{5,4},{6,5},{7,6},{8,11},{9,8},{10,9... | collective-permute-start | bytes 1572872 | tf_op jit(solution)/shard_map/ppermute | solution.py:53
  58.6 1.4 %collective-permute-done.7.refs_10_ = bf16[1024,512]{1,0:T(8,128)(2,1)S(1)} collective-permute-done((bf16[1024,512]{1,0:T(8,128)(2,1)S(1)}, bf16[1024,512]{1,0:T(8,128)(2,1)S(1)}, u32[]{:S(2)}, u32[]{:S(2)}) %collective-permute-start.7) | collective-permute-done | bytes 1048608 | tf_op jit(solution)/shard_map/ppermute | solution.py:53
  60.1 4.2 %project_last.1 = (bf16[256,512]{1,0:T(8,128)(2,1)S(1)}, bf16[1024,512]{1,0:T(8,128)(2,1)S(1)}, bf16[512,1024]{1,0:T(8,128)(2,1)S(1)}, bf16[512,256]{1,0:T(8,128)(2,1)S(1)}) custom-call(s32[24,128]{1,0:T(8,128)S(1)} %get-tuple-element.44.table_ref, s32[24,128]{1,0:T(8,128)S(1)} %get-tuple-element.45.spots_ref, ...), custom_call_target="tpu_custom_call" | custom-call | flops 10000000000 | bytes 10485760 | tf_op jit(solution)/shard_map/project_last/pallas_call | solution.py:232
  64.3 10.5 %shard_map.92.hidden_ref = bf16[256,512]{1,0:T(8,128)(2,1)S(1)} custom-call(bf16[1024,512]{1,0:T(8,128)(2,1)S(1)} %get-tuple-element.56.keys_ref, bf16[512,1024]{1,0:T(8,128)(2,1)S(1)} %get-tuple-element.57.values_ref, bf16[512,256]{1,0:T(8,128)(2,1)S(1)} %get-tuple-element.58.query_ref, bf16[256,512]{1,0:T(8,128)(2,1)S(1)} %get-tuple-element.59.refs_0_, ...), custom_call_target="tpu_custom_call" | custom-call | flops 32000000000 | bytes 5242880 | tf_op jit(solution)/shard_map/pallas_call | solution.py:323
  74.9 0.0 collective-permute-done.11.refs_3_
  74.9 0.0 collective-permute-done.12.refs_5_
  74.9 0.0 collective-permute-done.13.refs_6_
  74.9 1.6 %mlp.2 = (bf16[256,128]{1,0:T(8,128)(2,1)S(1)}, bf16[256,128]{1,0:T(8,128)(2,1)S(1)}, bf16[256,128]{1,0:T(8,128)(2,1)S(1)}, bf16[256,128]{1,0:T(8,128)(2,1)S(1)}) custom-call(bf16[256,512]{1,0:T(8,128)(2,1)S(1)} %shard_map.92.hidden_ref, f32[2,512]{1,0:T(2,128)S(1)} %copy-done.4, bf16[512,512]{1,0:T(8,128)(2,1)S(1)} %copy-done.1, ...), custom_call_target="tpu_custom_call" | custom-call | flops 1073741824 | bytes 5242880 | tf_op jit(solution)/shard_map/mlp/pallas_call | solution.py:374
  76.5 1.4 %collective-permute-start.14 = (bf16[256,128]{1,0:T(8,128)(2,1)S(1)}, bf16[256,128]{1,0:T(8,128)(2,1)S(1)}, u32[]{:S(2)}, u32[]{:S(2)}) collective-permute-start(bf16[256,128]{1,0:T(8,128)(2,1)S(1)} %get-tuple-element.62.refs_6_.rest_8_), channel_id=1, source_target_pairs={{0,4},{1,5},{2,6},{3,7},{4,8},{5,9},{6,10},{7,11},{8,12},{9,13},{1... | collective-permute-start | bytes 196616 | tf_op jit(solution)/shard_map/ppermute | solution.py:523
  78.0 0.0 collective-permute-start.15
  78.0 5.1 %collective-permute-start.16 = (bf16[256,128]{1,0:T(8,128)(2,1)S(1)}, bf16[256,128]{1,0:T(8,128)(2,1)S(1)}, u32[]{:S(2)}, u32[]{:S(2)}) collective-permute-start(bf16[256,128]{1,0:T(8,128)(2,1)S(1)} %get-tuple-element.64), channel_id=1, source_target_pairs={{0,6},{1,7},{2,4},{3,5},{4,10},{5,11},{6,8},{7,9},{8,14},{9,15},{1... | collective-permute-start | bytes 196616 | tf_op jit(solution)/shard_map/ppermute | solution.py:523
  83.0 0.3 collective-permute-start.17
  83.4 6.3 %shard_map.93.hidden_ref = bf16[256,512]{1,0:T(8,128)(2,1)S(1)} custom-call(bf16[1024,512]{1,0:T(8,128)(2,1)S(1)} %get-tuple-element.52.keys_ref, bf16[512,1024]{1,0:T(8,128)(2,1)S(1)} %get-tuple-element.53.values_ref, bf16[512,256]{1,0:T(8,128)(2,1)S(1)} %get-tuple-element.54.query_ref, bf16[256,512]{1,0:T(8,128)(2,1)S(1)} %get-tuple-element.66.refs_0_, ...), custom_call_target="tpu_custom_call" | custom-call | flops 16000000000 | bytes 5242880 | tf_op jit(solution)/shard_map/pallas_call | solution.py:323
  89.6 0.0 copy-start.6
  89.7 1.6 %mlp.3 = (bf16[256,128]{1,0:T(8,128)(2,1)S(1)}, bf16[256,128]{1,0:T(8,128)(2,1)S(1)}, bf16[256,128]{1,0:T(8,128)(2,1)S(1)}, bf16[256,128]{1,0:T(8,128)(2,1)S(1)}) custom-call(bf16[256,512]{1,0:T(8,128)(2,1)S(1)} %shard_map.93.hidden_ref, f32[2,512]{1,0:T(2,128)S(1)} %copy-done.4, bf16[512,512]{1,0:T(8,128)(2,1)S(1)} %copy-done.1, ...), custom_call_target="tpu_custom_call" | custom-call | flops 1073741824 | bytes 5242880 | tf_op jit(solution)/shard_map/mlp/pallas_call | solution.py:374
  91.3 1.2 %collective-permute-start.18 = (bf16[256,128]{1,0:T(8,128)(2,1)S(1)}, bf16[256,128]{1,0:T(8,128)(2,1)S(1)}, u32[]{:S(2)}, u32[]{:S(2)}) collective-permute-start(bf16[256,128]{1,0:T(8,128)(2,1)S(1)} %get-tuple-element.68), channel_id=1, source_target_pairs={{0,1},{1,2},{2,3},{3,0},{4,5},{5,6},{6,7},{7,4},{8,9},{9,10},{10,1... | collective-permute-start | bytes 196616 | tf_op jit(solution)/shard_map/ppermute | solution.py:53
  92.5 0.0 collective-permute-done.14.rest_0_
  92.5 0.3 collective-permute-start.21
  92.8 2.4 %collective-permute-start.19 = (bf16[256,128]{1,0:T(8,128)(2,1)S(1)}, bf16[256,128]{1,0:T(8,128)(2,1)S(1)}, u32[]{:S(2)}, u32[]{:S(2)}) collective-permute-start(bf16[256,128]{1,0:T(8,128)(2,1)S(1)} %get-tuple-element.69), channel_id=1, source_target_pairs={{0,2},{1,3},{2,0},{3,1},{4,6},{5,7},{6,4},{7,5},{8,10},{9,11},{10,... | collective-permute-start | bytes 196616 | tf_op jit(solution)/shard_map/ppermute | solution.py:53
  95.2 0.0 collective-permute-done.16.rest_2_
  95.2 0.1 collective-permute-start.20
  95.3 2.3 %collective-permute-start.22 = (bf16[256,128]{1,0:T(8,128)(2,1)S(1)}, bf16[256,128]{1,0:T(8,128)(2,1)S(1)}, u32[]{:S(2)}, u32[]{:S(2)}) collective-permute-start(bf16[256,128]{1,0:T(8,128)(2,1)S(1)} %get-tuple-element.64), channel_id=1, source_target_pairs={{0,2},{1,3},{2,0},{3,1},{4,6},{5,7},{6,4},{7,5},{8,10},{9,11},{10,... | collective-permute-start | bytes 196616 | tf_op jit(solution)/shard_map/ppermute | solution.py:53
  97.6 0.0 collective-permute-done.18.rest_5_
  97.6 1.5 %collective-permute-start.23 = (bf16[256,128]{1,0:T(8,128)(2,1)S(1)}, bf16[256,128]{1,0:T(8,128)(2,1)S(1)}, u32[]{:S(2)}, u32[]{:S(2)}) collective-permute-start(bf16[256,128]{1,0:T(8,128)(2,1)S(1)} %get-tuple-element.65), channel_id=1, source_target_pairs={{0,3},{1,0},{2,1},{3,2},{4,7},{5,4},{6,5},{7,6},{8,11},{9,8},{10,9... | collective-permute-start | bytes 196616 | tf_op jit(solution)/shard_map/ppermute | solution.py:53
  99.1 0.0 collective-permute-done.19.rest_6_
  99.1 0.0 collective-permute-done.20.rest_7_
  99.1 0.8 collective-permute-done.22.rest_10_
  99.9 1.7 %collective-permute-done.23.rest_11_ = bf16[256,128]{1,0:T(8,128)(2,1)S(1)} collective-permute-done((bf16[256,128]{1,0:T(8,128)(2,1)S(1)}, bf16[256,128]{1,0:T(8,128)(2,1)S(1)}, u32[]{:S(2)}, u32[]{:S(2)}) %collective-permute-start.23) | collective-permute-done | bytes 65568 | tf_op jit(solution)/shard_map/ppermute | solution.py:53
  101.7 1.9 %pack_lanes.1 = (bf16[784,128]{1,0:T(8,128)(2,1)S(1)}, bf16[784,128]{1,0:T(8,128)(2,1)S(1)}, bf16[784,128]{1,0:T(8,128)(2,1)S(1)}, bf16[784,128]{1,0:T(8,128)(2,1)S(1)}) custom-call(s32[1]{0:T(128)S(6)} %copy.10.shift_ref, s32[24,128]{1,0:T(8,128)S(1)} %get-tuple-element.44.table_ref, s32[24,128]{1,0:T(8,128)S(1)} %get-tuple-element.45.spots_ref, ...), custom_call_target="tpu_custom_call" | custom-call | tf_op jit(solution)/shard_map/pack_lanes/pallas_call | solution.py:420
  103.6 2.0 %collective-permute-start.24 = (bf16[784,128]{1,0:T(8,128)(2,1)S(1)}, bf16[784,128]{1,0:T(8,128)(2,1)S(1)}, u32[]{:S(2)}, u32[]{:S(2)}) collective-permute-start(bf16[784,128]{1,0:T(8,128)(2,1)S(1)} %get-tuple-element.71), channel_id=1, source_target_pairs={{0,252},{4,0},{8,4},{12,8},{16,12},{20,16},{24,20},{28,24},{32,28}... | collective-permute-start | bytes 602120 | tf_op jit(solution)/shard_map/ppermute | solution.py:53
  105.6 4.1 %collective-permute-start.25 = (bf16[784,128]{1,0:T(8,128)(2,1)S(1)}, bf16[784,128]{1,0:T(8,128)(2,1)S(1)}, u32[]{:S(2)}, u32[]{:S(2)}) collective-permute-start(bf16[784,128]{1,0:T(8,128)(2,1)S(1)} %get-tuple-element.73), channel_id=1, source_target_pairs={{0,4},{4,8},{8,12},{12,16},{16,20},{20,24},{24,28},{28,32},{32,36}... | collective-permute-start | bytes 602120 | tf_op jit(solution)/shard_map/ppermute | solution.py:53
  109.7 1.3 %collective-permute-start.26 = (bf16[784,128]{1,0:T(8,128)(2,1)S(1)}, bf16[784,128]{1,0:T(8,128)(2,1)S(1)}, u32[]{:S(2)}, u32[]{:S(2)}) collective-permute-start(bf16[784,128]{1,0:T(8,128)(2,1)S(1)} %get-tuple-element.74), channel_id=1, source_target_pairs={{0,8},{4,12},{8,16},{12,20},{16,24},{20,28},{24,32},{28,36},{32,40... | collective-permute-start | bytes 602120 | tf_op jit(solution)/shard_map/ppermute | solution.py:53
  111.0 2.0 %collective-permute-done.24.refs_0_ = bf16[784,128]{1,0:T(8,128)(2,1)S(1)} collective-permute-done((bf16[784,128]{1,0:T(8,128)(2,1)S(1)}, bf16[784,128]{1,0:T(8,128)(2,1)S(1)}, u32[]{:S(2)}, u32[]{:S(2)}) %collective-permute-start.24) | collective-permute-done | bytes 200736 | tf_op jit(solution)/shard_map/ppermute | solution.py:53
  113.0 0.5 collective-permute-done.25.refs_2_
  113.5 6.4 %collective-permute-done.26.refs_3_ = bf16[784,128]{1,0:T(8,128)(2,1)S(1)} collective-permute-done((bf16[784,128]{1,0:T(8,128)(2,1)S(1)}, bf16[784,128]{1,0:T(8,128)(2,1)S(1)}, u32[]{:S(2)}, u32[]{:S(2)}) %collective-permute-start.26) | collective-permute-done | bytes 200736 | tf_op jit(solution)/shard_map/ppermute | solution.py:53
  119.9 2.0 %place_rows.1 = bf16[3072,128]{1,0:T(8,128)(2,1)} custom-call(s32[2,4]{1,0:T(2,128)S(1)} %copy-done.6, bf16[784,128]{1,0:T(8,128)(2,1)S(1)} %collective-permute-done.24.refs_0_, bf16[784,128]{1,0:T(8,128)(2,1)S(1)} %get-tuple-element.72.refs_1_, bf16[784,128]{1,0:T(8,128)(2,1)S(1)} %collective-permute-done.25.refs_2_, ...), custom_call_target="tpu_custom_call" | custom-call | tf_op jit(solution)/shard_map/place_rows/pallas_call | solution.py:449
  (23 shorter events, 0.1 us)
Async XLA Ops:
  0.0 14.3 %copy-start = (bf16[512,384]{1,0:T(8,128)(2,1)S(1)}, bf16[512,384]{1,0:T(8,128)(2,1)}, u32[]{:S(2)}) copy-start(bf16[512,384]{1,0:T(8,128)(2,1)} %param.13) | copy-start | bytes 1179652
  0.0 14.7 %copy-start.7 = (bf16[128,512]{1,0:T(8,128)(2,1)S(1)}, bf16[128,512]{1,0:T(8,128)(2,1)}, u32[]{:S(2)}) copy-start(bf16[128,512]{1,0:T(8,128)(2,1)} %param.14) | copy-start | bytes 393220
  0.0 31.2 %copy-start.5 = (s32[2048]{0:T(1024)S(1)}, s32[2048]{0:T(1024)}, u32[]{:S(2)}) copy-start(s32[2048]{0:T(1024)} %param.11) | copy-start | bytes 24580
  0.0 34.1 %copy-start.1 = (bf16[512,512]{1,0:T(8,128)(2,1)S(1)}, bf16[512,512]{1,0:T(8,128)(2,1)}, u32[]{:S(2)}) copy-start(bf16[512,512]{1,0:T(8,128)(2,1)} %refs_0_.3) | copy-start | bytes 1572868
  0.0 36.9 %copy-start.2 = (bf16[512,512]{1,0:T(8,128)(2,1)S(1)}, bf16[512,512]{1,0:T(8,128)(2,1)}, u32[]{:S(2)}) copy-start(bf16[512,512]{1,0:T(8,128)(2,1)} %refs_4_.7) | copy-start | bytes 1572868
  4.6 33.8 %copy-start.3 = (bf16[784,512]{1,0:T(8,128)(2,1)S(1)}, bf16[784,512]{1,0:T(8,128)(2,1)}, u32[]{:S(2)}) copy-start(bf16[784,512]{1,0:T(8,128)(2,1)} %get-tuple-element.47.refs_1_) | copy-start | bytes 2408452
  4.6 32.3 %collective-permute-start = (bf16[784,512]{1,0:T(8,128)(2,1)}, bf16[784,512]{1,0:T(8,128)(2,1)S(1)}, u32[]{:S(2)}, u32[]{:S(2)}) collective-permute-start(bf16[784,512]{1,0:T(8,128)(2,1)} %get-tuple-element.46), channel_id=1, source_target_pairs={{0,4},{4,8},{8,12},{12,16},{16,20},{20,24},{24,28},{28,32},{32,36}... | collective-permute-start | bytes 2408456 | tf_op jit(solution)/shard_map/ppermute | solution.py:53
  7.7 29.3 %collective-permute-start.1 = (bf16[784,512]{1,0:T(8,128)(2,1)}, bf16[784,512]{1,0:T(8,128)(2,1)S(1)}, u32[]{:S(2)}, u32[]{:S(2)}) collective-permute-start(bf16[784,512]{1,0:T(8,128)(2,1)} %get-tuple-element.48), channel_id=1, source_target_pairs={{0,252},{4,0},{8,4},{12,8},{16,12},{20,16},{24,20},{28,24},{32,28}... | collective-permute-start | bytes 2408456 | tf_op jit(solution)/shard_map/ppermute | solution.py:53
  8.0 30.5 %collective-permute-start.2 = (bf16[784,512]{1,0:T(8,128)(2,1)}, bf16[784,512]{1,0:T(8,128)(2,1)S(1)}, u32[]{:S(2)}, u32[]{:S(2)}) collective-permute-start(bf16[784,512]{1,0:T(8,128)(2,1)} %get-tuple-element.49), channel_id=1, source_target_pairs={{0,248},{4,252},{8,0},{12,4},{16,8},{20,12},{24,16},{28,20},{32,24... | collective-permute-start | bytes 2408456 | tf_op jit(solution)/shard_map/ppermute | solution.py:53
  14.8 30.7 %copy-start.4 = (f32[2,512]{1,0:T(2,128)S(1)}, f32[2,512]{1,0:T(2,128)}, u32[]{:S(2)}) copy-start(f32[2,512]{1,0:T(2,128)} %gain_ref.3) | copy-start | bytes 12292
  14.8 12.8 %collective-permute-start.3 = (bf16[512,512]{1,0:T(8,128)(2,1)S(1)}, bf16[512,512]{1,0:T(8,128)(2,1)S(1)}, u32[]{:S(2)}, u32[]{:S(2)}) collective-permute-start(bf16[512,512]{1,0:T(8,128)(2,1)S(1)} %pad_maximum_fusion.after_ref.refs_5_.refs_1_), channel_id=1, source_target_pairs={{0,1},{1,2},{2,3},{3,0},{4,5},{5,6},{6,7},{7,4},{8,9},{9,10},{10,1... | collective-permute-start | bytes 1572872 | tf_op jit(solution)/shard_map/ppermute | solution.py:53
  16.1 11.7 %collective-permute-start.5 = (bf16[512,512]{1,0:T(8,128)(2,1)S(1)}, bf16[512,512]{1,0:T(8,128)(2,1)S(1)}, u32[]{:S(2)}, u32[]{:S(2)}) collective-permute-start(bf16[512,512]{1,0:T(8,128)(2,1)S(1)} %pad_maximum_fusion.after_ref.refs_5_.refs_1_), channel_id=1, source_target_pairs={{0,3},{1,0},{2,1},{3,2},{4,7},{5,4},{6,5},{7,6},{8,11},{9,8},{10,9... | collective-permute-start | bytes 1572872 | tf_op jit(solution)/shard_map/ppermute | solution.py:53
  27.6 6.5 %collective-permute-start.4 = (bf16[256,512]{1,0:T(8,128)(2,1)S(1)}, bf16[256,512]{1,0:T(8,128)(2,1)S(1)}, u32[]{:S(2)}, u32[]{:S(2)}) collective-permute-start(bf16[256,512]{1,0:T(8,128)(2,1)S(1)} %slice.8), channel_id=1, source_target_pairs={{0,1},{1,2},{2,3},{3,0},{4,5},{5,6},{6,7},{7,4},{8,9},{9,10},{10,1... | collective-permute-start | bytes 786440 | tf_op jit(solution)/shard_map/ppermute | solution.py:53
  27.8 6.4 %collective-permute-start.6 = (bf16[256,512]{1,0:T(8,128)(2,1)S(1)}, bf16[256,512]{1,0:T(8,128)(2,1)S(1)}, u32[]{:S(2)}, u32[]{:S(2)}) collective-permute-start(bf16[256,512]{1,0:T(8,128)(2,1)S(1)} %slice.9), channel_id=1, source_target_pairs={{0,3},{1,0},{2,1},{3,2},{4,7},{5,4},{6,5},{7,6},{8,11},{9,8},{10,9... | collective-permute-start | bytes 786440 | tf_op jit(solution)/shard_map/ppermute | solution.py:53
  34.2 21.5 %collective-permute-start.8 = (bf16[512,512]{1,0:T(8,128)(2,1)S(1)}, bf16[512,512]{1,0:T(8,128)(2,1)S(1)}, u32[]{:S(2)}, u32[]{:S(2)}) collective-permute-start(bf16[512,512]{1,0:T(8,128)(2,1)S(1)} %copy-done.1), channel_id=1, source_target_pairs={{0,1},{1,2},{2,3},{3,0},{4,5},{5,6},{6,7},{7,4},{8,9},{9,10},{10,1... | collective-permute-start | bytes 1572872 | tf_op jit(solution)/shard_map/ppermute | solution.py:53
  34.2 40.7 %collective-permute-start.11 = (bf16[512,512]{1,0:T(8,128)(2,1)S(1)}, bf16[512,512]{1,0:T(8,128)(2,1)S(1)}, u32[]{:S(2)}, u32[]{:S(2)}) collective-permute-start(bf16[512,512]{1,0:T(8,128)(2,1)S(1)} %copy-done.1), channel_id=1, source_target_pairs={{0,3},{1,0},{2,1},{3,2},{4,7},{5,4},{6,5},{7,6},{8,11},{9,8},{10,9... | collective-permute-start | bytes 1572872 | tf_op jit(solution)/shard_map/ppermute | solution.py:53
  36.9 18.7 %collective-permute-start.9 = (bf16[512,512]{1,0:T(8,128)(2,1)S(1)}, bf16[512,512]{1,0:T(8,128)(2,1)S(1)}, u32[]{:S(2)}, u32[]{:S(2)}) collective-permute-start(bf16[512,512]{1,0:T(8,128)(2,1)S(1)} %copy-done.2), channel_id=1, source_target_pairs={{0,3},{1,0},{2,1},{3,2},{4,7},{5,4},{6,5},{7,6},{8,11},{9,8},{10,9... | collective-permute-start | bytes 1572872 | tf_op jit(solution)/shard_map/ppermute | solution.py:53
  37.0 37.9 %collective-permute-start.12 = (bf16[512,512]{1,0:T(8,128)(2,1)S(1)}, bf16[512,512]{1,0:T(8,128)(2,1)S(1)}, u32[]{:S(2)}, u32[]{:S(2)}) collective-permute-start(bf16[512,512]{1,0:T(8,128)(2,1)S(1)} %copy-done.2), channel_id=1, source_target_pairs={{0,1},{1,2},{2,3},{3,0},{4,5},{5,6},{6,7},{7,4},{8,9},{9,10},{10,1... | collective-permute-start | bytes 1572872 | tf_op jit(solution)/shard_map/ppermute | solution.py:53
  40.2 19.9 %collective-permute-start.7 = (bf16[1024,512]{1,0:T(8,128)(2,1)S(1)}, bf16[1024,512]{1,0:T(8,128)(2,1)S(1)}, u32[]{:S(2)}, u32[]{:S(2)}) collective-permute-start(bf16[1024,512]{1,0:T(8,128)(2,1)S(1)} %head_rows.1.refs_10_), channel_id=1, source_target_pairs={{0,252},{4,0},{8,4},{12,8},{16,12},{20,16},{24,20},{28,24},{32,28}... | collective-permute-start | bytes 3145736 | tf_op jit(solution)/shard_map/ppermute | solution.py:53
  55.6 19.3 %collective-permute-start.10 = (bf16[512,512]{1,0:T(8,128)(2,1)S(1)}, bf16[512,512]{1,0:T(8,128)(2,1)S(1)}, u32[]{:S(2)}, u32[]{:S(2)}) collective-permute-start(bf16[512,512]{1,0:T(8,128)(2,1)S(1)} %collective-permute-done.8.refs_1_), channel_id=1, source_target_pairs={{0,1},{1,2},{2,3},{3,0},{4,5},{5,6},{6,7},{7,4},{8,9},{9,10},{10,1... | collective-permute-start | bytes 1572872 | tf_op jit(solution)/shard_map/ppermute | solution.py:53
  56.2 18.7 %collective-permute-start.13 = (bf16[512,512]{1,0:T(8,128)(2,1)S(1)}, bf16[512,512]{1,0:T(8,128)(2,1)S(1)}, u32[]{:S(2)}, u32[]{:S(2)}) collective-permute-start(bf16[512,512]{1,0:T(8,128)(2,1)S(1)} %collective-permute-done.9.refs_7_), channel_id=1, source_target_pairs={{0,3},{1,0},{2,1},{3,2},{4,7},{5,4},{6,5},{7,6},{8,11},{9,8},{10,9... | collective-permute-start | bytes 1572872 | tf_op jit(solution)/shard_map/ppermute | solution.py:53
  76.5 16.0 %collective-permute-start.14 = (bf16[256,128]{1,0:T(8,128)(2,1)S(1)}, bf16[256,128]{1,0:T(8,128)(2,1)S(1)}, u32[]{:S(2)}, u32[]{:S(2)}) collective-permute-start(bf16[256,128]{1,0:T(8,128)(2,1)S(1)} %get-tuple-element.62.refs_6_.rest_8_), channel_id=1, source_target_pairs={{0,4},{1,5},{2,6},{3,7},{4,8},{5,9},{6,10},{7,11},{8,12},{9,13},{1... | collective-permute-start | bytes 196616 | tf_op jit(solution)/shard_map/ppermute | solution.py:523
  78.0 14.9 %collective-permute-start.15 = (bf16[256,128]{1,0:T(8,128)(2,1)S(1)}, bf16[256,128]{1,0:T(8,128)(2,1)S(1)}, u32[]{:S(2)}, u32[]{:S(2)}) collective-permute-start(bf16[256,128]{1,0:T(8,128)(2,1)S(1)} %get-tuple-element.63), channel_id=1, source_target_pairs={{0,5},{1,6},{2,7},{3,4},{4,9},{5,10},{6,11},{7,8},{8,13},{9,14},{1... | collective-permute-start | bytes 196616 | tf_op jit(solution)/shard_map/ppermute | solution.py:523
  78.0 17.3 %collective-permute-start.16 = (bf16[256,128]{1,0:T(8,128)(2,1)S(1)}, bf16[256,128]{1,0:T(8,128)(2,1)S(1)}, u32[]{:S(2)}, u32[]{:S(2)}) collective-permute-start(bf16[256,128]{1,0:T(8,128)(2,1)S(1)} %get-tuple-element.64), channel_id=1, source_target_pairs={{0,6},{1,7},{2,4},{3,5},{4,10},{5,11},{6,8},{7,9},{8,14},{9,15},{1... | collective-permute-start | bytes 196616 | tf_op jit(solution)/shard_map/ppermute | solution.py:523
  83.0 12.3 %collective-permute-start.17 = (bf16[256,128]{1,0:T(8,128)(2,1)S(1)}, bf16[256,128]{1,0:T(8,128)(2,1)S(1)}, u32[]{:S(2)}, u32[]{:S(2)}) collective-permute-start(bf16[256,128]{1,0:T(8,128)(2,1)S(1)} %get-tuple-element.65), channel_id=1, source_target_pairs={{0,7},{1,4},{2,5},{3,6},{4,11},{5,8},{6,9},{7,10},{8,15},{9,12},{1... | collective-permute-start | bytes 196616 | tf_op jit(solution)/shard_map/ppermute | solution.py:523
  89.6 30.3 %copy-start.6 = (s32[2,4]{1,0:T(2,128)S(1)}, s32[2,4]{1,0:T(2,128)}, u32[]{:S(2)}) copy-start(s32[2,4]{1,0:T(2,128)} %get-tuple-element.41.counts_ref) | copy-start | bytes 100
  91.3 6.3 %collective-permute-start.18 = (bf16[256,128]{1,0:T(8,128)(2,1)S(1)}, bf16[256,128]{1,0:T(8,128)(2,1)S(1)}, u32[]{:S(2)}, u32[]{:S(2)}) collective-permute-start(bf16[256,128]{1,0:T(8,128)(2,1)S(1)} %get-tuple-element.68), channel_id=1, source_target_pairs={{0,1},{1,2},{2,3},{3,0},{4,5},{5,6},{6,7},{7,4},{8,9},{9,10},{10,1... | collective-permute-start | bytes 196616 | tf_op jit(solution)/shard_map/ppermute | solution.py:53
  92.5 6.6 %collective-permute-start.21 = (bf16[256,128]{1,0:T(8,128)(2,1)S(1)}, bf16[256,128]{1,0:T(8,128)(2,1)S(1)}, u32[]{:S(2)}, u32[]{:S(2)}) collective-permute-start(bf16[256,128]{1,0:T(8,128)(2,1)S(1)} %get-tuple-element.63), channel_id=1, source_target_pairs={{0,1},{1,2},{2,3},{3,0},{4,5},{5,6},{6,7},{7,4},{8,9},{9,10},{10,1... | collective-permute-start | bytes 196616 | tf_op jit(solution)/shard_map/ppermute | solution.py:53
  92.8 6.3 %collective-permute-start.19 = (bf16[256,128]{1,0:T(8,128)(2,1)S(1)}, bf16[256,128]{1,0:T(8,128)(2,1)S(1)}, u32[]{:S(2)}, u32[]{:S(2)}) collective-permute-start(bf16[256,128]{1,0:T(8,128)(2,1)S(1)} %get-tuple-element.69), channel_id=1, source_target_pairs={{0,2},{1,3},{2,0},{3,1},{4,6},{5,7},{6,4},{7,5},{8,10},{9,11},{10,... | collective-permute-start | bytes 196616 | tf_op jit(solution)/shard_map/ppermute | solution.py:53
  95.2 3.9 %collective-permute-start.20 = (bf16[256,128]{1,0:T(8,128)(2,1)S(1)}, bf16[256,128]{1,0:T(8,128)(2,1)S(1)}, u32[]{:S(2)}, u32[]{:S(2)}) collective-permute-start(bf16[256,128]{1,0:T(8,128)(2,1)S(1)} %get-tuple-element.70), channel_id=1, source_target_pairs={{0,3},{1,0},{2,1},{3,2},{4,7},{5,4},{6,5},{7,6},{8,11},{9,8},{10,9... | collective-permute-start | bytes 196616 | tf_op jit(solution)/shard_map/ppermute | solution.py:53
  95.3 4.6 %collective-permute-start.22 = (bf16[256,128]{1,0:T(8,128)(2,1)S(1)}, bf16[256,128]{1,0:T(8,128)(2,1)S(1)}, u32[]{:S(2)}, u32[]{:S(2)}) collective-permute-start(bf16[256,128]{1,0:T(8,128)(2,1)S(1)} %get-tuple-element.64), channel_id=1, source_target_pairs={{0,2},{1,3},{2,0},{3,1},{4,6},{5,7},{6,4},{7,5},{8,10},{9,11},{10,... | collective-permute-start | bytes 196616 | tf_op jit(solution)/shard_map/ppermute | solution.py:53
  97.6 4.1 %collective-permute-start.23 = (bf16[256,128]{1,0:T(8,128)(2,1)S(1)}, bf16[256,128]{1,0:T(8,128)(2,1)S(1)}, u32[]{:S(2)}, u32[]{:S(2)}) collective-permute-start(bf16[256,128]{1,0:T(8,128)(2,1)S(1)} %get-tuple-element.65), channel_id=1, source_target_pairs={{0,3},{1,0},{2,1},{3,2},{4,7},{5,4},{6,5},{7,6},{8,11},{9,8},{10,9... | collective-permute-start | bytes 196616 | tf_op jit(solution)/shard_map/ppermute | solution.py:53
  103.6 9.4 %collective-permute-start.24 = (bf16[784,128]{1,0:T(8,128)(2,1)S(1)}, bf16[784,128]{1,0:T(8,128)(2,1)S(1)}, u32[]{:S(2)}, u32[]{:S(2)}) collective-permute-start(bf16[784,128]{1,0:T(8,128)(2,1)S(1)} %get-tuple-element.71), channel_id=1, source_target_pairs={{0,252},{4,0},{8,4},{12,8},{16,12},{20,16},{24,20},{28,24},{32,28}... | collective-permute-start | bytes 602120 | tf_op jit(solution)/shard_map/ppermute | solution.py:53
  105.6 7.9 %collective-permute-start.25 = (bf16[784,128]{1,0:T(8,128)(2,1)S(1)}, bf16[784,128]{1,0:T(8,128)(2,1)S(1)}, u32[]{:S(2)}, u32[]{:S(2)}) collective-permute-start(bf16[784,128]{1,0:T(8,128)(2,1)S(1)} %get-tuple-element.73), channel_id=1, source_target_pairs={{0,4},{4,8},{8,12},{12,16},{16,20},{20,24},{24,28},{28,32},{32,36}... | collective-permute-start | bytes 602120 | tf_op jit(solution)/shard_map/ppermute | solution.py:53
  109.7 10.2 %collective-permute-start.26 = (bf16[784,128]{1,0:T(8,128)(2,1)S(1)}, bf16[784,128]{1,0:T(8,128)(2,1)S(1)}, u32[]{:S(2)}, u32[]{:S(2)}) collective-permute-start(bf16[784,128]{1,0:T(8,128)(2,1)S(1)} %get-tuple-element.74), channel_id=1, source_target_pairs={{0,8},{4,12},{8,16},{12,20},{16,24},{20,28},{24,32},{28,36},{32,40... | collective-permute-start | bytes 602120 | tf_op jit(solution)/shard_map/ppermute | solution.py:53

commit v4 on v3

--- a/solution.py
+++ b/solution.py
@@ -92,9 +92,9 @@
         in_specs=[VMEM, HBM],
         out_specs=(VMEM,) * LANES + (SMEM,),
         scratch_shapes=[pltpu.SemaphoreType.DMA((LANES,))],
-        compiler_params=pltpu.CompilerParams(vmem_limit_bytes=60 << 20),
+        compiler_params=pltpu.CompilerParams(vmem_limit_bytes=8 << 20),
         name="cut_windows",
-    )(ranks, feats)
+    )(ranks, pltpu.with_memory_space_constraint(feats, pltpu.HBM))
 
 
 def index_kernel(bricks, capacity, shift_ref, order_ref, after_ref, spots_ref, table_ref, wide_ref):
@@ -335,8 +335,10 @@
     )(*operands, *after)
 
 
-def mlp_kernel(groups, hidden_ref, gain_ref, *refs):
-    up_refs, down_refs = refs[:groups], refs[groups : 2 * groups]
+def mlp_kernel(groups, hidden_ref, gain_ref, up_ref, down_ref, ahead_ref, far_up_ref, far_down_ref, behind_ref, *refs):
+    depth = hidden_ref.shape[1]
+    up_refs = (up_ref, ahead_ref.at[:depth], far_up_ref, behind_ref.at[:depth])
+    down_refs = (down_ref, ahead_ref.at[depth:], far_down_ref, behind_ref.at[depth:])
     wide_ref, before_ref, result_ref = refs[-3:]
     outs = refs[-3 - groups : -3]
     queries, width = hidden_ref.shape
@@ -367,14 +369,14 @@
         outs[step][...] = result_ref[:, pl.ds(column, cut)]
 
 
-def mlp(hidden, gains, up, down, after):
-    groups = len(up)
+def mlp(hidden, gains, weights):
+    groups = 4
     rows, width = hidden.shape
-    middle = up[0].shape[1]
+    middle = weights[0].shape[1]
     return pl.pallas_call(
         functools.partial(mlp_kernel, groups),
         out_shape=(jax.ShapeDtypeStruct((rows, width // groups), BF16),) * groups,
-        in_specs=[VMEM] * (2 + 2 * groups) + [ANY] * len(after),
+        in_specs=[VMEM] * 8,
         out_specs=(VMEM,) * groups,
         scratch_shapes=[
             pltpu.VMEM((groups, rows, middle), BF16),
@@ -386,19 +388,41 @@
         ),
         compiler_params=pltpu.CompilerParams(vmem_limit_bytes=16 << 20),
         name="mlp",
-    )(hidden, gains, *up, *down, *after)
-
-
-def pack_kernel(shift_ref, table_ref, spots_ref, *rest):
-    sources, rest = rest[:12], rest[12:]
-    outs, lanes_ref, rows_ref = rest[:LANES], rest[LANES], rest[LANES + 1]
+    )(hidden, gains, *weights)
+
+
+def collect_kernel(*refs):
+    sources, out_ref = refs[:4], refs[4]
+    collect(sources, out_ref, 0)
+
+
+def collect(sources, out_ref, base):
     queries = sources[0].shape[0]
-    lanes_ref[...] = jnp.zeros_like(lanes_ref)
     rank = lax.axis_index("mp")
     for index, source in enumerate(sources):
-        sender = lax.rem(rank - index % 4 + 4, 4)
-        at = pl.multiple_of(index // 4 * PATCH + sender * queries, queries)
-        rows_ref[pl.ds(at, queries), :] = source[...]
+        sender = lax.rem(rank - index + 4, 4)
+        at = pl.multiple_of(base + sender * queries, queries)
+        out_ref[pl.ds(at, queries), :] = source[...]
+
+
+def collect_rows(sources):
+    return pl.pallas_call(
+        collect_kernel,
+        out_shape=jax.ShapeDtypeStruct((PATCH, sources[0].shape[1]), BF16),
+        in_specs=[VMEM] * 4,
+        out_specs=VMEM,
+        compiler_params=pltpu.CompilerParams(vmem_limit_bytes=4 << 20),
+        name="collect_rows",
+    )(*sources)
+
+
+def pack_kernel(shift_ref, table_ref, spots_ref, *rest):
+    tail_ref, last_ref, sources, rest = rest[0], rest[1], rest[2:6], rest[6:]
+    outs, lanes_ref, rows_ref = rest[:LANES], rest[LANES], rest[LANES + 1]
+    lanes_ref[...] = jnp.zeros_like(lanes_ref)
+    rows_ref[:PATCH, :] = tail_ref[...]
+    rows_ref[2 * PATCH :, :] = last_ref[...]
+    collect(sources, rows_ref, PATCH)
     begin = lax.div(PATCH - shift_ref[0], BLOCK)
     for step in range(2 * BLOCKS + 1):
         place = jnp.minimum(begin + step, 3 * BLOCKS - 1)
@@ -492,11 +516,9 @@
     half = near.shape[0] // 2
     far_a, far_b = shifted(ahead[:half], "mp", 1), shifted(behind[half:], "mp", -1)
     early = (near, ahead, far_a, far_b, behind)
-    ahead, behind, up_out, down_out = lax.optimization_barrier(
-        (ahead, behind, up_weight, down_weight)
-    )
-    up_ahead, up_behind = shifted(up_out, "mp", 1), shifted(up_out, "mp", -1)
-    down_ahead, down_behind = shifted(down_out, "mp", 1), shifted(down_out, "mp", -1)
+    late = jnp.concatenate([up_weight, down_weight], axis=0)
+    late, ahead, behind = lax.optimization_barrier((late, ahead, behind))
+    late_ahead, late_behind = shifted(late, "mp", 1), shifted(late, "mp", -1)
 
     spots, table = index_tables(
         bricks, capacity, patch_shift, curve_order.reshape(shard // BLOCK, BLOCK), near
@@ -506,38 +528,28 @@
     common = (table, spots, lanes, norm_gains, early)
     patch0 = project(0, *common, (head,), queries)
     mixed = attend((0, 1), patch0, early, (), ())
-    up_ahead, down_behind, mixed = lax.optimization_barrier((up_ahead, down_behind, mixed))
-    up_far, down_far = shifted(up_ahead, "mp", 1), shifted(down_behind, "mp", -1)
-    up = (up_weight, up_ahead, up_far, up_behind)
-    down = (down_weight, down_ahead, down_far, down_behind)
+    late_ahead, late_behind, mixed = lax.optimization_barrier((late_ahead, late_behind, mixed))
+    middle = late.shape[0] // 2
+    far_up = shifted(late_ahead[:middle], "mp", 1)
+    far_down = shifted(late_behind[middle:], "mp", -1)
+    weights = (up_weight, down_weight, late_ahead, far_up, far_down, late_behind)
     patch1 = project(1, *common, (head_next, mixed), queries)
 
-    blocks = mlp(attend((0, 1, 2, 3), patch1, early, (), ()), norm_gains, up, down, ())
-
-    def onward(step):
-        pairs = [
-            (brick * parts + rank, (brick + 1) % bricks * parts + (rank + step) % parts)
-            for brick in range(bricks)
-            for rank in range(parts)
-        ]
-        return lax.ppermute(blocks[step], ("brick", "mp"), pairs)
-
-    tail, last = [], [blocks[0]]
-    for step in range(parts):
-        tail.append(onward(step))
-        if step:
-            last.append(shifted(blocks[step], "mp", step))
+    blocks = mlp(attend((0, 1, 2, 3), patch1, early, (), ()), norm_gains, weights)
+
+    last = [blocks[0]]
+    for step in range(1, parts):
+        last.append(shifted(blocks[step], "mp", step))
     hidden = attend((2, 3), patch0, early, (mixed,), (blocks[0],))
-    blocks = mlp(hidden, norm_gains, up, down, ())
+    last = collect_rows(last)
+    tail = shifted(last, "brick", 1)
+    blocks = mlp(hidden, norm_gains, weights)
     first = [blocks[0]] + [shifted(blocks[step], "mp", step) for step in range(1, parts)]
-    back0, back1, back2, back3 = pack_lanes(patch_shift, table, spots, (*tail, *first, *last))
-    pieces = (
-        shifted(back0, "brick", -1),
-        back1,
-        shifted(back2, "brick", 1),
-        shifted(back3, "brick", 2),
-    )
-    return place_rows(counts, pieces, capacity)
+    back0, back1, back2, back3 = pack_lanes(patch_shift, table, spots, (tail, last, *first))
+    back3 = shifted(back3, "brick", 2)
+    back2 = shifted(back2, "brick", 1)
+    back0 = shifted(back0, "brick", -1)
+    return place_rows(counts, (back0, back1, back2, back3), capacity)
 
 
 def solution(mesh):

time: 122 us -> 125 us (1.025)
  waiting for transfers between devices: 25.5 us -> 37.9 us
  starting transfers between devices: 49.8 us -> 40.8 us
  Pallas kernels: 45.2 us -> 43.4 us
    ppermute x23 -> x22, waiting for transfers between devices: 25.5 us -> 37.9 us  [shifted(): return lax.ppermute(value, axis, pairs)]
    ppermute x4 -> x0, starting transfers between devices: 6.84 us -> none  [onward(): return lax.ppermute(blocks[step], ('brick', 'mp'), pairs)]
    ppermute x23 -> x22, starting transfers between devices: 43 us -> 40.8 us  [shifted(): return lax.ppermute(value, axis, pairs)]
    pallas_call x1, Pallas kernels: 4.55 us -> 2.66 us  [cut_windows(): pl.pallas_call(functools.partial(cut_kernel, bricks, shard), out_shape=(p...]
  transfers between devices with their start and end apart: 27 -> 22, of which waited for: 8 -> 14; matrix products, arithmetic and copies ran while one was open for 0% -> 1% of each run, Pallas kernels for 29% -> 28%
where the time goes in v4:
time: 125 us; the launch traced here: 124 us
  Pallas kernels  43.4 us (35%)
  starting transfers between devices  40.8 us (33%)
  waiting for transfers between devices  37.9 us (30%)
    ppermute x22, starting transfers between devices, shifted(): return lax.ppermute(value, axis, pairs)  40.8 us
    ppermute x22, waiting for transfers between devices, shifted(): return lax.ppermute(value, axis, pairs)  37.9 us
    pallas_call x3, Pallas kernels, attend(): pl.pallas_call(functools.partial(attend_kernel, groups, final), out_shape...  22.7 us
    pallas_call x2, Pallas kernels, project(): pl.pallas_call(functools.partial(project_kernel, part), out_shape=(shape(...  8.5 us
    pallas_call x2, Pallas kernels, mlp(): pl.pallas_call(functools.partial(mlp_kernel, groups), out_shape=(jax.Shap...  3.28 us
    pallas_call x1, Pallas kernels, cut_windows(): pl.pallas_call(functools.partial(cut_kernel, bricks, shard), out_shape=(p...  2.66 us
  transfers between devices with their start and end apart: 22, of which 14 were waited for; matrix products, arithmetic and copies ran while one was open for 1% of the time, Pallas kernels for 28%

profile of v4, /device:TPU:1, one launch (start us, length us, event | category | flops | bytes accessed | tf_op | source)
XLA Modules:
  0.0 124.4 jit_solution(10807685794819110019)
XLA Ops:
  0.0 0.8 copy-done.4
  0.8 2.7 %cut_windows.1 = (bf16[784,512]{1,0:T(8,128)(2,1)S(1)}, bf16[784,512]{1,0:T(8,128)(2,1)S(1)}, bf16[784,512]{1,0:T(8,128)(2,1)S(1)}, bf16[784,512]{1,0:T(8,128)(2,1)S(1)}, s32[2,4]{1,0:T(2,128)S(1)}) custom-call(s32[24,128]{1,0:T(8,128)S(1)} %bitcast.3, bf16[3072,512]{1,0:T(8,128)(2,1)} %feats_ref.1), custom_call_target="tpu_custom_call" | custom-call | tf_op jit(solution)/shard_map/cut_windows/pallas_call | solution.py:89
  3.4 0.0 copy-start.5
  3.4 0.0 copy-start.1
  3.5 0.0 copy-start.2
  3.5 3.2 %collective-permute-start = (bf16[784,512]{1,0:T(8,128)(2,1)S(1)}, bf16[784,512]{1,0:T(8,128)(2,1)S(1)}, u32[]{:S(2)}, u32[]{:S(2)}) collective-permute-start(bf16[784,512]{1,0:T(8,128)(2,1)S(1)} %get-tuple-element.45), channel_id=1, source_target_pairs={{0,4},{4,8},{8,12},{12,16},{16,20},{20,24},{24,28},{28,32},{32,36}... | collective-permute-start | bytes 2408456 | tf_op jit(solution)/shard_map/ppermute | solution.py:53
  6.7 0.1 collective-permute-start.1
  6.8 6.5 %collective-permute-start.2 = (bf16[784,512]{1,0:T(8,128)(2,1)S(1)}, bf16[784,512]{1,0:T(8,128)(2,1)S(1)}, u32[]{:S(2)}, u32[]{:S(2)}) collective-permute-start(bf16[784,512]{1,0:T(8,128)(2,1)S(1)} %get-tuple-element.48), channel_id=1, source_target_pairs={{0,248},{4,252},{8,0},{12,4},{16,8},{20,12},{24,16},{28,20},{32,24... | collective-permute-start | bytes 2408456 | tf_op jit(solution)/shard_map/ppermute | solution.py:53
  13.3 0.4 convolution_convert_fusion
  13.8 2.6 %collective-permute-start.5 = (bf16[512,512]{1,0:T(8,128)(2,1)S(1)}, bf16[512,512]{1,0:T(8,128)(2,1)S(1)}, u32[]{:S(2)}, u32[]{:S(2)}) collective-permute-start(bf16[512,512]{1,0:T(8,128)(2,1)S(1)} %pad_maximum_fusion.1.after_ref.refs_5_.refs_1_), channel_id=1, source_target_pairs={{0,3},{1,0},{2,1},{3,2},{4,7},{5,4},{6,5},{7,6},{8,11},{9,8},{10,9... | collective-permute-start | bytes 1572872 | tf_op jit(solution)/shard_map/ppermute | solution.py:53
  16.3 0.0 collective-permute-start.3
  16.4 9.3 %collective-permute-done.5.refs_9_.refs_4_ = bf16[512,512]{1,0:T(8,128)(2,1)S(1)} collective-permute-done((bf16[512,512]{1,0:T(8,128)(2,1)S(1)}, bf16[512,512]{1,0:T(8,128)(2,1)S(1)}, u32[]{:S(2)}, u32[]{:S(2)}) %collective-permute-start.5) | collective-permute-done | bytes 524320 | tf_op jit(solution)/shard_map/ppermute | solution.py:53
  25.7 3.5 %collective-permute-start.6 = (bf16[256,512]{1,0:T(8,128)(2,1)S(1)}, bf16[256,512]{1,0:T(8,128)(2,1)S(1)}, u32[]{:S(2)}, u32[]{:S(2)}) collective-permute-start(bf16[256,512]{1,0:T(8,128)(2,1)S(1)} %slice.17), channel_id=1, source_target_pairs={{0,3},{1,0},{2,1},{3,2},{4,7},{5,4},{6,5},{7,6},{8,11},{9,8},{10,9... | collective-permute-start | bytes 786440 | tf_op jit(solution)/shard_map/ppermute | solution.py:53
  29.2 0.0 collective-permute-done.3.refs_6_.refs_2_
  29.2 0.1 collective-permute-start.4
  30.0 0.0 copy-done.5
  30.0 0.6 index_tables.1
  30.6 0.1 pad_maximum_fusion
  30.7 1.8 %collective-permute-done.6.refs_5_.refs_8_.refs_3_ = bf16[256,512]{1,0:T(8,128)(2,1)S(1)} collective-permute-done((bf16[256,512]{1,0:T(8,128)(2,1)S(1)}, bf16[256,512]{1,0:T(8,128)(2,1)S(1)}, u32[]{:S(2)}, u32[]{:S(2)}) %collective-permute-start.6) | collective-permute-done | bytes 262176 | tf_op jit(solution)/shard_map/ppermute | solution.py:53
  32.5 3.1 %collective-permute-start.9 = (bf16[1024,512]{1,0:T(8,128)(2,1)S(1)}, bf16[1024,512]{1,0:T(8,128)(2,1)S(1)}, u32[]{:S(2)}, u32[]{:S(2)}) collective-permute-start(bf16[1024,512]{1,0:T(8,128)(2,1)S(1)} %pad_maximum_fusion), channel_id=1, source_target_pairs={{0,3},{1,0},{2,1},{3,2},{4,7},{5,4},{6,5},{7,6},{8,11},{9,8},{10,9... | collective-permute-start | bytes 3145736 | tf_op jit(solution)/shard_map/ppermute | solution.py:53
  35.6 0.1 collective-permute-done.4.refs_4_.refs_7_
  35.7 0.0 collective-permute-start.8
  35.7 0.0 collective-permute-done.refs_0_
  35.7 0.0 collective-permute-done.1.refs_2_
  35.8 0.0 collective-permute-done.2.refs_3_
  35.8 0.0 copy-start.3
  35.8 1.8 %head_rows.1.refs_10_ = bf16[1024,512]{1,0:T(8,128)(2,1)S(1)} custom-call(s32[24,128]{1,0:T(8,128)S(1)} %get-tuple-element.43.table_ref, s32[24,128]{1,0:T(8,128)S(1)} %get-tuple-element.44.spots_ref, bf16[784,512]{1,0:T(8,128)(2,1)S(1)} %collective-permute-done.refs_0_, bf16[784,512]{1,0:T(8,128)(2,1)S(1)} %get-tuple-element.46.refs_1_, ...), custom_call_target="tpu_custom_call" | custom-call | flops 805306368 | bytes 5242880 | tf_op jit(solution)/shard_map/head_rows/pallas_call | solution.py:182
  37.5 4.5 %collective-permute-start.7 = (bf16[1024,512]{1,0:T(8,128)(2,1)S(1)}, bf16[1024,512]{1,0:T(8,128)(2,1)S(1)}, u32[]{:S(2)}, u32[]{:S(2)}) collective-permute-start(bf16[1024,512]{1,0:T(8,128)(2,1)S(1)} %head_rows.1.refs_10_), channel_id=1, source_target_pairs={{0,252},{4,0},{8,4},{12,8},{16,12},{20,16},{24,20},{28,24},{32,28}... | collective-permute-start | bytes 3145736 | tf_op jit(solution)/shard_map/ppermute | solution.py:53
  42.0 4.3 %project_first.1 = (bf16[256,512]{1,0:T(8,128)(2,1)S(1)}, bf16[1024,512]{1,0:T(8,128)(2,1)S(1)}, bf16[512,1024]{1,0:T(8,128)(2,1)S(1)}, bf16[512,256]{1,0:T(8,128)(2,1)S(1)}) custom-call(s32[24,128]{1,0:T(8,128)S(1)} %get-tuple-element.43.table_ref, s32[24,128]{1,0:T(8,128)S(1)} %get-tuple-element.44.spots_ref, ...), custom_call_target="tpu_custom_call" | custom-call | flops 10000000000 | bytes 10485760 | tf_op jit(solution)/shard_map/project_first/pallas_call | solution.py:232
  46.3 5.8 %shard_map.91.refs_11_.refs_5_ = bf16[256,256]{1,0:T(8,128)(2,1)S(1)} custom-call(bf16[1024,512]{1,0:T(8,128)(2,1)S(1)} %get-tuple-element.50.keys_ref, bf16[512,1024]{1,0:T(8,128)(2,1)S(1)} %get-tuple-element.51.values_ref, bf16[512,256]{1,0:T(8,128)(2,1)S(1)} %get-tuple-element.52.query_ref), custom_call_target="tpu_custom_call" | custom-call | flops 16000000000 | bytes 5242880 | tf_op jit(solution)/shard_map/pallas_call | solution.py:323
  52.1 2.1 %collective-permute-done.9.behind_ref = bf16[1024,512]{1,0:T(8,128)(2,1)S(1)} collective-permute-done((bf16[1024,512]{1,0:T(8,128)(2,1)S(1)}, bf16[1024,512]{1,0:T(8,128)(2,1)S(1)}, u32[]{:S(2)}, u32[]{:S(2)}) %collective-permute-start.9) | collective-permute-done | bytes 1048608 | tf_op jit(solution)/shard_map/ppermute | solution.py:53
  54.2 3.2 %collective-permute-done.8.ahead_ref = bf16[1024,512]{1,0:T(8,128)(2,1)S(1)} collective-permute-done((bf16[1024,512]{1,0:T(8,128)(2,1)S(1)}, bf16[1024,512]{1,0:T(8,128)(2,1)S(1)}, u32[]{:S(2)}, u32[]{:S(2)}) %collective-permute-start.8) | collective-permute-done | bytes 1048608 | tf_op jit(solution)/shard_map/ppermute | solution.py:53
  57.5 0.3 collective-permute-start.11
  57.8 1.3 %collective-permute-start.10 = (bf16[512,512]{1,0:T(8,128)(2,1)S(1)}, bf16[512,512]{1,0:T(8,128)(2,1)S(1)}, u32[]{:S(2)}, u32[]{:S(2)}) collective-permute-start(bf16[512,512]{1,0:T(8,128)(2,1)S(1)} %slice.14), channel_id=1, source_target_pairs={{0,1},{1,2},{2,3},{3,0},{4,5},{5,6},{6,7},{7,4},{8,9},{9,10},{10,1... | collective-permute-start | bytes 1572872 | tf_op jit(solution)/shard_map/ppermute | solution.py:53
  59.1 0.0 collective-permute-done.7.refs_10_
  59.1 4.2 %project_last.1 = (bf16[256,512]{1,0:T(8,128)(2,1)S(1)}, bf16[1024,512]{1,0:T(8,128)(2,1)S(1)}, bf16[512,1024]{1,0:T(8,128)(2,1)S(1)}, bf16[512,256]{1,0:T(8,128)(2,1)S(1)}) custom-call(s32[24,128]{1,0:T(8,128)S(1)} %get-tuple-element.43.table_ref, s32[24,128]{1,0:T(8,128)S(1)} %get-tuple-element.44.spots_ref, ...), custom_call_target="tpu_custom_call" | custom-call | flops 10000000000 | bytes 10485760 | tf_op jit(solution)/shard_map/project_last/pallas_call | solution.py:232
  63.3 10.6 %shard_map.92.hidden_ref = bf16[256,512]{1,0:T(8,128)(2,1)S(1)} custom-call(bf16[1024,512]{1,0:T(8,128)(2,1)S(1)} %get-tuple-element.54.keys_ref, bf16[512,1024]{1,0:T(8,128)(2,1)S(1)} %get-tuple-element.55.values_ref, bf16[512,256]{1,0:T(8,128)(2,1)S(1)} %get-tuple-element.56.query_ref, bf16[256,512]{1,0:T(8,128)(2,1)S(1)} %get-tuple-element.57.refs_0_, ...), custom_call_target="tpu_custom_call" | custom-call | flops 32000000000 | bytes 5242880 | tf_op jit(solution)/shard_map/pallas_call | solution.py:323
  73.9 0.0 collective-permute-done.11.far_down_ref
  73.9 0.0 collective-permute-done.10.far_up_ref
  73.9 1.6 %mlp.2 = (bf16[256,128]{1,0:T(8,128)(2,1)S(1)}, bf16[256,128]{1,0:T(8,128)(2,1)S(1)}, bf16[256,128]{1,0:T(8,128)(2,1)S(1)}, bf16[256,128]{1,0:T(8,128)(2,1)S(1)}) custom-call(bf16[256,512]{1,0:T(8,128)(2,1)S(1)} %shard_map.92.hidden_ref, f32[2,512]{1,0:T(2,128)S(1)} %copy-done.3, bf16[512,512]{1,0:T(8,128)(2,1)S(1)} %copy-done.1, ...), custom_call_target="tpu_custom_call" | custom-call | flops 1073741824 | bytes 5242880 | tf_op jit(solution)/shard_map/mlp/pallas_call | solution.py:376
  75.6 0.1 collective-permute-start.12
  75.7 2.6 %collective-permute-start.13 = (bf16[256,128]{1,0:T(8,128)(2,1)S(1)}, bf16[256,128]{1,0:T(8,128)(2,1)S(1)}, u32[]{:S(2)}, u32[]{:S(2)}) collective-permute-start(bf16[256,128]{1,0:T(8,128)(2,1)S(1)} %get-tuple-element.62), channel_id=1, source_target_pairs={{0,2},{1,3},{2,0},{3,1},{4,6},{5,7},{6,4},{7,5},{8,10},{9,11},{10,... | collective-permute-start | bytes 196616 | tf_op jit(solution)/shard_map/ppermute | solution.py:53
  78.3 0.1 collective-permute-start.14
  78.4 1.6 %collective-permute-done.12.refs_1_ = bf16[256,128]{1,0:T(8,128)(2,1)S(1)} collective-permute-done((bf16[256,128]{1,0:T(8,128)(2,1)S(1)}, bf16[256,128]{1,0:T(8,128)(2,1)S(1)}, u32[]{:S(2)}, u32[]{:S(2)}) %collective-permute-start.12) | collective-permute-done | bytes 65568 | tf_op jit(solution)/shard_map/ppermute | solution.py:53
  80.0 0.7 collective-permute-done.13.refs_2_
  80.7 0.7 collective-permute-done.14.refs_3_
  81.4 4.3 %collective-permute-start.15 = (bf16[1024,128]{1,0:T(8,128)(2,1)S(1)}, bf16[1024,128]{1,0:T(8,128)(2,1)S(1)}, u32[]{:S(2)}, u32[]{:S(2)}) collective-permute-start(bf16[1024,128]{1,0:T(8,128)(2,1)S(1)} %collect_rows.1.rest_1_), channel_id=1, source_target_pairs={{0,4},{4,8},{8,12},{12,16},{16,20},{20,24},{24,28},{28,32},{32,36}... | collective-permute-start | bytes 786440 | tf_op jit(solution)/shard_map/ppermute | solution.py:53
  85.7 6.3 %shard_map.93.hidden_ref = bf16[256,512]{1,0:T(8,128)(2,1)S(1)} custom-call(bf16[1024,512]{1,0:T(8,128)(2,1)S(1)} %get-tuple-element.50.keys_ref, bf16[512,1024]{1,0:T(8,128)(2,1)S(1)} %get-tuple-element.51.values_ref, bf16[512,256]{1,0:T(8,128)(2,1)S(1)} %get-tuple-element.52.query_ref, bf16[256,512]{1,0:T(8,128)(2,1)S(1)} %get-tuple-element.64.refs_0_, ...), custom_call_target="tpu_custom_call" | custom-call | flops 16000000000 | bytes 5242880 | tf_op jit(solution)/shard_map/pallas_call | solution.py:323
  92.0 1.6 %mlp.3 = (bf16[256,128]{1,0:T(8,128)(2,1)S(1)}, bf16[256,128]{1,0:T(8,128)(2,1)S(1)}, bf16[256,128]{1,0:T(8,128)(2,1)S(1)}, bf16[256,128]{1,0:T(8,128)(2,1)S(1)}) custom-call(bf16[256,512]{1,0:T(8,128)(2,1)S(1)} %shard_map.93.hidden_ref, f32[2,512]{1,0:T(2,128)S(1)} %copy-done.3, bf16[512,512]{1,0:T(8,128)(2,1)S(1)} %copy-done.1, ...), custom_call_target="tpu_custom_call" | custom-call | flops 1073741824 | bytes 5242880 | tf_op jit(solution)/shard_map/mlp/pallas_call | solution.py:376
  93.6 1.0 collective-permute-start.16
  94.6 2.3 %collective-permute-start.17 = (bf16[256,128]{1,0:T(8,128)(2,1)S(1)}, bf16[256,128]{1,0:T(8,128)(2,1)S(1)}, u32[]{:S(2)}, u32[]{:S(2)}) collective-permute-start(bf16[256,128]{1,0:T(8,128)(2,1)S(1)} %get-tuple-element.67), channel_id=1, source_target_pairs={{0,2},{1,3},{2,0},{3,1},{4,6},{5,7},{6,4},{7,5},{8,10},{9,11},{10,... | collective-permute-start | bytes 196616 | tf_op jit(solution)/shard_map/ppermute | solution.py:53
  96.9 0.2 collective-permute-start.18
  97.1 0.9 collective-permute-done.16.rest_3_
  98.0 1.2 collective-permute-done.17.rest_4_
  99.2 0.7 collective-permute-done.18.rest_5_
  100.0 0.0 collective-permute-done.15.rest_0_
  100.0 1.9 %pack_lanes.1 = (bf16[784,128]{1,0:T(8,128)(2,1)S(1)}, bf16[784,128]{1,0:T(8,128)(2,1)S(1)}, bf16[784,128]{1,0:T(8,128)(2,1)S(1)}, bf16[784,128]{1,0:T(8,128)(2,1)S(1)}) custom-call(s32[1]{0:T(128)S(6)} %copy.10.shift_ref, s32[24,128]{1,0:T(8,128)S(1)} %get-tuple-element.43.table_ref, s32[24,128]{1,0:T(8,128)S(1)} %get-tuple-element.44.spots_ref, ...), custom_call_target="tpu_custom_call" | custom-call | tf_op jit(solution)/shard_map/pack_lanes/pallas_call | solution.py:444
  101.9 5.1 %collective-permute-start.19 = (bf16[784,128]{1,0:T(8,128)(2,1)S(1)}, bf16[784,128]{1,0:T(8,128)(2,1)S(1)}, u32[]{:S(2)}, u32[]{:S(2)}) collective-permute-start(bf16[784,128]{1,0:T(8,128)(2,1)S(1)} %get-tuple-element.69), channel_id=1, source_target_pairs={{0,252},{4,0},{8,4},{12,8},{16,12},{20,16},{24,20},{28,24},{32,28}... | collective-permute-start | bytes 602120 | tf_op jit(solution)/shard_map/ppermute | solution.py:53
  107.0 0.0 collective-permute-start.20
  107.0 0.0 collective-permute-start.21
  107.0 1.1 collective-permute-done.19.refs_0_
  108.1 3.2 %collective-permute-done.20.refs_2_ = bf16[784,128]{1,0:T(8,128)(2,1)S(1)} collective-permute-done((bf16[784,128]{1,0:T(8,128)(2,1)S(1)}, bf16[784,128]{1,0:T(8,128)(2,1)S(1)}, u32[]{:S(2)}, u32[]{:S(2)}) %collective-permute-start.20) | collective-permute-done | bytes 200736 | tf_op jit(solution)/shard_map/ppermute | solution.py:53
  111.3 11.1 %collective-permute-done.21.refs_3_ = bf16[784,128]{1,0:T(8,128)(2,1)S(1)} collective-permute-done((bf16[784,128]{1,0:T(8,128)(2,1)S(1)}, bf16[784,128]{1,0:T(8,128)(2,1)S(1)}, u32[]{:S(2)}, u32[]{:S(2)}) %collective-permute-start.21) | collective-permute-done | bytes 200736 | tf_op jit(solution)/shard_map/ppermute | solution.py:53
  122.4 2.0 %place_rows.1 = bf16[3072,128]{1,0:T(8,128)(2,1)} custom-call(s32[2,4]{1,0:T(2,128)S(1)} %get-tuple-element.40.counts_ref, bf16[784,128]{1,0:T(8,128)(2,1)S(1)} %collective-permute-done.19.refs_0_, bf16[784,128]{1,0:T(8,128)(2,1)S(1)} %get-tuple-element.70.refs_1_, bf16[784,128]{1,0:T(8,128)(2,1)S(1)} %collective-permute-done.20.refs_2_, ...), custom_call_target="tpu_custom_call" | custom-call | tf_op jit(solution)/shard_map/place_rows/pallas_call | solution.py:473
  (15 shorter events, 0.2 us)
Async XLA Ops:
  0.0 13.3 %copy-start = (bf16[512,384]{1,0:T(8,128)(2,1)S(1)}, bf16[512,384]{1,0:T(8,128)(2,1)}, u32[]{:S(2)}) copy-start(bf16[512,384]{1,0:T(8,128)(2,1)} %param.13) | copy-start | bytes 1179652
  0.0 0.8 copy-start.4
  0.8 13.0 %copy-start.6 = (bf16[128,512]{1,0:T(8,128)(2,1)S(1)}, bf16[128,512]{1,0:T(8,128)(2,1)}, u32[]{:S(2)}) copy-start(bf16[128,512]{1,0:T(8,128)(2,1)} %param.14) | copy-start | bytes 393220
  3.4 26.5 %copy-start.5 = (s32[2048]{0:T(1024)S(1)}, s32[2048]{0:T(1024)}, u32[]{:S(2)}) copy-start(s32[2048]{0:T(1024)} %param.11) | copy-start | bytes 24580
  3.4 27.1 %copy-start.1 = (bf16[512,512]{1,0:T(8,128)(2,1)S(1)}, bf16[512,512]{1,0:T(8,128)(2,1)}, u32[]{:S(2)}) copy-start(bf16[512,512]{1,0:T(8,128)(2,1)} %up_ref.3) | copy-start | bytes 1572868
  3.5 27.1 %copy-start.2 = (bf16[512,512]{1,0:T(8,128)(2,1)S(1)}, bf16[512,512]{1,0:T(8,128)(2,1)}, u32[]{:S(2)}) copy-start(bf16[512,512]{1,0:T(8,128)(2,1)} %down_ref.3) | copy-start | bytes 1572868
  3.5 32.3 %collective-permute-start = (bf16[784,512]{1,0:T(8,128)(2,1)S(1)}, bf16[784,512]{1,0:T(8,128)(2,1)S(1)}, u32[]{:S(2)}, u32[]{:S(2)}) collective-permute-start(bf16[784,512]{1,0:T(8,128)(2,1)S(1)} %get-tuple-element.45), channel_id=1, source_target_pairs={{0,4},{4,8},{8,12},{12,16},{16,20},{20,24},{24,28},{28,32},{32,36}... | collective-permute-start | bytes 2408456 | tf_op jit(solution)/shard_map/ppermute | solution.py:53
  6.7 29.0 %collective-permute-start.1 = (bf16[784,512]{1,0:T(8,128)(2,1)S(1)}, bf16[784,512]{1,0:T(8,128)(2,1)S(1)}, u32[]{:S(2)}, u32[]{:S(2)}) collective-permute-start(bf16[784,512]{1,0:T(8,128)(2,1)S(1)} %get-tuple-element.47), channel_id=1, source_target_pairs={{0,252},{4,0},{8,4},{12,8},{16,12},{20,16},{24,20},{28,24},{32,28}... | collective-permute-start | bytes 2408456 | tf_op jit(solution)/shard_map/ppermute | solution.py:53
  6.8 28.9 %collective-permute-start.2 = (bf16[784,512]{1,0:T(8,128)(2,1)S(1)}, bf16[784,512]{1,0:T(8,128)(2,1)S(1)}, u32[]{:S(2)}, u32[]{:S(2)}) collective-permute-start(bf16[784,512]{1,0:T(8,128)(2,1)S(1)} %get-tuple-element.48), channel_id=1, source_target_pairs={{0,248},{4,252},{8,0},{12,4},{16,8},{20,12},{24,16},{28,20},{32,24... | collective-permute-start | bytes 2408456 | tf_op jit(solution)/shard_map/ppermute | solution.py:53
  13.8 11.9 %collective-permute-start.5 = (bf16[512,512]{1,0:T(8,128)(2,1)S(1)}, bf16[512,512]{1,0:T(8,128)(2,1)S(1)}, u32[]{:S(2)}, u32[]{:S(2)}) collective-permute-start(bf16[512,512]{1,0:T(8,128)(2,1)S(1)} %pad_maximum_fusion.1.after_ref.refs_5_.refs_1_), channel_id=1, source_target_pairs={{0,3},{1,0},{2,1},{3,2},{4,7},{5,4},{6,5},{7,6},{8,11},{9,8},{10,9... | collective-permute-start | bytes 1572872 | tf_op jit(solution)/shard_map/ppermute | solution.py:53
  16.3 12.9 %collective-permute-start.3 = (bf16[512,512]{1,0:T(8,128)(2,1)S(1)}, bf16[512,512]{1,0:T(8,128)(2,1)S(1)}, u32[]{:S(2)}, u32[]{:S(2)}) collective-permute-start(bf16[512,512]{1,0:T(8,128)(2,1)S(1)} %pad_maximum_fusion.1.after_ref.refs_5_.refs_1_), channel_id=1, source_target_pairs={{0,1},{1,2},{2,3},{3,0},{4,5},{5,6},{6,7},{7,4},{8,9},{9,10},{10,1... | collective-permute-start | bytes 1572872 | tf_op jit(solution)/shard_map/ppermute | solution.py:53
  25.7 6.8 %collective-permute-start.6 = (bf16[256,512]{1,0:T(8,128)(2,1)S(1)}, bf16[256,512]{1,0:T(8,128)(2,1)S(1)}, u32[]{:S(2)}, u32[]{:S(2)}) collective-permute-start(bf16[256,512]{1,0:T(8,128)(2,1)S(1)} %slice.17), channel_id=1, source_target_pairs={{0,3},{1,0},{2,1},{3,2},{4,7},{5,4},{6,5},{7,6},{8,11},{9,8},{10,9... | collective-permute-start | bytes 786440 | tf_op jit(solution)/shard_map/ppermute | solution.py:53
  29.2 6.5 %collective-permute-start.4 = (bf16[256,512]{1,0:T(8,128)(2,1)S(1)}, bf16[256,512]{1,0:T(8,128)(2,1)S(1)}, u32[]{:S(2)}, u32[]{:S(2)}) collective-permute-start(bf16[256,512]{1,0:T(8,128)(2,1)S(1)} %slice.16), channel_id=1, source_target_pairs={{0,1},{1,2},{2,3},{3,0},{4,5},{5,6},{6,7},{7,4},{8,9},{9,10},{10,1... | collective-permute-start | bytes 786440 | tf_op jit(solution)/shard_map/ppermute | solution.py:53
  32.5 21.7 %collective-permute-start.9 = (bf16[1024,512]{1,0:T(8,128)(2,1)S(1)}, bf16[1024,512]{1,0:T(8,128)(2,1)S(1)}, u32[]{:S(2)}, u32[]{:S(2)}) collective-permute-start(bf16[1024,512]{1,0:T(8,128)(2,1)S(1)} %pad_maximum_fusion), channel_id=1, source_target_pairs={{0,3},{1,0},{2,1},{3,2},{4,7},{5,4},{6,5},{7,6},{8,11},{9,8},{10,9... | collective-permute-start | bytes 3145736 | tf_op jit(solution)/shard_map/ppermute | solution.py:53
  35.7 21.7 %collective-permute-start.8 = (bf16[1024,512]{1,0:T(8,128)(2,1)S(1)}, bf16[1024,512]{1,0:T(8,128)(2,1)S(1)}, u32[]{:S(2)}, u32[]{:S(2)}) collective-permute-start(bf16[1024,512]{1,0:T(8,128)(2,1)S(1)} %pad_maximum_fusion), channel_id=1, source_target_pairs={{0,1},{1,2},{2,3},{3,0},{4,5},{5,6},{6,7},{7,4},{8,9},{9,10},{10,1... | collective-permute-start | bytes 3145736 | tf_op jit(solution)/shard_map/ppermute | solution.py:53
  35.8 6.3 %copy-start.3 = (f32[2,512]{1,0:T(2,128)S(1)}, f32[2,512]{1,0:T(2,128)}, u32[]{:S(2)}) copy-start(f32[2,512]{1,0:T(2,128)} %gain_ref.3) | copy-start | bytes 12292
  37.5 21.5 %collective-permute-start.7 = (bf16[1024,512]{1,0:T(8,128)(2,1)S(1)}, bf16[1024,512]{1,0:T(8,128)(2,1)S(1)}, u32[]{:S(2)}, u32[]{:S(2)}) collective-permute-start(bf16[1024,512]{1,0:T(8,128)(2,1)S(1)} %head_rows.1.refs_10_), channel_id=1, source_target_pairs={{0,252},{4,0},{8,4},{12,8},{16,12},{20,16},{24,20},{28,24},{32,28}... | collective-permute-start | bytes 3145736 | tf_op jit(solution)/shard_map/ppermute | solution.py:53
  57.5 16.4 %collective-permute-start.11 = (bf16[512,512]{1,0:T(8,128)(2,1)S(1)}, bf16[512,512]{1,0:T(8,128)(2,1)S(1)}, u32[]{:S(2)}, u32[]{:S(2)}) collective-permute-start(bf16[512,512]{1,0:T(8,128)(2,1)S(1)} %slice.15), channel_id=1, source_target_pairs={{0,3},{1,0},{2,1},{3,2},{4,7},{5,4},{6,5},{7,6},{8,11},{9,8},{10,9... | collective-permute-start | bytes 1572872 | tf_op jit(solution)/shard_map/ppermute | solution.py:53
  57.8 16.1 %collective-permute-start.10 = (bf16[512,512]{1,0:T(8,128)(2,1)S(1)}, bf16[512,512]{1,0:T(8,128)(2,1)S(1)}, u32[]{:S(2)}, u32[]{:S(2)}) collective-permute-start(bf16[512,512]{1,0:T(8,128)(2,1)S(1)} %slice.14), channel_id=1, source_target_pairs={{0,1},{1,2},{2,3},{3,0},{4,5},{5,6},{6,7},{7,4},{8,9},{9,10},{10,1... | collective-permute-start | bytes 1572872 | tf_op jit(solution)/shard_map/ppermute | solution.py:53
  75.6 4.4 %collective-permute-start.12 = (bf16[256,128]{1,0:T(8,128)(2,1)S(1)}, bf16[256,128]{1,0:T(8,128)(2,1)S(1)}, u32[]{:S(2)}, u32[]{:S(2)}) collective-permute-start(bf16[256,128]{1,0:T(8,128)(2,1)S(1)} %get-tuple-element.61), channel_id=1, source_target_pairs={{0,1},{1,2},{2,3},{3,0},{4,5},{5,6},{6,7},{7,4},{8,9},{9,10},{10,1... | collective-permute-start | bytes 196616 | tf_op jit(solution)/shard_map/ppermute | solution.py:53
  75.7 5.0 %collective-permute-start.13 = (bf16[256,128]{1,0:T(8,128)(2,1)S(1)}, bf16[256,128]{1,0:T(8,128)(2,1)S(1)}, u32[]{:S(2)}, u32[]{:S(2)}) collective-permute-start(bf16[256,128]{1,0:T(8,128)(2,1)S(1)} %get-tuple-element.62), channel_id=1, source_target_pairs={{0,2},{1,3},{2,0},{3,1},{4,6},{5,7},{6,4},{7,5},{8,10},{9,11},{10,... | collective-permute-start | bytes 196616 | tf_op jit(solution)/shard_map/ppermute | solution.py:53
  78.3 3.1 %collective-permute-start.14 = (bf16[256,128]{1,0:T(8,128)(2,1)S(1)}, bf16[256,128]{1,0:T(8,128)(2,1)S(1)}, u32[]{:S(2)}, u32[]{:S(2)}) collective-permute-start(bf16[256,128]{1,0:T(8,128)(2,1)S(1)} %get-tuple-element.63), channel_id=1, source_target_pairs={{0,3},{1,0},{2,1},{3,2},{4,7},{5,4},{6,5},{7,6},{8,11},{9,8},{10,9... | collective-permute-start | bytes 196616 | tf_op jit(solution)/shard_map/ppermute | solution.py:53
  81.4 18.6 %collective-permute-start.15 = (bf16[1024,128]{1,0:T(8,128)(2,1)S(1)}, bf16[1024,128]{1,0:T(8,128)(2,1)S(1)}, u32[]{:S(2)}, u32[]{:S(2)}) collective-permute-start(bf16[1024,128]{1,0:T(8,128)(2,1)S(1)} %collect_rows.1.rest_1_), channel_id=1, source_target_pairs={{0,4},{4,8},{8,12},{12,16},{16,20},{20,24},{24,28},{28,32},{32,36}... | collective-permute-start | bytes 786440 | tf_op jit(solution)/shard_map/ppermute | solution.py:53
  93.6 4.4 %collective-permute-start.16 = (bf16[256,128]{1,0:T(8,128)(2,1)S(1)}, bf16[256,128]{1,0:T(8,128)(2,1)S(1)}, u32[]{:S(2)}, u32[]{:S(2)}) collective-permute-start(bf16[256,128]{1,0:T(8,128)(2,1)S(1)} %get-tuple-element.66), channel_id=1, source_target_pairs={{0,1},{1,2},{2,3},{3,0},{4,5},{5,6},{6,7},{7,4},{8,9},{9,10},{10,1... | collective-permute-start | bytes 196616 | tf_op jit(solution)/shard_map/ppermute | solution.py:53
  94.6 4.6 %collective-permute-start.17 = (bf16[256,128]{1,0:T(8,128)(2,1)S(1)}, bf16[256,128]{1,0:T(8,128)(2,1)S(1)}, u32[]{:S(2)}, u32[]{:S(2)}) collective-permute-start(bf16[256,128]{1,0:T(8,128)(2,1)S(1)} %get-tuple-element.67), channel_id=1, source_target_pairs={{0,2},{1,3},{2,0},{3,1},{4,6},{5,7},{6,4},{7,5},{8,10},{9,11},{10,... | collective-permute-start | bytes 196616 | tf_op jit(solution)/shard_map/ppermute | solution.py:53
  96.9 3.1 %collective-permute-start.18 = (bf16[256,128]{1,0:T(8,128)(2,1)S(1)}, bf16[256,128]{1,0:T(8,128)(2,1)S(1)}, u32[]{:S(2)}, u32[]{:S(2)}) collective-permute-start(bf16[256,128]{1,0:T(8,128)(2,1)S(1)} %get-tuple-element.68), channel_id=1, source_target_pairs={{0,3},{1,0},{2,1},{3,2},{4,7},{5,4},{6,5},{7,6},{8,11},{9,8},{10,9... | collective-permute-start | bytes 196616 | tf_op jit(solution)/shard_map/ppermute | solution.py:53
  101.9 6.1 %collective-permute-start.19 = (bf16[784,128]{1,0:T(8,128)(2,1)S(1)}, bf16[784,128]{1,0:T(8,128)(2,1)S(1)}, u32[]{:S(2)}, u32[]{:S(2)}) collective-permute-start(bf16[784,128]{1,0:T(8,128)(2,1)S(1)} %get-tuple-element.69), channel_id=1, source_target_pairs={{0,252},{4,0},{8,4},{12,8},{16,12},{20,16},{24,20},{28,24},{32,28}... | collective-permute-start | bytes 602120 | tf_op jit(solution)/shard_map/ppermute | solution.py:53
  107.0 4.3 %collective-permute-start.20 = (bf16[784,128]{1,0:T(8,128)(2,1)S(1)}, bf16[784,128]{1,0:T(8,128)(2,1)S(1)}, u32[]{:S(2)}, u32[]{:S(2)}) collective-permute-start(bf16[784,128]{1,0:T(8,128)(2,1)S(1)} %get-tuple-element.71), channel_id=1, source_target_pairs={{0,4},{4,8},{8,12},{12,16},{16,20},{20,24},{24,28},{28,32},{32,36}... | collective-permute-start | bytes 602120 | tf_op jit(solution)/shard_map/ppermute | solution.py:53
  107.0 15.4 %collective-permute-start.21 = (bf16[784,128]{1,0:T(8,128)(2,1)S(1)}, bf16[784,128]{1,0:T(8,128)(2,1)S(1)}, u32[]{:S(2)}, u32[]{:S(2)}) collective-permute-start(bf16[784,128]{1,0:T(8,128)(2,1)S(1)} %get-tuple-element.72), channel_id=1, source_target_pairs={{0,8},{4,12},{8,16},{12,20},{16,24},{20,28},{24,32},{28,36},{32,40... | collective-permute-start | bytes 602120 | tf_op jit(solution)/shard_map/ppermute | solution.py:53

commit v5 on v4

--- a/solution.py
+++ b/solution.py
@@ -95,6 +95,45 @@
         compiler_params=pltpu.CompilerParams(vmem_limit_bytes=8 << 20),
         name="cut_windows",
     )(ranks, pltpu.with_memory_space_constraint(feats, pltpu.HBM))
+
+
+def weights_kernel(qkv_ref, proj_ref, up_ref, down_ref, after_ref, near_ref, half_ref):
+    span = GROUP_HEADS * HEAD_DIM
+    shape = (3 * span, 3 * span)
+    row = lax.broadcasted_iota(jnp.int32, shape, 0)
+    column = lax.broadcasted_iota(jnp.int32, shape, 1)
+    kind, rest = row // span, row % span
+    source = rest // HEAD_DIM * (3 * HEAD_DIM) + kind * HEAD_DIM + rest % HEAD_DIM
+    order = jnp.where(column == source, 1.0, 0.0).astype(BF16)
+    near_ref[: 3 * span, :] = nt_dot(order, qkv_ref[...]).astype(BF16)
+    near_ref[3 * span :, :] = proj_ref[...]
+    odd = lax.rem(lax.axis_index("brick"), 2) == 1
+
+    @pl.when(jnp.logical_not(odd))
+    def _():
+        half_ref[: 2 * span, :] = near_ref[: 2 * span, :]
+        half_ref[2 * span :, :] = up_ref[...]
+
+    @pl.when(odd)
+    def _():
+        half_ref[: 2 * span, :] = near_ref[2 * span :, :]
+        half_ref[2 * span :, :] = down_ref[...]
+
+
+def sort_weights(qkv, proj, up, down, after):
+    width = proj.shape[1]
+    span = GROUP_HEADS * HEAD_DIM
+    return pl.pallas_call(
+        weights_kernel,
+        out_shape=(
+            jax.ShapeDtypeStruct((4 * span, width), BF16),
+            jax.ShapeDtypeStruct((2 * span + up.shape[0], width), BF16),
+        ),
+        in_specs=[VMEM] * 4 + [ANY],
+        out_specs=(VMEM, VMEM),
+        compiler_params=pltpu.CompilerParams(vmem_limit_bytes=8 << 20),
+        name="sort_weights",
+    )(qkv, proj, up, down, after)
 
 
 def index_kernel(bricks, capacity, shift_ref, order_ref, after_ref, spots_ref, table_ref, wide_ref):
@@ -192,21 +231,39 @@
     )(table, spots, *lanes, *after)
 
 
+def by_core(fill, weight_refs):
+    odd = lax.rem(lax.axis_index("brick"), 2) == 1
+    ahead, far, _, behind, ahead_other, far_other, _, behind_other = weight_refs[1:]
+    mine, other = (ahead, far, behind), (ahead_other, far_other, behind_other)
+
+    @pl.when(jnp.logical_not(odd))
+    def _():
+        fill(mine, other)
+
+    @pl.when(odd)
+    def _():
+        fill(other, mine)
+
+
 def project_kernel(part, table_ref, spots_ref, *refs):
     lane_refs, gain_ref = refs[:LANES], refs[LANES]
-    near_ref, ahead_ref, far_a_ref, far_b_ref, behind_ref = refs[LANES + 1 : LANES + 6]
-    extra_ref = refs[LANES + 6]
+    weight_refs = refs[LANES + 1 : LANES + 10]
+    extra_ref = refs[LANES + 10]
     own_ref, keys_ref, values_ref, query_ref, rows_ref, normed_ref, stack_ref = refs[-7:]
     queries = own_ref.shape[0]
     span = GROUP_HEADS * HEAD_DIM
-    for group, ref in enumerate((near_ref, ahead_ref, None, behind_ref)):
-        for kind in range(3):
-            if ref is None:
-                source = (far_a_ref, far_b_ref)[kind // 2]
-                at = kind % 2 * span
-            else:
-                source, at = ref, kind * span
-            stack_ref[kind, group * span : (group + 1) * span, :] = source[at : at + span, :]
+    near_ref = weight_refs[0]
+    for kind in range(3):
+        stack_ref[kind, :span, :] = near_ref[kind * span : (kind + 1) * span, :]
+
+    def fill(evens, odds):
+        for group in range(1, 4):
+            rows = slice(group * span, (group + 1) * span)
+            stack_ref[0, rows, :] = evens[group - 1][:span, :]
+            stack_ref[1, rows, :] = evens[group - 1][span : 2 * span, :]
+            stack_ref[2, rows, :] = odds[group - 1][:span, :]
+
+    by_core(fill, weight_refs)
     gain = gain_ref[0:1, :]
     for quarter in range(4):
         for block in range(quarter * 2, quarter * 2 + 2):
@@ -232,7 +289,7 @@
     return pl.pallas_call(
         functools.partial(project_kernel, part),
         out_shape=(shape(queries, width), shape(PATCH, width), shape(width, PATCH), shape(width, queries)),
-        in_specs=[SMEM] + [VMEM] * (LANES + 7) + ([VMEM] + [ANY] * (len(extra) - 1) if part else [ANY] * len(extra)),
+        in_specs=[SMEM] + [VMEM] * (LANES + 11) + ([VMEM] + [ANY] * (len(extra) - 1) if part else [ANY] * len(extra)),
         out_specs=(VMEM,) * 4,
         scratch_shapes=[
             pltpu.VMEM((PATCH, width), BF16),
@@ -247,7 +304,7 @@
 
 def attend_kernel(groups, final, keys_ref, values_ref, query_ref, *refs):
     mixed_ref, score_ref = refs[-2:]
-    out_ref = refs[-3] if final else None
+    out_ref = refs[-4] if final else None
     queries = query_ref.shape[1]
     span = GROUP_HEADS * HEAD_DIM
     first = groups[0]
@@ -293,16 +350,23 @@
     lax.fori_loop(0, GROUP_HEADS, head_step, highest)
     if not final:
         return
-    own_ref, near_ref, ahead_ref, far_b_ref, behind_ref = refs[:5]
+    own_ref, weight_refs = refs[0], refs[1:10]
+    proj_ref = refs[-3]
+    near_ref = weight_refs[0]
+    proj_ref[0] = near_ref[3 * span :, :]
+
+    def fill(evens, odds):
+        for group in range(1, 4):
+            proj_ref[group] = odds[group - 1][span : 2 * span, :]
+
+    by_core(fill, weight_refs)
     mixed = None
     for group in range(4):
         if group < first:
-            held = refs[5][group * span : (group + 1) * span, :]
+            held = refs[10][group * span : (group + 1) * span, :]
         else:
             held = mixed_ref[(group - first) * span : (group - first + 1) * span, :]
-        weight = (near_ref, ahead_ref, far_b_ref, behind_ref)[group]
-        weight = weight[span : 2 * span, :] if group == 2 else weight[3 * span :, :]
-        term = tn_dot(held, weight).astype(BF16).astype(F32)
+        term = tn_dot(held, proj_ref[group]).astype(BF16).astype(F32)
         mixed = term if mixed is None else mixed + term
     out_ref[...] = (own_ref[...].astype(F32) + mixed).astype(BF16)
 
@@ -313,13 +377,15 @@
     span = GROUP_HEADS * HEAD_DIM
     height = len(groups) * span
     final = groups[-1] == 3
-    near, ahead, _, far_b, behind = early
     operands = [keys, values, query]
     if final:
-        operands += [own, near, ahead, far_b, behind, *prior]
+        operands += [own, *early, *prior]
     scratch = [pltpu.VMEM((2, PATCH, queries), F32)]
     if final:
-        scratch = [pltpu.VMEM((height, queries), BF16)] + scratch
+        scratch = [
+            pltpu.VMEM((4, span, width), BF16),
+            pltpu.VMEM((height, queries), BF16),
+        ] + scratch
     return pl.pallas_call(
         functools.partial(attend_kernel, groups, final),
         out_shape=jax.ShapeDtypeStruct((queries, width) if final else (height, queries), BF16),
@@ -335,10 +401,35 @@
     )(*operands, *after)
 
 
-def mlp_kernel(groups, hidden_ref, gain_ref, up_ref, down_ref, ahead_ref, far_up_ref, far_down_ref, behind_ref, *refs):
+def mlp_kernel(groups, hidden_ref, gain_ref, up_ref, down_ref, *refs):
+    weight_refs, refs = refs[:9], refs[9:]
+    refs, ups_ref, downs_ref = refs[:-2], refs[-2], refs[-1]
     depth = hidden_ref.shape[1]
-    up_refs = (up_ref, ahead_ref.at[:depth], far_up_ref, behind_ref.at[:depth])
-    down_refs = (down_ref, ahead_ref.at[depth:], far_down_ref, behind_ref.at[depth:])
+    split = weight_refs[2].shape[0]
+    lead = weight_refs[1].shape[0] - depth
+    ahead, far_a, far_b, behind, ahead_o, far_a_o, far_b_o, behind_o = weight_refs[1:]
+    mine, other = (ahead, far_a, far_b, behind), (ahead_o, far_a_o, far_b_o, behind_o)
+
+    def fill(out_ref, sources):
+        out_ref[0] = sources[0][lead:, :]
+        out_ref[1, : split - lead, :] = sources[1][lead:, :]
+        out_ref[1, split - lead :, :] = sources[2][...]
+        out_ref[2] = sources[3][lead:, :]
+
+    odd = lax.rem(lax.axis_index("brick"), 2) == 1
+
+    @pl.when(jnp.logical_not(odd))
+    def _():
+        fill(ups_ref, mine)
+        fill(downs_ref, other)
+
+    @pl.when(odd)
+    def _():
+        fill(ups_ref, other)
+        fill(downs_ref, mine)
+
+    up_refs = (up_ref,) + tuple(ups_ref.at[group] for group in range(3))
+    down_refs = (down_ref,) + tuple(downs_ref.at[group] for group in range(3))
     wide_ref, before_ref, result_ref = refs[-3:]
     outs = refs[-3 - groups : -3]
     queries, width = hidden_ref.shape
@@ -369,26 +460,28 @@
         outs[step][...] = result_ref[:, pl.ds(column, cut)]
 
 
-def mlp(hidden, gains, weights):
+def mlp(hidden, gains, up, down, weights):
     groups = 4
     rows, width = hidden.shape
-    middle = weights[0].shape[1]
+    middle = up.shape[1]
     return pl.pallas_call(
         functools.partial(mlp_kernel, groups),
         out_shape=(jax.ShapeDtypeStruct((rows, width // groups), BF16),) * groups,
-        in_specs=[VMEM] * 8,
+        in_specs=[VMEM] * 13,
         out_specs=(VMEM,) * groups,
         scratch_shapes=[
             pltpu.VMEM((groups, rows, middle), BF16),
             pltpu.VMEM((2, BLOCK, middle), F32),
             pltpu.VMEM((rows, width), BF16),
+            pltpu.VMEM((groups - 1, width, middle), BF16),
+            pltpu.VMEM((groups - 1, middle, width), BF16),
         ],
         cost_estimate=pl.CostEstimate(
             flops=4 * rows * width * middle * groups, bytes_accessed=5 << 20, transcendentals=0
         ),
-        compiler_params=pltpu.CompilerParams(vmem_limit_bytes=16 << 20),
+        compiler_params=pltpu.CompilerParams(vmem_limit_bytes=18 << 20),
         name="mlp",
-    )(hidden, gains, *weights)
+    )(hidden, gains, up, down, *weights)
 
 
 def collect_kernel(*refs):
@@ -504,46 +597,40 @@
     lane2 = shifted(piece2, "brick", -1)
     lane0 = shifted(piece0, "brick", 1)
     lanes = (lane0, own, lane2, lane3)
-    counts, qkv_weight, proj_weight = lax.optimization_barrier((counts, qkv_weight, proj_weight))
-
-    span = GROUP_HEADS * HEAD_DIM
-    column = jnp.arange(3 * span, dtype=jnp.int32)
-    place = (column // HEAD_DIM % 3) * span + column // (3 * HEAD_DIM) * HEAD_DIM + column % HEAD_DIM
-    order = (place[None, :] == column[:, None]).astype(BF16)
-    qkv_rows = nt_dot(order, qkv_weight).astype(BF16)
-    near = jnp.concatenate([qkv_rows, proj_weight], axis=0)
-    ahead, behind = shifted(near, "mp", 1), shifted(near, "mp", -1)
-    half = near.shape[0] // 2
-    far_a, far_b = shifted(ahead[:half], "mp", 1), shifted(behind[half:], "mp", -1)
-    early = (near, ahead, far_a, far_b, behind)
-    late = jnp.concatenate([up_weight, down_weight], axis=0)
-    late, ahead, behind = lax.optimization_barrier((late, ahead, behind))
-    late_ahead, late_behind = shifted(late, "mp", 1), shifted(late, "mp", -1)
+    near, half = sort_weights(qkv_weight, proj_weight, up_weight, down_weight, own)
+    middle = half.shape[0] // 2
+
+    def swapped(value):
+        return lax.ppermute(value, "brick", [(brick, brick ^ 1) for brick in range(bricks)])
+
+    ahead = shifted(half, "mp", 1)
+    behind = shifted(half, "mp", -1)
+    far_a = shifted(ahead[:middle], "mp", 1)
+    far_b = shifted(behind[middle:], "mp", -1)
+    ahead_other, behind_other = swapped(ahead), swapped(behind)
+    far_a_other = swapped(far_a)
+    far_b_other = swapped(far_b)
+    weights = (near, ahead, far_a, far_b, behind, ahead_other, far_a_other, far_b_other, behind_other)
 
     spots, table = index_tables(
         bricks, capacity, patch_shift, curve_order.reshape(shard // BLOCK, BLOCK), near
     )
     head = head_rows(table, spots, lanes, (far_a, far_b))
     head_next = shifted(head, "brick", -1)
-    common = (table, spots, lanes, norm_gains, early)
+    common = (table, spots, lanes, norm_gains, weights)
     patch0 = project(0, *common, (head,), queries)
-    mixed = attend((0, 1), patch0, early, (), ())
-    late_ahead, late_behind, mixed = lax.optimization_barrier((late_ahead, late_behind, mixed))
-    middle = late.shape[0] // 2
-    far_up = shifted(late_ahead[:middle], "mp", 1)
-    far_down = shifted(late_behind[middle:], "mp", -1)
-    weights = (up_weight, down_weight, late_ahead, far_up, far_down, late_behind)
+    mixed = attend((0, 1), patch0, weights, (), ())
     patch1 = project(1, *common, (head_next, mixed), queries)
 
-    blocks = mlp(attend((0, 1, 2, 3), patch1, early, (), ()), norm_gains, weights)
+    blocks = mlp(attend((0, 1, 2, 3), patch1, weights, (), ()), norm_gains, up_weight, down_weight, weights)
 
     last = [blocks[0]]
     for step in range(1, parts):
         last.append(shifted(blocks[step], "mp", step))
-    hidden = attend((2, 3), patch0, early, (mixed,), (blocks[0],))
+    hidden = attend((2, 3), patch0, weights, (mixed,), (blocks[0],))
     last = collect_rows(last)
     tail = shifted(last, "brick", 1)
-    blocks = mlp(hidden, norm_gains, weights)
+    blocks = mlp(hidden, norm_gains, up_weight, down_weight, weights)
     first = [blocks[0]] + [shifted(blocks[step], "mp", step) for step in range(1, parts)]
     back0, back1, back2, back3 = pack_lanes(patch_shift, table, spots, (tail, last, *first))
     back3 = shifted(back3, "brick", 2)

time: 125 us -> 124 us (level)
  waiting for transfers between devices: 37.9 us -> 29.7 us
  starting transfers between devices: 40.8 us -> 48.1 us
    ppermute x0 -> x4, starting transfers between devices: none -> 19.1 us  [swapped(): lax.ppermute(value, 'brick', [(brick, brick ^ 1) for brick in range(brick...]
    ppermute x22 -> x18, starting transfers between devices: 40.8 us -> 29.1 us  [shifted(): return lax.ppermute(value, axis, pairs)]
    ppermute x22 -> x18, waiting for transfers between devices: 37.9 us -> 29.7 us  [shifted(): return lax.ppermute(value, axis, pairs)]
  transfers between devices with their start and end apart: 22 -> 22, of which waited for: 14 -> 10; matrix products, arithmetic and copies ran while one was open for 1% -> 0% of each run, Pallas kernels for 28% -> 17%
where the time goes in v5:
time: 124 us
  starting transfers between devices  48.1 us (39%)
  Pallas kernels  44.6 us (36%)
  waiting for transfers between devices  29.7 us (24%)
    ppermute x18, waiting for transfers between devices, shifted(): return lax.ppermute(value, axis, pairs)  29.7 us
    ppermute x18, starting transfers between devices, shifted(): return lax.ppermute(value, axis, pairs)  29.1 us
    pallas_call x3, Pallas kernels, attend(): pl.pallas_call(functools.partial(attend_kernel, groups, final), out_shape...  22.7 us
    ppermute x4, starting transfers between devices, swapped(): lax.ppermute(value, 'brick', [(brick, brick ^ 1) for brick in range(brick...  19.1 us
    pallas_call x2, Pallas kernels, project(): pl.pallas_call(functools.partial(project_kernel, part), out_shape=(shape(...  8.89 us
    pallas_call x2, Pallas kernels, mlp(): pl.pallas_call(functools.partial(mlp_kernel, groups), out_shape=(jax.Shap...  3.55 us
    pallas_call x1, Pallas kernels, cut_windows(): pl.pallas_call(functools.partial(cut_kernel, bricks, shard), out_shape=(p...  2.66 us
  transfers between devices with their start and end apart: 22, of which 10 were waited for; matrix products, arithmetic and copies ran while one was open for 0% of the time, Pallas kernels for 17%

profile of v5, /device:TPU:1, one launch (start us, length us, event | category | flops | bytes accessed | tf_op | source)
XLA Modules:
  0.0 124.2 jit_solution(17264824017539673003)
XLA Ops:
  0.0 0.0 copy-start.2
  0.0 0.0 copy-start.5
  0.0 0.8 copy-done.5
  0.8 2.7 %cut_windows.1 = (bf16[784,512]{1,0:T(8,128)(2,1)S(1)}, bf16[784,512]{1,0:T(8,128)(2,1)S(1)}, bf16[784,512]{1,0:T(8,128)(2,1)S(1)}, bf16[784,512]{1,0:T(8,128)(2,1)S(1)}, s32[2,4]{1,0:T(2,128)S(1)}) custom-call(s32[24,128]{1,0:T(8,128)S(1)} %bitcast.2, bf16[3072,512]{1,0:T(8,128)(2,1)} %feats_ref.1), custom_call_target="tpu_custom_call" | custom-call | tf_op jit(solution)/shard_map/cut_windows/pallas_call | solution.py:89
  3.5 3.2 %collective-permute-start = (bf16[784,512]{1,0:T(8,128)(2,1)S(1)}, bf16[784,512]{1,0:T(8,128)(2,1)S(1)}, u32[]{:S(2)}, u32[]{:S(2)}) collective-permute-start(bf16[784,512]{1,0:T(8,128)(2,1)S(1)} %get-tuple-element.39), channel_id=1, source_target_pairs={{0,4},{4,8},{8,12},{12,16},{16,20},{20,24},{24,28},{28,32},{32,36}... | collective-permute-start | bytes 2408456 | tf_op jit(solution)/shard_map/ppermute | solution.py:53
  6.8 0.1 collective-permute-start.1
  6.8 0.0 copy-done.1
  6.8 0.0 copy-done
  6.9 0.0 copy-done.3
  6.9 0.5 sort_weights.1
  7.3 2.5 %collective-permute-start.5 = (bf16[768,512]{1,0:T(8,128)(2,1)S(1)}, bf16[768,512]{1,0:T(8,128)(2,1)S(1)}, u32[]{:S(2)}, u32[]{:S(2)}) collective-permute-start(bf16[768,512]{1,0:T(8,128)(2,1)S(1)} %get-tuple-element.42), channel_id=1, source_target_pairs={{0,3},{1,0},{2,1},{3,2},{4,7},{5,4},{6,5},{7,6},{8,11},{9,8},{10,9... | collective-permute-start | bytes 2359304 | tf_op jit(solution)/shard_map/ppermute | solution.py:53
  9.8 0.0 collective-permute-start.3
  9.8 6.6 %collective-permute-start.2 = (bf16[784,512]{1,0:T(8,128)(2,1)S(1)}, bf16[784,512]{1,0:T(8,128)(2,1)S(1)}, u32[]{:S(2)}, u32[]{:S(2)}) collective-permute-start(bf16[784,512]{1,0:T(8,128)(2,1)S(1)} %get-tuple-element.41), channel_id=1, source_target_pairs={{0,248},{4,252},{8,0},{12,4},{16,8},{20,12},{24,16},{28,20},{32,24... | collective-permute-start | bytes 2408456 | tf_op jit(solution)/shard_map/ppermute | solution.py:53
  16.4 4.0 %collective-permute-done.5.refs_9_.refs_5_.refs_4_ = bf16[768,512]{1,0:T(8,128)(2,1)S(1)} collective-permute-done((bf16[768,512]{1,0:T(8,128)(2,1)S(1)}, bf16[768,512]{1,0:T(8,128)(2,1)S(1)}, u32[]{:S(2)}, u32[]{:S(2)}) %collective-permute-start.5) | collective-permute-done | bytes 786464 | tf_op jit(solution)/shard_map/ppermute | solution.py:53
  20.5 0.0 copy-start.4
  20.5 3.5 %collective-permute-start.6 = (bf16[384,512]{1,0:T(8,128)(2,1)S(1)}, bf16[384,512]{1,0:T(8,128)(2,1)S(1)}, u32[]{:S(2)}, u32[]{:S(2)}) collective-permute-start(bf16[384,512]{1,0:T(8,128)(2,1)S(1)} %slice.9), channel_id=1, source_target_pairs={{0,3},{1,0},{2,1},{3,2},{4,7},{5,4},{6,5},{7,6},{8,11},{9,8},{10,9... | collective-permute-start | bytes 1179656 | tf_op jit(solution)/shard_map/ppermute | solution.py:53
  24.0 0.0 collective-permute-done.3.refs_6_.refs_2_.refs_1_
  24.0 0.1 collective-permute-start.4
  24.1 0.0 collective-permute-done.refs_0_
  24.1 10.2 %collective-permute-start.10 = (bf16[768,512]{1,0:T(8,128)(2,1)S(1)}, bf16[768,512]{1,0:T(8,128)(2,1)S(1)}, u32[]{:S(2)}, u32[]{:S(2)}) collective-permute-start(bf16[768,512]{1,0:T(8,128)(2,1)S(1)} %collective-permute-done.5.refs_9_.refs_5_.refs_4_), channel_id=1, source_target_pairs={{0,4},{4,0},{8,12},{12,8},{16,20},{20,16},{24,28},{28,24},{32,36},... | collective-permute-start | bytes 2359304 | tf_op jit(solution)/shard_map/ppermute | solution.py:604
  34.3 0.0 collective-permute-done.1.refs_2_
  34.3 0.1 collective-permute-start.7
  34.4 0.0 collective-permute-done.6.refs_5_.refs_8_.refs_4_.refs_3_
  34.4 5.0 %collective-permute-start.9 = (bf16[384,512]{1,0:T(8,128)(2,1)S(1)}, bf16[384,512]{1,0:T(8,128)(2,1)S(1)}, u32[]{:S(2)}, u32[]{:S(2)}) collective-permute-start(bf16[384,512]{1,0:T(8,128)(2,1)S(1)} %collective-permute-done.6.refs_5_.refs_8_.refs_4_.refs_3_), channel_id=1, source_target_pairs={{0,4},{4,0},{8,12},{12,8},{16,20},{20,16},{24,28},{28,24},{32,36},... | collective-permute-start | bytes 1179656 | tf_op jit(solution)/shard_map/ppermute | solution.py:604
  39.4 0.0 collective-permute-done.4.refs_4_.refs_7_.refs_3_.refs_2_
  39.4 3.8 %collective-permute-start.8 = (bf16[384,512]{1,0:T(8,128)(2,1)S(1)}, bf16[384,512]{1,0:T(8,128)(2,1)S(1)}, u32[]{:S(2)}, u32[]{:S(2)}) collective-permute-start(bf16[384,512]{1,0:T(8,128)(2,1)S(1)} %collective-permute-done.4.refs_4_.refs_7_.refs_3_.refs_2_), channel_id=1, source_target_pairs={{0,4},{4,0},{8,12},{12,8},{16,20},{20,16},{24,28},{28,24},{32,36},... | collective-permute-start | bytes 1179656 | tf_op jit(solution)/shard_map/ppermute | solution.py:604
  43.8 0.6 index_tables.1
  44.4 0.0 collective-permute-done.2.refs_3_
  44.4 1.8 %head_rows.1.refs_14_ = bf16[1024,512]{1,0:T(8,128)(2,1)S(1)} custom-call(s32[24,128]{1,0:T(8,128)S(1)} %get-tuple-element.37.table_ref, s32[24,128]{1,0:T(8,128)S(1)} %get-tuple-element.38.spots_ref, bf16[784,512]{1,0:T(8,128)(2,1)S(1)} %collective-permute-done.refs_0_, bf16[784,512]{1,0:T(8,128)(2,1)S(1)} %get-tuple-element.35.after_ref.refs_1_, ...), custom_call_target="tpu_custom_call" | custom-call | flops 805306368 | bytes 5242880 | tf_op jit(solution)/shard_map/head_rows/pallas_call | solution.py:221
  46.2 0.1 collective-permute-start.11
  46.3 0.0 collective-permute-done.9.refs_12_.refs_8_.refs_7_
  46.3 0.0 collective-permute-done.10.refs_13_.refs_9_.refs_8_
  46.3 0.0 collective-permute-done.8.refs_11_.refs_7_.refs_6_
  46.3 0.0 collective-permute-done.7.refs_10_.refs_6_.refs_5_
  46.3 4.6 %project_first.1 = (bf16[256,512]{1,0:T(8,128)(2,1)S(1)}, bf16[1024,512]{1,0:T(8,128)(2,1)S(1)}, bf16[512,1024]{1,0:T(8,128)(2,1)S(1)}, bf16[512,256]{1,0:T(8,128)(2,1)S(1)}) custom-call(s32[24,128]{1,0:T(8,128)S(1)} %get-tuple-element.37.table_ref, s32[24,128]{1,0:T(8,128)S(1)} %get-tuple-element.38.spots_ref, ...), custom_call_target="tpu_custom_call" | custom-call | flops 10000000000 | bytes 10485760 | tf_op jit(solution)/shard_map/project_first/pallas_call | solution.py:289
  50.9 5.8 %shard_map.91.refs_15_.refs_10_ = bf16[256,256]{1,0:T(8,128)(2,1)S(1)} custom-call(bf16[1024,512]{1,0:T(8,128)(2,1)S(1)} %get-tuple-element.43.keys_ref, bf16[512,1024]{1,0:T(8,128)(2,1)S(1)} %get-tuple-element.44.values_ref, bf16[512,256]{1,0:T(8,128)(2,1)S(1)} %get-tuple-element.45.query_ref), custom_call_target="tpu_custom_call" | custom-call | flops 16000000000 | bytes 5242880 | tf_op jit(solution)/shard_map/pallas_call | solution.py:389
  56.7 3.8 %collective-permute-done.11.refs_14_ = bf16[1024,512]{1,0:T(8,128)(2,1)S(1)} collective-permute-done((bf16[1024,512]{1,0:T(8,128)(2,1)S(1)}, bf16[1024,512]{1,0:T(8,128)(2,1)S(1)}, u32[]{:S(2)}, u32[]{:S(2)}) %collective-permute-start.11) | collective-permute-done | bytes 1048608 | tf_op jit(solution)/shard_map/ppermute | solution.py:53
  60.5 4.3 %project_last.1 = (bf16[256,512]{1,0:T(8,128)(2,1)S(1)}, bf16[1024,512]{1,0:T(8,128)(2,1)S(1)}, bf16[512,1024]{1,0:T(8,128)(2,1)S(1)}, bf16[512,256]{1,0:T(8,128)(2,1)S(1)}) custom-call(s32[24,128]{1,0:T(8,128)S(1)} %get-tuple-element.37.table_ref, s32[24,128]{1,0:T(8,128)S(1)} %get-tuple-element.38.spots_ref, ...), custom_call_target="tpu_custom_call" | custom-call | flops 10000000000 | bytes 10485760 | tf_op jit(solution)/shard_map/project_last/pallas_call | solution.py:289
  64.8 10.6 %shard_map.92.hidden_ref = bf16[256,512]{1,0:T(8,128)(2,1)S(1)} custom-call(bf16[1024,512]{1,0:T(8,128)(2,1)S(1)} %get-tuple-element.46.keys_ref, bf16[512,1024]{1,0:T(8,128)(2,1)S(1)} %get-tuple-element.47.values_ref, bf16[512,256]{1,0:T(8,128)(2,1)S(1)} %get-tuple-element.48.query_ref, bf16[256,512]{1,0:T(8,128)(2,1)S(1)} %get-tuple-element.49.refs_0_, ...), custom_call_target="tpu_custom_call" | custom-call | flops 32000000000 | bytes 5242880 | tf_op jit(solution)/shard_map/pallas_call | solution.py:389
  75.4 1.8 %mlp.2 = (bf16[256,128]{1,0:T(8,128)(2,1)S(1)}, bf16[256,128]{1,0:T(8,128)(2,1)S(1)}, bf16[256,128]{1,0:T(8,128)(2,1)S(1)}, bf16[256,128]{1,0:T(8,128)(2,1)S(1)}) custom-call(bf16[256,512]{1,0:T(8,128)(2,1)S(1)} %shard_map.92.hidden_ref, f32[2,512]{1,0:T(2,128)S(1)} %copy-done.4, bf16[512,512]{1,0:T(8,128)(2,1)S(1)} %copy-done, ...), custom_call_target="tpu_custom_call" | custom-call | flops 1073741824 | bytes 5242880 | tf_op jit(solution)/shard_map/mlp/pallas_call | solution.py:467
  77.2 0.1 collective-permute-start.12
  77.3 0.8 collective-permute-start.13
  78.1 1.8 %collective-permute-start.14 = (bf16[256,128]{1,0:T(8,128)(2,1)S(1)}, bf16[256,128]{1,0:T(8,128)(2,1)S(1)}, u32[]{:S(2)}, u32[]{:S(2)}) collective-permute-start(bf16[256,128]{1,0:T(8,128)(2,1)S(1)} %get-tuple-element.53), channel_id=1, source_target_pairs={{0,3},{1,0},{2,1},{3,2},{4,7},{5,4},{6,5},{7,6},{8,11},{9,8},{10,9... | collective-permute-start | bytes 196616 | tf_op jit(solution)/shard_map/ppermute | solution.py:53
  79.9 2.3 %collective-permute-done.12.refs_1_ = bf16[256,128]{1,0:T(8,128)(2,1)S(1)} collective-permute-done((bf16[256,128]{1,0:T(8,128)(2,1)S(1)}, bf16[256,128]{1,0:T(8,128)(2,1)S(1)}, u32[]{:S(2)}, u32[]{:S(2)}) %collective-permute-start.12) | collective-permute-done | bytes 65568 | tf_op jit(solution)/shard_map/ppermute | solution.py:53
  82.3 0.0 collective-permute-done.13.refs_2_
  82.3 0.6 collective-permute-done.14.refs_3_
  82.9 2.4 %collective-permute-start.15 = (bf16[1024,128]{1,0:T(8,128)(2,1)S(1)}, bf16[1024,128]{1,0:T(8,128)(2,1)S(1)}, u32[]{:S(2)}, u32[]{:S(2)}) collective-permute-start(bf16[1024,128]{1,0:T(8,128)(2,1)S(1)} %collect_rows.1.rest_1_), channel_id=1, source_target_pairs={{0,4},{4,8},{8,12},{12,16},{16,20},{20,24},{24,28},{28,32},{32,36}... | collective-permute-start | bytes 786440 | tf_op jit(solution)/shard_map/ppermute | solution.py:53
  85.3 6.3 %shard_map.93.hidden_ref = bf16[256,512]{1,0:T(8,128)(2,1)S(1)} custom-call(bf16[1024,512]{1,0:T(8,128)(2,1)S(1)} %get-tuple-element.43.keys_ref, bf16[512,1024]{1,0:T(8,128)(2,1)S(1)} %get-tuple-element.44.values_ref, bf16[512,256]{1,0:T(8,128)(2,1)S(1)} %get-tuple-element.45.query_ref, bf16[256,512]{1,0:T(8,128)(2,1)S(1)} %get-tuple-element.54.refs_0_, ...), custom_call_target="tpu_custom_call" | custom-call | flops 16000000000 | bytes 5242880 | tf_op jit(solution)/shard_map/pallas_call | solution.py:389
  91.7 1.8 %mlp.3 = (bf16[256,128]{1,0:T(8,128)(2,1)S(1)}, bf16[256,128]{1,0:T(8,128)(2,1)S(1)}, bf16[256,128]{1,0:T(8,128)(2,1)S(1)}, bf16[256,128]{1,0:T(8,128)(2,1)S(1)}) custom-call(bf16[256,512]{1,0:T(8,128)(2,1)S(1)} %shard_map.93.hidden_ref, f32[2,512]{1,0:T(2,128)S(1)} %copy-done.4, bf16[512,512]{1,0:T(8,128)(2,1)S(1)} %copy-done, ...), custom_call_target="tpu_custom_call" | custom-call | flops 1073741824 | bytes 5242880 | tf_op jit(solution)/shard_map/mlp/pallas_call | solution.py:467
  93.4 0.6 collective-permute-start.16
  94.1 2.7 %collective-permute-start.17 = (bf16[256,128]{1,0:T(8,128)(2,1)S(1)}, bf16[256,128]{1,0:T(8,128)(2,1)S(1)}, u32[]{:S(2)}, u32[]{:S(2)}) collective-permute-start(bf16[256,128]{1,0:T(8,128)(2,1)S(1)} %get-tuple-element.57), channel_id=1, source_target_pairs={{0,2},{1,3},{2,0},{3,1},{4,6},{5,7},{6,4},{7,5},{8,10},{9,11},{10,... | collective-permute-start | bytes 196616 | tf_op jit(solution)/shard_map/ppermute | solution.py:53
  96.8 0.0 collective-permute-start.18
  96.8 1.1 collective-permute-done.16.rest_3_
  97.8 1.3 %collective-permute-done.17.rest_4_ = bf16[256,128]{1,0:T(8,128)(2,1)S(1)} collective-permute-done((bf16[256,128]{1,0:T(8,128)(2,1)S(1)}, bf16[256,128]{1,0:T(8,128)(2,1)S(1)}, u32[]{:S(2)}, u32[]{:S(2)}) %collective-permute-start.17) | collective-permute-done | bytes 65568 | tf_op jit(solution)/shard_map/ppermute | solution.py:53
  99.1 0.8 collective-permute-done.18.rest_5_
  99.9 0.0 collective-permute-done.15.rest_0_
  99.9 1.9 %pack_lanes.1 = (bf16[784,128]{1,0:T(8,128)(2,1)S(1)}, bf16[784,128]{1,0:T(8,128)(2,1)S(1)}, bf16[784,128]{1,0:T(8,128)(2,1)S(1)}, bf16[784,128]{1,0:T(8,128)(2,1)S(1)}) custom-call(s32[1]{0:T(128)S(6)} %copy.10.shift_ref, s32[24,128]{1,0:T(8,128)S(1)} %get-tuple-element.37.table_ref, s32[24,128]{1,0:T(8,128)S(1)} %get-tuple-element.38.spots_ref, ...), custom_call_target="tpu_custom_call" | custom-call | tf_op jit(solution)/shard_map/pack_lanes/pallas_call | solution.py:537
  101.8 4.2 %collective-permute-start.19 = (bf16[784,128]{1,0:T(8,128)(2,1)S(1)}, bf16[784,128]{1,0:T(8,128)(2,1)S(1)}, u32[]{:S(2)}, u32[]{:S(2)}) collective-permute-start(bf16[784,128]{1,0:T(8,128)(2,1)S(1)} %get-tuple-element.59), channel_id=1, source_target_pairs={{0,252},{4,0},{8,4},{12,8},{16,12},{20,16},{24,20},{28,24},{32,28}... | collective-permute-start | bytes 602120 | tf_op jit(solution)/shard_map/ppermute | solution.py:53
  106.1 0.0 collective-permute-start.20
  106.1 0.3 collective-permute-start.21
  106.4 0.8 collective-permute-done.19.refs_0_
  107.2 3.9 %collective-permute-done.20.refs_2_ = bf16[784,128]{1,0:T(8,128)(2,1)S(1)} collective-permute-done((bf16[784,128]{1,0:T(8,128)(2,1)S(1)}, bf16[784,128]{1,0:T(8,128)(2,1)S(1)}, u32[]{:S(2)}, u32[]{:S(2)}) %collective-permute-start.20) | collective-permute-done | bytes 200736 | tf_op jit(solution)/shard_map/ppermute | solution.py:53
  111.1 11.1 %collective-permute-done.21.refs_3_ = bf16[784,128]{1,0:T(8,128)(2,1)S(1)} collective-permute-done((bf16[784,128]{1,0:T(8,128)(2,1)S(1)}, bf16[784,128]{1,0:T(8,128)(2,1)S(1)}, u32[]{:S(2)}, u32[]{:S(2)}) %collective-permute-start.21) | collective-permute-done | bytes 200736 | tf_op jit(solution)/shard_map/ppermute | solution.py:53
  122.2 2.0 %place_rows.1 = bf16[3072,128]{1,0:T(8,128)(2,1)} custom-call(s32[2,4]{1,0:T(2,128)S(1)} %get-tuple-element.34.counts_ref, bf16[784,128]{1,0:T(8,128)(2,1)S(1)} %collective-permute-done.19.refs_0_, bf16[784,128]{1,0:T(8,128)(2,1)S(1)} %get-tuple-element.60.refs_1_, bf16[784,128]{1,0:T(8,128)(2,1)S(1)} %collective-permute-done.20.refs_2_, ...), custom_call_target="tpu_custom_call" | custom-call | tf_op jit(solution)/shard_map/place_rows/pallas_call | solution.py:566
  (10 shorter events, 0.1 us)
Async XLA Ops:
  0.0 6.8 %copy-start.1 = (bf16[512,512]{1,0:T(8,128)(2,1)S(1)}, bf16[512,512]{1,0:T(8,128)(2,1)}, u32[]{:S(2)}) copy-start(bf16[512,512]{1,0:T(8,128)(2,1)} %down_ref.5) | copy-start | bytes 1572868
  0.0 6.8 %copy-start = (bf16[512,512]{1,0:T(8,128)(2,1)S(1)}, bf16[512,512]{1,0:T(8,128)(2,1)}, u32[]{:S(2)}) copy-start(bf16[512,512]{1,0:T(8,128)(2,1)} %up_ref.5) | copy-start | bytes 1572868
  0.0 6.8 %copy-start.3 = (bf16[128,512]{1,0:T(8,128)(2,1)S(1)}, bf16[128,512]{1,0:T(8,128)(2,1)}, u32[]{:S(2)}) copy-start(bf16[128,512]{1,0:T(8,128)(2,1)} %proj_ref.1) | copy-start | bytes 393220
  0.0 6.8 %copy-start.2 = (bf16[512,384]{1,0:T(8,128)(2,1)S(1)}, bf16[512,384]{1,0:T(8,128)(2,1)}, u32[]{:S(2)}) copy-start(bf16[512,384]{1,0:T(8,128)(2,1)} %qkv_ref.1) | copy-start | bytes 1179652
  0.0 0.8 copy-start.5
  0.8 43.0 %copy-start.6 = (s32[2048]{0:T(1024)S(1)}, s32[2048]{0:T(1024)}, u32[]{:S(2)}) copy-start(s32[2048]{0:T(1024)} %param.11) | copy-start | bytes 24580
  3.5 20.6 %collective-permute-start = (bf16[784,512]{1,0:T(8,128)(2,1)S(1)}, bf16[784,512]{1,0:T(8,128)(2,1)S(1)}, u32[]{:S(2)}, u32[]{:S(2)}) collective-permute-start(bf16[784,512]{1,0:T(8,128)(2,1)S(1)} %get-tuple-element.39), channel_id=1, source_target_pairs={{0,4},{4,8},{8,12},{12,16},{16,20},{20,24},{24,28},{28,32},{32,36}... | collective-permute-start | bytes 2408456 | tf_op jit(solution)/shard_map/ppermute | solution.py:53
  6.8 27.5 %collective-permute-start.1 = (bf16[784,512]{1,0:T(8,128)(2,1)S(1)}, bf16[784,512]{1,0:T(8,128)(2,1)S(1)}, u32[]{:S(2)}, u32[]{:S(2)}) collective-permute-start(bf16[784,512]{1,0:T(8,128)(2,1)S(1)} %get-tuple-element.40), channel_id=1, source_target_pairs={{0,252},{4,0},{8,4},{12,8},{16,12},{20,16},{24,20},{28,24},{32,28}... | collective-permute-start | bytes 2408456 | tf_op jit(solution)/shard_map/ppermute | solution.py:53
  7.3 13.1 %collective-permute-start.5 = (bf16[768,512]{1,0:T(8,128)(2,1)S(1)}, bf16[768,512]{1,0:T(8,128)(2,1)S(1)}, u32[]{:S(2)}, u32[]{:S(2)}) collective-permute-start(bf16[768,512]{1,0:T(8,128)(2,1)S(1)} %get-tuple-element.42), channel_id=1, source_target_pairs={{0,3},{1,0},{2,1},{3,2},{4,7},{5,4},{6,5},{7,6},{8,11},{9,8},{10,9... | collective-permute-start | bytes 2359304 | tf_op jit(solution)/shard_map/ppermute | solution.py:53
  9.8 14.2 %collective-permute-start.3 = (bf16[768,512]{1,0:T(8,128)(2,1)S(1)}, bf16[768,512]{1,0:T(8,128)(2,1)S(1)}, u32[]{:S(2)}, u32[]{:S(2)}) collective-permute-start(bf16[768,512]{1,0:T(8,128)(2,1)S(1)} %get-tuple-element.42), channel_id=1, source_target_pairs={{0,1},{1,2},{2,3},{3,0},{4,5},{5,6},{6,7},{7,4},{8,9},{9,10},{10,1... | collective-permute-start | bytes 2359304 | tf_op jit(solution)/shard_map/ppermute | solution.py:53
  9.8 34.6 %collective-permute-start.2 = (bf16[784,512]{1,0:T(8,128)(2,1)S(1)}, bf16[784,512]{1,0:T(8,128)(2,1)S(1)}, u32[]{:S(2)}, u32[]{:S(2)}) collective-permute-start(bf16[784,512]{1,0:T(8,128)(2,1)S(1)} %get-tuple-element.41), channel_id=1, source_target_pairs={{0,248},{4,252},{8,0},{12,4},{16,8},{20,12},{24,16},{28,20},{32,24... | collective-permute-start | bytes 2408456 | tf_op jit(solution)/shard_map/ppermute | solution.py:53
  20.5 25.9 %copy-start.4 = (f32[2,512]{1,0:T(2,128)S(1)}, f32[2,512]{1,0:T(2,128)}, u32[]{:S(2)}) copy-start(f32[2,512]{1,0:T(2,128)} %gain_ref.3) | copy-start | bytes 12292
  20.5 13.9 %collective-permute-start.6 = (bf16[384,512]{1,0:T(8,128)(2,1)S(1)}, bf16[384,512]{1,0:T(8,128)(2,1)S(1)}, u32[]{:S(2)}, u32[]{:S(2)}) collective-permute-start(bf16[384,512]{1,0:T(8,128)(2,1)S(1)} %slice.9), channel_id=1, source_target_pairs={{0,3},{1,0},{2,1},{3,2},{4,7},{5,4},{6,5},{7,6},{8,11},{9,8},{10,9... | collective-permute-start | bytes 1179656 | tf_op jit(solution)/shard_map/ppermute | solution.py:53
  24.0 15.4 %collective-permute-start.4 = (bf16[384,512]{1,0:T(8,128)(2,1)S(1)}, bf16[384,512]{1,0:T(8,128)(2,1)S(1)}, u32[]{:S(2)}, u32[]{:S(2)}) collective-permute-start(bf16[384,512]{1,0:T(8,128)(2,1)S(1)} %slice.8), channel_id=1, source_target_pairs={{0,1},{1,2},{2,3},{3,0},{4,5},{5,6},{6,7},{7,4},{8,9},{9,10},{10,1... | collective-permute-start | bytes 1179656 | tf_op jit(solution)/shard_map/ppermute | solution.py:53
  24.1 22.2 %collective-permute-start.10 = (bf16[768,512]{1,0:T(8,128)(2,1)S(1)}, bf16[768,512]{1,0:T(8,128)(2,1)S(1)}, u32[]{:S(2)}, u32[]{:S(2)}) collective-permute-start(bf16[768,512]{1,0:T(8,128)(2,1)S(1)} %collective-permute-done.5.refs_9_.refs_5_.refs_4_), channel_id=1, source_target_pairs={{0,4},{4,0},{8,12},{12,8},{16,20},{20,16},{24,28},{28,24},{32,36},... | collective-permute-start | bytes 2359304 | tf_op jit(solution)/shard_map/ppermute | solution.py:604
  34.3 12.0 %collective-permute-start.7 = (bf16[768,512]{1,0:T(8,128)(2,1)S(1)}, bf16[768,512]{1,0:T(8,128)(2,1)S(1)}, u32[]{:S(2)}, u32[]{:S(2)}) collective-permute-start(bf16[768,512]{1,0:T(8,128)(2,1)S(1)} %collective-permute-done.3.refs_6_.refs_2_.refs_1_), channel_id=1, source_target_pairs={{0,4},{4,0},{8,12},{12,8},{16,20},{20,16},{24,28},{28,24},{32,36},... | collective-permute-start | bytes 2359304 | tf_op jit(solution)/shard_map/ppermute | solution.py:604
  34.4 11.9 %collective-permute-start.9 = (bf16[384,512]{1,0:T(8,128)(2,1)S(1)}, bf16[384,512]{1,0:T(8,128)(2,1)S(1)}, u32[]{:S(2)}, u32[]{:S(2)}) collective-permute-start(bf16[384,512]{1,0:T(8,128)(2,1)S(1)} %collective-permute-done.6.refs_5_.refs_8_.refs_4_.refs_3_), channel_id=1, source_target_pairs={{0,4},{4,0},{8,12},{12,8},{16,20},{20,16},{24,28},{28,24},{32,36},... | collective-permute-start | bytes 1179656 | tf_op jit(solution)/shard_map/ppermute | solution.py:604
  39.4 7.0 %collective-permute-start.8 = (bf16[384,512]{1,0:T(8,128)(2,1)S(1)}, bf16[384,512]{1,0:T(8,128)(2,1)S(1)}, u32[]{:S(2)}, u32[]{:S(2)}) collective-permute-start(bf16[384,512]{1,0:T(8,128)(2,1)S(1)} %collective-permute-done.4.refs_4_.refs_7_.refs_3_.refs_2_), channel_id=1, source_target_pairs={{0,4},{4,0},{8,12},{12,8},{16,20},{20,16},{24,28},{28,24},{32,36},... | collective-permute-start | bytes 1179656 | tf_op jit(solution)/shard_map/ppermute | solution.py:604
  46.2 14.3 %collective-permute-start.11 = (bf16[1024,512]{1,0:T(8,128)(2,1)S(1)}, bf16[1024,512]{1,0:T(8,128)(2,1)S(1)}, u32[]{:S(2)}, u32[]{:S(2)}) collective-permute-start(bf16[1024,512]{1,0:T(8,128)(2,1)S(1)} %head_rows.1.refs_14_), channel_id=1, source_target_pairs={{0,252},{4,0},{8,4},{12,8},{16,12},{20,16},{24,20},{28,24},{32,28}... | collective-permute-start | bytes 3145736 | tf_op jit(solution)/shard_map/ppermute | solution.py:53
  77.2 5.1 %collective-permute-start.12 = (bf16[256,128]{1,0:T(8,128)(2,1)S(1)}, bf16[256,128]{1,0:T(8,128)(2,1)S(1)}, u32[]{:S(2)}, u32[]{:S(2)}) collective-permute-start(bf16[256,128]{1,0:T(8,128)(2,1)S(1)} %get-tuple-element.51), channel_id=1, source_target_pairs={{0,1},{1,2},{2,3},{3,0},{4,5},{5,6},{6,7},{7,4},{8,9},{9,10},{10,1... | collective-permute-start | bytes 196616 | tf_op jit(solution)/shard_map/ppermute | solution.py:53
  77.3 5.0 %collective-permute-start.13 = (bf16[256,128]{1,0:T(8,128)(2,1)S(1)}, bf16[256,128]{1,0:T(8,128)(2,1)S(1)}, u32[]{:S(2)}, u32[]{:S(2)}) collective-permute-start(bf16[256,128]{1,0:T(8,128)(2,1)S(1)} %get-tuple-element.52), channel_id=1, source_target_pairs={{0,2},{1,3},{2,0},{3,1},{4,6},{5,7},{6,4},{7,5},{8,10},{9,11},{10,... | collective-permute-start | bytes 196616 | tf_op jit(solution)/shard_map/ppermute | solution.py:53
  78.1 4.8 %collective-permute-start.14 = (bf16[256,128]{1,0:T(8,128)(2,1)S(1)}, bf16[256,128]{1,0:T(8,128)(2,1)S(1)}, u32[]{:S(2)}, u32[]{:S(2)}) collective-permute-start(bf16[256,128]{1,0:T(8,128)(2,1)S(1)} %get-tuple-element.53), channel_id=1, source_target_pairs={{0,3},{1,0},{2,1},{3,2},{4,7},{5,4},{6,5},{7,6},{8,11},{9,8},{10,9... | collective-permute-start | bytes 196616 | tf_op jit(solution)/shard_map/ppermute | solution.py:53
  82.9 17.0 %collective-permute-start.15 = (bf16[1024,128]{1,0:T(8,128)(2,1)S(1)}, bf16[1024,128]{1,0:T(8,128)(2,1)S(1)}, u32[]{:S(2)}, u32[]{:S(2)}) collective-permute-start(bf16[1024,128]{1,0:T(8,128)(2,1)S(1)} %collect_rows.1.rest_1_), channel_id=1, source_target_pairs={{0,4},{4,8},{8,12},{12,16},{16,20},{20,24},{24,28},{28,32},{32,36}... | collective-permute-start | bytes 786440 | tf_op jit(solution)/shard_map/ppermute | solution.py:53
  93.4 4.4 %collective-permute-start.16 = (bf16[256,128]{1,0:T(8,128)(2,1)S(1)}, bf16[256,128]{1,0:T(8,128)(2,1)S(1)}, u32[]{:S(2)}, u32[]{:S(2)}) collective-permute-start(bf16[256,128]{1,0:T(8,128)(2,1)S(1)} %get-tuple-element.56), channel_id=1, source_target_pairs={{0,1},{1,2},{2,3},{3,0},{4,5},{5,6},{6,7},{7,4},{8,9},{9,10},{10,1... | collective-permute-start | bytes 196616 | tf_op jit(solution)/shard_map/ppermute | solution.py:53
  94.1 5.0 %collective-permute-start.17 = (bf16[256,128]{1,0:T(8,128)(2,1)S(1)}, bf16[256,128]{1,0:T(8,128)(2,1)S(1)}, u32[]{:S(2)}, u32[]{:S(2)}) collective-permute-start(bf16[256,128]{1,0:T(8,128)(2,1)S(1)} %get-tuple-element.57), channel_id=1, source_target_pairs={{0,2},{1,3},{2,0},{3,1},{4,6},{5,7},{6,4},{7,5},{8,10},{9,11},{10,... | collective-permute-start | bytes 196616 | tf_op jit(solution)/shard_map/ppermute | solution.py:53
  96.8 3.1 %collective-permute-start.18 = (bf16[256,128]{1,0:T(8,128)(2,1)S(1)}, bf16[256,128]{1,0:T(8,128)(2,1)S(1)}, u32[]{:S(2)}, u32[]{:S(2)}) collective-permute-start(bf16[256,128]{1,0:T(8,128)(2,1)S(1)} %get-tuple-element.58), channel_id=1, source_target_pairs={{0,3},{1,0},{2,1},{3,2},{4,7},{5,4},{6,5},{7,6},{8,11},{9,8},{10,9... | collective-permute-start | bytes 196616 | tf_op jit(solution)/shard_map/ppermute | solution.py:53
  101.8 5.3 %collective-permute-start.19 = (bf16[784,128]{1,0:T(8,128)(2,1)S(1)}, bf16[784,128]{1,0:T(8,128)(2,1)S(1)}, u32[]{:S(2)}, u32[]{:S(2)}) collective-permute-start(bf16[784,128]{1,0:T(8,128)(2,1)S(1)} %get-tuple-element.59), channel_id=1, source_target_pairs={{0,252},{4,0},{8,4},{12,8},{16,12},{20,16},{24,20},{28,24},{32,28}... | collective-permute-start | bytes 602120 | tf_op jit(solution)/shard_map/ppermute | solution.py:53
  106.1 5.0 %collective-permute-start.20 = (bf16[784,128]{1,0:T(8,128)(2,1)S(1)}, bf16[784,128]{1,0:T(8,128)(2,1)S(1)}, u32[]{:S(2)}, u32[]{:S(2)}) collective-permute-start(bf16[784,128]{1,0:T(8,128)(2,1)S(1)} %get-tuple-element.61), channel_id=1, source_target_pairs={{0,4},{4,8},{8,12},{12,16},{16,20},{20,24},{24,28},{28,32},{32,36}... | collective-permute-start | bytes 602120 | tf_op jit(solution)/shard_map/ppermute | solution.py:53
  106.1 16.1 %collective-permute-start.21 = (bf16[784,128]{1,0:T(8,128)(2,1)S(1)}, bf16[784,128]{1,0:T(8,128)(2,1)S(1)}, u32[]{:S(2)}, u32[]{:S(2)}) collective-permute-start(bf16[784,128]{1,0:T(8,128)(2,1)S(1)} %get-tuple-element.62), channel_id=1, source_target_pairs={{0,8},{4,12},{8,16},{12,20},{16,24},{20,28},{24,32},{28,36},{32,40... | collective-permute-start | bytes 602120 | tf_op jit(solution)/shard_map/ppermute | solution.py:53

commit v6 on v5

--- a/solution.py
+++ b/solution.py
@@ -65,18 +65,19 @@
 
 
 def cut_kernel(bricks, shard, ranks_ref, feats_ref, *rest):
-    outs, counts_ref, sems = rest[:LANES], rest[LANES], rest[LANES + 1]
+    outs, counts_ref, sems = rest[:3], rest[3], rest[4]
     capacity = feats_ref.shape[0]
     me = lax.axis_index("brick")
     ranks = ranks_ref[...]
     loads = []
-    for lane in (3, 2, 0, 1):
+    for index, lane in enumerate((3, 2, 0)):
         target = lax.rem(me - lane + 1 + bricks, bricks)
         first = jnp.sum((ranks < target * shard).astype(jnp.int32))
         counts_ref[0, lane] = first
         rows = pl.ds(window_start(first, capacity), PIECE)
-        loads.append(pltpu.make_async_copy(feats_ref.at[rows], outs[lane], sems.at[lane]))
+        loads.append(pltpu.make_async_copy(feats_ref.at[rows], outs[index], sems.at[index]))
         loads[-1].start()
+    counts_ref[0, 1] = jnp.sum((ranks < me * shard).astype(jnp.int32))
     for lane in range(LANES):
         target = lax.rem(me - lane + 1 + bricks, bricks)
         counts_ref[1, lane] = jnp.sum((ranks < (target + 1) * shard).astype(jnp.int32))
@@ -88,10 +89,10 @@
     piece = jax.ShapeDtypeStruct((PIECE, feats.shape[1]), feats.dtype)
     return pl.pallas_call(
         functools.partial(cut_kernel, bricks, shard),
-        out_shape=(piece,) * LANES + (jax.ShapeDtypeStruct((2, LANES), jnp.int32),),
+        out_shape=(piece,) * 3 + (jax.ShapeDtypeStruct((2, LANES), jnp.int32),),
         in_specs=[VMEM, HBM],
-        out_specs=(VMEM,) * LANES + (SMEM,),
-        scratch_shapes=[pltpu.SemaphoreType.DMA((LANES,))],
+        out_specs=(VMEM,) * 3 + (SMEM,),
+        scratch_shapes=[pltpu.SemaphoreType.DMA((3,))],
         compiler_params=pltpu.CompilerParams(vmem_limit_bytes=8 << 20),
         name="cut_windows",
     )(ranks, pltpu.with_memory_space_constraint(feats, pltpu.HBM))
@@ -136,7 +137,13 @@
     )(qkv, proj, up, down, after)
 
 
-def index_kernel(bricks, capacity, shift_ref, order_ref, after_ref, spots_ref, table_ref, wide_ref):
+def index_kernel(
+    bricks, shift_ref, counts_ref, order_ref, feats_ref, after_ref, spots_ref, table_ref, own_ref, wide_ref, sem
+):
+    capacity = feats_ref.shape[0]
+    rows = pl.ds(window_start(counts_ref[0, 1], capacity), PIECE)
+    load = pltpu.make_async_copy(feats_ref.at[rows], own_ref, sem)
+    load.start()
     me = lax.axis_index("brick")
     order = order_ref[...]
     rows = order.shape[0]
@@ -179,20 +186,24 @@
     for lane in range(LANES):
         spots = jnp.where(lane_wide == lane, spot_wide - table[:, lane : lane + 1], spots)
     spots_ref[...] = jnp.where(lane_wide < 0, -1, spots)
-
-
-def index_tables(bricks, capacity, shift, order, after):
+    load.wait()
+
+
+def index_tables(bricks, shift, counts, order, feats, after):
     height = 3 * BLOCKS
     table = jax.ShapeDtypeStruct((height, BLOCK), jnp.int32)
     return pl.pallas_call(
-        functools.partial(index_kernel, bricks, capacity),
-        out_shape=(table, table),
-        in_specs=[SMEM, VMEM, HBM],
-        out_specs=(VMEM, VMEM),
-        scratch_shapes=[pltpu.VMEM((2, 2, height + 2 * BLOCKS, BLOCK), jnp.int32)],
+        functools.partial(index_kernel, bricks),
+        out_shape=(table, table, jax.ShapeDtypeStruct((PIECE, feats.shape[1]), feats.dtype)),
+        in_specs=[SMEM, SMEM, VMEM, HBM, ANY],
+        out_specs=(VMEM,) * 3,
+        scratch_shapes=[
+            pltpu.VMEM((2, 2, height + 2 * BLOCKS, BLOCK), jnp.int32),
+            pltpu.SemaphoreType.DMA,
+        ],
         compiler_params=pltpu.CompilerParams(vmem_limit_bytes=4 << 20),
         name="index_tables",
-    )(shift, order, after)
+    )(shift, counts, order, pltpu.with_memory_space_constraint(feats, pltpu.HBM), after)
 
 
 def hot_rows(spots):
@@ -590,14 +601,13 @@
     shard = curve_order.shape[0]
     queries = PATCH // parts
 
-    piece0, own, piece2, piece3, counts = cut_windows(
+    piece3, piece2, piece0, counts = cut_windows(
         bricks, shard, slot_rank.reshape(capacity // 128, 128), voxel_feats
     )
     lane3 = shifted(piece3, "brick", -2)
     lane2 = shifted(piece2, "brick", -1)
     lane0 = shifted(piece0, "brick", 1)
-    lanes = (lane0, own, lane2, lane3)
-    near, half = sort_weights(qkv_weight, proj_weight, up_weight, down_weight, own)
+    near, half = sort_weights(qkv_weight, proj_weight, up_weight, down_weight, piece0)
     middle = half.shape[0] // 2
 
     def swapped(value):
@@ -607,15 +617,17 @@
     behind = shifted(half, "mp", -1)
     far_a = shifted(ahead[:middle], "mp", 1)
     far_b = shifted(behind[middle:], "mp", -1)
-    ahead_other, behind_other = swapped(ahead), swapped(behind)
+    ahead_other = swapped(ahead)
+    behind_other = swapped(behind)
     far_a_other = swapped(far_a)
     far_b_other = swapped(far_b)
     weights = (near, ahead, far_a, far_b, behind, ahead_other, far_a_other, far_b_other, behind_other)
 
-    spots, table = index_tables(
-        bricks, capacity, patch_shift, curve_order.reshape(shard // BLOCK, BLOCK), near
+    spots, table, own = index_tables(
+        bricks, patch_shift, counts, curve_order.reshape(shard // BLOCK, BLOCK), voxel_feats, near
     )
-    head = head_rows(table, spots, lanes, (far_a, far_b))
+    lanes = (lane0, own, lane2, lane3)
+    head = head_rows(table, spots, lanes, ())
     head_next = shifted(head, "brick", -1)
     common = (table, spots, lanes, norm_gains, weights)
     patch0 = project(0, *common, (head,), queries)

time: 124 us -> 128 us (1.032)
  waiting for transfers between devices: 29.7 us -> 45.1 us
  starting transfers between devices: 48.1 us -> 34.5 us
  Pallas kernels: 44.6 us -> 45.9 us
    ppermute x18, waiting for transfers between devices: 29.7 us -> 45.1 us  [shifted(): return lax.ppermute(value, axis, pairs)]
    ppermute x4, starting transfers between devices: 19.1 us -> 8.49 us  [swapped(): lax.ppermute(value, 'brick', [(brick, brick ^ 1) for brick in range(brick...]
    ppermute x18, starting transfers between devices: 29.1 us -> 26.1 us  [shifted(): return lax.ppermute(value, axis, pairs)]
    pallas_call x1, Pallas kernels: 0.59 us -> 2.21 us  [index_tables(): pl.pallas_call(functools.partial(index_kernel, bricks), out_shape=(table,...]
  transfers between devices with their start and end apart: 22 -> 22, of which waited for: 10 -> 12; matrix products, arithmetic and copies ran while one was open for 0% -> 0% of each run, Pallas kernels for 17% -> 18%
where the time goes in v6:
time: 128 us; the launch traced here: 127 us
  Pallas kernels  45.9 us (36%)
  waiting for transfers between devices  45.1 us (35%)
  starting transfers between devices  34.5 us (27%)
    ppermute x18, waiting for transfers between devices, shifted(): return lax.ppermute(value, axis, pairs)  45.1 us
    ppermute x18, starting transfers between devices, shifted(): return lax.ppermute(value, axis, pairs)  26.1 us
    pallas_call x3, Pallas kernels, attend(): pl.pallas_call(functools.partial(attend_kernel, groups, final), out_shape...  22.7 us
    pallas_call x2, Pallas kernels, project(): pl.pallas_call(functools.partial(project_kernel, part), out_shape=(shape(...  8.86 us
    ppermute x4, starting transfers between devices, swapped(): lax.ppermute(value, 'brick', [(brick, brick ^ 1) for brick in range(brick...  8.49 us
    pallas_call x2, Pallas kernels, mlp(): pl.pallas_call(functools.partial(mlp_kernel, groups), out_shape=(jax.Shap...  3.55 us
  transfers between devices with their start and end apart: 22, of which 12 were waited for; matrix products, arithmetic and copies ran while one was open for 0% of the time, Pallas kernels for 18%

profile of v6, /device:TPU:1, one launch (start us, length us, event | category | flops | bytes accessed | tf_op | source)
XLA Modules:
  0.0 127.4 jit_solution(18174750525308806348)
XLA Ops:
  0.0 0.0 copy-start.2
  0.0 0.0 copy-start.5
  0.0 0.8 copy-done.5
  0.8 2.4 %cut_windows.1 = (bf16[784,512]{1,0:T(8,128)(2,1)S(1)}, bf16[784,512]{1,0:T(8,128)(2,1)S(1)}, bf16[784,512]{1,0:T(8,128)(2,1)S(1)}, s32[2,4]{1,0:T(2,128)S(1)}) custom-call(s32[24,128]{1,0:T(8,128)S(1)} %bitcast.2, bf16[3072,512]{1,0:T(8,128)(2,1)} %feats_ref.3), custom_call_target="tpu_custom_call" | custom-call | tf_op jit(solution)/shard_map/cut_windows/pallas_call | solution.py:90
  3.2 3.3 %collective-permute-start.1 = (bf16[784,512]{1,0:T(8,128)(2,1)S(1)}, bf16[784,512]{1,0:T(8,128)(2,1)S(1)}, u32[]{:S(2)}, u32[]{:S(2)}) collective-permute-start(bf16[784,512]{1,0:T(8,128)(2,1)S(1)} %get-tuple-element.40), channel_id=1, source_target_pairs={{0,252},{4,0},{8,4},{12,8},{16,12},{20,16},{24,20},{28,24},{32,28}... | collective-permute-start | bytes 2408456 | tf_op jit(solution)/shard_map/ppermute | solution.py:53
  6.5 6.5 %collective-permute-start.2 = (bf16[784,512]{1,0:T(8,128)(2,1)S(1)}, bf16[784,512]{1,0:T(8,128)(2,1)S(1)}, u32[]{:S(2)}, u32[]{:S(2)}) collective-permute-start(bf16[784,512]{1,0:T(8,128)(2,1)S(1)} %get-tuple-element.41), channel_id=1, source_target_pairs={{0,248},{4,252},{8,0},{12,4},{16,8},{20,12},{24,16},{28,20},{32,24... | collective-permute-start | bytes 2408456 | tf_op jit(solution)/shard_map/ppermute | solution.py:53
  13.0 0.0 copy-done.1
  13.0 0.0 copy-done.3
  13.0 0.5 sort_weights.1
  13.5 2.6 %collective-permute-start.5 = (bf16[768,512]{1,0:T(8,128)(2,1)S(1)}, bf16[768,512]{1,0:T(8,128)(2,1)S(1)}, u32[]{:S(2)}, u32[]{:S(2)}) collective-permute-start(bf16[768,512]{1,0:T(8,128)(2,1)S(1)} %get-tuple-element.42), channel_id=1, source_target_pairs={{0,3},{1,0},{2,1},{3,2},{4,7},{5,4},{6,5},{7,6},{8,11},{9,8},{10,9... | collective-permute-start | bytes 2359304 | tf_op jit(solution)/shard_map/ppermute | solution.py:53
  16.0 0.0 collective-permute-start.3
  16.0 1.7 %collective-permute-start = (bf16[784,512]{1,0:T(8,128)(2,1)S(1)}, bf16[784,512]{1,0:T(8,128)(2,1)S(1)}, u32[]{:S(2)}, u32[]{:S(2)}) collective-permute-start(bf16[784,512]{1,0:T(8,128)(2,1)S(1)} %get-tuple-element.35.after_ref), channel_id=1, source_target_pairs={{0,4},{4,8},{8,12},{12,16},{16,20},{20,24},{24,28},{28,32},{32,36}... | collective-permute-start | bytes 2408456 | tf_op jit(solution)/shard_map/ppermute | solution.py:53
  17.7 14.6 %collective-permute-done.5.refs_9_.refs_5_.refs_4_ = bf16[768,512]{1,0:T(8,128)(2,1)S(1)} collective-permute-done((bf16[768,512]{1,0:T(8,128)(2,1)S(1)}, bf16[768,512]{1,0:T(8,128)(2,1)S(1)}, u32[]{:S(2)}, u32[]{:S(2)}) %collective-permute-start.5) | collective-permute-done | bytes 786464 | tf_op jit(solution)/shard_map/ppermute | solution.py:53
  32.4 3.5 %collective-permute-start.6 = (bf16[384,512]{1,0:T(8,128)(2,1)S(1)}, bf16[384,512]{1,0:T(8,128)(2,1)S(1)}, u32[]{:S(2)}, u32[]{:S(2)}) collective-permute-start(bf16[384,512]{1,0:T(8,128)(2,1)S(1)} %slice.9), channel_id=1, source_target_pairs={{0,3},{1,0},{2,1},{3,2},{4,7},{5,4},{6,5},{7,6},{8,11},{9,8},{10,9... | collective-permute-start | bytes 1179656 | tf_op jit(solution)/shard_map/ppermute | solution.py:53
  35.9 0.0 collective-permute-done.3.refs_6_.refs_2_.refs_1_
  35.9 0.1 collective-permute-start.4
  36.0 0.0 collective-permute-done.1.refs_2_
  36.0 1.8 %collective-permute-start.10 = (bf16[768,512]{1,0:T(8,128)(2,1)S(1)}, bf16[768,512]{1,0:T(8,128)(2,1)S(1)}, u32[]{:S(2)}, u32[]{:S(2)}) collective-permute-start(bf16[768,512]{1,0:T(8,128)(2,1)S(1)} %collective-permute-done.5.refs_9_.refs_5_.refs_4_), channel_id=1, source_target_pairs={{0,4},{4,0},{8,12},{12,8},{16,20},{20,16},{24,28},{28,24},{32,36},... | collective-permute-start | bytes 2359304 | tf_op jit(solution)/shard_map/ppermute | solution.py:614
  37.8 0.0 collective-permute-done.2.refs_3_
  37.8 1.9 %collective-permute-start.7 = (bf16[768,512]{1,0:T(8,128)(2,1)S(1)}, bf16[768,512]{1,0:T(8,128)(2,1)S(1)}, u32[]{:S(2)}, u32[]{:S(2)}) collective-permute-start(bf16[768,512]{1,0:T(8,128)(2,1)S(1)} %collective-permute-done.3.refs_6_.refs_2_.refs_1_), channel_id=1, source_target_pairs={{0,4},{4,0},{8,12},{12,8},{16,20},{20,16},{24,28},{28,24},{32,36},... | collective-permute-start | bytes 2359304 | tf_op jit(solution)/shard_map/ppermute | solution.py:614
  39.7 3.3 %collective-permute-done.6.refs_8_.refs_4_.refs_3_ = bf16[384,512]{1,0:T(8,128)(2,1)S(1)} collective-permute-done((bf16[384,512]{1,0:T(8,128)(2,1)S(1)}, bf16[384,512]{1,0:T(8,128)(2,1)S(1)}, u32[]{:S(2)}, u32[]{:S(2)}) %collective-permute-start.6) | collective-permute-done | bytes 393248 | tf_op jit(solution)/shard_map/ppermute | solution.py:53
  42.9 2.3 %collective-permute-start.9 = (bf16[384,512]{1,0:T(8,128)(2,1)S(1)}, bf16[384,512]{1,0:T(8,128)(2,1)S(1)}, u32[]{:S(2)}, u32[]{:S(2)}) collective-permute-start(bf16[384,512]{1,0:T(8,128)(2,1)S(1)} %collective-permute-done.6.refs_8_.refs_4_.refs_3_), channel_id=1, source_target_pairs={{0,4},{4,0},{8,12},{12,8},{16,20},{20,16},{24,28},{28,24},{32,36},... | collective-permute-start | bytes 1179656 | tf_op jit(solution)/shard_map/ppermute | solution.py:614
  45.2 1.0 collective-permute-done.4.refs_7_.refs_3_.refs_2_
  46.2 2.6 %collective-permute-start.8 = (bf16[384,512]{1,0:T(8,128)(2,1)S(1)}, bf16[384,512]{1,0:T(8,128)(2,1)S(1)}, u32[]{:S(2)}, u32[]{:S(2)}) collective-permute-start(bf16[384,512]{1,0:T(8,128)(2,1)S(1)} %collective-permute-done.4.refs_7_.refs_3_.refs_2_), channel_id=1, source_target_pairs={{0,4},{4,0},{8,12},{12,8},{16,20},{20,16},{24,28},{28,24},{32,36},... | collective-permute-start | bytes 1179656 | tf_op jit(solution)/shard_map/ppermute | solution.py:614
  49.4 0.0 copy-start.4
  49.4 2.2 %index_tables.1 = (s32[24,128]{1,0:T(8,128)S(1)}, s32[24,128]{1,0:T(8,128)S(1)}, bf16[784,512]{1,0:T(8,128)(2,1)S(1)}) custom-call(s32[1]{0:T(128)S(6)} %copy.10.shift_ref, s32[2,4]{1,0:T(2,128)S(1)} %get-tuple-element.34.counts_ref, s32[16,128]{1,0:T(8,128)S(1)} %bitcast.3, bf16[3072,512]{1,0:T(8,128)(2,1)} %feats_ref.3, ...), custom_call_target="tpu_custom_call" | custom-call | tf_op jit(solution)/shard_map/index_tables/pallas_call | solution.py:195
  51.6 0.0 collective-permute-done.refs_0_
  51.6 1.8 %head_rows.1.refs_14_ = bf16[1024,512]{1,0:T(8,128)(2,1)S(1)} custom-call(s32[24,128]{1,0:T(8,128)S(1)} %get-tuple-element.37.table_ref, s32[24,128]{1,0:T(8,128)S(1)} %get-tuple-element.38.spots_ref, bf16[784,512]{1,0:T(8,128)(2,1)S(1)} %collective-permute-done.refs_0_, bf16[784,512]{1,0:T(8,128)(2,1)S(1)} %get-tuple-element.39.refs_1_, ...), custom_call_target="tpu_custom_call" | custom-call | flops 805306368 | bytes 5242880 | tf_op jit(solution)/shard_map/head_rows/pallas_call | solution.py:232
  53.4 0.1 collective-permute-start.11
  53.5 0.0 collective-permute-done.9.refs_12_.refs_8_.refs_7_
  53.5 0.0 collective-permute-done.10.refs_13_.refs_9_.refs_8_
  53.5 0.0 collective-permute-done.8.refs_11_.refs_7_.refs_6_
  53.5 0.0 collective-permute-done.7.refs_10_.refs_6_.refs_5_
  53.5 0.0 copy-done.4
  53.5 4.5 %project_first.1 = (bf16[256,512]{1,0:T(8,128)(2,1)S(1)}, bf16[1024,512]{1,0:T(8,128)(2,1)S(1)}, bf16[512,1024]{1,0:T(8,128)(2,1)S(1)}, bf16[512,256]{1,0:T(8,128)(2,1)S(1)}) custom-call(s32[24,128]{1,0:T(8,128)S(1)} %get-tuple-element.37.table_ref, s32[24,128]{1,0:T(8,128)S(1)} %get-tuple-element.38.spots_ref, ...), custom_call_target="tpu_custom_call" | custom-call | flops 10000000000 | bytes 10485760 | tf_op jit(solution)/shard_map/project_first/pallas_call | solution.py:300
  58.1 5.8 %shard_map.91.refs_15_.refs_10_ = bf16[256,256]{1,0:T(8,128)(2,1)S(1)} custom-call(bf16[1024,512]{1,0:T(8,128)(2,1)S(1)} %get-tuple-element.43.keys_ref, bf16[512,1024]{1,0:T(8,128)(2,1)S(1)} %get-tuple-element.44.values_ref, bf16[512,256]{1,0:T(8,128)(2,1)S(1)} %get-tuple-element.45.query_ref), custom_call_target="tpu_custom_call" | custom-call | flops 16000000000 | bytes 5242880 | tf_op jit(solution)/shard_map/pallas_call | solution.py:400
  63.9 3.8 %collective-permute-done.11.refs_14_ = bf16[1024,512]{1,0:T(8,128)(2,1)S(1)} collective-permute-done((bf16[1024,512]{1,0:T(8,128)(2,1)S(1)}, bf16[1024,512]{1,0:T(8,128)(2,1)S(1)}, u32[]{:S(2)}, u32[]{:S(2)}) %collective-permute-start.11) | collective-permute-done | bytes 1048608 | tf_op jit(solution)/shard_map/ppermute | solution.py:53
  67.7 4.3 %project_last.1 = (bf16[256,512]{1,0:T(8,128)(2,1)S(1)}, bf16[1024,512]{1,0:T(8,128)(2,1)S(1)}, bf16[512,1024]{1,0:T(8,128)(2,1)S(1)}, bf16[512,256]{1,0:T(8,128)(2,1)S(1)}) custom-call(s32[24,128]{1,0:T(8,128)S(1)} %get-tuple-element.37.table_ref, s32[24,128]{1,0:T(8,128)S(1)} %get-tuple-element.38.spots_ref, ...), custom_call_target="tpu_custom_call" | custom-call | flops 10000000000 | bytes 10485760 | tf_op jit(solution)/shard_map/project_last/pallas_call | solution.py:300
  72.0 10.6 %shard_map.92.hidden_ref = bf16[256,512]{1,0:T(8,128)(2,1)S(1)} custom-call(bf16[1024,512]{1,0:T(8,128)(2,1)S(1)} %get-tuple-element.46.keys_ref, bf16[512,1024]{1,0:T(8,128)(2,1)S(1)} %get-tuple-element.47.values_ref, bf16[512,256]{1,0:T(8,128)(2,1)S(1)} %get-tuple-element.48.query_ref, bf16[256,512]{1,0:T(8,128)(2,1)S(1)} %get-tuple-element.49.refs_0_, ...), custom_call_target="tpu_custom_call" | custom-call | flops 32000000000 | bytes 5242880 | tf_op jit(solution)/shard_map/pallas_call | solution.py:400
  82.6 1.8 %mlp.2 = (bf16[256,128]{1,0:T(8,128)(2,1)S(1)}, bf16[256,128]{1,0:T(8,128)(2,1)S(1)}, bf16[256,128]{1,0:T(8,128)(2,1)S(1)}, bf16[256,128]{1,0:T(8,128)(2,1)S(1)}) custom-call(bf16[256,512]{1,0:T(8,128)(2,1)S(1)} %shard_map.92.hidden_ref, f32[2,512]{1,0:T(2,128)S(1)} %copy-done.4, bf16[512,512]{1,0:T(8,128)(2,1)S(1)} %copy-done, ...), custom_call_target="tpu_custom_call" | custom-call | flops 1073741824 | bytes 5242880 | tf_op jit(solution)/shard_map/mlp/pallas_call | solution.py:478
  84.4 0.1 collective-permute-start.12
  84.5 1.1 collective-permute-start.13
  85.6 1.6 %collective-permute-start.14 = (bf16[256,128]{1,0:T(8,128)(2,1)S(1)}, bf16[256,128]{1,0:T(8,128)(2,1)S(1)}, u32[]{:S(2)}, u32[]{:S(2)}) collective-permute-start(bf16[256,128]{1,0:T(8,128)(2,1)S(1)} %get-tuple-element.53), channel_id=1, source_target_pairs={{0,3},{1,0},{2,1},{3,2},{4,7},{5,4},{6,5},{7,6},{8,11},{9,8},{10,9... | collective-permute-start | bytes 196616 | tf_op jit(solution)/shard_map/ppermute | solution.py:53
  87.1 3.1 %collective-permute-done.12.refs_1_ = bf16[256,128]{1,0:T(8,128)(2,1)S(1)} collective-permute-done((bf16[256,128]{1,0:T(8,128)(2,1)S(1)}, bf16[256,128]{1,0:T(8,128)(2,1)S(1)}, u32[]{:S(2)}, u32[]{:S(2)}) %collective-permute-start.12) | collective-permute-done | bytes 65568 | tf_op jit(solution)/shard_map/ppermute | solution.py:53
  90.3 0.0 collective-permute-done.13.refs_2_
  90.3 0.9 collective-permute-done.14.refs_3_
  91.2 0.2 collective-permute-start.15
  91.4 6.3 %shard_map.93.hidden_ref = bf16[256,512]{1,0:T(8,128)(2,1)S(1)} custom-call(bf16[1024,512]{1,0:T(8,128)(2,1)S(1)} %get-tuple-element.43.keys_ref, bf16[512,1024]{1,0:T(8,128)(2,1)S(1)} %get-tuple-element.44.values_ref, bf16[512,256]{1,0:T(8,128)(2,1)S(1)} %get-tuple-element.45.query_ref, bf16[256,512]{1,0:T(8,128)(2,1)S(1)} %get-tuple-element.54.refs_0_, ...), custom_call_target="tpu_custom_call" | custom-call | flops 16000000000 | bytes 5242880 | tf_op jit(solution)/shard_map/pallas_call | solution.py:400
  97.8 1.8 %mlp.3 = (bf16[256,128]{1,0:T(8,128)(2,1)S(1)}, bf16[256,128]{1,0:T(8,128)(2,1)S(1)}, bf16[256,128]{1,0:T(8,128)(2,1)S(1)}, bf16[256,128]{1,0:T(8,128)(2,1)S(1)}) custom-call(bf16[256,512]{1,0:T(8,128)(2,1)S(1)} %shard_map.93.hidden_ref, f32[2,512]{1,0:T(2,128)S(1)} %copy-done.4, bf16[512,512]{1,0:T(8,128)(2,1)S(1)} %copy-done, ...), custom_call_target="tpu_custom_call" | custom-call | flops 1073741824 | bytes 5242880 | tf_op jit(solution)/shard_map/mlp/pallas_call | solution.py:478
  99.6 1.1 collective-permute-start.16
  100.7 2.3 %collective-permute-start.17 = (bf16[256,128]{1,0:T(8,128)(2,1)S(1)}, bf16[256,128]{1,0:T(8,128)(2,1)S(1)}, u32[]{:S(2)}, u32[]{:S(2)}) collective-permute-start(bf16[256,128]{1,0:T(8,128)(2,1)S(1)} %get-tuple-element.57), channel_id=1, source_target_pairs={{0,2},{1,3},{2,0},{3,1},{4,6},{5,7},{6,4},{7,5},{8,10},{9,11},{10,... | collective-permute-start | bytes 196616 | tf_op jit(solution)/shard_map/ppermute | solution.py:53
  102.9 0.2 collective-permute-start.18
  103.2 0.8 collective-permute-done.16.rest_3_
  104.0 2.0 %collective-permute-done.17.rest_4_ = bf16[256,128]{1,0:T(8,128)(2,1)S(1)} collective-permute-done((bf16[256,128]{1,0:T(8,128)(2,1)S(1)}, bf16[256,128]{1,0:T(8,128)(2,1)S(1)}, u32[]{:S(2)}, u32[]{:S(2)}) %collective-permute-start.17) | collective-permute-done | bytes 65568 | tf_op jit(solution)/shard_map/ppermute | solution.py:53
  106.0 0.7 collective-permute-done.18.rest_5_
  106.6 0.0 collective-permute-done.15.rest_0_
  106.6 1.9 %pack_lanes.1 = (bf16[784,128]{1,0:T(8,128)(2,1)S(1)}, bf16[784,128]{1,0:T(8,128)(2,1)S(1)}, bf16[784,128]{1,0:T(8,128)(2,1)S(1)}, bf16[784,128]{1,0:T(8,128)(2,1)S(1)}) custom-call(s32[1]{0:T(128)S(6)} %copy.10.shift_ref, s32[24,128]{1,0:T(8,128)S(1)} %get-tuple-element.37.table_ref, s32[24,128]{1,0:T(8,128)S(1)} %get-tuple-element.38.spots_ref, ...), custom_call_target="tpu_custom_call" | custom-call | tf_op jit(solution)/shard_map/pack_lanes/pallas_call | solution.py:548
  108.6 1.5 %collective-permute-start.19 = (bf16[784,128]{1,0:T(8,128)(2,1)S(1)}, bf16[784,128]{1,0:T(8,128)(2,1)S(1)}, u32[]{:S(2)}, u32[]{:S(2)}) collective-permute-start(bf16[784,128]{1,0:T(8,128)(2,1)S(1)} %get-tuple-element.59), channel_id=1, source_target_pairs={{0,252},{4,0},{8,4},{12,8},{16,12},{20,16},{24,20},{28,24},{32,28}... | collective-permute-start | bytes 602120 | tf_op jit(solution)/shard_map/ppermute | solution.py:53
  110.1 0.3 collective-permute-start.20
  110.4 0.0 collective-permute-start.21
  110.4 3.4 %collective-permute-done.19.refs_0_ = bf16[784,128]{1,0:T(8,128)(2,1)S(1)} collective-permute-done((bf16[784,128]{1,0:T(8,128)(2,1)S(1)}, bf16[784,128]{1,0:T(8,128)(2,1)S(1)}, u32[]{:S(2)}, u32[]{:S(2)}) %collective-permute-start.19) | collective-permute-done | bytes 200736 | tf_op jit(solution)/shard_map/ppermute | solution.py:53
  113.8 0.4 collective-permute-done.20.refs_2_
  114.2 11.1 %collective-permute-done.21.refs_3_ = bf16[784,128]{1,0:T(8,128)(2,1)S(1)} collective-permute-done((bf16[784,128]{1,0:T(8,128)(2,1)S(1)}, bf16[784,128]{1,0:T(8,128)(2,1)S(1)}, u32[]{:S(2)}, u32[]{:S(2)}) %collective-permute-start.21) | collective-permute-done | bytes 200736 | tf_op jit(solution)/shard_map/ppermute | solution.py:53
  125.4 2.0 %place_rows.1 = bf16[3072,128]{1,0:T(8,128)(2,1)} custom-call(s32[2,4]{1,0:T(2,128)S(1)} %get-tuple-element.34.counts_ref, bf16[784,128]{1,0:T(8,128)(2,1)S(1)} %collective-permute-done.19.refs_0_, bf16[784,128]{1,0:T(8,128)(2,1)S(1)} %get-tuple-element.60.refs_1_, bf16[784,128]{1,0:T(8,128)(2,1)S(1)} %collective-permute-done.20.refs_2_, ...), custom_call_target="tpu_custom_call" | custom-call | tf_op jit(solution)/shard_map/place_rows/pallas_call | solution.py:577
  (10 shorter events, 0.1 us)
Async XLA Ops:
  0.0 13.0 %copy-start.1 = (bf16[512,512]{1,0:T(8,128)(2,1)S(1)}, bf16[512,512]{1,0:T(8,128)(2,1)}, u32[]{:S(2)}) copy-start(bf16[512,512]{1,0:T(8,128)(2,1)} %down_ref.5) | copy-start | bytes 1572868
  0.0 13.0 %copy-start = (bf16[512,512]{1,0:T(8,128)(2,1)S(1)}, bf16[512,512]{1,0:T(8,128)(2,1)}, u32[]{:S(2)}) copy-start(bf16[512,512]{1,0:T(8,128)(2,1)} %up_ref.5) | copy-start | bytes 1572868
  0.0 13.0 %copy-start.3 = (bf16[128,512]{1,0:T(8,128)(2,1)S(1)}, bf16[128,512]{1,0:T(8,128)(2,1)}, u32[]{:S(2)}) copy-start(bf16[128,512]{1,0:T(8,128)(2,1)} %proj_ref.1) | copy-start | bytes 393220
  0.0 13.0 %copy-start.2 = (bf16[512,384]{1,0:T(8,128)(2,1)S(1)}, bf16[512,384]{1,0:T(8,128)(2,1)}, u32[]{:S(2)}) copy-start(bf16[512,384]{1,0:T(8,128)(2,1)} %qkv_ref.1) | copy-start | bytes 1179652
  0.0 0.8 copy-start.5
  0.8 48.5 %copy-start.6 = (s32[2048]{0:T(1024)S(1)}, s32[2048]{0:T(1024)}, u32[]{:S(2)}) copy-start(s32[2048]{0:T(1024)} %param.11) | copy-start | bytes 24580
  3.2 32.8 %collective-permute-start.1 = (bf16[784,512]{1,0:T(8,128)(2,1)S(1)}, bf16[784,512]{1,0:T(8,128)(2,1)S(1)}, u32[]{:S(2)}, u32[]{:S(2)}) collective-permute-start(bf16[784,512]{1,0:T(8,128)(2,1)S(1)} %get-tuple-element.40), channel_id=1, source_target_pairs={{0,252},{4,0},{8,4},{12,8},{16,12},{20,16},{24,20},{28,24},{32,28}... | collective-permute-start | bytes 2408456 | tf_op jit(solution)/shard_map/ppermute | solution.py:53
  6.5 31.3 %collective-permute-start.2 = (bf16[784,512]{1,0:T(8,128)(2,1)S(1)}, bf16[784,512]{1,0:T(8,128)(2,1)S(1)}, u32[]{:S(2)}, u32[]{:S(2)}) collective-permute-start(bf16[784,512]{1,0:T(8,128)(2,1)S(1)} %get-tuple-element.41), channel_id=1, source_target_pairs={{0,248},{4,252},{8,0},{12,4},{16,8},{20,12},{24,16},{28,20},{32,24... | collective-permute-start | bytes 2408456 | tf_op jit(solution)/shard_map/ppermute | solution.py:53
  13.5 18.9 %collective-permute-start.5 = (bf16[768,512]{1,0:T(8,128)(2,1)S(1)}, bf16[768,512]{1,0:T(8,128)(2,1)S(1)}, u32[]{:S(2)}, u32[]{:S(2)}) collective-permute-start(bf16[768,512]{1,0:T(8,128)(2,1)S(1)} %get-tuple-element.42), channel_id=1, source_target_pairs={{0,3},{1,0},{2,1},{3,2},{4,7},{5,4},{6,5},{7,6},{8,11},{9,8},{10,9... | collective-permute-start | bytes 2359304 | tf_op jit(solution)/shard_map/ppermute | solution.py:53
  16.0 19.9 %collective-permute-start.3 = (bf16[768,512]{1,0:T(8,128)(2,1)S(1)}, bf16[768,512]{1,0:T(8,128)(2,1)S(1)}, u32[]{:S(2)}, u32[]{:S(2)}) collective-permute-start(bf16[768,512]{1,0:T(8,128)(2,1)S(1)} %get-tuple-element.42), channel_id=1, source_target_pairs={{0,1},{1,2},{2,3},{3,0},{4,5},{5,6},{6,7},{7,4},{8,9},{9,10},{10,1... | collective-permute-start | bytes 2359304 | tf_op jit(solution)/shard_map/ppermute | solution.py:53
  16.0 35.6 %collective-permute-start = (bf16[784,512]{1,0:T(8,128)(2,1)S(1)}, bf16[784,512]{1,0:T(8,128)(2,1)S(1)}, u32[]{:S(2)}, u32[]{:S(2)}) collective-permute-start(bf16[784,512]{1,0:T(8,128)(2,1)S(1)} %get-tuple-element.35.after_ref), channel_id=1, source_target_pairs={{0,4},{4,8},{8,12},{12,16},{16,20},{20,24},{24,28},{28,32},{32,36}... | collective-permute-start | bytes 2408456 | tf_op jit(solution)/shard_map/ppermute | solution.py:53
  32.4 10.5 %collective-permute-start.6 = (bf16[384,512]{1,0:T(8,128)(2,1)S(1)}, bf16[384,512]{1,0:T(8,128)(2,1)S(1)}, u32[]{:S(2)}, u32[]{:S(2)}) collective-permute-start(bf16[384,512]{1,0:T(8,128)(2,1)S(1)} %slice.9), channel_id=1, source_target_pairs={{0,3},{1,0},{2,1},{3,2},{4,7},{5,4},{6,5},{7,6},{8,11},{9,8},{10,9... | collective-permute-start | bytes 1179656 | tf_op jit(solution)/shard_map/ppermute | solution.py:53
  35.9 10.3 %collective-permute-start.4 = (bf16[384,512]{1,0:T(8,128)(2,1)S(1)}, bf16[384,512]{1,0:T(8,128)(2,1)S(1)}, u32[]{:S(2)}, u32[]{:S(2)}) collective-permute-start(bf16[384,512]{1,0:T(8,128)(2,1)S(1)} %slice.8), channel_id=1, source_target_pairs={{0,1},{1,2},{2,3},{3,0},{4,5},{5,6},{6,7},{7,4},{8,9},{9,10},{10,1... | collective-permute-start | bytes 1179656 | tf_op jit(solution)/shard_map/ppermute | solution.py:53
  36.0 17.5 %collective-permute-start.10 = (bf16[768,512]{1,0:T(8,128)(2,1)S(1)}, bf16[768,512]{1,0:T(8,128)(2,1)S(1)}, u32[]{:S(2)}, u32[]{:S(2)}) collective-permute-start(bf16[768,512]{1,0:T(8,128)(2,1)S(1)} %collective-permute-done.5.refs_9_.refs_5_.refs_4_), channel_id=1, source_target_pairs={{0,4},{4,0},{8,12},{12,8},{16,20},{20,16},{24,28},{28,24},{32,36},... | collective-permute-start | bytes 2359304 | tf_op jit(solution)/shard_map/ppermute | solution.py:614
  37.8 15.7 %collective-permute-start.7 = (bf16[768,512]{1,0:T(8,128)(2,1)S(1)}, bf16[768,512]{1,0:T(8,128)(2,1)S(1)}, u32[]{:S(2)}, u32[]{:S(2)}) collective-permute-start(bf16[768,512]{1,0:T(8,128)(2,1)S(1)} %collective-permute-done.3.refs_6_.refs_2_.refs_1_), channel_id=1, source_target_pairs={{0,4},{4,0},{8,12},{12,8},{16,20},{20,16},{24,28},{28,24},{32,36},... | collective-permute-start | bytes 2359304 | tf_op jit(solution)/shard_map/ppermute | solution.py:614
  42.9 10.6 %collective-permute-start.9 = (bf16[384,512]{1,0:T(8,128)(2,1)S(1)}, bf16[384,512]{1,0:T(8,128)(2,1)S(1)}, u32[]{:S(2)}, u32[]{:S(2)}) collective-permute-start(bf16[384,512]{1,0:T(8,128)(2,1)S(1)} %collective-permute-done.6.refs_8_.refs_4_.refs_3_), channel_id=1, source_target_pairs={{0,4},{4,0},{8,12},{12,8},{16,20},{20,16},{24,28},{28,24},{32,36},... | collective-permute-start | bytes 1179656 | tf_op jit(solution)/shard_map/ppermute | solution.py:614
  46.2 7.3 %collective-permute-start.8 = (bf16[384,512]{1,0:T(8,128)(2,1)S(1)}, bf16[384,512]{1,0:T(8,128)(2,1)S(1)}, u32[]{:S(2)}, u32[]{:S(2)}) collective-permute-start(bf16[384,512]{1,0:T(8,128)(2,1)S(1)} %collective-permute-done.4.refs_7_.refs_3_.refs_2_), channel_id=1, source_target_pairs={{0,4},{4,0},{8,12},{12,8},{16,20},{20,16},{24,28},{28,24},{32,36},... | collective-permute-start | bytes 1179656 | tf_op jit(solution)/shard_map/ppermute | solution.py:614
  49.4 4.1 %copy-start.4 = (f32[2,512]{1,0:T(2,128)S(1)}, f32[2,512]{1,0:T(2,128)}, u32[]{:S(2)}) copy-start(f32[2,512]{1,0:T(2,128)} %gain_ref.3) | copy-start | bytes 12292
  53.4 14.3 %collective-permute-start.11 = (bf16[1024,512]{1,0:T(8,128)(2,1)S(1)}, bf16[1024,512]{1,0:T(8,128)(2,1)S(1)}, u32[]{:S(2)}, u32[]{:S(2)}) collective-permute-start(bf16[1024,512]{1,0:T(8,128)(2,1)S(1)} %head_rows.1.refs_14_), channel_id=1, source_target_pairs={{0,252},{4,0},{8,4},{12,8},{16,12},{20,16},{24,20},{28,24},{32,28}... | collective-permute-start | bytes 3145736 | tf_op jit(solution)/shard_map/ppermute | solution.py:53
  84.4 5.9 %collective-permute-start.12 = (bf16[256,128]{1,0:T(8,128)(2,1)S(1)}, bf16[256,128]{1,0:T(8,128)(2,1)S(1)}, u32[]{:S(2)}, u32[]{:S(2)}) collective-permute-start(bf16[256,128]{1,0:T(8,128)(2,1)S(1)} %get-tuple-element.51), channel_id=1, source_target_pairs={{0,1},{1,2},{2,3},{3,0},{4,5},{5,6},{6,7},{7,4},{8,9},{9,10},{10,1... | collective-permute-start | bytes 196616 | tf_op jit(solution)/shard_map/ppermute | solution.py:53
  84.5 5.8 %collective-permute-start.13 = (bf16[256,128]{1,0:T(8,128)(2,1)S(1)}, bf16[256,128]{1,0:T(8,128)(2,1)S(1)}, u32[]{:S(2)}, u32[]{:S(2)}) collective-permute-start(bf16[256,128]{1,0:T(8,128)(2,1)S(1)} %get-tuple-element.52), channel_id=1, source_target_pairs={{0,2},{1,3},{2,0},{3,1},{4,6},{5,7},{6,4},{7,5},{8,10},{9,11},{10,... | collective-permute-start | bytes 196616 | tf_op jit(solution)/shard_map/ppermute | solution.py:53
  85.6 5.6 %collective-permute-start.14 = (bf16[256,128]{1,0:T(8,128)(2,1)S(1)}, bf16[256,128]{1,0:T(8,128)(2,1)S(1)}, u32[]{:S(2)}, u32[]{:S(2)}) collective-permute-start(bf16[256,128]{1,0:T(8,128)(2,1)S(1)} %get-tuple-element.53), channel_id=1, source_target_pairs={{0,3},{1,0},{2,1},{3,2},{4,7},{5,4},{6,5},{7,6},{8,11},{9,8},{10,9... | collective-permute-start | bytes 196616 | tf_op jit(solution)/shard_map/ppermute | solution.py:53
  91.2 15.4 %collective-permute-start.15 = (bf16[1024,128]{1,0:T(8,128)(2,1)S(1)}, bf16[1024,128]{1,0:T(8,128)(2,1)S(1)}, u32[]{:S(2)}, u32[]{:S(2)}) collective-permute-start(bf16[1024,128]{1,0:T(8,128)(2,1)S(1)} %collect_rows.1.rest_1_), channel_id=1, source_target_pairs={{0,4},{4,8},{8,12},{12,16},{16,20},{20,24},{24,28},{28,32},{32,36}... | collective-permute-start | bytes 786440 | tf_op jit(solution)/shard_map/ppermute | solution.py:53
  99.6 4.4 %collective-permute-start.16 = (bf16[256,128]{1,0:T(8,128)(2,1)S(1)}, bf16[256,128]{1,0:T(8,128)(2,1)S(1)}, u32[]{:S(2)}, u32[]{:S(2)}) collective-permute-start(bf16[256,128]{1,0:T(8,128)(2,1)S(1)} %get-tuple-element.56), channel_id=1, source_target_pairs={{0,1},{1,2},{2,3},{3,0},{4,5},{5,6},{6,7},{7,4},{8,9},{9,10},{10,1... | collective-permute-start | bytes 196616 | tf_op jit(solution)/shard_map/ppermute | solution.py:53
  100.7 5.3 %collective-permute-start.17 = (bf16[256,128]{1,0:T(8,128)(2,1)S(1)}, bf16[256,128]{1,0:T(8,128)(2,1)S(1)}, u32[]{:S(2)}, u32[]{:S(2)}) collective-permute-start(bf16[256,128]{1,0:T(8,128)(2,1)S(1)} %get-tuple-element.57), channel_id=1, source_target_pairs={{0,2},{1,3},{2,0},{3,1},{4,6},{5,7},{6,4},{7,5},{8,10},{9,11},{10,... | collective-permute-start | bytes 196616 | tf_op jit(solution)/shard_map/ppermute | solution.py:53
  102.9 3.7 %collective-permute-start.18 = (bf16[256,128]{1,0:T(8,128)(2,1)S(1)}, bf16[256,128]{1,0:T(8,128)(2,1)S(1)}, u32[]{:S(2)}, u32[]{:S(2)}) collective-permute-start(bf16[256,128]{1,0:T(8,128)(2,1)S(1)} %get-tuple-element.58), channel_id=1, source_target_pairs={{0,3},{1,0},{2,1},{3,2},{4,7},{5,4},{6,5},{7,6},{8,11},{9,8},{10,9... | collective-permute-start | bytes 196616 | tf_op jit(solution)/shard_map/ppermute | solution.py:53
  108.6 5.2 %collective-permute-start.19 = (bf16[784,128]{1,0:T(8,128)(2,1)S(1)}, bf16[784,128]{1,0:T(8,128)(2,1)S(1)}, u32[]{:S(2)}, u32[]{:S(2)}) collective-permute-start(bf16[784,128]{1,0:T(8,128)(2,1)S(1)} %get-tuple-element.59), channel_id=1, source_target_pairs={{0,252},{4,0},{8,4},{12,8},{16,12},{20,16},{24,20},{28,24},{32,28}... | collective-permute-start | bytes 602120 | tf_op jit(solution)/shard_map/ppermute | solution.py:53
  110.1 4.1 %collective-permute-start.20 = (bf16[784,128]{1,0:T(8,128)(2,1)S(1)}, bf16[784,128]{1,0:T(8,128)(2,1)S(1)}, u32[]{:S(2)}, u32[]{:S(2)}) collective-permute-start(bf16[784,128]{1,0:T(8,128)(2,1)S(1)} %get-tuple-element.61), channel_id=1, source_target_pairs={{0,4},{4,8},{8,12},{12,16},{16,20},{20,24},{24,28},{28,32},{32,36}... | collective-permute-start | bytes 602120 | tf_op jit(solution)/shard_map/ppermute | solution.py:53
  110.4 15.0 %collective-permute-start.21 = (bf16[784,128]{1,0:T(8,128)(2,1)S(1)}, bf16[784,128]{1,0:T(8,128)(2,1)S(1)}, u32[]{:S(2)}, u32[]{:S(2)}) collective-permute-start(bf16[784,128]{1,0:T(8,128)(2,1)S(1)} %get-tuple-element.62), channel_id=1, source_target_pairs={{0,8},{4,12},{8,16},{12,20},{16,24},{20,28},{24,32},{28,36},{32,40... | collective-permute-start | bytes 602120 | tf_op jit(solution)/shard_map/ppermute | solution.py:53

commit v7 on v6

--- a/solution.py
+++ b/solution.py
@@ -11,7 +11,9 @@
 HEAD_DIM = 16
 GROUP_HEADS = 8
 EPSILON = 1e-05
-LOG2E = 1.4426950408889634
+SCALE = HEAD_DIM ** (-0.5) * 1.4426950408889634
+SAFE_SCORE = 100.0
+SAFE_VALUE = 1e4
 
 TILE = 16
 BLOCK = 128
@@ -256,11 +258,17 @@
         fill(other, mine)
 
 
+def largest(values, top):
+    rows, columns = values.shape
+    found = jnp.max(jnp.abs(values).reshape(rows // 8, 8, columns), axis=0)
+    return found if top is None else jnp.maximum(top, found)
+
+
 def project_kernel(part, table_ref, spots_ref, *refs):
     lane_refs, gain_ref = refs[:LANES], refs[LANES]
     weight_refs = refs[LANES + 1 : LANES + 10]
     extra_ref = refs[LANES + 10]
-    own_ref, keys_ref, values_ref, query_ref, rows_ref, normed_ref, stack_ref = refs[-7:]
+    own_ref, keys_ref, values_ref, query_ref, bound_ref, rows_ref, normed_ref, stack_ref = refs[-8:]
     queries = own_ref.shape[0]
     span = GROUP_HEADS * HEAD_DIM
     near_ref = weight_refs[0]
@@ -276,6 +284,8 @@
 
     by_core(fill, weight_refs)
     gain = gain_ref[0:1, :]
+    value_top = None
+    key_top = None
     for quarter in range(4):
         for block in range(quarter * 2, quarter * 2 + 2):
             rows = slice(block * BLOCK, (block + 1) * BLOCK)
@@ -286,12 +296,21 @@
             normed_ref[rows, :] = layer_norm(found, gain)
         rows = slice(quarter * 256, (quarter + 1) * 256)
         normed = normed_ref[rows, :]
-        keys_ref[rows, :] = nt_dot(normed, stack_ref[1]).astype(BF16)
-        values_ref[:, rows] = nt_dot(stack_ref[2], normed).astype(BF16)
+        keys = nt_dot(normed, stack_ref[1])
+        keys_ref[rows, :] = keys.astype(BF16)
+        key_top = largest(keys, key_top)
+        values = nt_dot(stack_ref[2], normed)
+        values_ref[:, rows] = values.astype(BF16)
+        value_top = largest(values, value_top)
     own_rows = pl.ds(pl.multiple_of(lax.axis_index("mp") * queries, queries), queries)
     own_ref[...] = rows_ref[own_rows, :]
     query = nt_dot(stack_ref[0], normed_ref[own_rows, :])
-    query_ref[...] = (query * (HEAD_DIM ** (-0.5) * LOG2E)).astype(BF16)
+    query_ref[...] = query.astype(BF16)
+    query = jnp.minimum(jnp.abs(query), 1e9)
+    query_top = jnp.max(jnp.sum((query * query).reshape(-1, HEAD_DIM, queries), axis=1))
+    key_top = jnp.minimum(jnp.max(key_top), 1e9)
+    bound = 1.05 * SCALE**2 * HEAD_DIM * query_top * (key_top * key_top)
+    bound_ref[0] = jnp.where(jnp.max(value_top) < SAFE_VALUE, bound, 2.0 * SAFE_SCORE**2)
 
 
 def project(part, table, spots, lanes, gains, early, extra, queries):
@@ -299,9 +318,15 @@
     shape = lambda *dims: jax.ShapeDtypeStruct(dims, BF16)
     return pl.pallas_call(
         functools.partial(project_kernel, part),
-        out_shape=(shape(queries, width), shape(PATCH, width), shape(width, PATCH), shape(width, queries)),
+        out_shape=(
+            shape(queries, width),
+            shape(PATCH, width),
+            shape(width, PATCH),
+            shape(width, queries),
+            jax.ShapeDtypeStruct((1,), F32),
+        ),
         in_specs=[SMEM] + [VMEM] * (LANES + 11) + ([VMEM] + [ANY] * (len(extra) - 1) if part else [ANY] * len(extra)),
-        out_specs=(VMEM,) * 4,
+        out_specs=(VMEM,) * 4 + (SMEM,),
         scratch_shapes=[
             pltpu.VMEM((PATCH, width), BF16),
             pltpu.VMEM((PATCH, width), BF16),
@@ -313,7 +338,7 @@
     )(table, spots, *lanes, gains, *early, *extra)
 
 
-def attend_kernel(groups, final, keys_ref, values_ref, query_ref, *refs):
+def attend_kernel(groups, final, bound_ref, keys_ref, values_ref, query_ref, *refs):
     mixed_ref, score_ref = refs[-2:]
     out_ref = refs[-4] if final else None
     queries = query_ref.shape[1]
@@ -327,38 +352,65 @@
         query = query_ref[group * span : (group + 1) * span, :]
         return jnp.where(head_of_row == head, query, jnp.zeros_like(query))
 
-    def score(slot, group, query, chunk, highest):
+    def score(slot, group, query, chunk):
         rows = slice(chunk * BLOCK, (chunk + 1) * BLOCK)
         scores = nn_dot(keys_ref[rows, group * span : (group + 1) * span], query)
         score_ref[slot, rows, :] = scores
-        top = jnp.max(scores.reshape(BLOCK // 8, 8, queries), axis=0)
-        return top if highest is None else jnp.maximum(highest, top)
-
-    highest = None
-    query = query_of(first, 0)
-    for chunk in range(BLOCKS):
-        highest = score(0, first, query, chunk, highest)
-
-    def head_step(head, highest):
+
+    def head_step(head, carry):
         for index, group in enumerate(groups):
-            top = jnp.max(highest, axis=0, keepdims=True)
             last = index + 1 == len(groups)
             later = groups[0] if last else groups[index + 1]
             query = query_of(later, jnp.minimum(head + 1, GROUP_HEADS - 1) if last else head)
             rows = pl.ds(pl.multiple_of(group * span + head * HEAD_DIM, HEAD_DIM), HEAD_DIM)
-            total, highest = None, None
+            total = None
             for chunk in range(BLOCKS):
                 keys = slice(chunk * BLOCK, (chunk + 1) * BLOCK)
-                highest = score((index + 1) % 2, later, query, chunk, highest)
-                weights = jnp.exp2(score_ref[index % 2, keys, :] - top).astype(BF16)
+                score((index + 1) % 2, later, query, chunk)
+                weights = jnp.exp2(score_ref[index % 2, keys, :] * SCALE).astype(BF16)
                 values = jnp.concatenate([values_ref[rows, keys], ones], axis=0)
                 term = nn_dot(values, weights)
                 total = term if total is None else total + term
             held = pl.ds(pl.multiple_of((group - first) * span + head * HEAD_DIM, HEAD_DIM), HEAD_DIM)
             mixed_ref[held, :] = (total[:HEAD_DIM] / total[HEAD_DIM : HEAD_DIM + 1]).astype(BF16)
-        return highest
-
-    lax.fori_loop(0, GROUP_HEADS, head_step, highest)
+        return carry
+
+    safe = bound_ref[0] < SAFE_SCORE * SAFE_SCORE
+
+    @pl.when(safe)
+    def _():
+        query = query_of(first, 0)
+        for chunk in range(BLOCKS):
+            score(0, first, query, chunk)
+        lax.fori_loop(0, GROUP_HEADS, head_step, 0)
+
+    def careful_step(index, carry):
+        base = pl.multiple_of((first + index // GROUP_HEADS) * span, span)
+        head = index % GROUP_HEADS
+        query = query_ref[pl.ds(base, span), :]
+        query = jnp.where(head_of_row == head, query, jnp.zeros_like(query))
+        top, total = None, None
+        for chunk in range(BLOCKS):
+            keys = slice(chunk * BLOCK, (chunk + 1) * BLOCK)
+            scores = nn_dot(keys_ref[keys, pl.ds(base, span)], query)
+            score_ref[0, keys, :] = scores
+            high = jnp.max(scores, axis=0, keepdims=True)
+            top = high if top is None else jnp.maximum(top, high)
+        rows = pl.ds(pl.multiple_of(base + head * HEAD_DIM, HEAD_DIM), HEAD_DIM)
+        for chunk in range(BLOCKS):
+            keys = slice(chunk * BLOCK, (chunk + 1) * BLOCK)
+            weights = jnp.exp2((score_ref[0, keys, :] - top) * SCALE).astype(BF16)
+            values = jnp.concatenate([values_ref[rows, keys], ones], axis=0)
+            term = nn_dot(values, weights)
+            total = term if total is None else total + term
+        held = pl.ds(pl.multiple_of(index * HEAD_DIM, HEAD_DIM), HEAD_DIM)
+        mixed_ref[held, :] = (total[:HEAD_DIM] / total[HEAD_DIM : HEAD_DIM + 1]).astype(BF16)
+        return carry
+
+    @pl.when(jnp.logical_not(safe))
+    def _():
+        lax.fori_loop(0, len(groups) * GROUP_HEADS, careful_step, 0)
+
     if not final:
         return
     own_ref, weight_refs = refs[0], refs[1:10]
@@ -383,12 +435,12 @@
 
 
 def attend(groups, projected, early, prior, after):
-    own, keys, values, query = projected
+    own, keys, values, query, bound = projected
     queries, width = own.shape
     span = GROUP_HEADS * HEAD_DIM
     height = len(groups) * span
     final = groups[-1] == 3
-    operands = [keys, values, query]
+    operands = [bound, keys, values, query]
     if final:
         operands += [own, *early, *prior]
     scratch = [pltpu.VMEM((2, PATCH, queries), F32)]
@@ -400,7 +452,7 @@
     return pl.pallas_call(
         functools.partial(attend_kernel, groups, final),
         out_shape=jax.ShapeDtypeStruct((queries, width) if final else (height, queries), BF16),
-        in_specs=[VMEM] * len(operands) + [ANY] * len(after),
+        in_specs=[SMEM] + [VMEM] * (len(operands) - 1) + [ANY] * len(after),
         out_specs=VMEM,
         scratch_shapes=scratch,
         cost_estimate=pl.CostEstimate(

time: 128 us -> 147 us (1.15)
  Pallas kernels: 45.9 us -> 68.5 us
  waiting for transfers between devices: 45.1 us -> 39.5 us
  starting transfers between devices: 34.5 us -> 37.2 us
    pallas_call x3, Pallas kernels: 22.7 us -> 43.9 us  [attend(): pl.pallas_call(functools.partial(attend_kernel, groups, final), out_shape...]
    ppermute x18, waiting for transfers between devices: 45.1 us -> 39.5 us  [shifted(): return lax.ppermute(value, axis, pairs)]
    ppermute x18, starting transfers between devices: 26.1 us -> 28.7 us  [shifted(): return lax.ppermute(value, axis, pairs)]
  transfers between devices with their start and end apart: 22 -> 22, of which waited for: 12 -> 11; matrix products, arithmetic and copies ran while one was open for 0% -> 0% of each run, Pallas kernels for 18% -> 23%
where the time goes in v7:
time: 147 us
  Pallas kernels  68.5 us (47%)
  waiting for transfers between devices  39.5 us (27%)
  starting transfers between devices  37.2 us (25%)
    pallas_call x3, Pallas kernels, attend(): pl.pallas_call(functools.partial(attend_kernel, groups, final), out_shape...  43.9 us
    ppermute x18, waiting for transfers between devices, shifted(): return lax.ppermute(value, axis, pairs)  39.5 us
    ppermute x18, starting transfers between devices, shifted(): return lax.ppermute(value, axis, pairs)  28.7 us
    pallas_call x2, Pallas kernels, project(): pl.pallas_call(functools.partial(project_kernel, part), out_shape=(shape(...  10.2 us
    ppermute x4, starting transfers between devices, swapped(): lax.ppermute(value, 'brick', [(brick, brick ^ 1) for brick in range(brick...  8.49 us
    pallas_call x2, Pallas kernels, mlp(): pl.pallas_call(functools.partial(mlp_kernel, groups), out_shape=(jax.Shap...  3.51 us
  transfers between devices with their start and end apart: 22, of which 11 were waited for; matrix products, arithmetic and copies ran while one was open for 0% of the time, Pallas kernels for 23%

profile of v7, /device:TPU:1, one launch (start us, length us, event | category | flops | bytes accessed | tf_op | source)
XLA Modules:
  0.0 146.9 jit_solution(13082629521477050965)
XLA Ops:
  0.0 0.0 copy-start.2
  0.0 0.0 copy-start.5
  0.0 0.8 copy-done.5
  0.8 2.4 %cut_windows.1 = (bf16[784,512]{1,0:T(8,128)(2,1)S(1)}, bf16[784,512]{1,0:T(8,128)(2,1)S(1)}, bf16[784,512]{1,0:T(8,128)(2,1)S(1)}, s32[2,4]{1,0:T(2,128)S(1)}) custom-call(s32[24,128]{1,0:T(8,128)S(1)} %bitcast.2, bf16[3072,512]{1,0:T(8,128)(2,1)} %feats_ref.3), custom_call_target="tpu_custom_call" | custom-call | tf_op jit(solution)/shard_map/cut_windows/pallas_call | solution.py:92
  3.2 3.3 %collective-permute-start.1 = (bf16[784,512]{1,0:T(8,128)(2,1)S(1)}, bf16[784,512]{1,0:T(8,128)(2,1)S(1)}, u32[]{:S(2)}, u32[]{:S(2)}) collective-permute-start(bf16[784,512]{1,0:T(8,128)(2,1)S(1)} %get-tuple-element.42), channel_id=1, source_target_pairs={{0,252},{4,0},{8,4},{12,8},{16,12},{20,16},{24,20},{28,24},{32,28}... | collective-permute-start | bytes 2408456 | tf_op jit(solution)/shard_map/ppermute | solution.py:55
  6.5 6.5 %collective-permute-start.2 = (bf16[784,512]{1,0:T(8,128)(2,1)S(1)}, bf16[784,512]{1,0:T(8,128)(2,1)S(1)}, u32[]{:S(2)}, u32[]{:S(2)}) collective-permute-start(bf16[784,512]{1,0:T(8,128)(2,1)S(1)} %get-tuple-element.43), channel_id=1, source_target_pairs={{0,248},{4,252},{8,0},{12,4},{16,8},{20,12},{24,16},{28,20},{32,24... | collective-permute-start | bytes 2408456 | tf_op jit(solution)/shard_map/ppermute | solution.py:55
  13.0 0.0 copy-done.1
  13.0 0.0 copy-done.3
  13.0 0.5 sort_weights.1
  13.5 2.6 %collective-permute-start.5 = (bf16[768,512]{1,0:T(8,128)(2,1)S(1)}, bf16[768,512]{1,0:T(8,128)(2,1)S(1)}, u32[]{:S(2)}, u32[]{:S(2)}) collective-permute-start(bf16[768,512]{1,0:T(8,128)(2,1)S(1)} %get-tuple-element.44), channel_id=1, source_target_pairs={{0,3},{1,0},{2,1},{3,2},{4,7},{5,4},{6,5},{7,6},{8,11},{9,8},{10,9... | collective-permute-start | bytes 2359304 | tf_op jit(solution)/shard_map/ppermute | solution.py:55
  16.0 0.0 collective-permute-start.3
  16.0 1.7 %collective-permute-start = (bf16[784,512]{1,0:T(8,128)(2,1)S(1)}, bf16[784,512]{1,0:T(8,128)(2,1)S(1)}, u32[]{:S(2)}, u32[]{:S(2)}) collective-permute-start(bf16[784,512]{1,0:T(8,128)(2,1)S(1)} %get-tuple-element.37.after_ref), channel_id=1, source_target_pairs={{0,4},{4,8},{8,12},{12,16},{16,20},{20,24},{24,28},{28,32},{32,36}... | collective-permute-start | bytes 2408456 | tf_op jit(solution)/shard_map/ppermute | solution.py:55
  17.7 14.6 %collective-permute-done.5.refs_9_.refs_5_.refs_4_ = bf16[768,512]{1,0:T(8,128)(2,1)S(1)} collective-permute-done((bf16[768,512]{1,0:T(8,128)(2,1)S(1)}, bf16[768,512]{1,0:T(8,128)(2,1)S(1)}, u32[]{:S(2)}, u32[]{:S(2)}) %collective-permute-start.5) | collective-permute-done | bytes 786464 | tf_op jit(solution)/shard_map/ppermute | solution.py:55
  32.4 3.5 %collective-permute-start.6 = (bf16[384,512]{1,0:T(8,128)(2,1)S(1)}, bf16[384,512]{1,0:T(8,128)(2,1)S(1)}, u32[]{:S(2)}, u32[]{:S(2)}) collective-permute-start(bf16[384,512]{1,0:T(8,128)(2,1)S(1)} %slice.9), channel_id=1, source_target_pairs={{0,3},{1,0},{2,1},{3,2},{4,7},{5,4},{6,5},{7,6},{8,11},{9,8},{10,9... | collective-permute-start | bytes 1179656 | tf_op jit(solution)/shard_map/ppermute | solution.py:55
  35.9 0.0 collective-permute-done.3.refs_6_.refs_2_.refs_1_
  35.9 0.1 collective-permute-start.4
  36.0 0.0 collective-permute-done.1.refs_2_
  36.0 1.8 %collective-permute-start.10 = (bf16[768,512]{1,0:T(8,128)(2,1)S(1)}, bf16[768,512]{1,0:T(8,128)(2,1)S(1)}, u32[]{:S(2)}, u32[]{:S(2)}) collective-permute-start(bf16[768,512]{1,0:T(8,128)(2,1)S(1)} %collective-permute-done.5.refs_9_.refs_5_.refs_4_), channel_id=1, source_target_pairs={{0,4},{4,0},{8,12},{12,8},{16,20},{20,16},{24,28},{28,24},{32,36},... | collective-permute-start | bytes 2359304 | tf_op jit(solution)/shard_map/ppermute | solution.py:666
  37.8 0.0 collective-permute-done.2.refs_3_
  37.8 1.9 %collective-permute-start.7 = (bf16[768,512]{1,0:T(8,128)(2,1)S(1)}, bf16[768,512]{1,0:T(8,128)(2,1)S(1)}, u32[]{:S(2)}, u32[]{:S(2)}) collective-permute-start(bf16[768,512]{1,0:T(8,128)(2,1)S(1)} %collective-permute-done.3.refs_6_.refs_2_.refs_1_), channel_id=1, source_target_pairs={{0,4},{4,0},{8,12},{12,8},{16,20},{20,16},{24,28},{28,24},{32,36},... | collective-permute-start | bytes 2359304 | tf_op jit(solution)/shard_map/ppermute | solution.py:666
  39.7 3.3 %collective-permute-done.6.refs_8_.refs_4_.refs_3_ = bf16[384,512]{1,0:T(8,128)(2,1)S(1)} collective-permute-done((bf16[384,512]{1,0:T(8,128)(2,1)S(1)}, bf16[384,512]{1,0:T(8,128)(2,1)S(1)}, u32[]{:S(2)}, u32[]{:S(2)}) %collective-permute-start.6) | collective-permute-done | bytes 393248 | tf_op jit(solution)/shard_map/ppermute | solution.py:55
  42.9 2.3 %collective-permute-start.9 = (bf16[384,512]{1,0:T(8,128)(2,1)S(1)}, bf16[384,512]{1,0:T(8,128)(2,1)S(1)}, u32[]{:S(2)}, u32[]{:S(2)}) collective-permute-start(bf16[384,512]{1,0:T(8,128)(2,1)S(1)} %collective-permute-done.6.refs_8_.refs_4_.refs_3_), channel_id=1, source_target_pairs={{0,4},{4,0},{8,12},{12,8},{16,20},{20,16},{24,28},{28,24},{32,36},... | collective-permute-start | bytes 1179656 | tf_op jit(solution)/shard_map/ppermute | solution.py:666
  45.2 1.0 collective-permute-done.4.refs_7_.refs_3_.refs_2_
  46.2 2.6 %collective-permute-start.8 = (bf16[384,512]{1,0:T(8,128)(2,1)S(1)}, bf16[384,512]{1,0:T(8,128)(2,1)S(1)}, u32[]{:S(2)}, u32[]{:S(2)}) collective-permute-start(bf16[384,512]{1,0:T(8,128)(2,1)S(1)} %collective-permute-done.4.refs_7_.refs_3_.refs_2_), channel_id=1, source_target_pairs={{0,4},{4,0},{8,12},{12,8},{16,20},{20,16},{24,28},{28,24},{32,36},... | collective-permute-start | bytes 1179656 | tf_op jit(solution)/shard_map/ppermute | solution.py:666
  49.4 0.0 copy-start.4
  49.4 2.2 %index_tables.1 = (s32[24,128]{1,0:T(8,128)S(1)}, s32[24,128]{1,0:T(8,128)S(1)}, bf16[784,512]{1,0:T(8,128)(2,1)S(1)}) custom-call(s32[1]{0:T(128)S(6)} %copy.10.shift_ref, s32[2,4]{1,0:T(2,128)S(1)} %get-tuple-element.36.counts_ref, s32[16,128]{1,0:T(8,128)S(1)} %bitcast.3, bf16[3072,512]{1,0:T(8,128)(2,1)} %feats_ref.3, ...), custom_call_target="tpu_custom_call" | custom-call | tf_op jit(solution)/shard_map/index_tables/pallas_call | solution.py:197
  51.6 0.0 collective-permute-done.refs_0_
  51.6 1.8 %head_rows.1.refs_14_ = bf16[1024,512]{1,0:T(8,128)(2,1)S(1)} custom-call(s32[24,128]{1,0:T(8,128)S(1)} %get-tuple-element.39.table_ref, s32[24,128]{1,0:T(8,128)S(1)} %get-tuple-element.40.spots_ref, bf16[784,512]{1,0:T(8,128)(2,1)S(1)} %collective-permute-done.refs_0_, bf16[784,512]{1,0:T(8,128)(2,1)S(1)} %get-tuple-element.41.refs_1_, ...), custom_call_target="tpu_custom_call" | custom-call | flops 805306368 | bytes 5242880 | tf_op jit(solution)/shard_map/head_rows/pallas_call | solution.py:234
  53.4 0.1 collective-permute-start.11
  53.5 0.0 collective-permute-done.9.refs_12_.refs_8_.refs_7_
  53.5 0.0 collective-permute-done.10.refs_13_.refs_9_.refs_8_
  53.5 0.0 collective-permute-done.8.refs_11_.refs_7_.refs_6_
  53.5 0.0 collective-permute-done.7.refs_10_.refs_6_.refs_5_
  53.5 0.0 copy-done.4
  53.5 5.2 %project_first.1 = (bf16[256,512]{1,0:T(8,128)(2,1)S(1)}, bf16[1024,512]{1,0:T(8,128)(2,1)S(1)}, bf16[512,1024]{1,0:T(8,128)(2,1)S(1)}, bf16[512,256]{1,0:T(8,128)(2,1)S(1)}, f32[1]{0:T(128)}) custom-call(s32[24,128]{1,0:T(8,128)S(1)} %get-tuple-element.39.table_ref, s32[24,128]{1,0:T(8,128)S(1)} %get-tuple-element.40.spots_ref, ...), custom_call_target="tpu_custom_call" | custom-call | flops 10000000000 | bytes 10485760 | tf_op jit(solution)/shard_map/project_first/pallas_call | solution.py:319
  58.8 10.8 %shard_map.91.refs_15_.refs_10_ = bf16[256,256]{1,0:T(8,128)(2,1)S(1)} custom-call(f32[1]{0:T(128)} %get-tuple-element.45.bound_ref, bf16[1024,512]{1,0:T(8,128)(2,1)S(1)} %get-tuple-element.46.keys_ref, bf16[512,1024]{1,0:T(8,128)(2,1)S(1)} %get-tuple-element.47.values_ref, bf16[512,256]{1,0:T(8,128)(2,1)S(1)} %get-tuple-element.48.query_ref), custom_call_target="tpu_custom_call" | custom-call | flops 16000000000 | bytes 5242880 | tf_op jit(solution)/shard_map/pallas_call | solution.py:452
  69.6 0.0 collective-permute-done.11.refs_14_
  69.6 5.0 %project_last.1 = (bf16[256,512]{1,0:T(8,128)(2,1)S(1)}, bf16[1024,512]{1,0:T(8,128)(2,1)S(1)}, bf16[512,1024]{1,0:T(8,128)(2,1)S(1)}, bf16[512,256]{1,0:T(8,128)(2,1)S(1)}, f32[1]{0:T(128)}) custom-call(s32[24,128]{1,0:T(8,128)S(1)} %get-tuple-element.39.table_ref, s32[24,128]{1,0:T(8,128)S(1)} %get-tuple-element.40.spots_ref, ...), custom_call_target="tpu_custom_call" | custom-call | flops 10000000000 | bytes 10485760 | tf_op jit(solution)/shard_map/project_last/pallas_call | solution.py:319
  74.6 21.7 %shard_map.92.hidden_ref = bf16[256,512]{1,0:T(8,128)(2,1)S(1)} custom-call(f32[1]{0:T(128)} %get-tuple-element.49.bound_ref, bf16[1024,512]{1,0:T(8,128)(2,1)S(1)} %get-tuple-element.50.keys_ref, bf16[512,1024]{1,0:T(8,128)(2,1)S(1)} %get-tuple-element.51.values_ref, bf16[512,256]{1,0:T(8,128)(2,1)S(1)} %get-tuple-element.52.query_ref, ...), custom_call_target="tpu_custom_call" | custom-call | flops 32000000000 | bytes 5242880 | tf_op jit(solution)/shard_map/pallas_call | solution.py:452
  96.3 1.7 %mlp.2 = (bf16[256,128]{1,0:T(8,128)(2,1)S(1)}, bf16[256,128]{1,0:T(8,128)(2,1)S(1)}, bf16[256,128]{1,0:T(8,128)(2,1)S(1)}, bf16[256,128]{1,0:T(8,128)(2,1)S(1)}) custom-call(bf16[256,512]{1,0:T(8,128)(2,1)S(1)} %shard_map.92.hidden_ref, f32[2,512]{1,0:T(2,128)S(1)} %copy-done.4, bf16[512,512]{1,0:T(8,128)(2,1)S(1)} %copy-done, ...), custom_call_target="tpu_custom_call" | custom-call | flops 1073741824 | bytes 5242880 | tf_op jit(solution)/shard_map/mlp/pallas_call | solution.py:530
  98.1 0.1 collective-permute-start.12
  98.2 1.6 %collective-permute-start.13 = (bf16[256,128]{1,0:T(8,128)(2,1)S(1)}, bf16[256,128]{1,0:T(8,128)(2,1)S(1)}, u32[]{:S(2)}, u32[]{:S(2)}) collective-permute-start(bf16[256,128]{1,0:T(8,128)(2,1)S(1)} %get-tuple-element.56), channel_id=1, source_target_pairs={{0,2},{1,3},{2,0},{3,1},{4,6},{5,7},{6,4},{7,5},{8,10},{9,11},{10,... | collective-permute-start | bytes 196616 | tf_op jit(solution)/shard_map/ppermute | solution.py:55
  99.7 1.1 collective-permute-start.14
  100.8 1.7 %collective-permute-done.12.refs_1_ = bf16[256,128]{1,0:T(8,128)(2,1)S(1)} collective-permute-done((bf16[256,128]{1,0:T(8,128)(2,1)S(1)}, bf16[256,128]{1,0:T(8,128)(2,1)S(1)}, u32[]{:S(2)}, u32[]{:S(2)}) %collective-permute-start.12) | collective-permute-done | bytes 65568 | tf_op jit(solution)/shard_map/ppermute | solution.py:55
  102.5 0.7 collective-permute-done.13.refs_2_
  103.2 0.9 collective-permute-done.14.refs_3_
  104.1 2.9 %collective-permute-start.15 = (bf16[1024,128]{1,0:T(8,128)(2,1)S(1)}, bf16[1024,128]{1,0:T(8,128)(2,1)S(1)}, u32[]{:S(2)}, u32[]{:S(2)}) collective-permute-start(bf16[1024,128]{1,0:T(8,128)(2,1)S(1)} %collect_rows.1.rest_1_), channel_id=1, source_target_pairs={{0,4},{4,8},{8,12},{12,16},{16,20},{20,24},{24,28},{28,32},{32,36}... | collective-permute-start | bytes 786440 | tf_op jit(solution)/shard_map/ppermute | solution.py:55
  107.0 11.4 %shard_map.93.hidden_ref = bf16[256,512]{1,0:T(8,128)(2,1)S(1)} custom-call(f32[1]{0:T(128)} %get-tuple-element.45.bound_ref, bf16[1024,512]{1,0:T(8,128)(2,1)S(1)} %get-tuple-element.46.keys_ref, bf16[512,1024]{1,0:T(8,128)(2,1)S(1)} %get-tuple-element.47.values_ref, bf16[512,256]{1,0:T(8,128)(2,1)S(1)} %get-tuple-element.48.query_ref, ...), custom_call_target="tpu_custom_call" | custom-call | flops 16000000000 | bytes 5242880 | tf_op jit(solution)/shard_map/pallas_call | solution.py:452
  118.4 1.8 %mlp.3 = (bf16[256,128]{1,0:T(8,128)(2,1)S(1)}, bf16[256,128]{1,0:T(8,128)(2,1)S(1)}, bf16[256,128]{1,0:T(8,128)(2,1)S(1)}, bf16[256,128]{1,0:T(8,128)(2,1)S(1)}) custom-call(bf16[256,512]{1,0:T(8,128)(2,1)S(1)} %shard_map.93.hidden_ref, f32[2,512]{1,0:T(2,128)S(1)} %copy-done.4, bf16[512,512]{1,0:T(8,128)(2,1)S(1)} %copy-done, ...), custom_call_target="tpu_custom_call" | custom-call | flops 1073741824 | bytes 5242880 | tf_op jit(solution)/shard_map/mlp/pallas_call | solution.py:530
  120.2 1.1 collective-permute-start.16
  121.3 2.3 %collective-permute-start.17 = (bf16[256,128]{1,0:T(8,128)(2,1)S(1)}, bf16[256,128]{1,0:T(8,128)(2,1)S(1)}, u32[]{:S(2)}, u32[]{:S(2)}) collective-permute-start(bf16[256,128]{1,0:T(8,128)(2,1)S(1)} %get-tuple-element.61), channel_id=1, source_target_pairs={{0,2},{1,3},{2,0},{3,1},{4,6},{5,7},{6,4},{7,5},{8,10},{9,11},{10,... | collective-permute-start | bytes 196616 | tf_op jit(solution)/shard_map/ppermute | solution.py:55
  123.6 0.2 collective-permute-start.18
  123.8 1.0 collective-permute-done.16.rest_3_
  124.8 2.0 %collective-permute-done.17.rest_4_ = bf16[256,128]{1,0:T(8,128)(2,1)S(1)} collective-permute-done((bf16[256,128]{1,0:T(8,128)(2,1)S(1)}, bf16[256,128]{1,0:T(8,128)(2,1)S(1)}, u32[]{:S(2)}, u32[]{:S(2)}) %collective-permute-start.17) | collective-permute-done | bytes 65568 | tf_op jit(solution)/shard_map/ppermute | solution.py:55
  126.9 0.7 collective-permute-done.18.rest_5_
  127.5 0.0 collective-permute-done.15.rest_0_
  127.5 1.9 %pack_lanes.1 = (bf16[784,128]{1,0:T(8,128)(2,1)S(1)}, bf16[784,128]{1,0:T(8,128)(2,1)S(1)}, bf16[784,128]{1,0:T(8,128)(2,1)S(1)}, bf16[784,128]{1,0:T(8,128)(2,1)S(1)}) custom-call(s32[1]{0:T(128)S(6)} %copy.10.shift_ref, s32[24,128]{1,0:T(8,128)S(1)} %get-tuple-element.39.table_ref, s32[24,128]{1,0:T(8,128)S(1)} %get-tuple-element.40.spots_ref, ...), custom_call_target="tpu_custom_call" | custom-call | tf_op jit(solution)/shard_map/pack_lanes/pallas_call | solution.py:600
  129.5 0.6 collective-permute-start.19
  130.1 1.2 collective-permute-start.20
  131.3 0.0 collective-permute-start.21
  131.3 3.4 %collective-permute-done.19.refs_0_ = bf16[784,128]{1,0:T(8,128)(2,1)S(1)} collective-permute-done((bf16[784,128]{1,0:T(8,128)(2,1)S(1)}, bf16[784,128]{1,0:T(8,128)(2,1)S(1)}, u32[]{:S(2)}, u32[]{:S(2)}) %collective-permute-start.19) | collective-permute-done | bytes 200736 | tf_op jit(solution)/shard_map/ppermute | solution.py:55
  134.7 0.0 collective-permute-done.20.refs_2_
  134.7 10.2 %collective-permute-done.21.refs_3_ = bf16[784,128]{1,0:T(8,128)(2,1)S(1)} collective-permute-done((bf16[784,128]{1,0:T(8,128)(2,1)S(1)}, bf16[784,128]{1,0:T(8,128)(2,1)S(1)}, u32[]{:S(2)}, u32[]{:S(2)}) %collective-permute-start.21) | collective-permute-done | bytes 200736 | tf_op jit(solution)/shard_map/ppermute | solution.py:55
  144.9 2.0 %place_rows.1 = bf16[3072,128]{1,0:T(8,128)(2,1)} custom-call(s32[2,4]{1,0:T(2,128)S(1)} %get-tuple-element.36.counts_ref, bf16[784,128]{1,0:T(8,128)(2,1)S(1)} %collective-permute-done.19.refs_0_, bf16[784,128]{1,0:T(8,128)(2,1)S(1)} %get-tuple-element.64.refs_1_, bf16[784,128]{1,0:T(8,128)(2,1)S(1)} %collective-permute-done.20.refs_2_, ...), custom_call_target="tpu_custom_call" | custom-call | tf_op jit(solution)/shard_map/place_rows/pallas_call | solution.py:629
  (10 shorter events, 0.1 us)
Async XLA Ops:
  0.0 13.0 %copy-start.1 = (bf16[512,512]{1,0:T(8,128)(2,1)S(1)}, bf16[512,512]{1,0:T(8,128)(2,1)}, u32[]{:S(2)}) copy-start(bf16[512,512]{1,0:T(8,128)(2,1)} %down_ref.5) | copy-start | bytes 1572868
  0.0 13.0 %copy-start = (bf16[512,512]{1,0:T(8,128)(2,1)S(1)}, bf16[512,512]{1,0:T(8,128)(2,1)}, u32[]{:S(2)}) copy-start(bf16[512,512]{1,0:T(8,128)(2,1)} %up_ref.5) | copy-start | bytes 1572868
  0.0 13.0 %copy-start.3 = (bf16[128,512]{1,0:T(8,128)(2,1)S(1)}, bf16[128,512]{1,0:T(8,128)(2,1)}, u32[]{:S(2)}) copy-start(bf16[128,512]{1,0:T(8,128)(2,1)} %proj_ref.1) | copy-start | bytes 393220
  0.0 13.0 %copy-start.2 = (bf16[512,384]{1,0:T(8,128)(2,1)S(1)}, bf16[512,384]{1,0:T(8,128)(2,1)}, u32[]{:S(2)}) copy-start(bf16[512,384]{1,0:T(8,128)(2,1)} %qkv_ref.1) | copy-start | bytes 1179652
  0.0 0.8 copy-start.5
  0.8 48.5 %copy-start.6 = (s32[2048]{0:T(1024)S(1)}, s32[2048]{0:T(1024)}, u32[]{:S(2)}) copy-start(s32[2048]{0:T(1024)} %param.11) | copy-start | bytes 24580
  3.2 32.8 %collective-permute-start.1 = (bf16[784,512]{1,0:T(8,128)(2,1)S(1)}, bf16[784,512]{1,0:T(8,128)(2,1)S(1)}, u32[]{:S(2)}, u32[]{:S(2)}) collective-permute-start(bf16[784,512]{1,0:T(8,128)(2,1)S(1)} %get-tuple-element.42), channel_id=1, source_target_pairs={{0,252},{4,0},{8,4},{12,8},{16,12},{20,16},{24,20},{28,24},{32,28}... | collective-permute-start | bytes 2408456 | tf_op jit(solution)/shard_map/ppermute | solution.py:55
  6.5 31.3 %collective-permute-start.2 = (bf16[784,512]{1,0:T(8,128)(2,1)S(1)}, bf16[784,512]{1,0:T(8,128)(2,1)S(1)}, u32[]{:S(2)}, u32[]{:S(2)}) collective-permute-start(bf16[784,512]{1,0:T(8,128)(2,1)S(1)} %get-tuple-element.43), channel_id=1, source_target_pairs={{0,248},{4,252},{8,0},{12,4},{16,8},{20,12},{24,16},{28,20},{32,24... | collective-permute-start | bytes 2408456 | tf_op jit(solution)/shard_map/ppermute | solution.py:55
  13.5 18.9 %collective-permute-start.5 = (bf16[768,512]{1,0:T(8,128)(2,1)S(1)}, bf16[768,512]{1,0:T(8,128)(2,1)S(1)}, u32[]{:S(2)}, u32[]{:S(2)}) collective-permute-start(bf16[768,512]{1,0:T(8,128)(2,1)S(1)} %get-tuple-element.44), channel_id=1, source_target_pairs={{0,3},{1,0},{2,1},{3,2},{4,7},{5,4},{6,5},{7,6},{8,11},{9,8},{10,9... | collective-permute-start | bytes 2359304 | tf_op jit(solution)/shard_map/ppermute | solution.py:55
  16.0 19.9 %collective-permute-start.3 = (bf16[768,512]{1,0:T(8,128)(2,1)S(1)}, bf16[768,512]{1,0:T(8,128)(2,1)S(1)}, u32[]{:S(2)}, u32[]{:S(2)}) collective-permute-start(bf16[768,512]{1,0:T(8,128)(2,1)S(1)} %get-tuple-element.44), channel_id=1, source_target_pairs={{0,1},{1,2},{2,3},{3,0},{4,5},{5,6},{6,7},{7,4},{8,9},{9,10},{10,1... | collective-permute-start | bytes 2359304 | tf_op jit(solution)/shard_map/ppermute | solution.py:55
  16.0 35.6 %collective-permute-start = (bf16[784,512]{1,0:T(8,128)(2,1)S(1)}, bf16[784,512]{1,0:T(8,128)(2,1)S(1)}, u32[]{:S(2)}, u32[]{:S(2)}) collective-permute-start(bf16[784,512]{1,0:T(8,128)(2,1)S(1)} %get-tuple-element.37.after_ref), channel_id=1, source_target_pairs={{0,4},{4,8},{8,12},{12,16},{16,20},{20,24},{24,28},{28,32},{32,36}... | collective-permute-start | bytes 2408456 | tf_op jit(solution)/shard_map/ppermute | solution.py:55
  32.4 10.5 %collective-permute-start.6 = (bf16[384,512]{1,0:T(8,128)(2,1)S(1)}, bf16[384,512]{1,0:T(8,128)(2,1)S(1)}, u32[]{:S(2)}, u32[]{:S(2)}) collective-permute-start(bf16[384,512]{1,0:T(8,128)(2,1)S(1)} %slice.9), channel_id=1, source_target_pairs={{0,3},{1,0},{2,1},{3,2},{4,7},{5,4},{6,5},{7,6},{8,11},{9,8},{10,9... | collective-permute-start | bytes 1179656 | tf_op jit(solution)/shard_map/ppermute | solution.py:55
  35.9 10.3 %collective-permute-start.4 = (bf16[384,512]{1,0:T(8,128)(2,1)S(1)}, bf16[384,512]{1,0:T(8,128)(2,1)S(1)}, u32[]{:S(2)}, u32[]{:S(2)}) collective-permute-start(bf16[384,512]{1,0:T(8,128)(2,1)S(1)} %slice.8), channel_id=1, source_target_pairs={{0,1},{1,2},{2,3},{3,0},{4,5},{5,6},{6,7},{7,4},{8,9},{9,10},{10,1... | collective-permute-start | bytes 1179656 | tf_op jit(solution)/shard_map/ppermute | solution.py:55
  36.0 17.5 %collective-permute-start.10 = (bf16[768,512]{1,0:T(8,128)(2,1)S(1)}, bf16[768,512]{1,0:T(8,128)(2,1)S(1)}, u32[]{:S(2)}, u32[]{:S(2)}) collective-permute-start(bf16[768,512]{1,0:T(8,128)(2,1)S(1)} %collective-permute-done.5.refs_9_.refs_5_.refs_4_), channel_id=1, source_target_pairs={{0,4},{4,0},{8,12},{12,8},{16,20},{20,16},{24,28},{28,24},{32,36},... | collective-permute-start | bytes 2359304 | tf_op jit(solution)/shard_map/ppermute | solution.py:666
  37.8 15.7 %collective-permute-start.7 = (bf16[768,512]{1,0:T(8,128)(2,1)S(1)}, bf16[768,512]{1,0:T(8,128)(2,1)S(1)}, u32[]{:S(2)}, u32[]{:S(2)}) collective-permute-start(bf16[768,512]{1,0:T(8,128)(2,1)S(1)} %collective-permute-done.3.refs_6_.refs_2_.refs_1_), channel_id=1, source_target_pairs={{0,4},{4,0},{8,12},{12,8},{16,20},{20,16},{24,28},{28,24},{32,36},... | collective-permute-start | bytes 2359304 | tf_op jit(solution)/shard_map/ppermute | solution.py:666
  42.9 10.6 %collective-permute-start.9 = (bf16[384,512]{1,0:T(8,128)(2,1)S(1)}, bf16[384,512]{1,0:T(8,128)(2,1)S(1)}, u32[]{:S(2)}, u32[]{:S(2)}) collective-permute-start(bf16[384,512]{1,0:T(8,128)(2,1)S(1)} %collective-permute-done.6.refs_8_.refs_4_.refs_3_), channel_id=1, source_target_pairs={{0,4},{4,0},{8,12},{12,8},{16,20},{20,16},{24,28},{28,24},{32,36},... | collective-permute-start | bytes 1179656 | tf_op jit(solution)/shard_map/ppermute | solution.py:666
  46.2 7.3 %collective-permute-start.8 = (bf16[384,512]{1,0:T(8,128)(2,1)S(1)}, bf16[384,512]{1,0:T(8,128)(2,1)S(1)}, u32[]{:S(2)}, u32[]{:S(2)}) collective-permute-start(bf16[384,512]{1,0:T(8,128)(2,1)S(1)} %collective-permute-done.4.refs_7_.refs_3_.refs_2_), channel_id=1, source_target_pairs={{0,4},{4,0},{8,12},{12,8},{16,20},{20,16},{24,28},{28,24},{32,36},... | collective-permute-start | bytes 1179656 | tf_op jit(solution)/shard_map/ppermute | solution.py:666
  49.4 4.1 %copy-start.4 = (f32[2,512]{1,0:T(2,128)S(1)}, f32[2,512]{1,0:T(2,128)}, u32[]{:S(2)}) copy-start(f32[2,512]{1,0:T(2,128)} %gain_ref.3) | copy-start | bytes 12292
  53.4 16.2 %collective-permute-start.11 = (bf16[1024,512]{1,0:T(8,128)(2,1)S(1)}, bf16[1024,512]{1,0:T(8,128)(2,1)S(1)}, u32[]{:S(2)}, u32[]{:S(2)}) collective-permute-start(bf16[1024,512]{1,0:T(8,128)(2,1)S(1)} %head_rows.1.refs_14_), channel_id=1, source_target_pairs={{0,252},{4,0},{8,4},{12,8},{16,12},{20,16},{24,20},{28,24},{32,28}... | collective-permute-start | bytes 3145736 | tf_op jit(solution)/shard_map/ppermute | solution.py:55
  98.1 4.4 %collective-permute-start.12 = (bf16[256,128]{1,0:T(8,128)(2,1)S(1)}, bf16[256,128]{1,0:T(8,128)(2,1)S(1)}, u32[]{:S(2)}, u32[]{:S(2)}) collective-permute-start(bf16[256,128]{1,0:T(8,128)(2,1)S(1)} %get-tuple-element.55), channel_id=1, source_target_pairs={{0,1},{1,2},{2,3},{3,0},{4,5},{5,6},{6,7},{7,4},{8,9},{9,10},{10,1... | collective-permute-start | bytes 196616 | tf_op jit(solution)/shard_map/ppermute | solution.py:55
  98.2 5.0 %collective-permute-start.13 = (bf16[256,128]{1,0:T(8,128)(2,1)S(1)}, bf16[256,128]{1,0:T(8,128)(2,1)S(1)}, u32[]{:S(2)}, u32[]{:S(2)}) collective-permute-start(bf16[256,128]{1,0:T(8,128)(2,1)S(1)} %get-tuple-element.56), channel_id=1, source_target_pairs={{0,2},{1,3},{2,0},{3,1},{4,6},{5,7},{6,4},{7,5},{8,10},{9,11},{10,... | collective-permute-start | bytes 196616 | tf_op jit(solution)/shard_map/ppermute | solution.py:55
  99.7 4.3 %collective-permute-start.14 = (bf16[256,128]{1,0:T(8,128)(2,1)S(1)}, bf16[256,128]{1,0:T(8,128)(2,1)S(1)}, u32[]{:S(2)}, u32[]{:S(2)}) collective-permute-start(bf16[256,128]{1,0:T(8,128)(2,1)S(1)} %get-tuple-element.57), channel_id=1, source_target_pairs={{0,3},{1,0},{2,1},{3,2},{4,7},{5,4},{6,5},{7,6},{8,11},{9,8},{10,9... | collective-permute-start | bytes 196616 | tf_op jit(solution)/shard_map/ppermute | solution.py:55
  104.1 23.4 %collective-permute-start.15 = (bf16[1024,128]{1,0:T(8,128)(2,1)S(1)}, bf16[1024,128]{1,0:T(8,128)(2,1)S(1)}, u32[]{:S(2)}, u32[]{:S(2)}) collective-permute-start(bf16[1024,128]{1,0:T(8,128)(2,1)S(1)} %collect_rows.1.rest_1_), channel_id=1, source_target_pairs={{0,4},{4,8},{8,12},{12,16},{16,20},{20,24},{24,28},{28,32},{32,36}... | collective-permute-start | bytes 786440 | tf_op jit(solution)/shard_map/ppermute | solution.py:55
  120.2 4.6 %collective-permute-start.16 = (bf16[256,128]{1,0:T(8,128)(2,1)S(1)}, bf16[256,128]{1,0:T(8,128)(2,1)S(1)}, u32[]{:S(2)}, u32[]{:S(2)}) collective-permute-start(bf16[256,128]{1,0:T(8,128)(2,1)S(1)} %get-tuple-element.60), channel_id=1, source_target_pairs={{0,1},{1,2},{2,3},{3,0},{4,5},{5,6},{6,7},{7,4},{8,9},{9,10},{10,1... | collective-permute-start | bytes 196616 | tf_op jit(solution)/shard_map/ppermute | solution.py:55
  121.3 5.6 %collective-permute-start.17 = (bf16[256,128]{1,0:T(8,128)(2,1)S(1)}, bf16[256,128]{1,0:T(8,128)(2,1)S(1)}, u32[]{:S(2)}, u32[]{:S(2)}) collective-permute-start(bf16[256,128]{1,0:T(8,128)(2,1)S(1)} %get-tuple-element.61), channel_id=1, source_target_pairs={{0,2},{1,3},{2,0},{3,1},{4,6},{5,7},{6,4},{7,5},{8,10},{9,11},{10,... | collective-permute-start | bytes 196616 | tf_op jit(solution)/shard_map/ppermute | solution.py:55
  123.6 4.0 %collective-permute-start.18 = (bf16[256,128]{1,0:T(8,128)(2,1)S(1)}, bf16[256,128]{1,0:T(8,128)(2,1)S(1)}, u32[]{:S(2)}, u32[]{:S(2)}) collective-permute-start(bf16[256,128]{1,0:T(8,128)(2,1)S(1)} %get-tuple-element.62), channel_id=1, source_target_pairs={{0,3},{1,0},{2,1},{3,2},{4,7},{5,4},{6,5},{7,6},{8,11},{9,8},{10,9... | collective-permute-start | bytes 196616 | tf_op jit(solution)/shard_map/ppermute | solution.py:55
  129.5 5.2 %collective-permute-start.19 = (bf16[784,128]{1,0:T(8,128)(2,1)S(1)}, bf16[784,128]{1,0:T(8,128)(2,1)S(1)}, u32[]{:S(2)}, u32[]{:S(2)}) collective-permute-start(bf16[784,128]{1,0:T(8,128)(2,1)S(1)} %get-tuple-element.63), channel_id=1, source_target_pairs={{0,252},{4,0},{8,4},{12,8},{16,12},{20,16},{24,20},{28,24},{32,28}... | collective-permute-start | bytes 602120 | tf_op jit(solution)/shard_map/ppermute | solution.py:55
  130.1 4.6 %collective-permute-start.20 = (bf16[784,128]{1,0:T(8,128)(2,1)S(1)}, bf16[784,128]{1,0:T(8,128)(2,1)S(1)}, u32[]{:S(2)}, u32[]{:S(2)}) collective-permute-start(bf16[784,128]{1,0:T(8,128)(2,1)S(1)} %get-tuple-element.65), channel_id=1, source_target_pairs={{0,4},{4,8},{8,12},{12,16},{16,20},{20,24},{24,28},{28,32},{32,36}... | collective-permute-start | bytes 602120 | tf_op jit(solution)/shard_map/ppermute | solution.py:55
  131.3 13.6 %collective-permute-start.21 = (bf16[784,128]{1,0:T(8,128)(2,1)S(1)}, bf16[784,128]{1,0:T(8,128)(2,1)S(1)}, u32[]{:S(2)}, u32[]{:S(2)}) collective-permute-start(bf16[784,128]{1,0:T(8,128)(2,1)S(1)} %get-tuple-element.66), channel_id=1, source_target_pairs={{0,8},{4,12},{8,16},{12,20},{16,24},{20,28},{24,32},{28,36},{32,40... | collective-permute-start | bytes 602120 | tf_op jit(solution)/shard_map/ppermute | solution.py:55
